TPU v7x, 512 devices: a whole 4x4x16 slice. The times are simulated.
512 devices in a mesh: gx: 8 (over y, core), gy: 4 (over x), gz: 16 (over z).
Axes of the slice: x: 4, y: 4, z: 16, core: 2. Of those that a mesh axis runs over, the one named last changes fastest.
Arguments:
- conc: float32 [128, 64, 2048], P('gx', 'gy', 'gz'), may hold values from 0 to 1
- right_side: float32 [128, 64, 2048], P('gx', 'gy', 'gz'), may hold values from -6144 to 6144
- order_field: bfloat16 [8, 128, 64, 2048], P(None, 'gx', 'gy', 'gz'), may hold values from 0 to 1
- grain_ids: int32 [8, 4, 128, 8], P('gx', 'gy', 'gz'), may hold values from 0 to 4095, as said below
Outputs:
- solution: float32 [128, 64, 2048], P('gx', 'gy', 'gz')
- mobility: float32 [128, 64, 2048], P('gx', 'gy', 'gz')
Inputs may be any that keep to these rules, and one draw needn't show every extreme that they name: `grain_ids`: the 8 ids of one block are distinct; neighbouring blocks share some grains, usually in other slots.
All inputs are finite; a program needn't handle non-finite values.
Results may differ from a plain program's by a relative error of at most 0.0019.
Values may be sent and summed in bfloat16 or wider, within the bound.
No kernel may reach another device: no remote copies, remote signals or barrier semaphores. Data moves between devices by JAX's collectives and lax.ppermute only.
A program may use at most 128 MiB of HBM per device.

v0:
```python
import jax
import jax.numpy as jnp
from jax import lax
from jax.sharding import PartitionSpec as P

SLOTS = 8
BRICK = 16
SMOOTH = 2
COARSE_SWEEPS = 8


OMEGA = 0.8
TAU_FINE = 256.0


def with_halo(cells, sides, width):
    for axis, dim in sides:
        count = lax.axis_size(axis)
        head = lax.slice_in_dim(cells, 0, width, axis=dim)
        tail = lax.slice_in_dim(cells, cells.shape[dim] - width, cells.shape[dim], axis=dim)
        cells = jnp.concatenate(
            [
                lax.ppermute(tail, axis, [(i, (i + 1) % count) for i in range(count)]),
                cells,
                lax.ppermute(head, axis, [((i + 1) % count, i) for i in range(count)]),
            ],
            axis=dim,
        )
    return cells


def neighbour_view(padded, lead, spatial, direction):
    index = [slice(None)] * lead
    for across in range(3):
        extent = padded.shape[lead + across]
        if across == spatial:
            index.append(slice(1 + direction, extent - 1 + direction))
        else:
            index.append(slice(1, extent - 1))
    return padded[tuple(index)]


def apply_operator(values, padded, coeffs, diag, step):
    summed = None
    for spatial in range(3):
        plus_cell = neighbour_view(padded, 0, spatial, 1)
        minus_cell = neighbour_view(padded, 0, spatial, -1)
        term = coeffs[2 * spatial] * plus_cell + coeffs[2 * spatial + 1] * minus_cell
        summed = term if summed is None else summed + term
    return diag * values - step * summed


def diagonal_of(coeffs, step):
    summed = coeffs[0]
    for coeff in coeffs[1:]:
        summed = summed + coeff
    return 1.0 + step * summed


def jacobi_sweep(values, source, coeffs, diag, step, faces):
    if values is None:
        return OMEGA * source / diag
    padded = faces(values)
    return values + OMEGA * (source - apply_operator(values, padded, coeffs, diag, step)) / diag


def residual_of(values, source, coeffs, diag, step, faces):
    return source - apply_operator(values, faces(values), coeffs, diag, step)


def restrict_field(field):
    extent = field.shape
    grouped = field.reshape(extent[0] // 2, 2, extent[1] // 2, 2, extent[2] // 2, 2)
    return jnp.mean(grouped, axis=(1, 3, 5))


def restrict_coeffs(coeffs):
    result = []
    for position, coeff in enumerate(coeffs):
        spatial = position // 2
        pick = 1 if position % 2 == 0 else 0
        extent = coeff.shape
        grouped = coeff.reshape(extent[0] // 2, 2, extent[1] // 2, 2, extent[2] // 2, 2)
        chosen = jnp.take(grouped, pick, axis=2 * spatial + 1)
        remaining = tuple(
            (
                pair_axis if pair_axis < 2 * spatial + 1 else pair_axis - 1
                for pair_axis in (1, 3, 5)
                if pair_axis != 2 * spatial + 1
            )
        )
        result.append(jnp.mean(chosen, axis=remaining))
    return tuple(result)


def prolong_field(field):
    return jnp.repeat(jnp.repeat(jnp.repeat(field, 2, axis=0), 2, axis=1), 2, axis=2)


def spread_faces(values):
    return with_halo(values, (("gx", 0), ("gy", 1), ("gz", 2)), 1)


def mobility_field(conc, order_field, grain_ids):
    ids_padded = with_halo(grain_ids, (("gx", 0), ("gy", 1), ("gz", 2)), 1)
    own_ids = ids_padded[1:-1, 1:-1, 1:-1]
    order_padded = with_halo(order_field, (("gx", 1), ("gy", 2), ("gz", 3)), 1)
    center = order_padded[:, 1:-1, 1:-1, 1:-1].astype(jnp.float32)
    summed = jnp.zeros(conc.shape, jnp.float32)
    for spatial in range(3):
        for direction in (1, -1):
            edge = BRICK - 1 if direction == 1 else 0
            beside_ids = neighbour_view(ids_padded, 0, spatial, direction)
            matches = (own_ids[..., :, None] == beside_ids[..., None, :]).astype(jnp.float32)
            for across in range(3):
                if across != spatial:
                    matches = jnp.repeat(matches, BRICK, axis=across)
            shifted = neighbour_view(order_padded, 1, spatial, direction).astype(jnp.float32)
            differ = shifted - center
            plain = jnp.sum(differ * differ, axis=0)
            extent = shifted.shape
            split = (
                extent[: spatial + 1]
                + (extent[spatial + 1] // BRICK, BRICK)
                + extent[spatial + 2 :]
            )
            boundary = jnp.take(shifted.reshape(split), edge, axis=spatial + 2)
            center_edge = jnp.take(center.reshape(split), edge, axis=spatial + 2)
            remapped = jnp.zeros(boundary.shape, jnp.float32)
            for other in range(SLOTS):
                remapped = (
                    remapped + jnp.moveaxis(matches[..., other], -1, 0) * boundary[other][None]
                )
            fixed = jnp.sum((remapped - center_edge) ** 2 - (boundary - center_edge) ** 2, axis=0)
            marker = (jnp.arange(BRICK) == edge).reshape((BRICK,) + (1,) * (2 - spatial))
            plain_split = plain.reshape(split[1:])
            plain = jnp.where(
                marker, plain_split + jnp.expand_dims(fixed, spatial + 1), plain_split
            ).reshape(conc.shape)
            summed = summed + plain
    return 1.0 + 8.0 * (conc * (1.0 - conc)) ** 2 + summed


def body(conc, right_side, order_field, grain_ids):
    mobility = mobility_field(conc, order_field, grain_ids)
    step_fine = TAU_FINE
    mobility_padded = with_halo(mobility, (("gx", 0), ("gy", 1), ("gz", 2)), 1)
    coeff_list = []
    for spatial in range(3):
        coeff_list.append(0.5 * (mobility + neighbour_view(mobility_padded, 0, spatial, 1)))
        coeff_list.append(0.5 * (mobility + neighbour_view(mobility_padded, 0, spatial, -1)))
    coeffs_fine = tuple(coeff_list)
    diag_fine = diagonal_of(coeffs_fine, step_fine)
    solution = conc
    for sweep_index in range(SMOOTH):
        solution = jacobi_sweep(
            solution, right_side, coeffs_fine, diag_fine, step_fine, spread_faces
        )
    fine_residual = residual_of(
        solution, right_side, coeffs_fine, diag_fine, step_fine, spread_faces
    )
    source_mid = restrict_field(fine_residual)
    coeffs_mid = restrict_coeffs(coeffs_fine)
    step_mid = TAU_FINE / 4.0
    diag_mid = diagonal_of(coeffs_mid, step_mid)
    error_mid = None
    for sweep_index in range(SMOOTH):
        error_mid = jacobi_sweep(
            error_mid, source_mid, coeffs_mid, diag_mid, step_mid, spread_faces
        )
    mid_residual = residual_of(error_mid, source_mid, coeffs_mid, diag_mid, step_mid, spread_faces)
    source_low = restrict_field(mid_residual)
    coeffs_low = restrict_coeffs(coeffs_mid)
    step_low = TAU_FINE / 16.0
    diag_low = diagonal_of(coeffs_low, step_low)
    error_low = None
    for sweep_index in range(COARSE_SWEEPS):
        error_low = jacobi_sweep(
            error_low, source_low, coeffs_low, diag_low, step_low, spread_faces
        )
    error_mid = error_mid + prolong_field(error_low)
    for sweep_index in range(SMOOTH):
        error_mid = jacobi_sweep(
            error_mid, source_mid, coeffs_mid, diag_mid, step_mid, spread_faces
        )
    solution = solution + prolong_field(error_mid)
    for sweep_index in range(SMOOTH):
        solution = jacobi_sweep(
            solution, right_side, coeffs_fine, diag_fine, step_fine, spread_faces
        )
    return (solution, mobility)


def solution(mesh):
    return jax.shard_map(
        body,
        mesh=mesh,
        in_specs=(
            P("gx", "gy", "gz"),
            P("gx", "gy", "gz"),
            P(None, "gx", "gy", "gz"),
            P("gx", "gy", "gz", None),
        ),
        out_specs=(P("gx", "gy", "gz"), P("gx", "gy", "gz")),
        check_vma=False,
    )
```

profile of v0, /device:TPU:32, one launch (start us, length us, event | category | flops | bytes accessed | tf_op | source)
XLA Modules:
  0.0 642.1 jit_solution(15381117889054198545)
XLA Ops:
  6.9 4.7 collective-permute-start.5
  18.4 3.8 collective-permute-start.11
  43.9 4.6 reshape.440
  51.6 3.2 collective-permute-start.6
  56.1 13.4 %fusion.387 = (f32[8,16,16,8,1]{4,3,2,0,1:T(8,128)}, f32[8,16,16,8,1]{4,3,2,0,1:T(8,128)}) fusion(f32[8,16,16,8,16]{4,3,2,0,1:T(8,128)} %reshape.440), kind=kLoop, calls=%fused_computation.970 | loop fusion | bytes 262144 | tf_op jit(solution)/shard_map/jit(_take) | solution.py:128
  73.5 8.6 %copy.367 = f32[8,16,16,8,1]{2,3,1,0,4:T(8,128)} copy(f32[8,16,16,8,1]{4,3,2,0,1:T(8,128)} %get-tuple-element.239) | data formatting | bytes 131072
  82.0 8.6 %copy.365 = f32[8,16,16,8,1]{2,3,1,0,4:T(8,128)} copy(f32[8,16,16,8,1]{4,3,2,0,1:T(8,128)} %get-tuple-element.240) | data formatting | bytes 131072
  93.9 7.3 %collective-permute-start.8 = (bf16[8,18,18,1]{2,0,3,1:T(8,128)(2,1)S(1)}, bf16[8,18,18,1]{2,0,3,1:T(8,128)(2,1)S(1)}, u32[]{:S(2)}, u32[]{:S(2)}) collective-permute-start(bf16[8,18,18,1]{2,0,3,1:T(8,128)(2,1)S(1)} %copy.325), channel_id=1, source_target_pairs={{1,0},{2,1},{3,2},{4,3},{5,4},{6,5},{7,6},{8,7},{9,8},{10,9},{11,1... | collective-permute-start | bytes 15560 | tf_op jit(solution)/shard_map/ppermute | solution.py:25
  111.4 4.2 fusion.11
  115.7 4.6 reshape.443
  120.3 7.9 %copy.366 = f32[8,16,16,8,1]{2,3,4,1,0:T(8,128)S(1)} copy(f32[8,16,16,8,1]{4,3,2,0,1:T(8,128)} %bitcast.634) | data formatting | bytes 131072
  129.7 4.6 reshape.425
  134.3 9.0 %slice.1912 = f32[8,16,16,8,1]{4,3,2,0,1:T(8,128)} slice(f32[8,16,16,8,16]{4,3,2,0,1:T(8,128)} %reshape.425), slice={[0:8], [0:16], [0:16], [0:8], [15:16]} | slice | bytes 131072 | tf_op jit(solution)/shard_map/jit(_take) | solution.py:127
  143.5 8.0 %copy.364 = f32[8,16,16,8,1]{2,3,4,1,0:T(8,128)S(1)} copy(f32[8,16,16,8,1]{4,3,2,0,1:T(8,128)} %slice.1912) | data formatting | bytes 131072
  154.7 4.2 collective-permute-start.20
  160.9 5.1 collective-permute-start.14
  168.1 4.7 collective-permute-start.22
  175.0 5.4 collective-permute-start.16
  184.8 5.7 collective-permute-done.17
  192.2 9.8 %reshape.462 = f32[8,2,8,2,64,2]{5,4,3,2,1,0:T(8,128)} reshape(f32[16,16,128]{2,1,0:T(8,128)S(1)} %get-tuple-element.234) | data formatting | bytes 262144 | tf_op jit(solution)/shard_map/reshape | solution.py:83
  204.8 9.8 %reshape.461 = f32[8,2,8,2,64,2]{5,4,3,2,1,0:T(8,128)} reshape(f32[16,16,128]{2,1,0:T(8,128)S(1)} %get-tuple-element.233) | data formatting | bytes 262144 | tf_op jit(solution)/shard_map/reshape | solution.py:83
  214.6 4.9 collective-permute-start.26
  224.2 9.8 %reshape.460 = f32[8,2,8,2,64,2]{5,4,3,2,1,0:T(8,128)} reshape(f32[16,16,128]{2,1,0:T(8,128)S(1)} %get-tuple-element.232) | data formatting | bytes 262144 | tf_op jit(solution)/shard_map/reshape | solution.py:83
  234.2 4.9 collective-permute-start.28
  243.8 9.8 %reshape.459 = f32[8,2,8,2,64,2]{5,4,3,2,1,0:T(8,128)} reshape(f32[16,16,128]{2,1,0:T(8,128)S(1)} %get-tuple-element.231) | data formatting | bytes 262144 | tf_op jit(solution)/shard_map/reshape | solution.py:83
  258.6 9.8 %reshape.463 = f32[8,2,8,2,64,2]{5,4,3,2,1,0:T(8,128)} reshape(f32[16,16,128]{2,1,0:T(8,128)S(1)} %get-tuple-element.235) | data formatting | bytes 262144 | tf_op jit(solution)/shard_map/reshape | solution.py:83
  268.4 9.0 %slice.1968 = f32[8,2,8,2,64,1]{5,4,3,2,1,0:T(8,128)} slice(f32[8,2,8,2,64,2]{5,4,3,2,1,0:T(8,128)} %reshape.463), slice={[0:8], [0:2], [0:8], [0:2], [0:64], [1:2]} | slice | bytes 131072 | tf_op jit(solution)/shard_map/jit(_take) | solution.py:84
  277.4 5.4 copy.353
  282.8 4.9 collective-permute-start.32
  289.6 9.8 %reshape.464 = f32[8,2,8,2,64,2]{5,4,3,2,1,0:T(8,128)} reshape(f32[16,16,128]{2,1,0:T(8,128)S(1)} %get-tuple-element.236) | data formatting | bytes 262144 | tf_op jit(solution)/shard_map/reshape | solution.py:83
  299.4 5.4 copy.354
  305.0 3.6 collective-permute-start.34
  314.1 3.4 collective-permute-done.35
  317.7 9.8 %reshape.458 = f32[8,2,8,2,64,2]{5,4,3,2,1,0:T(8,128)} reshape(f32[16,16,128]{2,1,0:T(8,128)S(1)} %fusion.92) | data formatting | bytes 262144 | tf_op jit(solution)/shard_map/reshape | solution.py:73
  327.5 4.0 reduce_sum.246
  338.2 5.3 collective-permute-start.38
  347.0 3.3 collective-permute-done.39
  350.4 4.1 collective-permute-start.40
  357.8 3.2 collective-permute-done.41
  367.3 3.9 collective-permute-start.45
  380.4 3.1 collective-permute-done.47
  391.2 3.9 collective-permute-start.51
  398.0 3.9 collective-permute-start.52
  403.8 3.8 collective-permute-done.53
  414.1 3.7 collective-permute-start.57
  420.9 4.1 collective-permute-start.58
  427.0 3.8 collective-permute-done.59
  441.0 3.6 collective-permute-done.63
  444.7 3.9 collective-permute-start.64
  450.5 3.8 collective-permute-done.65
  460.6 3.9 collective-permute-start.69
  482.6 3.9 collective-permute-start.75
  504.8 3.7 collective-permute-start.81
  511.6 3.9 collective-permute-start.82
  517.4 3.8 collective-permute-done.83
  531.4 3.6 collective-permute-done.87
  535.1 3.9 collective-permute-start.88
  541.1 3.6 collective-permute-done.89
  551.4 3.9 collective-permute-start.93
  564.6 3.1 collective-permute-done.95
  574.1 3.9 collective-permute-start.99
  587.2 3.1 collective-permute-done.101
  597.9 3.7 collective-permute-start.105
  626.2 3.6 collective-permute-done.111
  (472 shorter events, 298.1 us)
Async XLA Ops:
  0.7 6.2 collective-permute-start.1
  4.4 44.1 %collective-permute-start = (bf16[8,1,16,128]{3,2,0,1:T(8,128)(2,1)S(1)}, bf16[8,1,16,128]{3,2,0,1:T(8,128)(2,1)S(1)}, u32[]{:S(2)}, u32[]{:S(2)}) collective-permute-start(bf16[8,1,16,128]{3,2,0,1:T(8,128)(2,1)S(1)} %get-tuple-element.271), channel_id=1, source_target_pairs={{64,0},{128,64},{192,128},{256,192},{320,256},{384,320},{448,384},... | collective-permute-start | bytes 98312 | tf_op jit(solution)/shard_map/ppermute | solution.py:25
  4.6 37.0 %collective-permute-start.2 = (bf16[8,1,16,128]{3,2,0,1:T(8,128)(2,1)S(1)}, bf16[8,1,16,128]{3,2,0,1:T(8,128)(2,1)S(1)}, u32[]{:S(2)}, u32[]{:S(2)}) collective-permute-start(bf16[8,1,16,128]{3,2,0,1:T(8,128)(2,1)S(1)} %get-tuple-element.272), channel_id=1, source_target_pairs={{0,64},{64,128},{128,192},{192,256},{256,320},{320,384},{384,448},... | collective-permute-start | bytes 98312 | tf_op jit(solution)/shard_map/ppermute | solution.py:23
  6.2 35.3 %collective-permute-start.19 = (f32[1,16,128]{2,1,0:T(8,128)S(1)}, f32[1,16,128]{2,1,0:T(8,128)S(1)}, u32[]{:S(2)}, u32[]{:S(2)}) collective-permute-start(f32[1,16,128]{2,1,0:T(8,128)S(1)} %get-tuple-element.310), channel_id=1, source_target_pairs={{0,64},{64,128},{128,192},{192,256},{256,320},{320,384},{384,448},... | collective-permute-start | bytes 24584 | tf_op jit(solution)/shard_map/ppermute | solution.py:23
  6.9 9.0 %collective-permute-start.5 = (s32[3,1,8,8]{3,2,1,0:T(8,128)S(1)}, s32[3,1,8,8]{3,2,1,0:T(8,128)S(1)}, u32[]{:S(2)}, u32[]{:S(2)}) collective-permute-start(s32[3,1,8,8]{3,2,1,0:T(8,128)S(1)} %constant_dynamic-update-slice_fusion.3), channel_id=1, source_target_pairs={{16,0},{32,16},{48,32},{0,48},{17,1},{33,17},{49,33},{1,49},{18,2}... | collective-permute-start | bytes 2312 | tf_op jit(solution)/shard_map/ppermute | solution.py:25
  11.6 6.8 %collective-permute-start.7 = (s32[3,1,8,8]{3,2,1,0:T(8,128)S(1)}, s32[3,1,8,8]{3,2,1,0:T(8,128)S(1)}, u32[]{:S(2)}, u32[]{:S(2)}) collective-permute-start(s32[3,1,8,8]{3,2,1,0:T(8,128)S(1)} %constant_dynamic-update-slice_fusion.3), channel_id=1, source_target_pairs={{0,16},{16,32},{32,48},{48,0},{1,17},{17,33},{33,49},{49,1},{2,18}... | collective-permute-start | bytes 2312 | tf_op jit(solution)/shard_map/ppermute | solution.py:23
  18.4 6.7 %collective-permute-start.11 = (s32[3,3,1,8]{3,2,1,0:T(1,128)S(1)}, s32[3,3,1,8]{3,2,1,0:T(1,128)S(1)}, u32[]{:S(2)}, u32[]{:S(2)}) collective-permute-start(s32[3,3,1,8]{3,2,1,0:T(1,128)S(1)} %get-tuple-element.361), channel_id=1, source_target_pairs={{0,1},{1,2},{2,3},{3,4},{4,5},{5,6},{6,7},{7,8},{8,9},{9,10},{10,1... | collective-permute-start | bytes 872 | tf_op jit(solution)/shard_map/ppermute | solution.py:23
  25.1 128.9 %collective-permute-start.18 = (f32[1,16,128]{2,1,0:T(8,128)}, f32[1,16,128]{2,1,0:T(8,128)}, u32[]{:S(2)}, u32[]{:S(2)}) collective-permute-start(f32[1,16,128]{2,1,0:T(8,128)} %get-tuple-element.309), channel_id=1, source_target_pairs={{64,0},{128,64},{192,128},{256,192},{320,256},{384,320},{448,384},... | collective-permute-start | bytes 24584 | tf_op jit(solution)/shard_map/ppermute | solution.py:25
  49.0 41.7 %collective-permute-start.4 = (bf16[8,18,1,128]{3,2,0,1:T(2,128)(2,1)S(1)}, bf16[8,18,1,128]{3,2,0,1:T(2,128)(2,1)S(1)}, u32[]{:S(2)}, u32[]{:S(2)}) collective-permute-start(bf16[8,18,1,128]{3,2,0,1:T(2,128)(2,1)S(1)} %get-tuple-element.250), channel_id=1, source_target_pairs={{16,0},{32,16},{48,32},{0,48},{17,1},{33,17},{49,33},{1,49},{18,2}... | collective-permute-start | bytes 110600 | tf_op jit(solution)/shard_map/ppermute | solution.py:25
  51.6 39.0 %collective-permute-start.6 = (bf16[8,18,1,128]{3,2,0,1:T(2,128)(2,1)S(1)}, bf16[8,18,1,128]{3,2,0,1:T(2,128)(2,1)S(1)}, u32[]{:S(2)}, u32[]{:S(2)}) collective-permute-start(bf16[8,18,1,128]{3,2,0,1:T(2,128)(2,1)S(1)} %get-tuple-element.249), channel_id=1, source_target_pairs={{0,16},{16,32},{32,48},{48,0},{1,17},{17,33},{33,49},{49,1},{2,18}... | collective-permute-start | bytes 110600 | tf_op jit(solution)/shard_map/ppermute | solution.py:23
  93.9 13.3 %collective-permute-start.8 = (bf16[8,18,18,1]{2,0,3,1:T(8,128)(2,1)S(1)}, bf16[8,18,18,1]{2,0,3,1:T(8,128)(2,1)S(1)}, u32[]{:S(2)}, u32[]{:S(2)}) collective-permute-start(bf16[8,18,18,1]{2,0,3,1:T(8,128)(2,1)S(1)} %copy.325), channel_id=1, source_target_pairs={{1,0},{2,1},{3,2},{4,3},{5,4},{6,5},{7,6},{8,7},{9,8},{10,9},{11,1... | collective-permute-start | bytes 15560 | tf_op jit(solution)/shard_map/ppermute | solution.py:25
  102.2 7.3 %collective-permute-start.10 = (bf16[8,18,18,1]{2,0,3,1:T(8,128)(2,1)S(1)}, bf16[8,18,18,1]{2,0,3,1:T(8,128)(2,1)S(1)}, u32[]{:S(2)}, u32[]{:S(2)}) collective-permute-start(bf16[8,18,18,1]{2,0,3,1:T(8,128)(2,1)S(1)} %copy.339), channel_id=1, source_target_pairs={{0,1},{1,2},{2,3},{3,4},{4,5},{5,6},{6,7},{7,8},{8,9},{9,10},{10,1... | collective-permute-start | bytes 15560 | tf_op jit(solution)/shard_map/ppermute | solution.py:23
  153.4 7.5 %collective-permute-start.12 = (f32[1,16,128]{2,1,0:T(8,128)S(1)}, f32[1,16,128]{2,1,0:T(8,128)S(1)}, u32[]{:S(2)}, u32[]{:S(2)}) collective-permute-start(f32[1,16,128]{2,1,0:T(8,128)S(1)} %get-tuple-element.306), channel_id=1, source_target_pairs={{64,0},{128,64},{192,128},{256,192},{320,256},{384,320},{448,384},... | collective-permute-start | bytes 24584 | tf_op jit(solution)/shard_map/ppermute | solution.py:25
  154.0 6.8 %collective-permute-start.13 = (f32[1,16,128]{2,1,0:T(8,128)S(1)}, f32[1,16,128]{2,1,0:T(8,128)S(1)}, u32[]{:S(2)}, u32[]{:S(2)}) collective-permute-start(f32[1,16,128]{2,1,0:T(8,128)S(1)} %get-tuple-element.305), channel_id=1, source_target_pairs={{0,64},{64,128},{128,192},{192,256},{256,320},{320,384},{384,448},... | collective-permute-start | bytes 24584 | tf_op jit(solution)/shard_map/ppermute | solution.py:23
  154.7 13.2 %collective-permute-start.20 = (f32[18,1,128]{2,1,0:T(1,128)S(1)}, f32[18,1,128]{2,1,0:T(1,128)S(1)}, u32[]{:S(2)}, u32[]{:S(2)}) collective-permute-start(f32[18,1,128]{2,1,0:T(1,128)S(1)} %get-tuple-element.296), channel_id=1, source_target_pairs={{16,0},{32,16},{48,32},{0,48},{17,1},{33,17},{49,33},{1,49},{18,2}... | collective-permute-start | bytes 27656 | tf_op jit(solution)/shard_map/ppermute | solution.py:25
  158.9 9.1 %collective-permute-start.21 = (f32[18,1,128]{2,1,0:T(1,128)S(1)}, f32[18,1,128]{2,1,0:T(1,128)S(1)}, u32[]{:S(2)}, u32[]{:S(2)}) collective-permute-start(f32[18,1,128]{2,1,0:T(1,128)S(1)} %get-tuple-element.295), channel_id=1, source_target_pairs={{0,16},{16,32},{32,48},{48,0},{1,17},{17,33},{33,49},{49,1},{2,18}... | collective-permute-start | bytes 27656 | tf_op jit(solution)/shard_map/ppermute | solution.py:23
  160.9 13.9 %collective-permute-start.14 = (f32[18,1,128]{2,1,0:T(1,128)S(1)}, f32[18,1,128]{2,1,0:T(1,128)S(1)}, u32[]{:S(2)}, u32[]{:S(2)}) collective-permute-start(f32[18,1,128]{2,1,0:T(1,128)S(1)} %get-tuple-element.294), channel_id=1, source_target_pairs={{16,0},{32,16},{48,32},{0,48},{17,1},{33,17},{49,33},{1,49},{18,2}... | collective-permute-start | bytes 27656 | tf_op jit(solution)/shard_map/ppermute | solution.py:25
  166.0 8.8 %collective-permute-start.15 = (f32[18,1,128]{2,1,0:T(1,128)S(1)}, f32[18,1,128]{2,1,0:T(1,128)S(1)}, u32[]{:S(2)}, u32[]{:S(2)}) collective-permute-start(f32[18,1,128]{2,1,0:T(1,128)S(1)} %get-tuple-element.293), channel_id=1, source_target_pairs={{0,16},{16,32},{32,48},{48,0},{1,17},{17,33},{33,49},{49,1},{2,18}... | collective-permute-start | bytes 27656 | tf_op jit(solution)/shard_map/ppermute | solution.py:23
  168.1 14.1 %collective-permute-start.22 = (f32[18,18,1]{2,1,0:T(8,128)S(1)}, f32[18,18,1]{2,1,0:T(8,128)S(1)}, u32[]{:S(2)}, u32[]{:S(2)}) collective-permute-start(f32[18,18,1]{2,1,0:T(8,128)S(1)} %get-tuple-element.283), channel_id=1, source_target_pairs={{1,0},{2,1},{3,2},{4,3},{5,4},{6,5},{7,6},{8,7},{9,8},{10,9},{11,1... | collective-permute-start | bytes 3896 | tf_op jit(solution)/shard_map/ppermute | solution.py:25
  172.9 10.6 %collective-permute-start.23 = (f32[18,18,1]{2,1,0:T(8,128)S(1)}, f32[18,18,1]{2,1,0:T(8,128)S(1)}, u32[]{:S(2)}, u32[]{:S(2)}) collective-permute-start(f32[18,18,1]{2,1,0:T(8,128)S(1)} %get-tuple-element.284), channel_id=1, source_target_pairs={{0,1},{1,2},{2,3},{3,4},{4,5},{5,6},{6,7},{7,8},{8,9},{9,10},{10,1... | collective-permute-start | bytes 3896 | tf_op jit(solution)/shard_map/ppermute | solution.py:23
  175.0 9.9 %collective-permute-start.16 = (f32[18,18,1]{2,1,0:T(8,128)S(1)}, f32[18,18,1]{2,1,0:T(8,128)S(1)}, u32[]{:S(2)}, u32[]{:S(2)}) collective-permute-start(f32[18,18,1]{2,1,0:T(8,128)S(1)} %get-tuple-element.282), channel_id=1, source_target_pairs={{1,0},{2,1},{3,2},{4,3},{5,4},{6,5},{7,6},{8,7},{9,8},{10,9},{11,1... | collective-permute-start | bytes 3896 | tf_op jit(solution)/shard_map/ppermute | solution.py:25
  180.3 10.2 %collective-permute-start.17 = (f32[18,18,1]{2,1,0:T(8,128)S(1)}, f32[18,18,1]{2,1,0:T(8,128)S(1)}, u32[]{:S(2)}, u32[]{:S(2)}) collective-permute-start(f32[18,18,1]{2,1,0:T(8,128)S(1)} %get-tuple-element.281), channel_id=1, source_target_pairs={{0,1},{1,2},{2,3},{3,4},{4,5},{5,6},{6,7},{7,8},{8,9},{9,10},{10,1... | collective-permute-start | bytes 3896 | tf_op jit(solution)/shard_map/ppermute | solution.py:23
  191.7 22.9 %collective-permute-start.24 = (f32[1,16,128]{2,1,0:T(8,128)S(1)}, f32[1,16,128]{2,1,0:T(8,128)S(1)}, u32[]{:S(2)}, u32[]{:S(2)}) collective-permute-start(f32[1,16,128]{2,1,0:T(8,128)S(1)} %get-tuple-element.304), channel_id=1, source_target_pairs={{64,0},{128,64},{192,128},{256,192},{320,256},{384,320},{448,384},... | collective-permute-start | bytes 24584 | tf_op jit(solution)/shard_map/ppermute | solution.py:25
  191.7 22.9 %collective-permute-start.25 = (f32[1,16,128]{2,1,0:T(8,128)S(1)}, f32[1,16,128]{2,1,0:T(8,128)S(1)}, u32[]{:S(2)}, u32[]{:S(2)}) collective-permute-start(f32[1,16,128]{2,1,0:T(8,128)S(1)} %get-tuple-element.303), channel_id=1, source_target_pairs={{0,64},{64,128},{128,192},{192,256},{256,320},{320,384},{384,448},... | collective-permute-start | bytes 24584 | tf_op jit(solution)/shard_map/ppermute | solution.py:23
  214.6 19.4 %collective-permute-start.26 = (f32[18,1,128]{2,1,0:T(1,128)S(1)}, f32[18,1,128]{2,1,0:T(1,128)S(1)}, u32[]{:S(2)}, u32[]{:S(2)}) collective-permute-start(f32[18,1,128]{2,1,0:T(1,128)S(1)} %get-tuple-element.292), channel_id=1, source_target_pairs={{16,0},{32,16},{48,32},{0,48},{17,1},{33,17},{49,33},{1,49},{18,2}... | collective-permute-start | bytes 27656 | tf_op jit(solution)/shard_map/ppermute | solution.py:25
  219.5 14.5 %collective-permute-start.27 = (f32[18,1,128]{2,1,0:T(1,128)S(1)}, f32[18,1,128]{2,1,0:T(1,128)S(1)}, u32[]{:S(2)}, u32[]{:S(2)}) collective-permute-start(f32[18,1,128]{2,1,0:T(1,128)S(1)} %get-tuple-element.291), channel_id=1, source_target_pairs={{0,16},{16,32},{32,48},{48,0},{1,17},{17,33},{33,49},{49,1},{2,18}... | collective-permute-start | bytes 27656 | tf_op jit(solution)/shard_map/ppermute | solution.py:23
  234.2 19.4 %collective-permute-start.28 = (f32[18,18,1]{2,1,0:T(8,128)S(1)}, f32[18,18,1]{2,1,0:T(8,128)S(1)}, u32[]{:S(2)}, u32[]{:S(2)}) collective-permute-start(f32[18,18,1]{2,1,0:T(8,128)S(1)} %get-tuple-element.279), channel_id=1, source_target_pairs={{1,0},{2,1},{3,2},{4,3},{5,4},{6,5},{7,6},{8,7},{9,8},{10,9},{11,1... | collective-permute-start | bytes 3896 | tf_op jit(solution)/shard_map/ppermute | solution.py:25
  239.1 14.5 %collective-permute-start.29 = (f32[18,18,1]{2,1,0:T(8,128)S(1)}, f32[18,18,1]{2,1,0:T(8,128)S(1)}, u32[]{:S(2)}, u32[]{:S(2)}) collective-permute-start(f32[18,18,1]{2,1,0:T(8,128)S(1)} %get-tuple-element.280), channel_id=1, source_target_pairs={{0,1},{1,2},{2,3},{3,4},{4,5},{5,6},{6,7},{7,8},{8,9},{9,10},{10,1... | collective-permute-start | bytes 3896 | tf_op jit(solution)/shard_map/ppermute | solution.py:23
  253.9 28.9 %collective-permute-start.30 = (f32[1,16,128]{2,1,0:T(8,128)S(1)}, f32[1,16,128]{2,1,0:T(8,128)S(1)}, u32[]{:S(2)}, u32[]{:S(2)}) collective-permute-start(f32[1,16,128]{2,1,0:T(8,128)S(1)} %get-tuple-element.302), channel_id=1, source_target_pairs={{64,0},{128,64},{192,128},{256,192},{320,256},{384,320},{448,384},... | collective-permute-start | bytes 24584 | tf_op jit(solution)/shard_map/ppermute | solution.py:25
  255.8 27.0 %collective-permute-start.31 = (f32[1,16,128]{2,1,0:T(8,128)S(1)}, f32[1,16,128]{2,1,0:T(8,128)S(1)}, u32[]{:S(2)}, u32[]{:S(2)}) collective-permute-start(f32[1,16,128]{2,1,0:T(8,128)S(1)} %get-tuple-element.301), channel_id=1, source_target_pairs={{0,64},{64,128},{128,192},{192,256},{256,320},{320,384},{384,448},... | collective-permute-start | bytes 24584 | tf_op jit(solution)/shard_map/ppermute | solution.py:23
  282.8 22.0 %collective-permute-start.32 = (f32[18,1,128]{2,1,0:T(1,128)S(1)}, f32[18,1,128]{2,1,0:T(1,128)S(1)}, u32[]{:S(2)}, u32[]{:S(2)}) collective-permute-start(f32[18,1,128]{2,1,0:T(1,128)S(1)} %get-tuple-element.290), channel_id=1, source_target_pairs={{16,0},{32,16},{48,32},{0,48},{17,1},{33,17},{49,33},{1,49},{18,2}... | collective-permute-start | bytes 27656 | tf_op jit(solution)/shard_map/ppermute | solution.py:25
  287.7 17.1 %collective-permute-start.33 = (f32[18,1,128]{2,1,0:T(1,128)S(1)}, f32[18,1,128]{2,1,0:T(1,128)S(1)}, u32[]{:S(2)}, u32[]{:S(2)}) collective-permute-start(f32[18,1,128]{2,1,0:T(1,128)S(1)} %get-tuple-element.289), channel_id=1, source_target_pairs={{0,16},{16,32},{32,48},{48,0},{1,17},{17,33},{33,49},{49,1},{2,18}... | collective-permute-start | bytes 27656 | tf_op jit(solution)/shard_map/ppermute | solution.py:23
  305.0 9.1 %collective-permute-start.34 = (f32[18,18,1]{2,1,0:T(8,128)S(1)}, f32[18,18,1]{2,1,0:T(8,128)S(1)}, u32[]{:S(2)}, u32[]{:S(2)}) collective-permute-start(f32[18,18,1]{2,1,0:T(8,128)S(1)} %get-tuple-element.277), channel_id=1, source_target_pairs={{1,0},{2,1},{3,2},{4,3},{5,4},{6,5},{7,6},{8,7},{9,8},{10,9},{11,1... | collective-permute-start | bytes 3896 | tf_op jit(solution)/shard_map/ppermute | solution.py:25
  308.6 8.9 %collective-permute-start.35 = (f32[18,18,1]{2,1,0:T(8,128)S(1)}, f32[18,18,1]{2,1,0:T(8,128)S(1)}, u32[]{:S(2)}, u32[]{:S(2)}) collective-permute-start(f32[18,18,1]{2,1,0:T(8,128)S(1)} %get-tuple-element.278), channel_id=1, source_target_pairs={{0,1},{1,2},{2,3},{3,4},{4,5},{5,6},{6,7},{7,8},{8,9},{9,10},{10,1... | collective-permute-start | bytes 3896 | tf_op jit(solution)/shard_map/ppermute | solution.py:23
  338.2 8.8 %collective-permute-start.38 = (f32[10,1,64]{2,1,0:T(1,128)S(1)}, f32[10,1,64]{2,1,0:T(1,128)S(1)}, u32[]{:S(2)}, u32[]{:S(2)}) collective-permute-start(f32[10,1,64]{2,1,0:T(1,128)S(1)} %get-tuple-element.358), channel_id=1, source_target_pairs={{16,0},{32,16},{48,32},{0,48},{17,1},{33,17},{49,33},{1,49},{18,2}... | collective-permute-start | bytes 7688 | tf_op jit(solution)/shard_map/ppermute | solution.py:25
  343.6 6.7 %collective-permute-start.39 = (f32[10,1,64]{2,1,0:T(1,128)S(1)}, f32[10,1,64]{2,1,0:T(1,128)S(1)}, u32[]{:S(2)}, u32[]{:S(2)}) collective-permute-start(f32[10,1,64]{2,1,0:T(1,128)S(1)} %get-tuple-element.357), channel_id=1, source_target_pairs={{0,16},{16,32},{32,48},{48,0},{1,17},{17,33},{33,49},{49,1},{2,18}... | collective-permute-start | bytes 7688 | tf_op jit(solution)/shard_map/ppermute | solution.py:23
  350.4 7.3 %collective-permute-start.40 = (f32[10,10,1]{2,1,0:T(8,128)S(1)}, f32[10,10,1]{2,1,0:T(8,128)S(1)}, u32[]{:S(2)}, u32[]{:S(2)}) collective-permute-start(f32[10,10,1]{2,1,0:T(8,128)S(1)} %get-tuple-element.317), channel_id=1, source_target_pairs={{1,0},{2,1},{3,2},{4,3},{5,4},{6,5},{7,6},{8,7},{9,8},{10,9},{11,1... | collective-permute-start | bytes 1208 | tf_op jit(solution)/shard_map/ppermute | solution.py:25
  354.6 6.3 collective-permute-start.41
  365.3 7.1 %collective-permute-start.44 = (f32[10,1,64]{2,1,0:T(1,128)S(1)}, f32[10,1,64]{2,1,0:T(1,128)S(1)}, u32[]{:S(2)}, u32[]{:S(2)}) collective-permute-start(f32[10,1,64]{2,1,0:T(1,128)S(1)} %get-tuple-element.356), channel_id=1, source_target_pairs={{16,0},{32,16},{48,32},{0,48},{17,1},{33,17},{49,33},{1,49},{18,2}... | collective-permute-start | bytes 7688 | tf_op jit(solution)/shard_map/ppermute | solution.py:25
  367.3 6.7 %collective-permute-start.45 = (f32[10,1,64]{2,1,0:T(1,128)S(1)}, f32[10,1,64]{2,1,0:T(1,128)S(1)}, u32[]{:S(2)}, u32[]{:S(2)}) collective-permute-start(f32[10,1,64]{2,1,0:T(1,128)S(1)} %get-tuple-element.355), channel_id=1, source_target_pairs={{0,16},{16,32},{32,48},{48,0},{1,17},{17,33},{33,49},{49,1},{2,18}... | collective-permute-start | bytes 7688 | tf_op jit(solution)/shard_map/ppermute | solution.py:23
  374.1 6.3 collective-permute-start.46
  377.3 6.3 collective-permute-start.47
  389.3 5.9 collective-permute-start.50
  391.2 6.7 %collective-permute-start.51 = (f32[6,1,32]{2,1,0:T(1,128)S(1)}, f32[6,1,32]{2,1,0:T(1,128)S(1)}, u32[]{:S(2)}, u32[]{:S(2)}) collective-permute-start(f32[6,1,32]{2,1,0:T(1,128)S(1)} %get-tuple-element.452), channel_id=1, source_target_pairs={{0,16},{16,32},{32,48},{48,0},{1,17},{17,33},{33,49},{49,1},{2,18}... | collective-permute-start | bytes 2312 | tf_op jit(solution)/shard_map/ppermute | solution.py:23
  414.1 6.7 %collective-permute-start.57 = (f32[6,1,32]{2,1,0:T(1,128)S(1)}, f32[6,1,32]{2,1,0:T(1,128)S(1)}, u32[]{:S(2)}, u32[]{:S(2)}) collective-permute-start(f32[6,1,32]{2,1,0:T(1,128)S(1)} %get-tuple-element.450), channel_id=1, source_target_pairs={{0,16},{16,32},{32,48},{48,0},{1,17},{17,33},{33,49},{49,1},{2,18}... | collective-permute-start | bytes 2312 | tf_op jit(solution)/shard_map/ppermute | solution.py:23
  420.9 6.1 collective-permute-start.58
  437.9 6.7 %collective-permute-start.63 = (f32[6,1,32]{2,1,0:T(1,128)S(1)}, f32[6,1,32]{2,1,0:T(1,128)S(1)}, u32[]{:S(2)}, u32[]{:S(2)}) collective-permute-start(f32[6,1,32]{2,1,0:T(1,128)S(1)} %get-tuple-element.448), channel_id=1, source_target_pairs={{0,16},{16,32},{32,48},{48,0},{1,17},{17,33},{33,49},{49,1},{2,18}... | collective-permute-start | bytes 2312 | tf_op jit(solution)/shard_map/ppermute | solution.py:23
  460.6 6.7 %collective-permute-start.69 = (f32[6,1,32]{2,1,0:T(1,128)S(1)}, f32[6,1,32]{2,1,0:T(1,128)S(1)}, u32[]{:S(2)}, u32[]{:S(2)}) collective-permute-start(f32[6,1,32]{2,1,0:T(1,128)S(1)} %get-tuple-element.446), channel_id=1, source_target_pairs={{0,16},{16,32},{32,48},{48,0},{1,17},{17,33},{33,49},{49,1},{2,18}... | collective-permute-start | bytes 2312 | tf_op jit(solution)/shard_map/ppermute | solution.py:23
  482.6 6.7 %collective-permute-start.75 = (f32[6,1,32]{2,1,0:T(1,128)S(1)}, f32[6,1,32]{2,1,0:T(1,128)S(1)}, u32[]{:S(2)}, u32[]{:S(2)}) collective-permute-start(f32[6,1,32]{2,1,0:T(1,128)S(1)} %get-tuple-element.444), channel_id=1, source_target_pairs={{0,16},{16,32},{32,48},{48,0},{1,17},{17,33},{33,49},{49,1},{2,18}... | collective-permute-start | bytes 2312 | tf_op jit(solution)/shard_map/ppermute | solution.py:23
  504.8 6.7 %collective-permute-start.81 = (f32[6,1,32]{2,1,0:T(1,128)S(1)}, f32[6,1,32]{2,1,0:T(1,128)S(1)}, u32[]{:S(2)}, u32[]{:S(2)}) collective-permute-start(f32[6,1,32]{2,1,0:T(1,128)S(1)} %get-tuple-element.442), channel_id=1, source_target_pairs={{0,16},{16,32},{32,48},{48,0},{1,17},{17,33},{33,49},{49,1},{2,18}... | collective-permute-start | bytes 2312 | tf_op jit(solution)/shard_map/ppermute | solution.py:23
  528.3 6.7 %collective-permute-start.87 = (f32[6,1,32]{2,1,0:T(1,128)S(1)}, f32[6,1,32]{2,1,0:T(1,128)S(1)}, u32[]{:S(2)}, u32[]{:S(2)}) collective-permute-start(f32[6,1,32]{2,1,0:T(1,128)S(1)} %get-tuple-element.440), channel_id=1, source_target_pairs={{0,16},{16,32},{32,48},{48,0},{1,17},{17,33},{33,49},{49,1},{2,18}... | collective-permute-start | bytes 2312 | tf_op jit(solution)/shard_map/ppermute | solution.py:23
  535.1 6.1 collective-permute-start.88
  551.4 6.7 %collective-permute-start.93 = (f32[10,1,64]{2,1,0:T(1,128)S(1)}, f32[10,1,64]{2,1,0:T(1,128)S(1)}, u32[]{:S(2)}, u32[]{:S(2)}) collective-permute-start(f32[10,1,64]{2,1,0:T(1,128)S(1)} %get-tuple-element.353), channel_id=1, source_target_pairs={{0,16},{16,32},{32,48},{48,0},{1,17},{17,33},{33,49},{49,1},{2,18}... | collective-permute-start | bytes 7688 | tf_op jit(solution)/shard_map/ppermute | solution.py:23
  558.2 6.3 collective-permute-start.94
  561.4 6.3 collective-permute-start.95
  574.1 6.7 %collective-permute-start.99 = (f32[10,1,64]{2,1,0:T(1,128)S(1)}, f32[10,1,64]{2,1,0:T(1,128)S(1)}, u32[]{:S(2)}, u32[]{:S(2)}) collective-permute-start(f32[10,1,64]{2,1,0:T(1,128)S(1)} %get-tuple-element.351), channel_id=1, source_target_pairs={{0,16},{16,32},{32,48},{48,0},{1,17},{17,33},{33,49},{49,1},{2,18}... | collective-permute-start | bytes 7688 | tf_op jit(solution)/shard_map/ppermute | solution.py:23
  580.9 6.3 collective-permute-start.100
  584.0 6.3 collective-permute-start.101
  597.9 6.8 %collective-permute-start.105 = (f32[18,1,128]{2,1,0:T(1,128)S(1)}, f32[18,1,128]{2,1,0:T(1,128)S(1)}, u32[]{:S(2)}, u32[]{:S(2)}) collective-permute-start(f32[18,1,128]{2,1,0:T(1,128)S(1)} %get-tuple-element.287), channel_id=1, source_target_pairs={{0,16},{16,32},{32,48},{48,0},{1,17},{17,33},{33,49},{49,1},{2,18}... | collective-permute-start | bytes 27656 | tf_op jit(solution)/shard_map/ppermute | solution.py:23
  604.8 7.8 %collective-permute-start.106 = (f32[18,18,1]{2,1,0:T(8,128)S(1)}, f32[18,18,1]{2,1,0:T(8,128)S(1)}, u32[]{:S(2)}, u32[]{:S(2)}) collective-permute-start(f32[18,18,1]{2,1,0:T(8,128)S(1)} %get-tuple-element.275), channel_id=1, source_target_pairs={{1,0},{2,1},{3,2},{4,3},{5,4},{6,5},{7,6},{8,7},{9,8},{10,9},{11,1... | collective-permute-start | bytes 3896 | tf_op jit(solution)/shard_map/ppermute | solution.py:25
  607.9 7.8 %collective-permute-start.107 = (f32[18,18,1]{2,1,0:T(8,128)S(1)}, f32[18,18,1]{2,1,0:T(8,128)S(1)}, u32[]{:S(2)}, u32[]{:S(2)}) collective-permute-start(f32[18,18,1]{2,1,0:T(8,128)S(1)} %get-tuple-element.276), channel_id=1, source_target_pairs={{0,1},{1,2},{2,3},{3,4},{4,5},{5,6},{6,7},{7,8},{8,9},{9,10},{10,1... | collective-permute-start | bytes 3896 | tf_op jit(solution)/shard_map/ppermute | solution.py:23
  623.1 6.8 %collective-permute-start.111 = (f32[18,1,128]{2,1,0:T(1,128)S(1)}, f32[18,1,128]{2,1,0:T(1,128)S(1)}, u32[]{:S(2)}, u32[]{:S(2)}) collective-permute-start(f32[18,1,128]{2,1,0:T(1,128)S(1)} %get-tuple-element.285), channel_id=1, source_target_pairs={{0,16},{16,32},{32,48},{48,0},{1,17},{17,33},{33,49},{49,1},{2,18}... | collective-permute-start | bytes 27656 | tf_op jit(solution)/shard_map/ppermute | solution.py:23
  630.0 7.8 %collective-permute-start.112 = (f32[18,18,1]{2,1,0:T(8,128)S(1)}, f32[18,18,1]{2,1,0:T(8,128)S(1)}, u32[]{:S(2)}, u32[]{:S(2)}) collective-permute-start(f32[18,18,1]{2,1,0:T(8,128)S(1)} %get-tuple-element.273), channel_id=1, source_target_pairs={{1,0},{2,1},{3,2},{4,3},{5,4},{6,5},{7,6},{8,7},{9,8},{10,9},{11,1... | collective-permute-start | bytes 3896 | tf_op jit(solution)/shard_map/ppermute | solution.py:25
  633.1 7.8 %collective-permute-start.113 = (f32[18,18,1]{2,1,0:T(8,128)S(1)}, f32[18,18,1]{2,1,0:T(8,128)S(1)}, u32[]{:S(2)}, u32[]{:S(2)}) collective-permute-start(f32[18,18,1]{2,1,0:T(8,128)S(1)} %get-tuple-element.274), channel_id=1, source_target_pairs={{0,1},{1,2},{2,3},{3,4},{4,5},{5,6},{6,7},{7,8},{8,9},{9,10},{10,1... | collective-permute-start | bytes 3896 | tf_op jit(solution)/shard_map/ppermute | solution.py:23
  (87 other events, 663.6 us)
where the time goes:
time: 652 us; the launch traced here: 642 us
  starting transfers between devices  252 us (39%)
  local copies, waits for them, and re-layouts  199 us (31%)
  waiting for transfers between devices  151 us (23%)
  other arithmetic  36.6 us (6%)
    ppermute x57, starting transfers between devices, with_halo(): lax.ppermute(head, axis, [((i + 1) % count, i) for i in range(count)])  142 us
    ppermute x57, waiting for transfers between devices, with_halo(): lax.ppermute(tail, axis, [(i, (i + 1) % count) for i in range(count)])  131 us
    ppermute x57, starting transfers between devices, with_halo(): lax.ppermute(tail, axis, [(i, (i + 1) % count) for i in range(count)])  110 us
    reshape x6, local copies, waits for them, and re-layouts, restrict_coeffs(): coeff.reshape(extent[0] // 2, 2, extent[1] // 2, 2, extent[2] // 2, 2)  58.7 us
    unnamed x83, local copies, waits for them, and re-layouts  35 us
    another operation x5, local copies, waits for them, and re-layouts, restrict_coeffs(): chosen = jnp.take(grouped, pick, axis=2 * spatial + 1)  20.9 us
    ppermute x57, waiting for transfers between devices, with_halo(): lax.ppermute(head, axis, [((i + 1) % count, i) for i in range(count)])  19.7 us
    another operation x2, local copies, waits for them, and re-layouts, mobility_field(): center_edge = jnp.take(center.reshape(split), edge, axis=spatial + 2)  14.7 us
  transfers between devices with their start and end apart: 114, of which 63 were waited for; matrix products, arithmetic and copies ran while one was open for 33% of the time, Pallas kernels for 0%

commit v1 on v0

v1 whole, which is shorter than its diff:
```python
import functools

import jax
import jax.numpy as jnp
from jax import lax
from jax.experimental import pallas as pl
from jax.experimental.pallas import tpu as pltpu
from jax.sharding import PartitionSpec as P

SLOTS = 8
BRICK = 16
OMEGA = 0.8
TAU = 256.0
LANES = 128
RING = 256
F32 = jnp.float32
BF16 = jnp.bfloat16
HIGH = lax.Precision.HIGHEST
VMEM = pl.BlockSpec(memory_space=pltpu.VMEM)
SMEM = pl.BlockSpec(memory_space=pltpu.SMEM)
COARSE = 51
COARSE_LOW = 10
MIDDLE = 70
MIDDLE_LOW = 3


def call(kernel, outs, args, scratch=(), specs=None):
    return pl.pallas_call(
        kernel,
        out_shape=[jax.ShapeDtypeStruct(shape, dtype) for shape, dtype in outs],
        in_specs=specs or [VMEM] * len(args),
        out_specs=[VMEM] * len(outs),
        scratch_shapes=[pltpu.VMEM(shape, dtype) for shape, dtype in scratch],
        compiler_params=pltpu.CompilerParams(vmem_limit_bytes=48 << 20),
    )(*args)


def roll(x, shift, axis):
    return pltpu.roll(x, shift % x.shape[axis], axis)


def iota(shape, axis):
    return lax.broadcasted_iota(jnp.int32, shape, axis)


def dot(a, b):
    return jnp.dot(a, b, precision=HIGH, preferred_element_type=F32)


def lane_ids(ids_ref):
    ids = ids_ref[0, 0].astype(F32)
    spread = (iota((8, LANES), 1) // BRICK == iota((8, LANES), 0)).astype(F32)
    grains = lax.dot_general(
        ids, spread, (((0,), (0,)), ((), ())), precision=HIGH, preferred_element_type=F32
    )
    return jnp.floor(grains + 0.5)


def split_ids(grains):
    high = jnp.floor(grains * (1.0 / 64.0))
    return jnp.concatenate([high, grains - 64.0 * high], axis=0).astype(BF16)


def join_ids(rows):
    rows = rows.astype(F32)
    return rows[:8] * 64.0 + rows[8:]


def faces_kernel(order_ref, ids_ref, xm_ref, xp_ref, ym_ref, yp_ref, zm_ref, zp_ref):
    grains = lane_ids(ids_ref)
    packed = split_ids(grains)
    for ref in (xm_ref, xp_ref, ym_ref, yp_ref):
        ref[SLOTS] = packed
    zm_ref[16] = split_ids(jnp.broadcast_to(grains[:, 0:1], (8, LANES)))
    zp_ref[16] = split_ids(jnp.broadcast_to(grains[:, LANES - 1 :], (8, LANES)))
    lane = iota((16, LANES), 1)
    low = [jnp.zeros((16, LANES), F32)] * 16
    high = [jnp.zeros((16, LANES), F32)] * 16
    for slot in range(SLOTS):
        cells = order_ref[slot].astype(F32)
        xm_ref[slot] = order_ref[slot, 0]
        xp_ref[slot] = order_ref[slot, 15]
        ym_ref[slot] = cells[:, 0, :].astype(BF16)
        yp_ref[slot] = cells[:, 15, :].astype(BF16)
        for x in range(16):
            low[x] = jnp.where(lane == slot, cells[x, :, 0:1], low[x])
            high[x] = jnp.where(lane == slot, cells[x, :, LANES - 1 :], high[x])
    for x in range(16):
        zm_ref[x] = low[x].astype(BF16)
        zp_ref[x] = high[x].astype(BF16)


def square(x):
    return x * x


def mobility_kernel(
    conc_ref, side_ref, order_ref, ids_ref, xm_ref, xp_ref, ym_ref, yp_ref, zm_ref, zp_ref,
    own_ym_ref, own_yp_ref, mob_ref, low_ref, high_ref, work, weights,
):
    own = lane_ids(ids_ref)
    lane = iota((16, LANES), 1)
    row = iota((16, LANES), 0)
    last = lane % BRICK == BRICK - 1
    edge = last | (lane % BRICK == 0)

    lane8 = iota((8, LANES), 1)
    after = jnp.where(
        lane8 >= LANES - BRICK, join_ids(zp_ref[16]), roll(own, -BRICK, 1)
    )
    before = jnp.where(lane8 < BRICK, join_ids(zm_ref[16]), roll(own, BRICK, 1))
    beside = jnp.where(lane8 % BRICK == BRICK - 1, after, before)
    for other in range(SLOTS):
        match = (own == beside[other : other + 1]).astype(F32)
        for slot in range(SLOTS):
            weights[slot * SLOTS + other] = jnp.broadcast_to(match[slot : slot + 1], (8, LANES))

    def across(face_ref, ids, center):
        facing = [face_ref[other].astype(F32) for other in range(SLOTS)]
        total = None
        for slot in range(SLOTS):
            value = None
            for other in range(SLOTS):
                match = (own[slot : slot + 1] == ids[other : other + 1]).astype(F32)
                term = match * facing[other]
                value = term if value is None else value + term
            part = square(value - center(slot))
            total = part if total is None else total + part
        return total

    def doubled(block):
        return jnp.concatenate([block, block], axis=0)

    def plane(x, below, carry_in):
        conc = conc_ref[x]
        base = 1.0 + 8.0 * square(conc * (1.0 - conc))
        zlow = zm_ref[x].astype(F32)
        zhigh = zp_ref[x].astype(F32)
        along_y = jnp.zeros((16, LANES), F32)
        along_z = jnp.zeros((16, LANES), F32)
        along_x = jnp.zeros((16, LANES), F32)
        centers = []
        facing = []
        above = jnp.minimum(x + 1, 15)
        for slot in range(SLOTS):
            here = order_ref[slot, x].astype(F32)
            there = order_ref[slot, above].astype(F32)
            centers.append(here)
            along_x = along_x + square(there - here)
            along_y = along_y + square(roll(here, -1, 0) - here)
            right = roll(here, -1, 1)
            along_z = along_z + square(right - here)
            right = jnp.where(lane == LANES - 1, zhigh[:, slot : slot + 1], right)
            left = jnp.where(lane == 0, zlow[:, slot : slot + 1], roll(here, 1, 1))
            facing.append(jnp.where(last, right, left))
        along_y = jnp.where(row == 15, 0.0, along_y)
        along_z = jnp.where(last, 0.0, along_z)
        remapped = jnp.zeros((16, LANES), F32)
        for slot in range(SLOTS):
            value = None
            for other in range(SLOTS):
                term = doubled(weights[slot * SLOTS + other]) * facing[other]
                value = term if value is None else value + term
            remapped = remapped + square(value - centers[slot])
        total = base + along_y + roll(along_y, 1, 0) + along_z + roll(along_z, 1, 1)
        total = total + jnp.where(edge, remapped, 0.0) + along_x + carry_in
        work[x] = total
        return along_x

    lax.fori_loop(0, 16, lambda x, c: plane(x, None, c), jnp.zeros((16, LANES), F32))
    work[0] = work[0] + across(
        xm_ref, join_ids(xm_ref[SLOTS]), lambda s: order_ref[s, 0].astype(F32)
    )
    work[15] = work[15] + across(
        xp_ref, join_ids(xp_ref[SLOTS]), lambda s: order_ref[s, 15].astype(F32)
    )
    bottom = across(ym_ref, join_ids(ym_ref[SLOTS]), lambda s: own_ym_ref[s].astype(F32))
    top = across(yp_ref, join_ids(yp_ref[SLOTS]), lambda s: own_yp_ref[s].astype(F32))
    for x in range(16):
        value = work[x]
        value = value + jnp.where(row == 0, bottom[x : x + 1], 0.0)
        value = value + jnp.where(row == 15, top[x : x + 1], 0.0)
        mob_ref[x] = value
        low_ref[0, x] = value[:8]
        high_ref[0, x] = value[8:]
        low_ref[1, x] = conc_ref[x, :8]
        high_ref[1, x] = conc_ref[x, 8:]
        low_ref[2, x] = side_ref[x, :8]
        high_ref[2, x] = side_ref[x, 8:]


def rows_kernel(below_ref, low_ref, high_ref, above_ref, xl_ref, xh_ref):
    for place, ref in enumerate((below_ref, low_ref, high_ref, above_ref)):
        rows = pl.ds(8 * place, 8)
        xl_ref[:, :, rows, :] = ref[:, :8]
        xh_ref[:, :, rows, :] = ref[:, 8:]


def lanes_kernel(xm_ref, xl_ref, xh_ref, xp_ref, zm_ref, zp_ref):
    lane = iota((32, LANES), 1)
    for place, ref in enumerate((xm_ref, xl_ref, xh_ref, xp_ref)):
        for x in range(8):
            mob, conc, side = ref[0, x], ref[1, x], ref[2, x]
            zm_ref[8 * place + x] = jnp.where(
                lane < 43, mob, jnp.where(lane < 86, roll(conc, 43, 1), roll(side, 86, 1))
            )
            zp_ref[8 * place + x] = jnp.where(
                lane >= 85, mob, jnp.where(lane >= 42, roll(conc, -43, 1), roll(side, -86, 1))
            )


def partner(x, step, axis):
    upper = (iota(x.shape, axis) & step) != 0
    return jnp.where(upper, roll(x, step, axis), roll(x, -step, axis))


def pair_sum(x, step, axis):
    return x + partner(x, step, axis)


def upper_of(x, step, axis):
    upper = (iota(x.shape, axis) & step) != 0
    return jnp.where(upper, x, roll(x, -step, axis))


def residual(value, source, flux_x, flux_x_before, ky, kz, step):
    flux_y = ky * (roll(value, -step, 0) - value)
    flux_z = kz * (roll(value, -step, 1) - value)
    total = (source - value) + (flux_x - flux_x_before)
    total = total + (flux_y - roll(flux_y, step, 0))
    return total + (flux_z - roll(flux_z, step, 1))


def sweep_planes(first, last, values, source, kx, ky, kz, step, use):
    before = kx[first - 1] * (values[first] - values[first - 1])

    def plane(x, flux_before):
        value = values[x]
        flux = kx[x] * (values[x + 1] - value)
        use(x, value, residual(value, source[x], flux, flux_before, ky[x], kz[x], step))
        return flux

    lax.fori_loop(first, last + 1, plane, before)


def down_kernel(
    xm_ref, xl_ref, xh_ref, xp_ref, zm_ref, zp_ref,
    v_ref, side_ref, kx_ref, ky_ref, kz_ref, wd_ref,
    f1_ref, k1x_ref, k1y_ref, k1z_ref, wd1_ref, chunk_ref,
    mob, v0, res, e0, e1, r1,
):
    lane = iota((32, LANES), 1)
    for place, ref in enumerate((xm_ref, xl_ref, xh_ref, xp_ref)):
        for i in range(8):
            x = 8 * place + i
            up, down = zp_ref[x], zm_ref[x]
            mob[x, :, :LANES] = ref[0, i]
            mob[x, :, LANES:] = jnp.where(lane < 43, up, jnp.where(lane >= 85, down, 1.0))
            v0[x, :, :LANES] = ref[1, i]
            v0[x, :, LANES:] = jnp.where(
                lane < 43, roll(up, -43, 1), jnp.where(lane >= 85, roll(down, 43, 1), 0.0)
            )
            side_ref[x, :, :LANES] = ref[2, i]
            side_ref[x, :, LANES:] = jnp.where(
                lane < 42, roll(up, -86, 1), jnp.where(lane >= 86, roll(down, 86, 1), 0.0)
            )

    half = TAU / 2

    def face_planes(x, before):
        here = mob[x]
        kx = half * (here + mob[x + 1])
        ky = half * (here + roll(here, -1, 0))
        kz = half * (here + roll(here, -1, 1))
        kx_ref[x] = kx
        ky_ref[x] = ky
        kz_ref[x] = kz
        total = (kx + before) + (ky + roll(ky, 1, 0)) + (kz + roll(kz, 1, 1))
        wd_ref[x] = OMEGA / (1.0 + total)
        return kx

    first = half * (mob[1] + mob[2])
    kx_ref[1] = first
    lax.fori_loop(2, 30, face_planes, first)

    def smooth(target, weight):
        def use(x, value, left):
            target[x] = value + weight[x] * left

        return use

    v_ref[1] = v0[1]
    for x in (0, 2, 29, 30, 31):
        v_ref[x] = v0[x]
    sweep_planes(2, 29, v0, side_ref, kx_ref, ky_ref, kz_ref, 1, smooth(res, wd_ref))
    sweep_planes(3, 28, res, side_ref, kx_ref, ky_ref, kz_ref, 1, smooth(v_ref, wd_ref))

    def keep(x, value, left):
        res[x] = left

    sweep_planes(4, 27, v_ref, side_ref, kx_ref, ky_ref, kz_ref, 1, keep)

    def pool(x):
        return pair_sum(pair_sum(x, 1, 0), 1, 1)

    for i in range(1, 14):
        x = 2 * i
        k1x_ref[i] = pool(kx_ref[x + 1]) * (1.0 / 16.0)
        if i == 1:
            continue
        f1_ref[i] = pool(res[x] + res[x + 1]) * 0.125
        along_y = pair_sum(ky_ref[x] + ky_ref[x + 1], 1, 1)
        k1y = upper_of(along_y, 1, 0) * (1.0 / 16.0)
        along_z = pair_sum(kz_ref[x] + kz_ref[x + 1], 1, 0)
        k1z = upper_of(along_z, 1, 1) * (1.0 / 16.0)
        k1y_ref[i] = k1y
        k1z_ref[i] = k1z
        total = (k1x_ref[i] + k1x_ref[i - 1]) + (k1y + roll(k1y, 2, 0)) + (k1z + roll(k1z, 2, 1))
        weight = OMEGA / (1.0 + total)
        wd1_ref[i] = weight
        e0[i] = weight * f1_ref[i]
    for ref in (f1_ref, k1x_ref, k1y_ref, k1z_ref, wd1_ref):
        for i in (0, 1, 14, 15):
            if i != 1 or ref is not k1x_ref:
                ref[i] = jnp.zeros((32, RING), F32)

    sweep_planes(3, 12, e0, f1_ref, k1x_ref, k1y_ref, k1z_ref, 2, smooth(e1, wd1_ref))

    def keep_middle(x, value, left):
        r1[x] = left

    sweep_planes(4, 11, e1, f1_ref, k1x_ref, k1y_ref, k1z_ref, 2, keep_middle)

    src = iota((RING, LANES), 0)
    dst = iota((RING, LANES), 1)
    cell = jnp.where(src < 192, src, src - RING)
    pick_low = (cell == 4 * (dst - COARSE_LOW)) & (dst < COARSE)
    pick_high = (cell == 4 * (dst - 64 - COARSE_LOW)) & (dst >= 64) & (dst < 64 + COARSE)
    pick_low = pick_low.astype(F32)
    pick_high = pick_high.astype(F32)
    pick_middle = ((cell == 2 * (dst - MIDDLE_LOW)) & (dst < MIDDLE)).astype(F32)
    for j in range(4):
        i = 4 + 2 * j
        f2 = pair_sum(pair_sum(r1[i] + r1[i + 1], 2, 0), 2, 1) * 0.125
        k2x = pair_sum(pair_sum(k1x_ref[i + 1], 2, 0), 2, 1) * (1.0 / 16.0)
        k2y = pair_sum(k1y_ref[i] + k1y_ref[i + 1], 2, 1)
        k2y = upper_of(k2y, 2, 0) * (1.0 / 16.0)
        k2z = pair_sum(k1z_ref[i] + k1z_ref[i + 1], 2, 0)
        k2z = upper_of(k2z, 2, 1) * (1.0 / 16.0)
        first = dot(f2, pick_low) + dot(k2x, pick_high)
        second = dot(k2y, pick_low) + dot(k2z, pick_high)
        for k in range(4):
            line = pl.ds(8 + 4 * k, 1)
            chunk_ref[0, pl.ds(4 * j + k, 1), :] = first[8 + 4 * k : 9 + 4 * k]
            chunk_ref[0, pl.ds(16 + 4 * j + k, 1), :] = second[8 + 4 * k : 9 + 4 * k]
    for i in range(8):
        middle = dot(e1[4 + i], pick_middle)
        for k in range(8):
            chunk_ref[0, pl.ds(32 + 8 * i + k, 1), :] = middle[8 + 2 * k : 9 + 2 * k]
    for k in range(1, 32):
        chunk_ref[k] = chunk_ref[0]


def up_kernel(
    place_ref, all_ref, v_ref, side_ref, kx_ref, ky_ref, kz_ref, wd_ref,
    f1_ref, k1x_ref, k1y_ref, k1z_ref, wd1_ref,
    out_ref,
    pair0, pair1, c2x, c2y, c2z, wd2, f2, ea, eb, mid, e1a, e1b, va, vb,
):
    gx = place_ref[0]
    gy = place_ref[1]

    def source(dx, dy):
        return ((gx + dx + 8) & 7) * 4 + ((gy + dy + 4) & 3)

    for p in range(8):
        for q in range(4):
            s = source(p - 1, q - 1)
            for i in range(4):
                pair0[4 * p + i, pl.ds(4 * q, 4), :] = all_ref[s, pl.ds(4 * i, 4), :]
                pair1[4 * p + i, pl.ds(4 * q, 4), :] = all_ref[s, pl.ds(16 + 4 * i, 4), :]
    for p in (-1, 0, 1):
        for q in (-1, 0, 1):
            s = source(p, q)
            for i in range(16):
                if (i - 4) // 8 != p or not 1 <= i <= 14:
                    continue
                start = 32 + 8 * ((i - 4) % 8)
                if q == -1:
                    mid[i, pl.ds(0, 4), :] = all_ref[s, pl.ds(start + 4, 4), :]
                elif q == 0:
                    mid[i, pl.ds(4, 8), :] = all_ref[s, pl.ds(start, 8), :]
                else:
                    mid[i, pl.ds(12, 4), :] = all_ref[s, pl.ds(start, 4), :]

    used = iota((16, LANES), 1) < COARSE
    for x in range(32):
        first = pair0[x]
        second = pair1[x]
        f2[x] = jnp.where(used, first, 0.0)
        c2x[x] = jnp.where(used, roll(first, 64, 1), 0.0)
        c2y[x] = jnp.where(used, second, 0.0)
        c2z[x] = jnp.where(used, roll(second, 64, 1), 0.0)
    for x in range(32):
        ky = c2y[x]
        kz = c2z[x]
        total = (c2x[x] + c2x[(x + 31) % 32]) + (ky + roll(ky, 1, 0)) + (kz + roll(kz, 1, 1))
        weight = OMEGA / (1.0 + total)
        wd2[x] = weight
        ea[x] = weight * f2[x]

    def coarse_sweep(old, new):
        before = c2x[31] * (old[0] - old[31])
        for x in range(32):
            value = old[x]
            flux = c2x[x] * (old[(x + 1) % 32] - value)
            left = residual(value, f2[x], flux, before, c2y[x], c2z[x], 1)
            new[x] = value + wd2[x] * left
            before = flux

    def two(_, c):
        coarse_sweep(ea, eb)
        coarse_sweep(eb, ea)
        return c

    lax.fori_loop(0, 3, two, 0)
    coarse_sweep(ea, eb)

    src = iota((LANES, RING), 0)
    dst = iota((LANES, RING), 1)
    cell = jnp.where(dst < 192, dst, dst - RING)
    spread2 = ((cell + 4 * COARSE_LOW) // 4 == src) & (src < COARSE) & (cell >= -4 * COARSE_LOW)
    spread2 = spread2.astype(F32)
    spread1 = ((cell + 2 * MIDDLE_LOW) // 2 == src) & (src < MIDDLE) & (cell >= -2 * MIDDLE_LOW)
    spread1 = spread1.astype(F32)
    line = iota((32, 16), 0)
    pick = iota((32, 16), 1)
    rows2 = (line // 4 + 2 == pick).astype(F32)
    rows1 = (line // 2 == pick).astype(F32)
    for j in range(8):
        coarse = dot(rows2, dot(eb[2 + j], spread2))
        for i in (2 * j, 2 * j + 1):
            if 1 <= i <= 14:
                e1a[i] = coarse + dot(rows1, dot(mid[i], spread1))

    def smooth(target, weight):
        def use(x, value, left):
            target[x] = value + weight[x] * left

        return use

    sweep_planes(2, 13, e1a, f1_ref, k1x_ref, k1y_ref, k1z_ref, 2, smooth(e1b, wd1_ref))
    sweep_planes(3, 12, e1b, f1_ref, k1x_ref, k1y_ref, k1z_ref, 2, smooth(e1a, wd1_ref))
    for x in range(6, 26):
        va[x] = v_ref[x] + e1a[x // 2]
    sweep_planes(7, 24, va, side_ref, kx_ref, ky_ref, kz_ref, 1, smooth(vb, wd_ref))

    def finish(x, value, left):
        new = value + wd_ref[x] * left
        out_ref[x - 8] = new[8:24, :LANES]

    sweep_planes(8, 23, vb, side_ref, kx_ref, ky_ref, kz_ref, 1, finish)


def shift(x, axis, direction):
    count = lax.axis_size(axis)
    return lax.ppermute(x, axis, [(i, (i + direction) % count) for i in range(count)])


def body(conc, right_side, order_field, grain_ids):
    face = ((9, 16, LANES), BF16)
    zface = ((17, 16, LANES), BF16)
    xm, xp, ym, yp, zm, zp = call(
        faces_kernel, [face] * 4 + [zface] * 2, (order_field, grain_ids)
    )
    faces = (
        shift(xp, "gx", 1), shift(xm, "gx", -1),
        shift(yp, "gy", 1), shift(ym, "gy", -1),
        shift(zp, "gz", 1), shift(zm, "gz", -1),
    )
    half = ((3, 16, 8, LANES), F32)
    mobility, low, high = call(
        mobility_kernel,
        [((16, 16, LANES), F32), half, half],
        (conc, right_side, order_field, grain_ids) + faces + (ym, yp),
        scratch=[((16, 16, LANES), F32), ((64, 8, LANES), F32)],
    )
    below = shift(high, "gy", 1)
    above = shift(low, "gy", -1)
    slab = ((3, 8, 32, LANES), F32)
    xl, xh = call(rows_kernel, [slab, slab], (below, low, high, above))
    before = shift(xh, "gx", 1)
    after = shift(xl, "gx", -1)
    wide = ((32, 32, LANES), F32)
    sm, sp = call(lanes_kernel, [wide, wide], (before, xl, xh, after))
    left = shift(sp, "gz", 1)
    right = shift(sm, "gz", -1)
    fine = ((32, 32, RING), F32)
    middle = ((16, 32, RING), F32)
    results = call(
        down_kernel,
        [fine] * 6 + [middle] * 5 + [((32, 96, LANES), F32)],
        (before, xl, xh, after, left, right),
        scratch=[fine] * 3 + [middle] * 3,
    )
    chunks = lax.all_to_all(results[-1], ("gx", "gy"), 0, 0, tiled=True)
    place = jnp.stack([lax.axis_index("gx"), lax.axis_index("gy")]).astype(jnp.int32)
    plane = ((32, 16, LANES), F32)
    (out,) = call(
        up_kernel,
        [((16, 16, LANES), F32)],
        (place, chunks) + tuple(results[:-1]),
        scratch=[plane] * 9 + [((16, 16, LANES), F32)] + [middle] * 2 + [fine] * 2,
        specs=[SMEM] + [VMEM] * 12,
    )
    return out, mobility


def solution(mesh):
    return jax.shard_map(
        body,
        mesh=mesh,
        in_specs=(
            P("gx", "gy", "gz"),
            P("gx", "gy", "gz"),
            P(None, "gx", "gy", "gz"),
            P("gx", "gy", "gz", None),
        ),
        out_specs=(P("gx", "gy", "gz"), P("gx", "gy", "gz")),
        check_vma=False,
    )
```

time: 652 us -> 157 us (0.24)
  the two profiles are of different devices: /device:TPU:32 before, /device:TPU:1 now
where the time goes in v1:
time: 157 us; the launch traced here: 156 us
  Pallas kernels  48.8 us (31%)
  starting transfers between devices  46.8 us (30%)
  waiting for transfers between devices  46.6 us (30%)
  local copies, waits for them, and re-layouts  12.7 us (8%)
    pallas_call x6, Pallas kernels, call(): pl.pallas_call(kernel, out_shape=[jax.ShapeDtypeStruct(shape, dtype) for...  48.8 us
    ppermute x12, starting transfers between devices, shift(): lax.ppermute(x, axis, [(i, (i + direction) % count) for i in range(count)])  37.6 us
    ppermute x12, waiting for transfers between devices, shift(): lax.ppermute(x, axis, [(i, (i + direction) % count) for i in range(count)])  25.2 us
    all_to_all x1, waiting for transfers between devices, body(): chunks = lax.all_to_all(results[-1], ('gx', 'gy'), 0, 0, tiled=True)  21.4 us
    unnamed x34, local copies, waits for them, and re-layouts  12.7 us
    all_to_all x1, starting transfers between devices, body(): chunks = lax.all_to_all(results[-1], ('gx', 'gy'), 0, 0, tiled=True)  9.26 us
  transfers between devices with their start and end apart: 13, of which 9 were waited for; matrix products, arithmetic and copies ran while one was open for 0% of the time, Pallas kernels for 0%

profile of v1, /device:TPU:1, one launch (start us, length us, event | category | flops | bytes accessed | tf_op | source)
XLA Modules:
  0.0 155.8 jit_solution(2083268258517758700)
XLA Ops:
  0.6 0.0 copy-start
  0.6 1.0 copy-done
  1.7 0.0 copy-start.16
  1.7 0.7 copy-done.16
  2.4 0.5 shard_map.59
  2.9 3.9 %collective-permute-start.2 = (bf16[9,16,128]{2,1,0:T(8,128)(2,1)S(1)}, bf16[9,16,128]{2,1,0:T(8,128)(2,1)S(1)}, u32[]{:S(2)}, u32[]{:S(2)}) collective-permute-start(bf16[9,16,128]{2,1,0:T(8,128)(2,1)S(1)} %get-tuple-element.29.own_yp_ref), channel_id=1, source_target_pairs={{0,16},{16,32},{32,48},{48,0},{1,17},{17,33},{33,49},{49,1},{2,18}... | collective-permute-start | bytes 110600 | tf_op jit(solution)/shard_map/ppermute | solution.py:467
  6.8 3.5 %collective-permute-start.4 = (bf16[17,16,128]{2,1,0:T(8,128)(2,1)S(1)}, bf16[17,16,128]{2,1,0:T(8,128)(2,1)S(1)}, u32[]{:S(2)}, u32[]{:S(2)}) collective-permute-start(bf16[17,16,128]{2,1,0:T(8,128)(2,1)S(1)} %get-tuple-element.31), channel_id=1, source_target_pairs={{0,1},{1,2},{2,3},{3,4},{4,5},{5,6},{6,7},{7,8},{8,9},{9,10},{10,1... | collective-permute-start | bytes 208904 | tf_op jit(solution)/shard_map/ppermute | solution.py:467
  10.4 9.5 %collective-permute-start.5 = (bf16[17,16,128]{2,1,0:T(8,128)(2,1)S(1)}, bf16[17,16,128]{2,1,0:T(8,128)(2,1)S(1)}, u32[]{:S(2)}, u32[]{:S(2)}) collective-permute-start(bf16[17,16,128]{2,1,0:T(8,128)(2,1)S(1)} %get-tuple-element.32), channel_id=1, source_target_pairs={{0,15},{1,0},{2,1},{3,2},{4,3},{5,4},{6,5},{7,6},{8,7},{9,8},{10,9... | collective-permute-start | bytes 208904 | tf_op jit(solution)/shard_map/ppermute | solution.py:467
  19.9 3.4 %collective-permute-start.3 = (bf16[9,16,128]{2,1,0:T(8,128)(2,1)S(1)}, bf16[9,16,128]{2,1,0:T(8,128)(2,1)S(1)}, u32[]{:S(2)}, u32[]{:S(2)}) collective-permute-start(bf16[9,16,128]{2,1,0:T(8,128)(2,1)S(1)} %get-tuple-element.30.own_ym_ref), channel_id=1, source_target_pairs={{0,48},{16,0},{32,16},{48,32},{1,49},{17,1},{33,17},{49,33},{2,50}... | collective-permute-start | bytes 110600 | tf_op jit(solution)/shard_map/ppermute | solution.py:467
  23.3 2.7 %collective-permute-start = (bf16[9,16,128]{2,1,0:T(8,128)(2,1)S(1)}, bf16[9,16,128]{2,1,0:T(8,128)(2,1)S(1)}, u32[]{:S(2)}, u32[]{:S(2)}) collective-permute-start(bf16[9,16,128]{2,1,0:T(8,128)(2,1)S(1)} %get-tuple-element.27), channel_id=1, source_target_pairs={{0,64},{64,128},{128,192},{192,256},{256,320},{320,384},{384,448},... | collective-permute-start | bytes 110600 | tf_op jit(solution)/shard_map/ppermute | solution.py:467
  26.0 0.0 collective-permute-done.2.ym_ref
  26.0 0.0 collective-permute-start.1
  26.0 0.0 collective-permute-done.3.yp_ref
  26.0 1.1 collective-permute-done.xm_ref
  27.0 2.3 %collective-permute-done.1.xp_ref = bf16[9,16,128]{2,1,0:T(8,128)(2,1)S(1)} collective-permute-done((bf16[9,16,128]{2,1,0:T(8,128)(2,1)S(1)}, bf16[9,16,128]{2,1,0:T(8,128)(2,1)S(1)}, u32[]{:S(2)}, u32[]{:S(2)}) %collective-permute-start.1) | collective-permute-done | bytes 36896 | tf_op jit(solution)/shard_map/ppermute | solution.py:467
  29.4 0.0 collective-permute-done.4.zm_ref
  29.4 0.0 collective-permute-done.5.zp_ref
  29.4 0.0 copy-start.14
  29.4 0.9 copy-done.14
  30.3 0.0 copy-start.15
  30.3 0.9 copy-done.15
  31.2 4.0 %shard_map.60 = (f32[16,16,128]{2,1,0:T(8,128)}, f32[3,16,8,128]{3,2,1,0:T(8,128)S(1)}, f32[3,16,8,128]{3,2,1,0:T(8,128)S(1)}) custom-call(f32[16,16,128]{2,1,0:T(8,128)S(1)} %copy-done.14, f32[16,16,128]{2,1,0:T(8,128)S(1)} %copy-done.15, bf16[8,16,16,128]{3,2,1,0:T(8,128)(2,1)S(1)} %copy-done, s32[1,1,8,8]{3,2,1,0:T(8,128)S(1)} %copy-done.16, ...), custom_call_target="tpu_custom_call" | custom-call | tf_op jit(solution)/shard_map/pallas_call | solution.py:28
  35.2 1.9 %collective-permute-start.6 = (f32[3,16,8,128]{3,2,1,0:T(8,128)S(1)}, f32[3,16,8,128]{3,2,1,0:T(8,128)S(1)}, u32[]{:S(2)}, u32[]{:S(2)}) collective-permute-start(f32[3,16,8,128]{3,2,1,0:T(8,128)S(1)} %get-tuple-element.33.high_ref), channel_id=1, source_target_pairs={{0,16},{16,32},{32,48},{48,0},{1,17},{17,33},{33,49},{49,1},{2,18}... | collective-permute-start | bytes 589832 | tf_op jit(solution)/shard_map/ppermute | solution.py:467
  37.1 4.6 %collective-permute-start.7 = (f32[3,16,8,128]{3,2,1,0:T(8,128)S(1)}, f32[3,16,8,128]{3,2,1,0:T(8,128)S(1)}, u32[]{:S(2)}, u32[]{:S(2)}) collective-permute-start(f32[3,16,8,128]{3,2,1,0:T(8,128)S(1)} %get-tuple-element.34.low_ref), channel_id=1, source_target_pairs={{0,48},{16,0},{32,16},{48,32},{1,49},{17,1},{33,17},{49,33},{2,50}... | collective-permute-start | bytes 589832 | tf_op jit(solution)/shard_map/ppermute | solution.py:467
  41.7 3.1 %collective-permute-done.6.below_ref = f32[3,16,8,128]{3,2,1,0:T(8,128)S(1)} collective-permute-done((f32[3,16,8,128]{3,2,1,0:T(8,128)S(1)}, f32[3,16,8,128]{3,2,1,0:T(8,128)S(1)}, u32[]{:S(2)}, u32[]{:S(2)}) %collective-permute-start.6) | collective-permute-done | bytes 196640 | tf_op jit(solution)/shard_map/ppermute | solution.py:467
  44.8 0.9 collective-permute-done.7.above_ref
  45.6 0.1 shard_map.61
  45.7 1.5 collective-permute-start.8
  47.2 0.0 collective-permute-start.9
  47.3 4.7 %collective-permute-done.8.xm_ref = f32[3,8,32,128]{3,2,1,0:T(8,128)S(1)} collective-permute-done((f32[3,8,32,128]{3,2,1,0:T(8,128)S(1)}, f32[3,8,32,128]{3,2,1,0:T(8,128)S(1)}, u32[]{:S(2)}, u32[]{:S(2)}) %collective-permute-start.8) | collective-permute-done | bytes 393248 | tf_op jit(solution)/shard_map/ppermute | solution.py:467
  52.0 2.8 %collective-permute-done.9.xp_ref = f32[3,8,32,128]{3,2,1,0:T(8,128)S(1)} collective-permute-done((f32[3,8,32,128]{3,2,1,0:T(8,128)S(1)}, f32[3,8,32,128]{3,2,1,0:T(8,128)S(1)}, u32[]{:S(2)}, u32[]{:S(2)}) %collective-permute-start.9) | collective-permute-done | bytes 393248 | tf_op jit(solution)/shard_map/ppermute | solution.py:467
  54.7 0.6 shard_map.62
  55.4 1.9 %collective-permute-start.10 = (f32[32,32,128]{2,1,0:T(8,128)S(1)}, f32[32,32,128]{2,1,0:T(8,128)S(1)}, u32[]{:S(2)}, u32[]{:S(2)}) collective-permute-start(f32[32,32,128]{2,1,0:T(8,128)S(1)} %get-tuple-element.37), channel_id=1, source_target_pairs={{0,1},{1,2},{2,3},{3,4},{4,5},{5,6},{6,7},{7,8},{8,9},{9,10},{10,1... | collective-permute-start | bytes 1572872 | tf_op jit(solution)/shard_map/ppermute | solution.py:467
  57.3 4.6 %collective-permute-start.11 = (f32[32,32,128]{2,1,0:T(8,128)S(1)}, f32[32,32,128]{2,1,0:T(8,128)S(1)}, u32[]{:S(2)}, u32[]{:S(2)}) collective-permute-start(f32[32,32,128]{2,1,0:T(8,128)S(1)} %get-tuple-element.38), channel_id=1, source_target_pairs={{0,15},{1,0},{2,1},{3,2},{4,3},{5,4},{6,5},{7,6},{8,7},{9,8},{10,9... | collective-permute-start | bytes 1572872 | tf_op jit(solution)/shard_map/ppermute | solution.py:467
  61.9 9.5 %collective-permute-done.10.zm_ref = f32[32,32,128]{2,1,0:T(8,128)S(1)} collective-permute-done((f32[32,32,128]{2,1,0:T(8,128)S(1)}, f32[32,32,128]{2,1,0:T(8,128)S(1)}, u32[]{:S(2)}, u32[]{:S(2)}) %collective-permute-start.10) | collective-permute-done | bytes 524320 | tf_op jit(solution)/shard_map/ppermute | solution.py:467
  71.4 0.9 collective-permute-done.11.zp_ref
  72.3 25.4 %shard_map.63 = (f32[32,32,256]{2,1,0:T(8,128)}, f32[32,32,256]{2,1,0:T(8,128)}, f32[32,32,256]{2,1,0:T(8,128)}, f32[32,32,256]{2,1,0:T(8,128)}, f32[32,32,256]{...) custom-call(f32[3,8,32,128]{3,2,1,0:T(8,128)S(1)} %collective-permut, ...), custom_call_target="tpu_custom_call" | custom-call | tf_op jit(solution)/shard_map/pallas_call | solution.py:28
  97.6 0.0 copy-start.4
  97.6 0.8 copy-done.4
  98.4 0.0 copy-start.6
  98.4 0.8 copy-done.6
  99.2 0.0 copy-start.8
  99.2 0.8 copy-done.8
  100.0 0.0 copy-start.10
  100.0 0.8 copy-done.10
  100.8 0.0 copy-start.12
  100.8 0.8 copy-done.12
  101.6 0.0 copy-start.1
  101.6 0.0 copy-start.2
  101.6 0.0 copy-start.3
  101.6 9.3 %all-to-all-start = ((f32[32,96,128]{2,1,0:T(8,128)}), f32[32,96,128]{2,1,0:T(8,128)}, u32[]{:S(2)}, u32[]{:S(2)}) async-start(f32[32,96,128]{2,1,0:T(8,128)} %get-tuple-element.39), calls=%async_computation | async-start | bytes 3145728 | tf_op jit(solution)/shard_map/all_to_all | solution.py:506
  110.9 0.1 pad_add_fusion.place_ref
  111.0 21.4 %all-to-all-done.all_ref = f32[32,96,128]{2,1,0:T(8,128)} async-done(((f32[32,96,128]{2,1,0:T(8,128)}), f32[32,96,128]{2,1,0:T(8,128)}, u32[]{:S(2)}, u32[]{:S(2)}) %all-to-all-start) | async-done | bytes 1572896 | tf_op jit(solution)/shard_map/all_to_all | solution.py:506
  132.3 0.0 copy-done.1
  132.3 0.0 copy-done.2
  132.3 0.0 copy-done.3
  132.3 0.0 copy-start.5
  132.4 1.0 copy-done.5
  133.4 0.0 copy-start.7
  133.4 1.0 copy-done.7
  134.4 1.0 copy-done.9
  135.5 1.0 copy-done.11
  136.5 1.0 copy-done.13
  137.6 18.2 %shard_map.64 = f32[16,16,128]{2,1,0:T(8,128)} custom-call(s32[2]{0:T(128)S(1)} %pad_add_fusion.place_ref, f32[32,96,128]{2,1,0:T(8,128)} %all-to-all-done.all_ref, f32[32,32,256]{2,1,0:T(8,128)S(1)} %copy-done.1, f32[32,32,256]{2,1,0:T(8,128)S(1)} %copy-done.2, f32[32,32,256]{2,1,0:T(8,128)S(1)} %copy-done.3, f32[32,32,256]{2,1,0:T(8,128)} %get-tuple-element.43.ky_ref, ...), custom_call_target="tpu_custom_call" | custom-call | tf_op jit(solution)/shard_map/pallas_call | solution.py:28
  (3 shorter events, 0.0 us)
Async XLA Ops:
  0.6 1.0 copy-start
  1.7 0.7 copy-start.16
  2.9 23.1 %collective-permute-start.2 = (bf16[9,16,128]{2,1,0:T(8,128)(2,1)S(1)}, bf16[9,16,128]{2,1,0:T(8,128)(2,1)S(1)}, u32[]{:S(2)}, u32[]{:S(2)}) collective-permute-start(bf16[9,16,128]{2,1,0:T(8,128)(2,1)S(1)} %get-tuple-element.29.own_yp_ref), channel_id=1, source_target_pairs={{0,16},{16,32},{32,48},{48,0},{1,17},{17,33},{33,49},{49,1},{2,18}... | collective-permute-start | bytes 110600 | tf_op jit(solution)/shard_map/ppermute | solution.py:467
  6.8 22.5 %collective-permute-start.4 = (bf16[17,16,128]{2,1,0:T(8,128)(2,1)S(1)}, bf16[17,16,128]{2,1,0:T(8,128)(2,1)S(1)}, u32[]{:S(2)}, u32[]{:S(2)}) collective-permute-start(bf16[17,16,128]{2,1,0:T(8,128)(2,1)S(1)} %get-tuple-element.31), channel_id=1, source_target_pairs={{0,1},{1,2},{2,3},{3,4},{4,5},{5,6},{6,7},{7,8},{8,9},{9,10},{10,1... | collective-permute-start | bytes 208904 | tf_op jit(solution)/shard_map/ppermute | solution.py:467
  10.4 19.0 %collective-permute-start.5 = (bf16[17,16,128]{2,1,0:T(8,128)(2,1)S(1)}, bf16[17,16,128]{2,1,0:T(8,128)(2,1)S(1)}, u32[]{:S(2)}, u32[]{:S(2)}) collective-permute-start(bf16[17,16,128]{2,1,0:T(8,128)(2,1)S(1)} %get-tuple-element.32), channel_id=1, source_target_pairs={{0,15},{1,0},{2,1},{3,2},{4,3},{5,4},{6,5},{7,6},{8,7},{9,8},{10,9... | collective-permute-start | bytes 208904 | tf_op jit(solution)/shard_map/ppermute | solution.py:467
  19.9 6.1 %collective-permute-start.3 = (bf16[9,16,128]{2,1,0:T(8,128)(2,1)S(1)}, bf16[9,16,128]{2,1,0:T(8,128)(2,1)S(1)}, u32[]{:S(2)}, u32[]{:S(2)}) collective-permute-start(bf16[9,16,128]{2,1,0:T(8,128)(2,1)S(1)} %get-tuple-element.30.own_ym_ref), channel_id=1, source_target_pairs={{0,48},{16,0},{32,16},{48,32},{1,49},{17,1},{33,17},{49,33},{2,50}... | collective-permute-start | bytes 110600 | tf_op jit(solution)/shard_map/ppermute | solution.py:467
  23.3 3.8 %collective-permute-start = (bf16[9,16,128]{2,1,0:T(8,128)(2,1)S(1)}, bf16[9,16,128]{2,1,0:T(8,128)(2,1)S(1)}, u32[]{:S(2)}, u32[]{:S(2)}) collective-permute-start(bf16[9,16,128]{2,1,0:T(8,128)(2,1)S(1)} %get-tuple-element.27), channel_id=1, source_target_pairs={{0,64},{64,128},{128,192},{192,256},{256,320},{320,384},{384,448},... | collective-permute-start | bytes 110600 | tf_op jit(solution)/shard_map/ppermute | solution.py:467
  26.0 3.4 %collective-permute-start.1 = (bf16[9,16,128]{2,1,0:T(8,128)(2,1)S(1)}, bf16[9,16,128]{2,1,0:T(8,128)(2,1)S(1)}, u32[]{:S(2)}, u32[]{:S(2)}) collective-permute-start(bf16[9,16,128]{2,1,0:T(8,128)(2,1)S(1)} %get-tuple-element.28), channel_id=1, source_target_pairs={{0,448},{64,0},{128,64},{192,128},{256,192},{320,256},{384,320},{4... | collective-permute-start | bytes 110600 | tf_op jit(solution)/shard_map/ppermute | solution.py:467
  29.4 0.9 copy-start.14
  30.3 0.9 copy-start.15
  35.2 9.6 %collective-permute-start.6 = (f32[3,16,8,128]{3,2,1,0:T(8,128)S(1)}, f32[3,16,8,128]{3,2,1,0:T(8,128)S(1)}, u32[]{:S(2)}, u32[]{:S(2)}) collective-permute-start(f32[3,16,8,128]{3,2,1,0:T(8,128)S(1)} %get-tuple-element.33.high_ref), channel_id=1, source_target_pairs={{0,16},{16,32},{32,48},{48,0},{1,17},{17,33},{33,49},{49,1},{2,18}... | collective-permute-start | bytes 589832 | tf_op jit(solution)/shard_map/ppermute | solution.py:467
  37.1 8.5 %collective-permute-start.7 = (f32[3,16,8,128]{3,2,1,0:T(8,128)S(1)}, f32[3,16,8,128]{3,2,1,0:T(8,128)S(1)}, u32[]{:S(2)}, u32[]{:S(2)}) collective-permute-start(f32[3,16,8,128]{3,2,1,0:T(8,128)S(1)} %get-tuple-element.34.low_ref), channel_id=1, source_target_pairs={{0,48},{16,0},{32,16},{48,32},{1,49},{17,1},{33,17},{49,33},{2,50}... | collective-permute-start | bytes 589832 | tf_op jit(solution)/shard_map/ppermute | solution.py:467
  45.7 6.2 %collective-permute-start.8 = (f32[3,8,32,128]{3,2,1,0:T(8,128)S(1)}, f32[3,8,32,128]{3,2,1,0:T(8,128)S(1)}, u32[]{:S(2)}, u32[]{:S(2)}) collective-permute-start(f32[3,8,32,128]{3,2,1,0:T(8,128)S(1)} %get-tuple-element.35.xh_ref), channel_id=1, source_target_pairs={{0,64},{64,128},{128,192},{192,256},{256,320},{320,384},{384,448},... | collective-permute-start | bytes 1179656 | tf_op jit(solution)/shard_map/ppermute | solution.py:467
  47.2 7.5 %collective-permute-start.9 = (f32[3,8,32,128]{3,2,1,0:T(8,128)S(1)}, f32[3,8,32,128]{3,2,1,0:T(8,128)S(1)}, u32[]{:S(2)}, u32[]{:S(2)}) collective-permute-start(f32[3,8,32,128]{3,2,1,0:T(8,128)S(1)} %get-tuple-element.36.xl_ref), channel_id=1, source_target_pairs={{0,448},{64,0},{128,64},{192,128},{256,192},{320,256},{384,320},{4... | collective-permute-start | bytes 1179656 | tf_op jit(solution)/shard_map/ppermute | solution.py:467
  55.4 16.0 %collective-permute-start.10 = (f32[32,32,128]{2,1,0:T(8,128)S(1)}, f32[32,32,128]{2,1,0:T(8,128)S(1)}, u32[]{:S(2)}, u32[]{:S(2)}) collective-permute-start(f32[32,32,128]{2,1,0:T(8,128)S(1)} %get-tuple-element.37), channel_id=1, source_target_pairs={{0,1},{1,2},{2,3},{3,4},{4,5},{5,6},{6,7},{7,8},{8,9},{9,10},{10,1... | collective-permute-start | bytes 1572872 | tf_op jit(solution)/shard_map/ppermute | solution.py:467
  57.3 15.0 %collective-permute-start.11 = (f32[32,32,128]{2,1,0:T(8,128)S(1)}, f32[32,32,128]{2,1,0:T(8,128)S(1)}, u32[]{:S(2)}, u32[]{:S(2)}) collective-permute-start(f32[32,32,128]{2,1,0:T(8,128)S(1)} %get-tuple-element.38), channel_id=1, source_target_pairs={{0,15},{1,0},{2,1},{3,2},{4,3},{5,4},{6,5},{7,6},{8,7},{9,8},{10,9... | collective-permute-start | bytes 1572872 | tf_op jit(solution)/shard_map/ppermute | solution.py:467
  97.6 0.8 copy-start.4
  98.4 0.8 copy-start.6
  99.2 0.8 copy-start.8
  100.0 0.8 copy-start.10
  100.8 0.8 copy-start.12
  101.6 30.7 %copy-start.1 = (f32[32,32,256]{2,1,0:T(8,128)S(1)}, f32[32,32,256]{2,1,0:T(8,128)}, u32[]{:S(2)}) copy-start(f32[32,32,256]{2,1,0:T(8,128)} %get-tuple-element.40.v_ref) | copy-start | bytes 3145732
  101.6 30.7 %copy-start.2 = (f32[32,32,256]{2,1,0:T(8,128)S(1)}, f32[32,32,256]{2,1,0:T(8,128)}, u32[]{:S(2)}) copy-start(f32[32,32,256]{2,1,0:T(8,128)} %get-tuple-element.41.side_ref) | copy-start | bytes 3145732
  101.6 30.7 %copy-start.3 = (f32[32,32,256]{2,1,0:T(8,128)S(1)}, f32[32,32,256]{2,1,0:T(8,128)}, u32[]{:S(2)}) copy-start(f32[32,32,256]{2,1,0:T(8,128)} %get-tuple-element.42.kx_ref) | copy-start | bytes 3145732
  101.6 30.7 %all-to-all-start = ((f32[32,96,128]{2,1,0:T(8,128)}), f32[32,96,128]{2,1,0:T(8,128)}, u32[]{:S(2)}, u32[]{:S(2)}) async-start(f32[32,96,128]{2,1,0:T(8,128)} %get-tuple-element.39), calls=%async_computation | async-start | bytes 3145728 | tf_op jit(solution)/shard_map/all_to_all | solution.py:506
  132.3 1.0 copy-start.5
  133.4 1.0 copy-start.7
  134.4 1.0 copy-start.9
  135.5 1.0 copy-start.11
  136.5 1.0 copy-start.13

commit v2 on v1

--- a/solution.py
+++ b/solution.py
@@ -17,21 +17,36 @@
 BF16 = jnp.bfloat16
 HIGH = lax.Precision.HIGHEST
 VMEM = pl.BlockSpec(memory_space=pltpu.VMEM)
+HBM = pl.BlockSpec(memory_space=pltpu.MemorySpace.HBM)
 SMEM = pl.BlockSpec(memory_space=pltpu.SMEM)
 COARSE = 51
 COARSE_LOW = 10
 MIDDLE = 70
 MIDDLE_LOW = 3
-
-
-def call(kernel, outs, args, scratch=(), specs=None):
+FINE_PLANES = pl.ds(6, 20)
+MIDDLE_PLANES = pl.ds(1, 13)
+
+
+def call(kernel, outs, args, scratch=(), specs=None, places=None, limit=16, semaphores=0):
+    specs = specs or [VMEM] * len(args)
+    places = places or [VMEM] * len(outs)
+    args = [
+        pltpu.with_memory_space_constraint(arg, pltpu.MemorySpace.HBM) if spec is HBM else arg
+        for arg, spec in zip(args, specs)
+    ]
+    scratches = [pltpu.VMEM(shape, dtype) for shape, dtype in scratch]
+    if semaphores:
+        scratches.append(pltpu.SemaphoreType.DMA((semaphores,)))
     return pl.pallas_call(
         kernel,
-        out_shape=[jax.ShapeDtypeStruct(shape, dtype) for shape, dtype in outs],
-        in_specs=specs or [VMEM] * len(args),
-        out_specs=[VMEM] * len(outs),
-        scratch_shapes=[pltpu.VMEM(shape, dtype) for shape, dtype in scratch],
-        compiler_params=pltpu.CompilerParams(vmem_limit_bytes=48 << 20),
+        out_shape=[
+            pltpu.MemorySpace.HBM(*out) if place is HBM else jax.ShapeDtypeStruct(*out)
+            for out, place in zip(outs, places)
+        ],
+        in_specs=specs,
+        out_specs=places,
+        scratch_shapes=scratches,
+        compiler_params=pltpu.CompilerParams(vmem_limit_bytes=limit << 20),
     )(*args)
 
 
@@ -43,8 +58,15 @@
     return lax.broadcasted_iota(jnp.int32, shape, axis)
 
 
-def dot(a, b):
-    return jnp.dot(a, b, precision=HIGH, preferred_element_type=F32)
+def select_dot(a, picks):
+    picks = picks.astype(BF16)
+    total = None
+    for _ in range(3):
+        part = a.astype(BF16)
+        a = a - part.astype(F32)
+        term = jnp.dot(part, picks, preferred_element_type=F32)
+        total = term if total is None else total + term
+    return total
 
 
 def lane_ids(ids_ref):
@@ -66,7 +88,18 @@
     return rows[:8] * 64.0 + rows[8:]
 
 
-def faces_kernel(order_ref, ids_ref, xm_ref, xp_ref, ym_ref, yp_ref, zm_ref, zp_ref):
+def faces_kernel(
+    conc_in, side_in, order_in, ids_in,
+    conc_ref, side_ref, order_ref, ids_ref, xm_ref, xp_ref, ym_ref, yp_ref, zm_ref, zp_ref, sems,
+):
+    pairs = (
+        (ids_in, ids_ref), (order_in, order_ref), (conc_in, conc_ref), (side_in, side_ref),
+    )
+    copies = [pltpu.make_async_copy(a, b, sems.at[k]) for k, (a, b) in enumerate(pairs)]
+    for copy in copies:
+        copy.start()
+    copies[0].wait()
+    copies[1].wait()
     grains = lane_ids(ids_ref)
     packed = split_ids(grains)
     for ref in (xm_ref, xp_ref, ym_ref, yp_ref):
@@ -88,6 +121,8 @@
     for x in range(16):
         zm_ref[x] = low[x].astype(BF16)
         zp_ref[x] = high[x].astype(BF16)
+    copies[2].wait()
+    copies[3].wait()
 
 
 def square(x):
@@ -96,7 +131,7 @@
 
 def mobility_kernel(
     conc_ref, side_ref, order_ref, ids_ref, xm_ref, xp_ref, ym_ref, yp_ref, zm_ref, zp_ref,
-    own_ym_ref, own_yp_ref, mob_ref, low_ref, high_ref, work, weights,
+    own_ym_ref, own_yp_ref, mob_ref, keep_ref, zm_out, zp_out, work, weights,
 ):
     own = lane_ids(ids_ref)
     lane = iota((16, LANES), 1)
@@ -131,7 +166,7 @@
     def doubled(block):
         return jnp.concatenate([block, block], axis=0)
 
-    def plane(x, below, carry_in):
+    def plane(x, carry_in):
         conc = conc_ref[x]
         base = 1.0 + 8.0 * square(conc * (1.0 - conc))
         zlow = zm_ref[x].astype(F32)
@@ -141,7 +176,7 @@
         along_x = jnp.zeros((16, LANES), F32)
         centers = []
         facing = []
-        above = jnp.minimum(x + 1, 15)
+        above = min(x + 1, 15)
         for slot in range(SLOTS):
             here = order_ref[slot, x].astype(F32)
             there = order_ref[slot, above].astype(F32)
@@ -167,7 +202,9 @@
         work[x] = total
         return along_x
 
-    lax.fori_loop(0, 16, lambda x, c: plane(x, None, c), jnp.zeros((16, LANES), F32))
+    carry = jnp.zeros((16, LANES), F32)
+    for x in range(16):
+        carry = plane(x, carry)
     work[0] = work[0] + across(
         xm_ref, join_ids(xm_ref[SLOTS]), lambda s: order_ref[s, 0].astype(F32)
     )
@@ -181,12 +218,20 @@
         value = value + jnp.where(row == 0, bottom[x : x + 1], 0.0)
         value = value + jnp.where(row == 15, top[x : x + 1], 0.0)
         mob_ref[x] = value
-        low_ref[0, x] = value[:8]
-        high_ref[0, x] = value[8:]
-        low_ref[1, x] = conc_ref[x, :8]
-        high_ref[1, x] = conc_ref[x, 8:]
-        low_ref[2, x] = side_ref[x, :8]
-        high_ref[2, x] = side_ref[x, 8:]
+        keep_ref[x] = value
+        conc, side = conc_ref[x], side_ref[x]
+        zm_out[x] = jnp.where(
+            lane < 43, value, jnp.where(lane < 86, roll(conc, 43, 1), roll(side, 86, 1))
+        )
+        zp_out[x] = jnp.where(
+            lane >= 85, value, jnp.where(lane >= 42, roll(conc, -43, 1), roll(side, -86, 1))
+        )
+
+
+def split_kernel(mob_ref, conc_ref, side_ref, zm_ref, zp_ref, low_ref, high_ref):
+    for place, ref in enumerate((mob_ref, conc_ref, side_ref, zm_ref, zp_ref)):
+        low_ref[place] = ref[:, :8]
+        high_ref[place] = ref[:, 8:]
 
 
 def rows_kernel(below_ref, low_ref, high_ref, above_ref, xl_ref, xh_ref):
@@ -194,19 +239,6 @@
         rows = pl.ds(8 * place, 8)
         xl_ref[:, :, rows, :] = ref[:, :8]
         xh_ref[:, :, rows, :] = ref[:, 8:]
-
-
-def lanes_kernel(xm_ref, xl_ref, xh_ref, xp_ref, zm_ref, zp_ref):
-    lane = iota((32, LANES), 1)
-    for place, ref in enumerate((xm_ref, xl_ref, xh_ref, xp_ref)):
-        for x in range(8):
-            mob, conc, side = ref[0, x], ref[1, x], ref[2, x]
-            zm_ref[8 * place + x] = jnp.where(
-                lane < 43, mob, jnp.where(lane < 86, roll(conc, 43, 1), roll(side, 86, 1))
-            )
-            zp_ref[8 * place + x] = jnp.where(
-                lane >= 85, mob, jnp.where(lane >= 42, roll(conc, -43, 1), roll(side, -86, 1))
-            )
 
 
 def partner(x, step, axis):
@@ -234,26 +266,34 @@
 def sweep_planes(first, last, values, source, kx, ky, kz, step, use):
     before = kx[first - 1] * (values[first] - values[first - 1])
 
-    def plane(x, flux_before):
-        value = values[x]
-        flux = kx[x] * (values[x + 1] - value)
-        use(x, value, residual(value, source[x], flux, flux_before, ky[x], kz[x], step))
-        return flux
-
-    lax.fori_loop(first, last + 1, plane, before)
+    value = values[first]
+    for x in range(first, last + 1):
+        above = values[x + 1]
+        flux = kx[x] * (above - value)
+        use(x, value, residual(value, source[x], flux, before, ky[x], kz[x], step))
+        before = flux
+        value = above
 
 
 def down_kernel(
-    xm_ref, xl_ref, xh_ref, xp_ref, zm_ref, zp_ref,
-    v_ref, side_ref, kx_ref, ky_ref, kz_ref, wd_ref,
-    f1_ref, k1x_ref, k1y_ref, k1z_ref, wd1_ref, chunk_ref,
-    mob, v0, res, e0, e1, r1,
+    xm_ref, xl_ref, xh_ref, xp_ref,
+    own_ref, chunk_ref, side_out, kx_out, ky_out, kz_out, wd_out, v_out,
+    k1x_out, k1y_out, k1z_out, wd1_out, f1_out,
+    mob, v0, res, v_ref, side_ref, kx_ref, ky_ref, kz_ref, wd_ref,
+    f1_ref, k1x_ref, k1y_ref, k1z_ref, wd1_ref, e0, e1, r1, rows, sems,
 ):
+    copies = []
+
+    def store(source, target, planes):
+        copy = pltpu.make_async_copy(source.at[planes], target.at[planes], sems.at[len(copies)])
+        copy.start()
+        copies.append(copy)
+
     lane = iota((32, LANES), 1)
     for place, ref in enumerate((xm_ref, xl_ref, xh_ref, xp_ref)):
         for i in range(8):
             x = 8 * place + i
-            up, down = zp_ref[x], zm_ref[x]
+            down, up = ref[3, i], ref[4, i]
             mob[x, :, :LANES] = ref[0, i]
             mob[x, :, LANES:] = jnp.where(lane < 43, up, jnp.where(lane >= 85, down, 1.0))
             v0[x, :, :LANES] = ref[1, i]
@@ -267,7 +307,9 @@
 
     half = TAU / 2
 
-    def face_planes(x, before):
+    before = half * (mob[1] + mob[2])
+    kx_ref[1] = before
+    for x in range(2, 30):
         here = mob[x]
         kx = half * (here + mob[x + 1])
         ky = half * (here + roll(here, -1, 0))
@@ -277,11 +319,13 @@
         kz_ref[x] = kz
         total = (kx + before) + (ky + roll(ky, 1, 0)) + (kz + roll(kz, 1, 1))
         wd_ref[x] = OMEGA / (1.0 + total)
-        return kx
-
-    first = half * (mob[1] + mob[2])
-    kx_ref[1] = first
-    lax.fori_loop(2, 30, face_planes, first)
+        before = kx
+
+    store(side_ref, side_out, FINE_PLANES)
+    store(kx_ref, kx_out, FINE_PLANES)
+    store(ky_ref, ky_out, FINE_PLANES)
+    store(kz_ref, kz_out, FINE_PLANES)
+    store(wd_ref, wd_out, FINE_PLANES)
 
     def smooth(target, weight):
         def use(x, value, left):
@@ -289,11 +333,10 @@
 
         return use
 
-    v_ref[1] = v0[1]
-    for x in (0, 2, 29, 30, 31):
-        v_ref[x] = v0[x]
     sweep_planes(2, 29, v0, side_ref, kx_ref, ky_ref, kz_ref, 1, smooth(res, wd_ref))
     sweep_planes(3, 28, res, side_ref, kx_ref, ky_ref, kz_ref, 1, smooth(v_ref, wd_ref))
+
+    store(v_ref, v_out, FINE_PLANES)
 
     def keep(x, value, left):
         res[x] = left
@@ -307,6 +350,8 @@
         x = 2 * i
         k1x_ref[i] = pool(kx_ref[x + 1]) * (1.0 / 16.0)
         if i == 1:
+            for ref in (f1_ref, k1y_ref, k1z_ref, wd1_ref):
+                ref[i] = jnp.zeros((32, RING), F32)
             continue
         f1_ref[i] = pool(res[x] + res[x + 1]) * 0.125
         along_y = pair_sum(ky_ref[x] + ky_ref[x + 1], 1, 1)
@@ -319,11 +364,11 @@
         weight = OMEGA / (1.0 + total)
         wd1_ref[i] = weight
         e0[i] = weight * f1_ref[i]
-    for ref in (f1_ref, k1x_ref, k1y_ref, k1z_ref, wd1_ref):
-        for i in (0, 1, 14, 15):
-            if i != 1 or ref is not k1x_ref:
-                ref[i] = jnp.zeros((32, RING), F32)
-
+    store(k1x_ref, k1x_out, MIDDLE_PLANES)
+    store(k1y_ref, k1y_out, MIDDLE_PLANES)
+    store(k1z_ref, k1z_out, MIDDLE_PLANES)
+    store(wd1_ref, wd1_out, MIDDLE_PLANES)
+    store(f1_ref, f1_out, MIDDLE_PLANES)
     sweep_planes(3, 12, e0, f1_ref, k1x_ref, k1y_ref, k1z_ref, 2, smooth(e1, wd1_ref))
 
     def keep_middle(x, value, left):
@@ -336,9 +381,10 @@
     cell = jnp.where(src < 192, src, src - RING)
     pick_low = (cell == 4 * (dst - COARSE_LOW)) & (dst < COARSE)
     pick_high = (cell == 4 * (dst - 64 - COARSE_LOW)) & (dst >= 64) & (dst < 64 + COARSE)
-    pick_low = pick_low.astype(F32)
-    pick_high = pick_high.astype(F32)
+    picks = jnp.concatenate([pick_low.astype(F32), pick_high.astype(F32)], axis=0)
     pick_middle = ((cell == 2 * (dst - MIDDLE_LOW)) & (dst < MIDDLE)).astype(F32)
+    firsts = []
+    seconds = []
     for j in range(4):
         i = 4 + 2 * j
         f2 = pair_sum(pair_sum(r1[i] + r1[i + 1], 2, 0), 2, 1) * 0.125
@@ -347,26 +393,49 @@
         k2y = upper_of(k2y, 2, 0) * (1.0 / 16.0)
         k2z = pair_sum(k1z_ref[i] + k1z_ref[i + 1], 2, 0)
         k2z = upper_of(k2z, 2, 1) * (1.0 / 16.0)
-        first = dot(f2, pick_low) + dot(k2x, pick_high)
-        second = dot(k2y, pick_low) + dot(k2z, pick_high)
-        for k in range(4):
-            line = pl.ds(8 + 4 * k, 1)
-            chunk_ref[0, pl.ds(4 * j + k, 1), :] = first[8 + 4 * k : 9 + 4 * k]
-            chunk_ref[0, pl.ds(16 + 4 * j + k, 1), :] = second[8 + 4 * k : 9 + 4 * k]
-    for i in range(8):
-        middle = dot(e1[4 + i], pick_middle)
-        for k in range(8):
-            chunk_ref[0, pl.ds(32 + 8 * i + k, 1), :] = middle[8 + 2 * k : 9 + 2 * k]
-    for k in range(1, 32):
-        chunk_ref[k] = chunk_ref[0]
+        firsts.append(jnp.concatenate([f2[8:24], k2x[8:24]], axis=1))
+        seconds.append(jnp.concatenate([k2y[8:24], k2z[8:24]], axis=1))
+    rows[...] = select_dot(jnp.concatenate(firsts + seconds, axis=0), picks)
+    coarse = rows[pl.ds(0, 32, stride=4), :]
+    rows[...] = select_dot(
+        jnp.concatenate([e1[4 + i, 8:24] for i in range(8)], axis=0), pick_middle
+    )
+    middle = rows[pl.ds(0, 64, stride=2), :]
+    own_ref[...] = middle
+    high = coarse.astype(BF16)
+    chunk = jnp.concatenate(
+        [high, (coarse - high.astype(F32)).astype(BF16), middle.astype(BF16)], axis=0
+    )
+    for k in range(32):
+        chunk_ref[k] = chunk
+    for copy in copies:
+        copy.wait()
 
 
 def up_kernel(
-    place_ref, all_ref, v_ref, side_ref, kx_ref, ky_ref, kz_ref, wd_ref,
-    f1_ref, k1x_ref, k1y_ref, k1z_ref, wd1_ref,
+    place_ref, all_ref, own_ref, side_in, kx_in, ky_in, kz_in, wd_in, v_in,
+    k1x_in, k1y_in, k1z_in, wd1_in, f1_in,
     out_ref,
-    pair0, pair1, c2x, c2y, c2z, wd2, f2, ea, eb, mid, e1a, e1b, va, vb,
+    side_ref, kx_ref, ky_ref, kz_ref, wd_ref, v_ref, k1x_ref, k1y_ref, k1z_ref, wd1_ref, f1_ref,
+    pair0, pair1, c2x, c2y, c2z, wd2, f2, ea, eb, mid, tall, lean, e1a, e1b, va, vb, sems,
 ):
+    copies = []
+    for planes, moves in (
+        (MIDDLE_PLANES, (
+            (k1x_in, k1x_ref), (k1y_in, k1y_ref), (k1z_in, k1z_ref), (wd1_in, wd1_ref),
+            (f1_in, f1_ref),
+        )),
+        (FINE_PLANES, (
+            (v_in, v_ref), (side_in, side_ref), (kx_in, kx_ref), (ky_in, ky_ref),
+            (kz_in, kz_ref), (wd_in, wd_ref),
+        )),
+    ):
+        for a, b in moves:
+            copies.append(
+                pltpu.make_async_copy(a.at[planes], b.at[planes], sems.at[len(copies)])
+            )
+    for copy in copies:
+        copy.start()
     gx = place_ref[0]
     gy = place_ref[1]
 
@@ -376,22 +445,28 @@
     for p in range(8):
         for q in range(4):
             s = source(p - 1, q - 1)
+            cells = all_ref[s, pl.ds(0, 32), :].astype(F32)
+            cells = cells + all_ref[s, pl.ds(32, 32), :].astype(F32)
             for i in range(4):
-                pair0[4 * p + i, pl.ds(4 * q, 4), :] = all_ref[s, pl.ds(4 * i, 4), :]
-                pair1[4 * p + i, pl.ds(4 * q, 4), :] = all_ref[s, pl.ds(16 + 4 * i, 4), :]
+                pair0[4 * p + i, pl.ds(4 * q, 4), :] = cells[4 * i : 4 * i + 4]
+                pair1[4 * p + i, pl.ds(4 * q, 4), :] = cells[16 + 4 * i : 20 + 4 * i]
     for p in (-1, 0, 1):
         for q in (-1, 0, 1):
-            s = source(p, q)
-            for i in range(16):
-                if (i - 4) // 8 != p or not 1 <= i <= 14:
+            if p == 0 and q == 0:
+                cells = own_ref[...]
+            else:
+                cells = all_ref[source(p, q), pl.ds(64, 64), :].astype(F32)
+            for i in range(1, 15):
+                if (i - 4) // 8 != p:
                     continue
-                start = 32 + 8 * ((i - 4) % 8)
+                start = 8 * ((i - 4) % 8)
+                block = cells[start : start + 8]
                 if q == -1:
-                    mid[i, pl.ds(0, 4), :] = all_ref[s, pl.ds(start + 4, 4), :]
+                    mid[i, pl.ds(0, 4), :] = block[4:]
                 elif q == 0:
-                    mid[i, pl.ds(4, 8), :] = all_ref[s, pl.ds(start, 8), :]
+                    mid[i, pl.ds(4, 8), :] = block
                 else:
-                    mid[i, pl.ds(12, 4), :] = all_ref[s, pl.ds(start, 4), :]
+                    mid[i, pl.ds(12, 4), :] = block[:4]
 
     used = iota((16, LANES), 1) < COARSE
     for x in range(32):
@@ -426,22 +501,29 @@
     lax.fori_loop(0, 3, two, 0)
     coarse_sweep(ea, eb)
 
+    lane = iota((8, LANES), 1)
+    for j in range(8):
+        line = roll(eb[2 + j, pl.ds(2, 8), :], MIDDLE, 1)
+        line = jnp.where((lane >= MIDDLE) & (lane < MIDDLE + COARSE), line, 0.0)
+        for k in range(4):
+            lean[j, pl.ds(k, 8, stride=4), :] = line
+    for i in range(1, 15):
+        line = mid[i]
+        for k in range(2):
+            tall[i, pl.ds(k, 16, stride=2), :] = line
     src = iota((LANES, RING), 0)
     dst = iota((LANES, RING), 1)
     cell = jnp.where(dst < 192, dst, dst - RING)
-    spread2 = ((cell + 4 * COARSE_LOW) // 4 == src) & (src < COARSE) & (cell >= -4 * COARSE_LOW)
-    spread2 = spread2.astype(F32)
-    spread1 = ((cell + 2 * MIDDLE_LOW) // 2 == src) & (src < MIDDLE) & (cell >= -2 * MIDDLE_LOW)
-    spread1 = spread1.astype(F32)
-    line = iota((32, 16), 0)
-    pick = iota((32, 16), 1)
-    rows2 = (line // 4 + 2 == pick).astype(F32)
-    rows1 = (line // 2 == pick).astype(F32)
-    for j in range(8):
-        coarse = dot(rows2, dot(eb[2 + j], spread2))
-        for i in (2 * j, 2 * j + 1):
-            if 1 <= i <= 14:
-                e1a[i] = coarse + dot(rows1, dot(mid[i], spread1))
+    middle = (cell >= -2 * MIDDLE_LOW) & (src < MIDDLE)
+    middle = middle & ((cell + 2 * MIDDLE_LOW) // 2 == src)
+    coarse = (cell >= -4 * COARSE_LOW) & (src >= MIDDLE) & (src < MIDDLE + COARSE)
+    coarse = coarse & ((cell + 4 * COARSE_LOW) // 4 == src - MIDDLE)
+    spread = (middle | coarse).astype(F32)
+    narrow = iota((32, LANES), 1) < MIDDLE
+    packed = [jnp.where(narrow, tall[i], lean[i // 2]) for i in range(1, 15)]
+    widened = select_dot(jnp.concatenate(packed, axis=0), spread)
+    for i in range(1, 15):
+        e1a[i] = widened[32 * (i - 1) : 32 * i]
 
     def smooth(target, weight):
         def use(x, value, left):
@@ -449,6 +531,8 @@
 
         return use
 
+    for copy in copies:
+        copy.wait()
     sweep_planes(2, 13, e1a, f1_ref, k1x_ref, k1y_ref, k1z_ref, 2, smooth(e1b, wd1_ref))
     sweep_planes(3, 12, e1b, f1_ref, k1x_ref, k1y_ref, k1z_ref, 2, smooth(e1a, wd1_ref))
     for x in range(6, 26):
@@ -470,48 +554,64 @@
 def body(conc, right_side, order_field, grain_ids):
     face = ((9, 16, LANES), BF16)
     zface = ((17, 16, LANES), BF16)
-    xm, xp, ym, yp, zm, zp = call(
-        faces_kernel, [face] * 4 + [zface] * 2, (order_field, grain_ids)
+    brick = ((16, 16, LANES), F32)
+    conc, side, order, ids, xm, xp, ym, yp, zm, zp = call(
+        faces_kernel,
+        [brick, brick, ((8, 16, 16, LANES), BF16), ((1, 1, 8, 8), jnp.int32)]
+        + [face] * 4
+        + [zface] * 2,
+        (conc, right_side, order_field, grain_ids),
+        specs=[HBM] * 4,
+        semaphores=4,
     )
     faces = (
         shift(xp, "gx", 1), shift(xm, "gx", -1),
         shift(yp, "gy", 1), shift(ym, "gy", -1),
         shift(zp, "gz", 1), shift(zm, "gz", -1),
     )
-    half = ((3, 16, 8, LANES), F32)
-    mobility, low, high = call(
+    mobility, keep, zm, zp = call(
         mobility_kernel,
-        [((16, 16, LANES), F32), half, half],
-        (conc, right_side, order_field, grain_ids) + faces + (ym, yp),
-        scratch=[((16, 16, LANES), F32), ((64, 8, LANES), F32)],
-    )
+        [brick] * 4,
+        (conc, side, order, ids) + faces + (ym, yp),
+        scratch=[brick, ((64, 8, LANES), F32)],
+    )
+    left = shift(zp, "gz", 1)
+    right = shift(zm, "gz", -1)
+    half = ((5, 16, 8, LANES), F32)
+    low, high = call(split_kernel, [half, half], (keep, conc, side, left, right))
     below = shift(high, "gy", 1)
     above = shift(low, "gy", -1)
-    slab = ((3, 8, 32, LANES), F32)
+    slab = ((5, 8, 32, LANES), F32)
     xl, xh = call(rows_kernel, [slab, slab], (below, low, high, above))
     before = shift(xh, "gx", 1)
     after = shift(xl, "gx", -1)
-    wide = ((32, 32, LANES), F32)
-    sm, sp = call(lanes_kernel, [wide, wide], (before, xl, xh, after))
-    left = shift(sp, "gz", 1)
-    right = shift(sm, "gz", -1)
     fine = ((32, 32, RING), F32)
     middle = ((16, 32, RING), F32)
-    results = call(
+    own, chunk, *kept = call(
         down_kernel,
-        [fine] * 6 + [middle] * 5 + [((32, 96, LANES), F32)],
-        (before, xl, xh, after, left, right),
-        scratch=[fine] * 3 + [middle] * 3,
-    )
-    chunks = lax.all_to_all(results[-1], ("gx", "gy"), 0, 0, tiled=True)
+        [((64, LANES), F32), ((32, LANES, LANES), BF16)] + [fine] * 6 + [middle] * 5,
+        (before, xl, xh, after),
+        scratch=[fine] * 9 + [middle] * 8 + [((LANES, LANES), F32)],
+        places=[VMEM] * 2 + [HBM] * 11,
+        limit=24,
+        semaphores=11,
+    )
+    chunks = lax.all_to_all(chunk, ("gx", "gy"), 0, 0, tiled=True)
     place = jnp.stack([lax.axis_index("gx"), lax.axis_index("gy")]).astype(jnp.int32)
     plane = ((32, 16, LANES), F32)
     (out,) = call(
         up_kernel,
-        [((16, 16, LANES), F32)],
-        (place, chunks) + tuple(results[:-1]),
-        scratch=[plane] * 9 + [((16, 16, LANES), F32)] + [middle] * 2 + [fine] * 2,
-        specs=[SMEM] + [VMEM] * 12,
+        [brick],
+        (place, chunks, own) + tuple(kept),
+        scratch=[fine] * 6
+        + [middle] * 5
+        + [plane] * 9
+        + [brick, ((16, 32, LANES), F32), ((8, 32, LANES), F32)]
+        + [middle] * 2
+        + [fine] * 2,
+        specs=[SMEM] + [VMEM] * 2 + [HBM] * 11,
+        limit=24,
+        semaphores=11,
     )
     return out, mobility
 

time: 157 us -> 116 us (0.74)
  Pallas kernels: 48.8 us -> 29.9 us
  local copies, waits for them, and re-layouts: 12.7 us -> 0 us
  waiting for transfers between devices: 46.6 us -> 37.4 us
    pallas_call x6, Pallas kernels: 48.8 us -> 29.9 us  [call(): pl.pallas_call(kernel, out_shape=[pltpu.MemorySpace.HBM(*out) if place is...]
    unnamed x34 -> x0, local copies, waits for them, and re-layouts: 12.7 us -> none
    all_to_all x1, waiting for transfers between devices: 21.4 us -> 15.9 us  [body(): chunks = lax.all_to_all(chunk, ('gx', 'gy'), 0, 0, tiled=True)]
    ppermute x12, waiting for transfers between devices: 25.2 us -> 21.5 us  [shift(): lax.ppermute(x, axis, [(i, (i + direction) % count) for i in range(count)])]
    ppermute x12, starting transfers between devices: 37.6 us -> 39.9 us  [shift(): lax.ppermute(x, axis, [(i, (i + direction) % count) for i in range(count)])]
    all_to_all x1, starting transfers between devices: 9.26 us -> 7.61 us  [body(): chunks = lax.all_to_all(chunk, ('gx', 'gy'), 0, 0, tiled=True)]
where the time goes in v2:
time: 116 us
  starting transfers between devices  47.5 us (41%)
  waiting for transfers between devices  37.4 us (32%)
  Pallas kernels  29.9 us (26%)
    ppermute x12, starting transfers between devices, shift(): lax.ppermute(x, axis, [(i, (i + direction) % count) for i in range(count)])  39.9 us
    pallas_call x6, Pallas kernels, call(): pl.pallas_call(kernel, out_shape=[pltpu.MemorySpace.HBM(*out) if place is...  29.9 us
    ppermute x12, waiting for transfers between devices, shift(): lax.ppermute(x, axis, [(i, (i + direction) % count) for i in range(count)])  21.5 us
    all_to_all x1, waiting for transfers between devices, body(): chunks = lax.all_to_all(chunk, ('gx', 'gy'), 0, 0, tiled=True)  15.9 us
    all_to_all x1, starting transfers between devices, body(): chunks = lax.all_to_all(chunk, ('gx', 'gy'), 0, 0, tiled=True)  7.61 us
  transfers between devices with their start and end apart: 13, of which 9 were waited for; matrix products, arithmetic and copies ran while one was open for 0% of the time, Pallas kernels for 0%

profile of v2, /device:TPU:1, one launch (start us, length us, event | category | flops | bytes accessed | tf_op | source)
XLA Modules:
  0.0 115.8 jit_solution(6286704885475800427)
XLA Ops:
  0.6 1.6 %shard_map.59 = (f32[16,16,128]{2,1,0:T(8,128)S(1)}, f32[16,16,128]{2,1,0:T(8,128)S(1)}, bf16[8,16,16,128]{3,2,1,0:T(8,128)(2,1)S(1)}, s32[1,1,8,8]{3,2,1,0:T(8,...) custom-call(f32[16,16,128]{2,1,0:T(8,128)} %conc_in.1, ...), custom_call_target="tpu_custom_call" | custom-call | tf_op jit(solution)/shard_map/pallas_call | solution.py:40
  2.2 3.9 %collective-permute-start.2 = (bf16[9,16,128]{2,1,0:T(8,128)(2,1)S(1)}, bf16[9,16,128]{2,1,0:T(8,128)(2,1)S(1)}, u32[]{:S(2)}, u32[]{:S(2)}) collective-permute-start(bf16[9,16,128]{2,1,0:T(8,128)(2,1)S(1)} %get-tuple-element.39.own_yp_ref), channel_id=1, source_target_pairs={{0,16},{16,32},{32,48},{48,0},{1,17},{17,33},{33,49},{49,1},{2,18}... | collective-permute-start | bytes 110600 | tf_op jit(solution)/shard_map/ppermute | solution.py:551
  6.2 3.5 %collective-permute-start.4 = (bf16[17,16,128]{2,1,0:T(8,128)(2,1)S(1)}, bf16[17,16,128]{2,1,0:T(8,128)(2,1)S(1)}, u32[]{:S(2)}, u32[]{:S(2)}) collective-permute-start(bf16[17,16,128]{2,1,0:T(8,128)(2,1)S(1)} %get-tuple-element.41), channel_id=1, source_target_pairs={{0,1},{1,2},{2,3},{3,4},{4,5},{5,6},{6,7},{7,8},{8,9},{9,10},{10,1... | collective-permute-start | bytes 208904 | tf_op jit(solution)/shard_map/ppermute | solution.py:551
  9.7 9.5 %collective-permute-start.5 = (bf16[17,16,128]{2,1,0:T(8,128)(2,1)S(1)}, bf16[17,16,128]{2,1,0:T(8,128)(2,1)S(1)}, u32[]{:S(2)}, u32[]{:S(2)}) collective-permute-start(bf16[17,16,128]{2,1,0:T(8,128)(2,1)S(1)} %get-tuple-element.42), channel_id=1, source_target_pairs={{0,15},{1,0},{2,1},{3,2},{4,3},{5,4},{6,5},{7,6},{8,7},{9,8},{10,9... | collective-permute-start | bytes 208904 | tf_op jit(solution)/shard_map/ppermute | solution.py:551
  19.2 3.4 %collective-permute-start.3 = (bf16[9,16,128]{2,1,0:T(8,128)(2,1)S(1)}, bf16[9,16,128]{2,1,0:T(8,128)(2,1)S(1)}, u32[]{:S(2)}, u32[]{:S(2)}) collective-permute-start(bf16[9,16,128]{2,1,0:T(8,128)(2,1)S(1)} %get-tuple-element.40.own_ym_ref), channel_id=1, source_target_pairs={{0,48},{16,0},{32,16},{48,32},{1,49},{17,1},{33,17},{49,33},{2,50}... | collective-permute-start | bytes 110600 | tf_op jit(solution)/shard_map/ppermute | solution.py:551
  22.6 2.7 %collective-permute-start = (bf16[9,16,128]{2,1,0:T(8,128)(2,1)S(1)}, bf16[9,16,128]{2,1,0:T(8,128)(2,1)S(1)}, u32[]{:S(2)}, u32[]{:S(2)}) collective-permute-start(bf16[9,16,128]{2,1,0:T(8,128)(2,1)S(1)} %get-tuple-element.37), channel_id=1, source_target_pairs={{0,64},{64,128},{128,192},{192,256},{256,320},{320,384},{384,448},... | collective-permute-start | bytes 110600 | tf_op jit(solution)/shard_map/ppermute | solution.py:551
  25.3 0.0 collective-permute-done.2.ym_ref
  25.3 0.0 collective-permute-start.1
  25.3 0.0 collective-permute-done.3.yp_ref
  25.4 1.1 collective-permute-done.xm_ref
  26.4 2.3 %collective-permute-done.1.xp_ref = bf16[9,16,128]{2,1,0:T(8,128)(2,1)S(1)} collective-permute-done((bf16[9,16,128]{2,1,0:T(8,128)(2,1)S(1)}, bf16[9,16,128]{2,1,0:T(8,128)(2,1)S(1)}, u32[]{:S(2)}, u32[]{:S(2)}) %collective-permute-start.1) | collective-permute-done | bytes 36896 | tf_op jit(solution)/shard_map/ppermute | solution.py:551
  28.7 0.0 collective-permute-done.4.zm_ref
  28.7 0.0 collective-permute-done.5.zp_ref
  28.7 2.8 %shard_map.60 = (f32[16,16,128]{2,1,0:T(8,128)}, f32[16,16,128]{2,1,0:T(8,128)S(1)}, f32[16,16,128]{2,1,0:T(8,128)S(1)}, f32[16,16,128]{2,1,0:T(8,128)S(1)}) custom-call(f32[16,16,128]{2,1,0:T(8,128)S(1)} %get-tuple-element.33.conc_ref, f32[16,16,128]{2,1,0:T(8,128)S(1)} %get-tuple-element.34.side_ref, ...), custom_call_target="tpu_custom_call" | custom-call | tf_op jit(solution)/shard_map/pallas_call | solution.py:40
  31.5 1.9 %collective-permute-start.6 = (f32[16,16,128]{2,1,0:T(8,128)S(1)}, f32[16,16,128]{2,1,0:T(8,128)S(1)}, u32[]{:S(2)}, u32[]{:S(2)}) collective-permute-start(f32[16,16,128]{2,1,0:T(8,128)S(1)} %get-tuple-element.44), channel_id=1, source_target_pairs={{0,1},{1,2},{2,3},{3,4},{4,5},{5,6},{6,7},{7,8},{8,9},{9,10},{10,1... | collective-permute-start | bytes 393224 | tf_op jit(solution)/shard_map/ppermute | solution.py:551
  33.4 4.6 %collective-permute-start.7 = (f32[16,16,128]{2,1,0:T(8,128)S(1)}, f32[16,16,128]{2,1,0:T(8,128)S(1)}, u32[]{:S(2)}, u32[]{:S(2)}) collective-permute-start(f32[16,16,128]{2,1,0:T(8,128)S(1)} %get-tuple-element.45), channel_id=1, source_target_pairs={{0,15},{1,0},{2,1},{3,2},{4,3},{5,4},{6,5},{7,6},{8,7},{9,8},{10,9... | collective-permute-start | bytes 393224 | tf_op jit(solution)/shard_map/ppermute | solution.py:551
  38.0 1.7 %collective-permute-done.6.zm_ref = f32[16,16,128]{2,1,0:T(8,128)S(1)} collective-permute-done((f32[16,16,128]{2,1,0:T(8,128)S(1)}, f32[16,16,128]{2,1,0:T(8,128)S(1)}, u32[]{:S(2)}, u32[]{:S(2)}) %collective-permute-start.6) | collective-permute-done | bytes 131104 | tf_op jit(solution)/shard_map/ppermute | solution.py:551
  39.7 0.9 collective-permute-done.7.zp_ref
  40.6 1.9 %collective-permute-start.8 = (f32[5,16,8,128]{3,2,1,0:T(8,128)S(1)}, f32[5,16,8,128]{3,2,1,0:T(8,128)S(1)}, u32[]{:S(2)}, u32[]{:S(2)}) collective-permute-start(f32[5,16,8,128]{3,2,1,0:T(8,128)S(1)} %get-tuple-element.46.high_ref), channel_id=1, source_target_pairs={{0,16},{16,32},{32,48},{48,0},{1,17},{17,33},{33,49},{49,1},{2,18}... | collective-permute-start | bytes 983048 | tf_op jit(solution)/shard_map/ppermute | solution.py:551
  42.5 4.6 %collective-permute-start.9 = (f32[5,16,8,128]{3,2,1,0:T(8,128)S(1)}, f32[5,16,8,128]{3,2,1,0:T(8,128)S(1)}, u32[]{:S(2)}, u32[]{:S(2)}) collective-permute-start(f32[5,16,8,128]{3,2,1,0:T(8,128)S(1)} %get-tuple-element.47.low_ref), channel_id=1, source_target_pairs={{0,48},{16,0},{32,16},{48,32},{1,49},{17,1},{33,17},{49,33},{2,50}... | collective-permute-start | bytes 983048 | tf_op jit(solution)/shard_map/ppermute | solution.py:551
  47.1 4.7 %collective-permute-done.8.below_ref = f32[5,16,8,128]{3,2,1,0:T(8,128)S(1)} collective-permute-done((f32[5,16,8,128]{3,2,1,0:T(8,128)S(1)}, f32[5,16,8,128]{3,2,1,0:T(8,128)S(1)}, u32[]{:S(2)}, u32[]{:S(2)}) %collective-permute-start.8) | collective-permute-done | bytes 327712 | tf_op jit(solution)/shard_map/ppermute | solution.py:551
  51.8 0.9 collective-permute-done.9.above_ref
  52.7 0.2 shard_map.62
  52.8 3.8 %collective-permute-start.10 = (f32[5,8,32,128]{3,2,1,0:T(8,128)S(1)}, f32[5,8,32,128]{3,2,1,0:T(8,128)S(1)}, u32[]{:S(2)}, u32[]{:S(2)}) collective-permute-start(f32[5,8,32,128]{3,2,1,0:T(8,128)S(1)} %get-tuple-element.48.xh_ref), channel_id=1, source_target_pairs={{0,64},{64,128},{128,192},{192,256},{256,320},{320,384},{384,448},... | collective-permute-start | bytes 1966088 | tf_op jit(solution)/shard_map/ppermute | solution.py:551
  56.7 0.0 collective-permute-start.11
  56.7 7.5 %collective-permute-done.10.xm_ref = f32[5,8,32,128]{3,2,1,0:T(8,128)S(1)} collective-permute-done((f32[5,8,32,128]{3,2,1,0:T(8,128)S(1)}, f32[5,8,32,128]{3,2,1,0:T(8,128)S(1)}, u32[]{:S(2)}, u32[]{:S(2)}) %collective-permute-start.10) | collective-permute-done | bytes 655392 | tf_op jit(solution)/shard_map/ppermute | solution.py:551
  64.2 2.5 %collective-permute-done.11.xp_ref = f32[5,8,32,128]{3,2,1,0:T(8,128)S(1)} collective-permute-done((f32[5,8,32,128]{3,2,1,0:T(8,128)S(1)}, f32[5,8,32,128]{3,2,1,0:T(8,128)S(1)}, u32[]{:S(2)}, u32[]{:S(2)}) %collective-permute-start.11) | collective-permute-done | bytes 655392 | tf_op jit(solution)/shard_map/ppermute | solution.py:551
  66.7 15.4 %shard_map.63 = (f32[64,128]{1,0:T(8,128)S(1)}, bf16[32,128,128]{2,1,0:T(8,128)(2,1)}, f32[32,32,256]{2,1,0:T(8,128)}, f32[32,32,256]{2,1,0:T(8,128)}, f32[32,32...) custom-call(f32[5,8,32,128]{3,2,1,0:T(8,128)S(1)} %collective-permut, ...), custom_call_target="tpu_custom_call" | custom-call | tf_op jit(solution)/shard_map/pallas_call | solution.py:40
  82.1 7.6 %all-to-all-start = ((bf16[32,128,128]{2,1,0:T(8,128)(2,1)}), bf16[32,128,128]{2,1,0:T(8,128)(2,1)S(1)}, u32[]{:S(2)}, u32[]{:S(2)}) async-start(bf16[32,128,128]{2,1,0:T(8,128)(2,1)} %get-tuple-element.50), calls=%async_computation | async-start | bytes 2097152 | tf_op jit(solution)/shard_map/all_to_all | solution.py:599
  89.8 0.1 pad_add_fusion.place_ref
  89.8 15.9 %all-to-all-done.all_ref = bf16[32,128,128]{2,1,0:T(8,128)(2,1)S(1)} async-done(((bf16[32,128,128]{2,1,0:T(8,128)(2,1)}), bf16[32,128,128]{2,1,0:T(8,128)(2,1)S(1)}, u32[]{:S(2)}, u32[]{:S(2)}) %all-to-all-start) | async-done | bytes 1048608 | tf_op jit(solution)/shard_map/all_to_all | solution.py:599
  105.8 9.9 %shard_map.64 = f32[16,16,128]{2,1,0:T(8,128)} custom-call(s32[2]{0:T(128)S(1)} %pad_add_fusion.place_ref, bf16[32,128,128]{2,1,0:T(8,128)(2,1)S(1)} %all-to-all-done.all_ref, f32[64,128]{1,0:T(8,128)S(1)} %get-tuple-element.51.own_ref, f32[32,32,256]{2,1,0:T(8,128)} %get-tuple-element.52.side_in, f32[32,32,256]{2,1,0:T(8,128)} %get-tuple-element.53.kx_in, ...), custom_call_target="tpu_custom_call" | custom-call | tf_op jit(solution)/shard_map/pallas_call | solution.py:40
  (1 shorter events, 0.0 us)
Async XLA Ops:
  2.2 23.1 %collective-permute-start.2 = (bf16[9,16,128]{2,1,0:T(8,128)(2,1)S(1)}, bf16[9,16,128]{2,1,0:T(8,128)(2,1)S(1)}, u32[]{:S(2)}, u32[]{:S(2)}) collective-permute-start(bf16[9,16,128]{2,1,0:T(8,128)(2,1)S(1)} %get-tuple-element.39.own_yp_ref), channel_id=1, source_target_pairs={{0,16},{16,32},{32,48},{48,0},{1,17},{17,33},{33,49},{49,1},{2,18}... | collective-permute-start | bytes 110600 | tf_op jit(solution)/shard_map/ppermute | solution.py:551
  6.2 22.5 %collective-permute-start.4 = (bf16[17,16,128]{2,1,0:T(8,128)(2,1)S(1)}, bf16[17,16,128]{2,1,0:T(8,128)(2,1)S(1)}, u32[]{:S(2)}, u32[]{:S(2)}) collective-permute-start(bf16[17,16,128]{2,1,0:T(8,128)(2,1)S(1)} %get-tuple-element.41), channel_id=1, source_target_pairs={{0,1},{1,2},{2,3},{3,4},{4,5},{5,6},{6,7},{7,8},{8,9},{9,10},{10,1... | collective-permute-start | bytes 208904 | tf_op jit(solution)/shard_map/ppermute | solution.py:551
  9.7 19.0 %collective-permute-start.5 = (bf16[17,16,128]{2,1,0:T(8,128)(2,1)S(1)}, bf16[17,16,128]{2,1,0:T(8,128)(2,1)S(1)}, u32[]{:S(2)}, u32[]{:S(2)}) collective-permute-start(bf16[17,16,128]{2,1,0:T(8,128)(2,1)S(1)} %get-tuple-element.42), channel_id=1, source_target_pairs={{0,15},{1,0},{2,1},{3,2},{4,3},{5,4},{6,5},{7,6},{8,7},{9,8},{10,9... | collective-permute-start | bytes 208904 | tf_op jit(solution)/shard_map/ppermute | solution.py:551
  19.2 6.1 %collective-permute-start.3 = (bf16[9,16,128]{2,1,0:T(8,128)(2,1)S(1)}, bf16[9,16,128]{2,1,0:T(8,128)(2,1)S(1)}, u32[]{:S(2)}, u32[]{:S(2)}) collective-permute-start(bf16[9,16,128]{2,1,0:T(8,128)(2,1)S(1)} %get-tuple-element.40.own_ym_ref), channel_id=1, source_target_pairs={{0,48},{16,0},{32,16},{48,32},{1,49},{17,1},{33,17},{49,33},{2,50}... | collective-permute-start | bytes 110600 | tf_op jit(solution)/shard_map/ppermute | solution.py:551
  22.6 3.8 %collective-permute-start = (bf16[9,16,128]{2,1,0:T(8,128)(2,1)S(1)}, bf16[9,16,128]{2,1,0:T(8,128)(2,1)S(1)}, u32[]{:S(2)}, u32[]{:S(2)}) collective-permute-start(bf16[9,16,128]{2,1,0:T(8,128)(2,1)S(1)} %get-tuple-element.37), channel_id=1, source_target_pairs={{0,64},{64,128},{128,192},{192,256},{256,320},{320,384},{384,448},... | collective-permute-start | bytes 110600 | tf_op jit(solution)/shard_map/ppermute | solution.py:551
  25.3 3.4 %collective-permute-start.1 = (bf16[9,16,128]{2,1,0:T(8,128)(2,1)S(1)}, bf16[9,16,128]{2,1,0:T(8,128)(2,1)S(1)}, u32[]{:S(2)}, u32[]{:S(2)}) collective-permute-start(bf16[9,16,128]{2,1,0:T(8,128)(2,1)S(1)} %get-tuple-element.38), channel_id=1, source_target_pairs={{0,448},{64,0},{128,64},{192,128},{256,192},{320,256},{384,320},{4... | collective-permute-start | bytes 110600 | tf_op jit(solution)/shard_map/ppermute | solution.py:551
  31.5 8.2 %collective-permute-start.6 = (f32[16,16,128]{2,1,0:T(8,128)S(1)}, f32[16,16,128]{2,1,0:T(8,128)S(1)}, u32[]{:S(2)}, u32[]{:S(2)}) collective-permute-start(f32[16,16,128]{2,1,0:T(8,128)S(1)} %get-tuple-element.44), channel_id=1, source_target_pairs={{0,1},{1,2},{2,3},{3,4},{4,5},{5,6},{6,7},{7,8},{8,9},{9,10},{10,1... | collective-permute-start | bytes 393224 | tf_op jit(solution)/shard_map/ppermute | solution.py:551
  33.4 7.1 %collective-permute-start.7 = (f32[16,16,128]{2,1,0:T(8,128)S(1)}, f32[16,16,128]{2,1,0:T(8,128)S(1)}, u32[]{:S(2)}, u32[]{:S(2)}) collective-permute-start(f32[16,16,128]{2,1,0:T(8,128)S(1)} %get-tuple-element.45), channel_id=1, source_target_pairs={{0,15},{1,0},{2,1},{3,2},{4,3},{5,4},{6,5},{7,6},{8,7},{9,8},{10,9... | collective-permute-start | bytes 393224 | tf_op jit(solution)/shard_map/ppermute | solution.py:551
  40.6 11.2 %collective-permute-start.8 = (f32[5,16,8,128]{3,2,1,0:T(8,128)S(1)}, f32[5,16,8,128]{3,2,1,0:T(8,128)S(1)}, u32[]{:S(2)}, u32[]{:S(2)}) collective-permute-start(f32[5,16,8,128]{3,2,1,0:T(8,128)S(1)} %get-tuple-element.46.high_ref), channel_id=1, source_target_pairs={{0,16},{16,32},{32,48},{48,0},{1,17},{17,33},{33,49},{49,1},{2,18}... | collective-permute-start | bytes 983048 | tf_op jit(solution)/shard_map/ppermute | solution.py:551
  42.5 10.1 %collective-permute-start.9 = (f32[5,16,8,128]{3,2,1,0:T(8,128)S(1)}, f32[5,16,8,128]{3,2,1,0:T(8,128)S(1)}, u32[]{:S(2)}, u32[]{:S(2)}) collective-permute-start(f32[5,16,8,128]{3,2,1,0:T(8,128)S(1)} %get-tuple-element.47.low_ref), channel_id=1, source_target_pairs={{0,48},{16,0},{32,16},{48,32},{1,49},{17,1},{33,17},{49,33},{2,50}... | collective-permute-start | bytes 983048 | tf_op jit(solution)/shard_map/ppermute | solution.py:551
  52.8 11.4 %collective-permute-start.10 = (f32[5,8,32,128]{3,2,1,0:T(8,128)S(1)}, f32[5,8,32,128]{3,2,1,0:T(8,128)S(1)}, u32[]{:S(2)}, u32[]{:S(2)}) collective-permute-start(f32[5,8,32,128]{3,2,1,0:T(8,128)S(1)} %get-tuple-element.48.xh_ref), channel_id=1, source_target_pairs={{0,64},{64,128},{128,192},{192,256},{256,320},{320,384},{384,448},... | collective-permute-start | bytes 1966088 | tf_op jit(solution)/shard_map/ppermute | solution.py:551
  56.7 10.0 %collective-permute-start.11 = (f32[5,8,32,128]{3,2,1,0:T(8,128)S(1)}, f32[5,8,32,128]{3,2,1,0:T(8,128)S(1)}, u32[]{:S(2)}, u32[]{:S(2)}) collective-permute-start(f32[5,8,32,128]{3,2,1,0:T(8,128)S(1)} %get-tuple-element.49.xl_ref), channel_id=1, source_target_pairs={{0,448},{64,0},{128,64},{192,128},{256,192},{320,256},{384,320},{4... | collective-permute-start | bytes 1966088 | tf_op jit(solution)/shard_map/ppermute | solution.py:551
  82.1 23.6 %all-to-all-start = ((bf16[32,128,128]{2,1,0:T(8,128)(2,1)}), bf16[32,128,128]{2,1,0:T(8,128)(2,1)S(1)}, u32[]{:S(2)}, u32[]{:S(2)}) async-start(bf16[32,128,128]{2,1,0:T(8,128)(2,1)} %get-tuple-element.50), calls=%async_computation | async-start | bytes 2097152 | tf_op jit(solution)/shard_map/all_to_all | solution.py:599

commit v3 on v2

--- a/solution.py
+++ b/solution.py
@@ -23,6 +23,7 @@
 COARSE_LOW = 10
 MIDDLE = 70
 MIDDLE_LOW = 3
+CHUNK = 112
 FINE_PLANES = pl.ds(6, 20)
 MIDDLE_PLANES = pl.ds(1, 13)
 
@@ -220,18 +221,20 @@
         mob_ref[x] = value
         keep_ref[x] = value
         conc, side = conc_ref[x], side_ref[x]
-        zm_out[x] = jnp.where(
+        first = jnp.where(
             lane < 43, value, jnp.where(lane < 86, roll(conc, 43, 1), roll(side, 86, 1))
         )
-        zp_out[x] = jnp.where(
+        zm_out[x] = first.astype(BF16)
+        final = jnp.where(
             lane >= 85, value, jnp.where(lane >= 42, roll(conc, -43, 1), roll(side, -86, 1))
         )
+        zp_out[x] = final.astype(BF16)
 
 
 def split_kernel(mob_ref, conc_ref, side_ref, zm_ref, zp_ref, low_ref, high_ref):
     for place, ref in enumerate((mob_ref, conc_ref, side_ref, zm_ref, zp_ref)):
-        low_ref[place] = ref[:, :8]
-        high_ref[place] = ref[:, 8:]
+        low_ref[place] = ref[:, :8].astype(BF16)
+        high_ref[place] = ref[:, 8:].astype(BF16)
 
 
 def rows_kernel(below_ref, low_ref, high_ref, above_ref, xl_ref, xh_ref):
@@ -276,7 +279,7 @@
 
 
 def down_kernel(
-    xm_ref, xl_ref, xh_ref, xp_ref,
+    mob_in, conc_in, side_in, zm_ref, zp_ref, below_ref, above_ref, xm_ref, xp_ref,
     own_ref, chunk_ref, side_out, kx_out, ky_out, kz_out, wd_out, v_out,
     k1x_out, k1y_out, k1z_out, wd1_out, f1_out,
     mob, v0, res, v_ref, side_ref, kx_ref, ky_ref, kz_ref, wd_ref,
@@ -290,20 +293,29 @@
         copies.append(copy)
 
     lane = iota((32, LANES), 1)
-    for place, ref in enumerate((xm_ref, xl_ref, xh_ref, xp_ref)):
-        for i in range(8):
-            x = 8 * place + i
-            down, up = ref[3, i], ref[4, i]
-            mob[x, :, :LANES] = ref[0, i]
-            mob[x, :, LANES:] = jnp.where(lane < 43, up, jnp.where(lane >= 85, down, 1.0))
-            v0[x, :, :LANES] = ref[1, i]
-            v0[x, :, LANES:] = jnp.where(
-                lane < 43, roll(up, -43, 1), jnp.where(lane >= 85, roll(down, 43, 1), 0.0)
-            )
-            side_ref[x, :, :LANES] = ref[2, i]
-            side_ref[x, :, LANES:] = jnp.where(
-                lane < 42, roll(up, -86, 1), jnp.where(lane >= 86, roll(down, 86, 1), 0.0)
-            )
+
+    def own_plane(x, place, ref):
+        parts = (below_ref[place, x], ref[x], above_ref[place, x])
+        return jnp.concatenate([part.astype(F32) for part in parts], axis=0)
+
+    own = (mob_in, conc_in, side_in, zm_ref, zp_ref)
+    for x in range(32):
+        if 8 <= x < 24:
+            parts = [own_plane(x - 8, place, ref) for place, ref in enumerate(own)]
+        else:
+            ref = xm_ref if x < 8 else xp_ref
+            parts = [ref[place, x % 8].astype(F32) for place in range(5)]
+        mob[x, :, :LANES] = parts[0]
+        v0[x, :, :LANES] = parts[1]
+        side_ref[x, :, :LANES] = parts[2]
+        down, up = parts[3], parts[4]
+        mob[x, :, LANES:] = jnp.where(lane < 43, up, jnp.where(lane >= 85, down, 1.0))
+        v0[x, :, LANES:] = jnp.where(
+            lane < 43, roll(up, -43, 1), jnp.where(lane >= 85, roll(down, 43, 1), 0.0)
+        )
+        side_ref[x, :, LANES:] = jnp.where(
+            lane < 42, roll(up, -86, 1), jnp.where(lane >= 86, roll(down, 86, 1), 0.0)
+        )
 
     half = TAU / 2
 
@@ -403,9 +415,8 @@
     middle = rows[pl.ds(0, 64, stride=2), :]
     own_ref[...] = middle
     high = coarse.astype(BF16)
-    chunk = jnp.concatenate(
-        [high, (coarse - high.astype(F32)).astype(BF16), middle.astype(BF16)], axis=0
-    )
+    low = (coarse[:16] - high[:16].astype(F32)).astype(BF16)
+    chunk = jnp.concatenate([high, low, middle.astype(BF16)], axis=0)
     for k in range(32):
         chunk_ref[k] = chunk
     for copy in copies:
@@ -442,20 +453,21 @@
     def source(dx, dy):
         return ((gx + dx + 8) & 7) * 4 + ((gy + dy + 4) & 3)
 
-    for p in range(8):
+    for p in (0, 1, 2, 3, 4, 6, 7):
         for q in range(4):
             s = source(p - 1, q - 1)
-            cells = all_ref[s, pl.ds(0, 32), :].astype(F32)
-            cells = cells + all_ref[s, pl.ds(32, 32), :].astype(F32)
+            first = all_ref[s, pl.ds(0, 16), :].astype(F32)
+            first = first + all_ref[s, pl.ds(32, 16), :].astype(F32)
+            second = all_ref[s, pl.ds(16, 16), :].astype(F32)
             for i in range(4):
-                pair0[4 * p + i, pl.ds(4 * q, 4), :] = cells[4 * i : 4 * i + 4]
-                pair1[4 * p + i, pl.ds(4 * q, 4), :] = cells[16 + 4 * i : 20 + 4 * i]
+                pair0[4 * p + i, pl.ds(4 * q, 4), :] = first[4 * i : 4 * i + 4]
+                pair1[4 * p + i, pl.ds(4 * q, 4), :] = second[4 * i : 4 * i + 4]
     for p in (-1, 0, 1):
         for q in (-1, 0, 1):
             if p == 0 and q == 0:
                 cells = own_ref[...]
             else:
-                cells = all_ref[source(p, q), pl.ds(64, 64), :].astype(F32)
+                cells = all_ref[source(p, q), pl.ds(48, 64), :].astype(F32)
             for i in range(1, 15):
                 if (i - 4) // 8 != p:
                     continue
@@ -469,41 +481,42 @@
                     mid[i, pl.ds(12, 4), :] = block[:4]
 
     used = iota((16, LANES), 1) < COARSE
-    for x in range(32):
-        first = pair0[x]
-        second = pair1[x]
-        f2[x] = jnp.where(used, first, 0.0)
-        c2x[x] = jnp.where(used, roll(first, 64, 1), 0.0)
-        c2y[x] = jnp.where(used, second, 0.0)
-        c2z[x] = jnp.where(used, roll(second, 64, 1), 0.0)
-    for x in range(32):
-        ky = c2y[x]
-        kz = c2z[x]
-        total = (c2x[x] + c2x[(x + 31) % 32]) + (ky + roll(ky, 1, 0)) + (kz + roll(kz, 1, 1))
+    for x in range(-6, 17):
+        k = x % 32
+        first = pair0[k]
+        second = pair1[k]
+        f2[k] = jnp.where(used, first, 0.0)
+        c2x[k] = jnp.where(used, roll(first, 64, 1), 0.0)
+        c2y[k] = jnp.where(used, second, 0.0)
+        c2z[k] = jnp.where(used, roll(second, 64, 1), 0.0)
+    for x in range(-5, 17):
+        k = x % 32
+        ky = c2y[k]
+        kz = c2z[k]
+        total = (c2x[k] + c2x[(x - 1) % 32]) + (ky + roll(ky, 1, 0)) + (kz + roll(kz, 1, 1))
         weight = OMEGA / (1.0 + total)
-        wd2[x] = weight
-        ea[x] = weight * f2[x]
-
-    def coarse_sweep(old, new):
-        before = c2x[31] * (old[0] - old[31])
-        for x in range(32):
-            value = old[x]
-            flux = c2x[x] * (old[(x + 1) % 32] - value)
-            left = residual(value, f2[x], flux, before, c2y[x], c2z[x], 1)
-            new[x] = value + wd2[x] * left
+        wd2[k] = weight
+        ea[k] = weight * f2[k]
+
+    old, new = ea, eb
+    for reach in range(6, -1, -1):
+        first = 2 - reach
+        value = old[first % 32]
+        below = (first - 1) % 32
+        before = c2x[below] * (value - old[below])
+        for x in range(first, 10 + reach):
+            k = x % 32
+            above = old[(x + 1) % 32]
+            flux = c2x[k] * (above - value)
+            left = residual(value, f2[k], flux, before, c2y[k], c2z[k], 1)
+            new[k] = value + wd2[k] * left
             before = flux
-
-    def two(_, c):
-        coarse_sweep(ea, eb)
-        coarse_sweep(eb, ea)
-        return c
-
-    lax.fori_loop(0, 3, two, 0)
-    coarse_sweep(ea, eb)
+            value = above
+        old, new = new, old
 
     lane = iota((8, LANES), 1)
     for j in range(8):
-        line = roll(eb[2 + j, pl.ds(2, 8), :], MIDDLE, 1)
+        line = roll(old[2 + j, pl.ds(2, 8), :], MIDDLE, 1)
         line = jnp.where((lane >= MIDDLE) & (lane < MIDDLE + COARSE), line, 0.0)
         for k in range(4):
             lean[j, pl.ds(k, 8, stride=4), :] = line
@@ -569,19 +582,20 @@
         shift(yp, "gy", 1), shift(ym, "gy", -1),
         shift(zp, "gz", 1), shift(zm, "gz", -1),
     )
+    pack = ((16, 16, LANES), BF16)
     mobility, keep, zm, zp = call(
         mobility_kernel,
-        [brick] * 4,
+        [brick, brick, pack, pack],
         (conc, side, order, ids) + faces + (ym, yp),
         scratch=[brick, ((64, 8, LANES), F32)],
     )
     left = shift(zp, "gz", 1)
     right = shift(zm, "gz", -1)
-    half = ((5, 16, 8, LANES), F32)
+    half = ((5, 16, 8, LANES), BF16)
     low, high = call(split_kernel, [half, half], (keep, conc, side, left, right))
     below = shift(high, "gy", 1)
     above = shift(low, "gy", -1)
-    slab = ((5, 8, 32, LANES), F32)
+    slab = ((5, 8, 32, LANES), BF16)
     xl, xh = call(rows_kernel, [slab, slab], (below, low, high, above))
     before = shift(xh, "gx", 1)
     after = shift(xl, "gx", -1)
@@ -589,15 +603,16 @@
     middle = ((16, 32, RING), F32)
     own, chunk, *kept = call(
         down_kernel,
-        [((64, LANES), F32), ((32, LANES, LANES), BF16)] + [fine] * 6 + [middle] * 5,
-        (before, xl, xh, after),
+        [((64, LANES), F32), ((32, CHUNK, LANES), BF16)] + [fine] * 6 + [middle] * 5,
+        (keep, conc, side, left, right, below, above, before, after),
         scratch=[fine] * 9 + [middle] * 8 + [((LANES, LANES), F32)],
         places=[VMEM] * 2 + [HBM] * 11,
         limit=24,
         semaphores=11,
     )
+    place = jnp.stack([lax.axis_index("gx"), lax.axis_index("gy")]).astype(jnp.int32)
+    chunk, place = lax.optimization_barrier((chunk, place))
     chunks = lax.all_to_all(chunk, ("gx", "gy"), 0, 0, tiled=True)
-    place = jnp.stack([lax.axis_index("gx"), lax.axis_index("gy")]).astype(jnp.int32)
     plane = ((32, 16, LANES), F32)
     (out,) = call(
         up_kernel,

time: 116 us -> 104 us (0.90)
  waiting for transfers between devices: 37.4 us -> 13.4 us
  blocking collectives: 0 us -> 22.2 us
  starting transfers between devices: 47.5 us -> 39.5 us
  Pallas kernels: 29.9 us -> 27.7 us
    all_to_all x0 -> x1, blocking collectives: none -> 22.2 us  [body(): chunks = lax.all_to_all(chunk, ('gx', 'gy'), 0, 0, tiled=True)]
    all_to_all x1 -> x0, waiting for transfers between devices: 15.9 us -> none  [body(): chunks = lax.all_to_all(chunk, ('gx', 'gy'), 0, 0, tiled=True)]
    ppermute x12, waiting for transfers between devices: 21.5 us -> 13.4 us  [shift(): lax.ppermute(x, axis, [(i, (i + direction) % count) for i in range(count)])]
    all_to_all x1 -> x0, starting transfers between devices: 7.61 us -> none  [body(): chunks = lax.all_to_all(chunk, ('gx', 'gy'), 0, 0, tiled=True)]
    pallas_call x6, Pallas kernels: 29.9 us -> 27.7 us  [call(): pl.pallas_call(kernel, out_shape=[pltpu.MemorySpace.HBM(*out) if place is...]
  transfers between devices with their start and end apart: 13 -> 12, of which waited for: 9 -> 8; matrix products, arithmetic and copies ran while one was open for 0% -> 0% of each run, Pallas kernels for 0% -> 0%
where the time goes in v3:
time: 104 us
  starting transfers between devices  39.5 us (38%)
  Pallas kernels  27.7 us (27%)
  blocking collectives  22.2 us (21%)
  waiting for transfers between devices  13.4 us (13%)
    ppermute x12, starting transfers between devices, shift(): lax.ppermute(x, axis, [(i, (i + direction) % count) for i in range(count)])  39.5 us
    pallas_call x6, Pallas kernels, call(): pl.pallas_call(kernel, out_shape=[pltpu.MemorySpace.HBM(*out) if place is...  27.7 us
    all_to_all x1, blocking collectives, body(): chunks = lax.all_to_all(chunk, ('gx', 'gy'), 0, 0, tiled=True)  22.2 us
    ppermute x12, waiting for transfers between devices, shift(): lax.ppermute(x, axis, [(i, (i + direction) % count) for i in range(count)])  13.4 us
  transfers between devices with their start and end apart: 12, of which 8 were waited for; matrix products, arithmetic and copies ran while one was open for 0% of the time, Pallas kernels for 0%

profile of v3, /device:TPU:1, one launch (start us, length us, event | category | flops | bytes accessed | tf_op | source)
XLA Modules:
  0.0 103.7 jit_solution(18192542451257907616)
XLA Ops:
  0.6 1.6 %shard_map.59 = (f32[16,16,128]{2,1,0:T(8,128)S(1)}, f32[16,16,128]{2,1,0:T(8,128)S(1)}, bf16[8,16,16,128]{3,2,1,0:T(8,128)(2,1)S(1)}, s32[1,1,8,8]{3,2,1,0:T(8,...) custom-call(f32[16,16,128]{2,1,0:T(8,128)} %conc_in.1, ...), custom_call_target="tpu_custom_call" | custom-call | tf_op jit(solution)/shard_map/pallas_call | solution.py:41
  2.2 3.9 %collective-permute-start.2 = (bf16[9,16,128]{2,1,0:T(8,128)(2,1)S(1)}, bf16[9,16,128]{2,1,0:T(8,128)(2,1)S(1)}, u32[]{:S(2)}, u32[]{:S(2)}) collective-permute-start(bf16[9,16,128]{2,1,0:T(8,128)(2,1)S(1)} %get-tuple-element.41.own_yp_ref), channel_id=1, source_target_pairs={{0,16},{16,32},{32,48},{48,0},{1,17},{17,33},{33,49},{49,1},{2,18}... | collective-permute-start | bytes 110600 | tf_op jit(solution)/shard_map/ppermute | solution.py:564
  6.2 3.5 %collective-permute-start.4 = (bf16[17,16,128]{2,1,0:T(8,128)(2,1)S(1)}, bf16[17,16,128]{2,1,0:T(8,128)(2,1)S(1)}, u32[]{:S(2)}, u32[]{:S(2)}) collective-permute-start(bf16[17,16,128]{2,1,0:T(8,128)(2,1)S(1)} %get-tuple-element.43), channel_id=1, source_target_pairs={{0,1},{1,2},{2,3},{3,4},{4,5},{5,6},{6,7},{7,8},{8,9},{9,10},{10,1... | collective-permute-start | bytes 208904 | tf_op jit(solution)/shard_map/ppermute | solution.py:564
  9.7 9.5 %collective-permute-start.5 = (bf16[17,16,128]{2,1,0:T(8,128)(2,1)S(1)}, bf16[17,16,128]{2,1,0:T(8,128)(2,1)S(1)}, u32[]{:S(2)}, u32[]{:S(2)}) collective-permute-start(bf16[17,16,128]{2,1,0:T(8,128)(2,1)S(1)} %get-tuple-element.44), channel_id=1, source_target_pairs={{0,15},{1,0},{2,1},{3,2},{4,3},{5,4},{6,5},{7,6},{8,7},{9,8},{10,9... | collective-permute-start | bytes 208904 | tf_op jit(solution)/shard_map/ppermute | solution.py:564
  19.2 3.4 %collective-permute-start.3 = (bf16[9,16,128]{2,1,0:T(8,128)(2,1)S(1)}, bf16[9,16,128]{2,1,0:T(8,128)(2,1)S(1)}, u32[]{:S(2)}, u32[]{:S(2)}) collective-permute-start(bf16[9,16,128]{2,1,0:T(8,128)(2,1)S(1)} %get-tuple-element.42.own_ym_ref), channel_id=1, source_target_pairs={{0,48},{16,0},{32,16},{48,32},{1,49},{17,1},{33,17},{49,33},{2,50}... | collective-permute-start | bytes 110600 | tf_op jit(solution)/shard_map/ppermute | solution.py:564
  22.6 2.7 %collective-permute-start = (bf16[9,16,128]{2,1,0:T(8,128)(2,1)S(1)}, bf16[9,16,128]{2,1,0:T(8,128)(2,1)S(1)}, u32[]{:S(2)}, u32[]{:S(2)}) collective-permute-start(bf16[9,16,128]{2,1,0:T(8,128)(2,1)S(1)} %get-tuple-element.39), channel_id=1, source_target_pairs={{0,64},{64,128},{128,192},{192,256},{256,320},{320,384},{384,448},... | collective-permute-start | bytes 110600 | tf_op jit(solution)/shard_map/ppermute | solution.py:564
  25.3 0.0 collective-permute-done.2.ym_ref
  25.3 0.0 collective-permute-start.1
  25.3 0.0 collective-permute-done.3.yp_ref
  25.4 1.1 %collective-permute-done.xm_ref = bf16[9,16,128]{2,1,0:T(8,128)(2,1)S(1)} collective-permute-done((bf16[9,16,128]{2,1,0:T(8,128)(2,1)S(1)}, bf16[9,16,128]{2,1,0:T(8,128)(2,1)S(1)}, u32[]{:S(2)}, u32[]{:S(2)}) %collective-permute-start) | collective-permute-done | bytes 36896 | tf_op jit(solution)/shard_map/ppermute | solution.py:564
  26.4 2.3 %collective-permute-done.1.xp_ref = bf16[9,16,128]{2,1,0:T(8,128)(2,1)S(1)} collective-permute-done((bf16[9,16,128]{2,1,0:T(8,128)(2,1)S(1)}, bf16[9,16,128]{2,1,0:T(8,128)(2,1)S(1)}, u32[]{:S(2)}, u32[]{:S(2)}) %collective-permute-start.1) | collective-permute-done | bytes 36896 | tf_op jit(solution)/shard_map/ppermute | solution.py:564
  28.7 0.0 collective-permute-done.4.zm_ref
  28.7 0.0 collective-permute-done.5.zp_ref
  28.7 2.8 %shard_map.60 = (f32[16,16,128]{2,1,0:T(8,128)}, f32[16,16,128]{2,1,0:T(8,128)S(1)}, bf16[16,16,128]{2,1,0:T(8,128)(2,1)S(1)}, bf16[16,16,128]{2,1,0:T(8,128)(2,1)S(1)}) custom-call(f32[16,16,128]{2,1,0:T(8,128)S(1)} %get-tuple-element.35.conc_ref.conc_in, f32[16,16,128]{2,1,0:T(8,128)S(1)} %get-tuple-element.36.side_ref.side_in, ...), custom_call_target="tpu_custom_call" | custom-call | tf_op jit(solution)/shard_map/pallas_call | solution.py:41
  31.5 1.9 %collective-permute-start.6 = (bf16[16,16,128]{2,1,0:T(8,128)(2,1)S(1)}, bf16[16,16,128]{2,1,0:T(8,128)(2,1)S(1)}, u32[]{:S(2)}, u32[]{:S(2)}) collective-permute-start(bf16[16,16,128]{2,1,0:T(8,128)(2,1)S(1)} %get-tuple-element.46), channel_id=1, source_target_pairs={{0,1},{1,2},{2,3},{3,4},{4,5},{5,6},{6,7},{7,8},{8,9},{9,10},{10,1... | collective-permute-start | bytes 196616 | tf_op jit(solution)/shard_map/ppermute | solution.py:564
  33.4 4.6 %collective-permute-start.7 = (bf16[16,16,128]{2,1,0:T(8,128)(2,1)S(1)}, bf16[16,16,128]{2,1,0:T(8,128)(2,1)S(1)}, u32[]{:S(2)}, u32[]{:S(2)}) collective-permute-start(bf16[16,16,128]{2,1,0:T(8,128)(2,1)S(1)} %get-tuple-element.47), channel_id=1, source_target_pairs={{0,15},{1,0},{2,1},{3,2},{4,3},{5,4},{6,5},{7,6},{8,7},{9,8},{10,9... | collective-permute-start | bytes 196616 | tf_op jit(solution)/shard_map/ppermute | solution.py:564
  38.0 0.3 collective-permute-done.6.zm_ref
  38.3 1.0 collective-permute-done.7.zp_ref
  39.3 1.9 %collective-permute-start.8 = (bf16[5,16,8,128]{3,2,1,0:T(8,128)(2,1)S(1)}, bf16[5,16,8,128]{3,2,1,0:T(8,128)(2,1)S(1)}, u32[]{:S(2)}, u32[]{:S(2)}) collective-permute-start(bf16[5,16,8,128]{3,2,1,0:T(8,128)(2,1)S(1)} %get-tuple-element.48.high_ref), channel_id=1, source_target_pairs={{0,16},{16,32},{32,48},{48,0},{1,17},{17,33},{33,49},{49,1},{2,18}... | collective-permute-start | bytes 491528 | tf_op jit(solution)/shard_map/ppermute | solution.py:564
  41.3 4.6 %collective-permute-start.9 = (bf16[5,16,8,128]{3,2,1,0:T(8,128)(2,1)S(1)}, bf16[5,16,8,128]{3,2,1,0:T(8,128)(2,1)S(1)}, u32[]{:S(2)}, u32[]{:S(2)}) collective-permute-start(bf16[5,16,8,128]{3,2,1,0:T(8,128)(2,1)S(1)} %get-tuple-element.49.low_ref), channel_id=1, source_target_pairs={{0,48},{16,0},{32,16},{48,32},{1,49},{17,1},{33,17},{49,33},{2,50}... | collective-permute-start | bytes 491528 | tf_op jit(solution)/shard_map/ppermute | solution.py:564
  45.9 1.1 %collective-permute-done.8.below_ref = bf16[5,16,8,128]{3,2,1,0:T(8,128)(2,1)S(1)} collective-permute-done((bf16[5,16,8,128]{3,2,1,0:T(8,128)(2,1)S(1)}, bf16[5,16,8,128]{3,2,1,0:T(8,128)(2,1)S(1)}, u32[]{:S(2)}, u32[]{:S(2)}) %collective-permute-start.8) | collective-permute-done | bytes 163872 | tf_op jit(solution)/shard_map/ppermute | solution.py:564
  47.0 1.1 %collective-permute-done.9.above_ref = bf16[5,16,8,128]{3,2,1,0:T(8,128)(2,1)S(1)} collective-permute-done((bf16[5,16,8,128]{3,2,1,0:T(8,128)(2,1)S(1)}, bf16[5,16,8,128]{3,2,1,0:T(8,128)(2,1)S(1)}, u32[]{:S(2)}, u32[]{:S(2)}) %collective-permute-start.9) | collective-permute-done | bytes 163872 | tf_op jit(solution)/shard_map/ppermute | solution.py:564
  48.1 0.1 shard_map.62
  48.2 3.5 %collective-permute-start.10 = (bf16[5,8,32,128]{3,2,1,0:T(8,128)(2,1)S(1)}, bf16[5,8,32,128]{3,2,1,0:T(8,128)(2,1)S(1)}, u32[]{:S(2)}, u32[]{:S(2)}) collective-permute-start(bf16[5,8,32,128]{3,2,1,0:T(8,128)(2,1)S(1)} %get-tuple-element.50), channel_id=1, source_target_pairs={{0,64},{64,128},{128,192},{192,256},{256,320},{320,384},{384,448},... | collective-permute-start | bytes 983048 | tf_op jit(solution)/shard_map/ppermute | solution.py:564
  51.7 0.0 collective-permute-start.11
  51.7 0.1 pad_add_fusion.place_ref
  51.8 3.9 %collective-permute-done.10.xm_ref = bf16[5,8,32,128]{3,2,1,0:T(8,128)(2,1)S(1)} collective-permute-done((bf16[5,8,32,128]{3,2,1,0:T(8,128)(2,1)S(1)}, bf16[5,8,32,128]{3,2,1,0:T(8,128)(2,1)S(1)}, u32[]{:S(2)}, u32[]{:S(2)}) %collective-permute-start.10) | collective-permute-done | bytes 327712 | tf_op jit(solution)/shard_map/ppermute | solution.py:564
  55.7 2.5 %collective-permute-done.11.xp_ref = bf16[5,8,32,128]{3,2,1,0:T(8,128)(2,1)S(1)} collective-permute-done((bf16[5,8,32,128]{3,2,1,0:T(8,128)(2,1)S(1)}, bf16[5,8,32,128]{3,2,1,0:T(8,128)(2,1)S(1)}, u32[]{:S(2)}, u32[]{:S(2)}) %collective-permute-start.11) | collective-permute-done | bytes 327712 | tf_op jit(solution)/shard_map/ppermute | solution.py:564
  58.2 14.2 %shard_map.63 = (f32[64,128]{1,0:T(8,128)S(1)}, bf16[32,112,128]{2,1,0:T(8,128)(2,1)S(1)}, f32[32,32,256]{2,1,0:T(8,128)}, f32[32,32,256]{2,1,0:T(8,128)}, f32[3...) custom-call(f32[16,16,128]{2,1,0:T(8,128)S(1)} %get-tuple-element.45, ...), custom_call_target="tpu_custom_call" | custom-call | tf_op jit(solution)/shard_map/pallas_call | solution.py:41
  72.4 22.2 %all_to_all.5.all_ref = bf16[32,112,128]{2,1,0:T(8,128)(2,1)S(1)} all-to-all(bf16[32,112,128]{2,1,0:T(8,128)(2,1)S(1)} %get-tuple-element.54), channel_id=1, replica_groups=mesh['gx'=8,'gy'=4,'gz'=16] {'gx','gy'}, dimensions={0} | all-to-all | bytes 1835008 | tf_op jit(solution)/shard_map/all_to_all | solution.py:615
  94.6 9.0 %shard_map.64 = f32[16,16,128]{2,1,0:T(8,128)} custom-call(s32[2]{0:T(128)S(1)} %pad_add_fusion.place_ref, bf16[32,112,128]{2,1,0:T(8,128)(2,1)S(1)} %all_to_all.5.all_ref, f32[64,128]{1,0:T(8,128)S(1)} %get-tuple-element.55.own_ref, f32[32,32,256]{2,1,0:T(8,128)} %get-tuple-element.56.side_in, f32[32,32,256]{2,1,0:T(8,128)} %get-tuple-element.57.kx_in, ...), custom_call_target="tpu_custom_call" | custom-call | tf_op jit(solution)/shard_map/pallas_call | solution.py:41
  (1 shorter events, 0.0 us)
Async XLA Ops:
  2.2 23.1 %collective-permute-start.2 = (bf16[9,16,128]{2,1,0:T(8,128)(2,1)S(1)}, bf16[9,16,128]{2,1,0:T(8,128)(2,1)S(1)}, u32[]{:S(2)}, u32[]{:S(2)}) collective-permute-start(bf16[9,16,128]{2,1,0:T(8,128)(2,1)S(1)} %get-tuple-element.41.own_yp_ref), channel_id=1, source_target_pairs={{0,16},{16,32},{32,48},{48,0},{1,17},{17,33},{33,49},{49,1},{2,18}... | collective-permute-start | bytes 110600 | tf_op jit(solution)/shard_map/ppermute | solution.py:564
  6.2 22.5 %collective-permute-start.4 = (bf16[17,16,128]{2,1,0:T(8,128)(2,1)S(1)}, bf16[17,16,128]{2,1,0:T(8,128)(2,1)S(1)}, u32[]{:S(2)}, u32[]{:S(2)}) collective-permute-start(bf16[17,16,128]{2,1,0:T(8,128)(2,1)S(1)} %get-tuple-element.43), channel_id=1, source_target_pairs={{0,1},{1,2},{2,3},{3,4},{4,5},{5,6},{6,7},{7,8},{8,9},{9,10},{10,1... | collective-permute-start | bytes 208904 | tf_op jit(solution)/shard_map/ppermute | solution.py:564
  9.7 19.0 %collective-permute-start.5 = (bf16[17,16,128]{2,1,0:T(8,128)(2,1)S(1)}, bf16[17,16,128]{2,1,0:T(8,128)(2,1)S(1)}, u32[]{:S(2)}, u32[]{:S(2)}) collective-permute-start(bf16[17,16,128]{2,1,0:T(8,128)(2,1)S(1)} %get-tuple-element.44), channel_id=1, source_target_pairs={{0,15},{1,0},{2,1},{3,2},{4,3},{5,4},{6,5},{7,6},{8,7},{9,8},{10,9... | collective-permute-start | bytes 208904 | tf_op jit(solution)/shard_map/ppermute | solution.py:564
  19.2 6.1 %collective-permute-start.3 = (bf16[9,16,128]{2,1,0:T(8,128)(2,1)S(1)}, bf16[9,16,128]{2,1,0:T(8,128)(2,1)S(1)}, u32[]{:S(2)}, u32[]{:S(2)}) collective-permute-start(bf16[9,16,128]{2,1,0:T(8,128)(2,1)S(1)} %get-tuple-element.42.own_ym_ref), channel_id=1, source_target_pairs={{0,48},{16,0},{32,16},{48,32},{1,49},{17,1},{33,17},{49,33},{2,50}... | collective-permute-start | bytes 110600 | tf_op jit(solution)/shard_map/ppermute | solution.py:564
  22.6 3.8 %collective-permute-start = (bf16[9,16,128]{2,1,0:T(8,128)(2,1)S(1)}, bf16[9,16,128]{2,1,0:T(8,128)(2,1)S(1)}, u32[]{:S(2)}, u32[]{:S(2)}) collective-permute-start(bf16[9,16,128]{2,1,0:T(8,128)(2,1)S(1)} %get-tuple-element.39), channel_id=1, source_target_pairs={{0,64},{64,128},{128,192},{192,256},{256,320},{320,384},{384,448},... | collective-permute-start | bytes 110600 | tf_op jit(solution)/shard_map/ppermute | solution.py:564
  25.3 3.4 %collective-permute-start.1 = (bf16[9,16,128]{2,1,0:T(8,128)(2,1)S(1)}, bf16[9,16,128]{2,1,0:T(8,128)(2,1)S(1)}, u32[]{:S(2)}, u32[]{:S(2)}) collective-permute-start(bf16[9,16,128]{2,1,0:T(8,128)(2,1)S(1)} %get-tuple-element.40), channel_id=1, source_target_pairs={{0,448},{64,0},{128,64},{192,128},{256,192},{320,256},{384,320},{4... | collective-permute-start | bytes 110600 | tf_op jit(solution)/shard_map/ppermute | solution.py:564
  31.5 6.8 %collective-permute-start.6 = (bf16[16,16,128]{2,1,0:T(8,128)(2,1)S(1)}, bf16[16,16,128]{2,1,0:T(8,128)(2,1)S(1)}, u32[]{:S(2)}, u32[]{:S(2)}) collective-permute-start(bf16[16,16,128]{2,1,0:T(8,128)(2,1)S(1)} %get-tuple-element.46), channel_id=1, source_target_pairs={{0,1},{1,2},{2,3},{3,4},{4,5},{5,6},{6,7},{7,8},{8,9},{9,10},{10,1... | collective-permute-start | bytes 196616 | tf_op jit(solution)/shard_map/ppermute | solution.py:564
  33.4 5.9 %collective-permute-start.7 = (bf16[16,16,128]{2,1,0:T(8,128)(2,1)S(1)}, bf16[16,16,128]{2,1,0:T(8,128)(2,1)S(1)}, u32[]{:S(2)}, u32[]{:S(2)}) collective-permute-start(bf16[16,16,128]{2,1,0:T(8,128)(2,1)S(1)} %get-tuple-element.47), channel_id=1, source_target_pairs={{0,15},{1,0},{2,1},{3,2},{4,3},{5,4},{6,5},{7,6},{8,7},{9,8},{10,9... | collective-permute-start | bytes 196616 | tf_op jit(solution)/shard_map/ppermute | solution.py:564
  39.3 7.6 %collective-permute-start.8 = (bf16[5,16,8,128]{3,2,1,0:T(8,128)(2,1)S(1)}, bf16[5,16,8,128]{3,2,1,0:T(8,128)(2,1)S(1)}, u32[]{:S(2)}, u32[]{:S(2)}) collective-permute-start(bf16[5,16,8,128]{3,2,1,0:T(8,128)(2,1)S(1)} %get-tuple-element.48.high_ref), channel_id=1, source_target_pairs={{0,16},{16,32},{32,48},{48,0},{1,17},{17,33},{33,49},{49,1},{2,18}... | collective-permute-start | bytes 491528 | tf_op jit(solution)/shard_map/ppermute | solution.py:564
  41.3 6.8 %collective-permute-start.9 = (bf16[5,16,8,128]{3,2,1,0:T(8,128)(2,1)S(1)}, bf16[5,16,8,128]{3,2,1,0:T(8,128)(2,1)S(1)}, u32[]{:S(2)}, u32[]{:S(2)}) collective-permute-start(bf16[5,16,8,128]{3,2,1,0:T(8,128)(2,1)S(1)} %get-tuple-element.49.low_ref), channel_id=1, source_target_pairs={{0,48},{16,0},{32,16},{48,32},{1,49},{17,1},{33,17},{49,33},{2,50}... | collective-permute-start | bytes 491528 | tf_op jit(solution)/shard_map/ppermute | solution.py:564
  48.2 7.5 %collective-permute-start.10 = (bf16[5,8,32,128]{3,2,1,0:T(8,128)(2,1)S(1)}, bf16[5,8,32,128]{3,2,1,0:T(8,128)(2,1)S(1)}, u32[]{:S(2)}, u32[]{:S(2)}) collective-permute-start(bf16[5,8,32,128]{3,2,1,0:T(8,128)(2,1)S(1)} %get-tuple-element.50), channel_id=1, source_target_pairs={{0,64},{64,128},{128,192},{192,256},{256,320},{320,384},{384,448},... | collective-permute-start | bytes 983048 | tf_op jit(solution)/shard_map/ppermute | solution.py:564
  51.7 6.5 %collective-permute-start.11 = (bf16[5,8,32,128]{3,2,1,0:T(8,128)(2,1)S(1)}, bf16[5,8,32,128]{3,2,1,0:T(8,128)(2,1)S(1)}, u32[]{:S(2)}, u32[]{:S(2)}) collective-permute-start(bf16[5,8,32,128]{3,2,1,0:T(8,128)(2,1)S(1)} %get-tuple-element.51), channel_id=1, source_target_pairs={{0,448},{64,0},{128,64},{192,128},{256,192},{320,256},{384,320},{4... | collective-permute-start | bytes 983048 | tf_op jit(solution)/shard_map/ppermute | solution.py:564

commit v4 on v3

--- a/solution.py
+++ b/solution.py
@@ -258,24 +258,29 @@
     return jnp.where(upper, x, roll(x, -step, axis))
 
 
-def residual(value, source, flux_x, flux_x_before, ky, kz, step):
-    flux_y = ky * (roll(value, -step, 0) - value)
-    flux_z = kz * (roll(value, -step, 1) - value)
-    total = (source - value) + (flux_x - flux_x_before)
-    total = total + (flux_y - roll(flux_y, step, 0))
-    return total + (flux_z - roll(flux_z, step, 1))
-
-
-def sweep_planes(first, last, values, source, kx, ky, kz, step, use):
-    before = kx[first - 1] * (values[first] - values[first - 1])
-
-    value = values[first]
-    for x in range(first, last + 1):
-        above = values[x + 1]
-        flux = kx[x] * (above - value)
-        use(x, value, residual(value, source[x], flux, before, ky[x], kz[x], step))
-        before = flux
-        value = above
+def groups(items, size):
+    items = list(items)
+    return [items[k : k + size] for k in range(0, len(items), size)]
+
+
+def sweep_planes(first, last, values, source, kx, ky, kz, step, use, size=8, planes=None):
+    at = (lambda x: x) if planes is None else (lambda x: x % planes)
+    before = kx[at(first - 1)] * (values[at(first)] - values[at(first - 1)])
+    for xs in groups(range(first, last + 1), size):
+        cells = [values[at(x)] for x in xs + [xs[-1] + 1]]
+        flux_z = [kz[at(x)] * (roll(v, -step, 1) - v) for x, v in zip(xs, cells)]
+        back_z = [roll(flux, step, 1) for flux in flux_z]
+        left = []
+        for k, x in enumerate(xs):
+            value = cells[k]
+            flux_x = kx[at(x)] * (cells[k + 1] - value)
+            flux_y = ky[at(x)] * (roll(value, -step, 0) - value)
+            total = (source[at(x)] - value) + (flux_x - before)
+            total = total + (flux_y - roll(flux_y, step, 0))
+            left.append(total + (flux_z[k] - back_z[k]))
+            before = flux_x
+        for k, x in enumerate(xs):
+            use(at(x), cells[k], left[k])
 
 
 def down_kernel(
@@ -299,39 +304,49 @@
         return jnp.concatenate([part.astype(F32) for part in parts], axis=0)
 
     own = (mob_in, conc_in, side_in, zm_ref, zp_ref)
-    for x in range(32):
-        if 8 <= x < 24:
-            parts = [own_plane(x - 8, place, ref) for place, ref in enumerate(own)]
-        else:
-            ref = xm_ref if x < 8 else xp_ref
-            parts = [ref[place, x % 8].astype(F32) for place in range(5)]
-        mob[x, :, :LANES] = parts[0]
-        v0[x, :, :LANES] = parts[1]
-        side_ref[x, :, :LANES] = parts[2]
-        down, up = parts[3], parts[4]
-        mob[x, :, LANES:] = jnp.where(lane < 43, up, jnp.where(lane >= 85, down, 1.0))
-        v0[x, :, LANES:] = jnp.where(
-            lane < 43, roll(up, -43, 1), jnp.where(lane >= 85, roll(down, 43, 1), 0.0)
-        )
-        side_ref[x, :, LANES:] = jnp.where(
-            lane < 42, roll(up, -86, 1), jnp.where(lane >= 86, roll(down, 86, 1), 0.0)
-        )
+    for xs in groups(range(32), 8):
+        planes = []
+        for x in xs:
+            if 8 <= x < 24:
+                parts = [own_plane(x - 8, place, ref) for place, ref in enumerate(own)]
+            else:
+                ref = xm_ref if x < 8 else xp_ref
+                parts = [ref[place, x % 8].astype(F32) for place in range(5)]
+            down, up = parts[3], parts[4]
+            beyond = jnp.where(lane < 43, up, jnp.where(lane >= 85, down, 1.0))
+            iterate = jnp.where(
+                lane < 43, roll(up, -43, 1), jnp.where(lane >= 85, roll(down, 43, 1), 0.0)
+            )
+            right = jnp.where(
+                lane < 42, roll(up, -86, 1), jnp.where(lane >= 86, roll(down, 86, 1), 0.0)
+            )
+            planes.append((parts, beyond, iterate, right))
+        for x, (parts, beyond, iterate, right) in zip(xs, planes):
+            mob[x, :, :LANES] = parts[0]
+            v0[x, :, :LANES] = parts[1]
+            side_ref[x, :, :LANES] = parts[2]
+            mob[x, :, LANES:] = beyond
+            v0[x, :, LANES:] = iterate
+            side_ref[x, :, LANES:] = right
 
     half = TAU / 2
 
     before = half * (mob[1] + mob[2])
     kx_ref[1] = before
-    for x in range(2, 30):
-        here = mob[x]
-        kx = half * (here + mob[x + 1])
-        ky = half * (here + roll(here, -1, 0))
-        kz = half * (here + roll(here, -1, 1))
-        kx_ref[x] = kx
-        ky_ref[x] = ky
-        kz_ref[x] = kz
-        total = (kx + before) + (ky + roll(ky, 1, 0)) + (kz + roll(kz, 1, 1))
-        wd_ref[x] = OMEGA / (1.0 + total)
-        before = kx
+    for xs in groups(range(2, 30), 7):
+        here = [mob[x] for x in xs + [xs[-1] + 1]]
+        kz = [half * (cells + roll(cells, -1, 1)) for cells in here[:-1]]
+        back = [roll(k, 1, 1) for k in kz]
+        done = []
+        for k, x in enumerate(xs):
+            kx = half * (here[k] + here[k + 1])
+            ky = half * (here[k] + roll(here[k], -1, 0))
+            total = (kx + before) + (ky + roll(ky, 1, 0)) + (kz[k] + back[k])
+            done.append((kx, ky, OMEGA / (1.0 + total)))
+            before = kx
+        for k, x in enumerate(xs):
+            kx_ref[x], ky_ref[x], wd_ref[x] = done[k]
+            kz_ref[x] = kz[k]
 
     store(side_ref, side_out, FINE_PLANES)
     store(kx_ref, kx_out, FINE_PLANES)
@@ -358,24 +373,27 @@
     def pool(x):
         return pair_sum(pair_sum(x, 1, 0), 1, 1)
 
-    for i in range(1, 14):
-        x = 2 * i
-        k1x_ref[i] = pool(kx_ref[x + 1]) * (1.0 / 16.0)
-        if i == 1:
-            for ref in (f1_ref, k1y_ref, k1z_ref, wd1_ref):
-                ref[i] = jnp.zeros((32, RING), F32)
-            continue
-        f1_ref[i] = pool(res[x] + res[x + 1]) * 0.125
-        along_y = pair_sum(ky_ref[x] + ky_ref[x + 1], 1, 1)
-        k1y = upper_of(along_y, 1, 0) * (1.0 / 16.0)
-        along_z = pair_sum(kz_ref[x] + kz_ref[x + 1], 1, 0)
-        k1z = upper_of(along_z, 1, 1) * (1.0 / 16.0)
-        k1y_ref[i] = k1y
-        k1z_ref[i] = k1z
-        total = (k1x_ref[i] + k1x_ref[i - 1]) + (k1y + roll(k1y, 2, 0)) + (k1z + roll(k1z, 2, 1))
-        weight = OMEGA / (1.0 + total)
-        wd1_ref[i] = weight
-        e0[i] = weight * f1_ref[i]
+    for xs in groups(range(1, 14), 7):
+        done = [pool(kx_ref[2 * i + 1]) * (1.0 / 16.0) for i in xs]
+        for i, value in zip(xs, done):
+            k1x_ref[i] = value
+    for ref in (f1_ref, k1y_ref, k1z_ref, wd1_ref):
+        ref[1] = jnp.zeros((32, RING), F32)
+    for xs in groups(range(2, 14), 6):
+        done = []
+        for i in xs:
+            x = 2 * i
+            f1 = pool(res[x] + res[x + 1]) * 0.125
+            along_y = pair_sum(ky_ref[x] + ky_ref[x + 1], 1, 1)
+            k1y = upper_of(along_y, 1, 0) * (1.0 / 16.0)
+            along_z = pair_sum(kz_ref[x] + kz_ref[x + 1], 1, 0)
+            k1z = upper_of(along_z, 1, 1) * (1.0 / 16.0)
+            total = k1x_ref[i] + k1x_ref[i - 1]
+            total = total + (k1y + roll(k1y, 2, 0)) + (k1z + roll(k1z, 2, 1))
+            weight = OMEGA / (1.0 + total)
+            done.append((f1, k1y, k1z, weight, weight * f1))
+        for i, value in zip(xs, done):
+            f1_ref[i], k1y_ref[i], k1z_ref[i], wd1_ref[i], e0[i] = value
     store(k1x_ref, k1x_out, MIDDLE_PLANES)
     store(k1y_ref, k1y_out, MIDDLE_PLANES)
     store(k1z_ref, k1z_out, MIDDLE_PLANES)
@@ -489,29 +507,30 @@
         c2x[k] = jnp.where(used, roll(first, 64, 1), 0.0)
         c2y[k] = jnp.where(used, second, 0.0)
         c2z[k] = jnp.where(used, roll(second, 64, 1), 0.0)
-    for x in range(-5, 17):
-        k = x % 32
-        ky = c2y[k]
-        kz = c2z[k]
-        total = (c2x[k] + c2x[(x - 1) % 32]) + (ky + roll(ky, 1, 0)) + (kz + roll(kz, 1, 1))
-        weight = OMEGA / (1.0 + total)
-        wd2[k] = weight
-        ea[k] = weight * f2[k]
+    for xs in groups(range(-5, 17), 11):
+        done = []
+        for x in xs:
+            k = x % 32
+            ky = c2y[k]
+            kz = c2z[k]
+            total = c2x[k] + c2x[(x - 1) % 32]
+            total = total + (ky + roll(ky, 1, 0)) + (kz + roll(kz, 1, 1))
+            weight = OMEGA / (1.0 + total)
+            done.append((weight, weight * f2[k]))
+        for x, value in zip(xs, done):
+            wd2[x % 32], ea[x % 32] = value
+
+    def smooth(target, weight):
+        def use(x, value, left):
+            target[x] = value + weight[x] * left
+
+        return use
 
     old, new = ea, eb
     for reach in range(6, -1, -1):
-        first = 2 - reach
-        value = old[first % 32]
-        below = (first - 1) % 32
-        before = c2x[below] * (value - old[below])
-        for x in range(first, 10 + reach):
-            k = x % 32
-            above = old[(x + 1) % 32]
-            flux = c2x[k] * (above - value)
-            left = residual(value, f2[k], flux, before, c2y[k], c2z[k], 1)
-            new[k] = value + wd2[k] * left
-            before = flux
-            value = above
+        sweep_planes(
+            2 - reach, 9 + reach, old, f2, c2x, c2y, c2z, 1, smooth(new, wd2), 10, 32
+        )
         old, new = new, old
 
     lane = iota((8, LANES), 1)
@@ -538,12 +557,6 @@
     for i in range(1, 15):
         e1a[i] = widened[32 * (i - 1) : 32 * i]
 
-    def smooth(target, weight):
-        def use(x, value, left):
-            target[x] = value + weight[x] * left
-
-        return use
-
     for copy in copies:
         copy.wait()
     sweep_planes(2, 13, e1a, f1_ref, k1x_ref, k1y_ref, k1z_ref, 2, smooth(e1b, wd1_ref))

time: 104 us -> 95.3 us (0.916)
  Pallas kernels: 27.7 us -> 18.9 us
    pallas_call x6, Pallas kernels: 27.7 us -> 18.9 us  [call(): pl.pallas_call(kernel, out_shape=[pltpu.MemorySpace.HBM(*out) if place is...]
where the time goes in v4:
time: 95.3 us; the launch traced here: 94.9 us
  starting transfers between devices  39.5 us (41%)
  blocking collectives  22.2 us (23%)
  Pallas kernels  18.9 us (20%)
  waiting for transfers between devices  13.4 us (14%)
    ppermute x12, starting transfers between devices, shift(): lax.ppermute(x, axis, [(i, (i + direction) % count) for i in range(count)])  39.5 us
    all_to_all x1, blocking collectives, body(): chunks = lax.all_to_all(chunk, ('gx', 'gy'), 0, 0, tiled=True)  22.2 us
    pallas_call x6, Pallas kernels, call(): pl.pallas_call(kernel, out_shape=[pltpu.MemorySpace.HBM(*out) if place is...  18.9 us
    ppermute x12, waiting for transfers between devices, shift(): lax.ppermute(x, axis, [(i, (i + direction) % count) for i in range(count)])  13.4 us
  transfers between devices with their start and end apart: 12, of which 8 were waited for; matrix products, arithmetic and copies ran while one was open for 0% of the time, Pallas kernels for 0%

profile of v4, /device:TPU:1, one launch (start us, length us, event | category | flops | bytes accessed | tf_op | source)
XLA Modules:
  0.0 94.9 jit_solution(12705996532960938311)
XLA Ops:
  0.6 1.6 %shard_map.59 = (f32[16,16,128]{2,1,0:T(8,128)S(1)}, f32[16,16,128]{2,1,0:T(8,128)S(1)}, bf16[8,16,16,128]{3,2,1,0:T(8,128)(2,1)S(1)}, s32[1,1,8,8]{3,2,1,0:T(8,...) custom-call(f32[16,16,128]{2,1,0:T(8,128)} %conc_in.1, ...), custom_call_target="tpu_custom_call" | custom-call | tf_op jit(solution)/shard_map/pallas_call | solution.py:41
  2.2 3.9 %collective-permute-start.2 = (bf16[9,16,128]{2,1,0:T(8,128)(2,1)S(1)}, bf16[9,16,128]{2,1,0:T(8,128)(2,1)S(1)}, u32[]{:S(2)}, u32[]{:S(2)}) collective-permute-start(bf16[9,16,128]{2,1,0:T(8,128)(2,1)S(1)} %get-tuple-element.41.own_yp_ref), channel_id=1, source_target_pairs={{0,16},{16,32},{32,48},{48,0},{1,17},{17,33},{33,49},{49,1},{2,18}... | collective-permute-start | bytes 110600 | tf_op jit(solution)/shard_map/ppermute | solution.py:577
  6.2 3.5 %collective-permute-start.4 = (bf16[17,16,128]{2,1,0:T(8,128)(2,1)S(1)}, bf16[17,16,128]{2,1,0:T(8,128)(2,1)S(1)}, u32[]{:S(2)}, u32[]{:S(2)}) collective-permute-start(bf16[17,16,128]{2,1,0:T(8,128)(2,1)S(1)} %get-tuple-element.43), channel_id=1, source_target_pairs={{0,1},{1,2},{2,3},{3,4},{4,5},{5,6},{6,7},{7,8},{8,9},{9,10},{10,1... | collective-permute-start | bytes 208904 | tf_op jit(solution)/shard_map/ppermute | solution.py:577
  9.7 9.5 %collective-permute-start.5 = (bf16[17,16,128]{2,1,0:T(8,128)(2,1)S(1)}, bf16[17,16,128]{2,1,0:T(8,128)(2,1)S(1)}, u32[]{:S(2)}, u32[]{:S(2)}) collective-permute-start(bf16[17,16,128]{2,1,0:T(8,128)(2,1)S(1)} %get-tuple-element.44), channel_id=1, source_target_pairs={{0,15},{1,0},{2,1},{3,2},{4,3},{5,4},{6,5},{7,6},{8,7},{9,8},{10,9... | collective-permute-start | bytes 208904 | tf_op jit(solution)/shard_map/ppermute | solution.py:577
  19.2 3.4 %collective-permute-start.3 = (bf16[9,16,128]{2,1,0:T(8,128)(2,1)S(1)}, bf16[9,16,128]{2,1,0:T(8,128)(2,1)S(1)}, u32[]{:S(2)}, u32[]{:S(2)}) collective-permute-start(bf16[9,16,128]{2,1,0:T(8,128)(2,1)S(1)} %get-tuple-element.42.own_ym_ref), channel_id=1, source_target_pairs={{0,48},{16,0},{32,16},{48,32},{1,49},{17,1},{33,17},{49,33},{2,50}... | collective-permute-start | bytes 110600 | tf_op jit(solution)/shard_map/ppermute | solution.py:577
  22.6 2.7 %collective-permute-start = (bf16[9,16,128]{2,1,0:T(8,128)(2,1)S(1)}, bf16[9,16,128]{2,1,0:T(8,128)(2,1)S(1)}, u32[]{:S(2)}, u32[]{:S(2)}) collective-permute-start(bf16[9,16,128]{2,1,0:T(8,128)(2,1)S(1)} %get-tuple-element.39), channel_id=1, source_target_pairs={{0,64},{64,128},{128,192},{192,256},{256,320},{320,384},{384,448},... | collective-permute-start | bytes 110600 | tf_op jit(solution)/shard_map/ppermute | solution.py:577
  25.3 0.0 collective-permute-done.2.ym_ref
  25.3 0.0 collective-permute-start.1
  25.3 0.0 collective-permute-done.3.yp_ref
  25.4 1.1 %collective-permute-done.xm_ref = bf16[9,16,128]{2,1,0:T(8,128)(2,1)S(1)} collective-permute-done((bf16[9,16,128]{2,1,0:T(8,128)(2,1)S(1)}, bf16[9,16,128]{2,1,0:T(8,128)(2,1)S(1)}, u32[]{:S(2)}, u32[]{:S(2)}) %collective-permute-start) | collective-permute-done | bytes 36896 | tf_op jit(solution)/shard_map/ppermute | solution.py:577
  26.4 2.3 %collective-permute-done.1.xp_ref = bf16[9,16,128]{2,1,0:T(8,128)(2,1)S(1)} collective-permute-done((bf16[9,16,128]{2,1,0:T(8,128)(2,1)S(1)}, bf16[9,16,128]{2,1,0:T(8,128)(2,1)S(1)}, u32[]{:S(2)}, u32[]{:S(2)}) %collective-permute-start.1) | collective-permute-done | bytes 36896 | tf_op jit(solution)/shard_map/ppermute | solution.py:577
  28.7 0.0 collective-permute-done.4.zm_ref
  28.7 0.0 collective-permute-done.5.zp_ref
  28.7 2.8 %shard_map.60 = (f32[16,16,128]{2,1,0:T(8,128)}, f32[16,16,128]{2,1,0:T(8,128)S(1)}, bf16[16,16,128]{2,1,0:T(8,128)(2,1)S(1)}, bf16[16,16,128]{2,1,0:T(8,128)(2,1)S(1)}) custom-call(f32[16,16,128]{2,1,0:T(8,128)S(1)} %get-tuple-element.35.conc_ref.conc_in, f32[16,16,128]{2,1,0:T(8,128)S(1)} %get-tuple-element.36.side_ref.side_in, ...), custom_call_target="tpu_custom_call" | custom-call | tf_op jit(solution)/shard_map/pallas_call | solution.py:41
  31.5 1.9 %collective-permute-start.6 = (bf16[16,16,128]{2,1,0:T(8,128)(2,1)S(1)}, bf16[16,16,128]{2,1,0:T(8,128)(2,1)S(1)}, u32[]{:S(2)}, u32[]{:S(2)}) collective-permute-start(bf16[16,16,128]{2,1,0:T(8,128)(2,1)S(1)} %get-tuple-element.46), channel_id=1, source_target_pairs={{0,1},{1,2},{2,3},{3,4},{4,5},{5,6},{6,7},{7,8},{8,9},{9,10},{10,1... | collective-permute-start | bytes 196616 | tf_op jit(solution)/shard_map/ppermute | solution.py:577
  33.4 4.6 %collective-permute-start.7 = (bf16[16,16,128]{2,1,0:T(8,128)(2,1)S(1)}, bf16[16,16,128]{2,1,0:T(8,128)(2,1)S(1)}, u32[]{:S(2)}, u32[]{:S(2)}) collective-permute-start(bf16[16,16,128]{2,1,0:T(8,128)(2,1)S(1)} %get-tuple-element.47), channel_id=1, source_target_pairs={{0,15},{1,0},{2,1},{3,2},{4,3},{5,4},{6,5},{7,6},{8,7},{9,8},{10,9... | collective-permute-start | bytes 196616 | tf_op jit(solution)/shard_map/ppermute | solution.py:577
  38.0 0.3 collective-permute-done.6.zm_ref
  38.3 1.0 %collective-permute-done.7.zp_ref = bf16[16,16,128]{2,1,0:T(8,128)(2,1)S(1)} collective-permute-done((bf16[16,16,128]{2,1,0:T(8,128)(2,1)S(1)}, bf16[16,16,128]{2,1,0:T(8,128)(2,1)S(1)}, u32[]{:S(2)}, u32[]{:S(2)}) %collective-permute-start.7) | collective-permute-done | bytes 65568 | tf_op jit(solution)/shard_map/ppermute | solution.py:577
  39.3 1.9 %collective-permute-start.8 = (bf16[5,16,8,128]{3,2,1,0:T(8,128)(2,1)S(1)}, bf16[5,16,8,128]{3,2,1,0:T(8,128)(2,1)S(1)}, u32[]{:S(2)}, u32[]{:S(2)}) collective-permute-start(bf16[5,16,8,128]{3,2,1,0:T(8,128)(2,1)S(1)} %get-tuple-element.48.high_ref), channel_id=1, source_target_pairs={{0,16},{16,32},{32,48},{48,0},{1,17},{17,33},{33,49},{49,1},{2,18}... | collective-permute-start | bytes 491528 | tf_op jit(solution)/shard_map/ppermute | solution.py:577
  41.3 4.6 %collective-permute-start.9 = (bf16[5,16,8,128]{3,2,1,0:T(8,128)(2,1)S(1)}, bf16[5,16,8,128]{3,2,1,0:T(8,128)(2,1)S(1)}, u32[]{:S(2)}, u32[]{:S(2)}) collective-permute-start(bf16[5,16,8,128]{3,2,1,0:T(8,128)(2,1)S(1)} %get-tuple-element.49.low_ref), channel_id=1, source_target_pairs={{0,48},{16,0},{32,16},{48,32},{1,49},{17,1},{33,17},{49,33},{2,50}... | collective-permute-start | bytes 491528 | tf_op jit(solution)/shard_map/ppermute | solution.py:577
  45.9 1.1 %collective-permute-done.8.below_ref = bf16[5,16,8,128]{3,2,1,0:T(8,128)(2,1)S(1)} collective-permute-done((bf16[5,16,8,128]{3,2,1,0:T(8,128)(2,1)S(1)}, bf16[5,16,8,128]{3,2,1,0:T(8,128)(2,1)S(1)}, u32[]{:S(2)}, u32[]{:S(2)}) %collective-permute-start.8) | collective-permute-done | bytes 163872 | tf_op jit(solution)/shard_map/ppermute | solution.py:577
  47.0 1.1 %collective-permute-done.9.above_ref = bf16[5,16,8,128]{3,2,1,0:T(8,128)(2,1)S(1)} collective-permute-done((bf16[5,16,8,128]{3,2,1,0:T(8,128)(2,1)S(1)}, bf16[5,16,8,128]{3,2,1,0:T(8,128)(2,1)S(1)}, u32[]{:S(2)}, u32[]{:S(2)}) %collective-permute-start.9) | collective-permute-done | bytes 163872 | tf_op jit(solution)/shard_map/ppermute | solution.py:577
  48.1 0.1 shard_map.62
  48.2 3.5 %collective-permute-start.10 = (bf16[5,8,32,128]{3,2,1,0:T(8,128)(2,1)S(1)}, bf16[5,8,32,128]{3,2,1,0:T(8,128)(2,1)S(1)}, u32[]{:S(2)}, u32[]{:S(2)}) collective-permute-start(bf16[5,8,32,128]{3,2,1,0:T(8,128)(2,1)S(1)} %get-tuple-element.50), channel_id=1, source_target_pairs={{0,64},{64,128},{128,192},{192,256},{256,320},{320,384},{384,448},... | collective-permute-start | bytes 983048 | tf_op jit(solution)/shard_map/ppermute | solution.py:577
  51.7 0.0 collective-permute-start.11
  51.7 0.1 pad_add_fusion.place_ref
  51.8 3.9 %collective-permute-done.10.xm_ref = bf16[5,8,32,128]{3,2,1,0:T(8,128)(2,1)S(1)} collective-permute-done((bf16[5,8,32,128]{3,2,1,0:T(8,128)(2,1)S(1)}, bf16[5,8,32,128]{3,2,1,0:T(8,128)(2,1)S(1)}, u32[]{:S(2)}, u32[]{:S(2)}) %collective-permute-start.10) | collective-permute-done | bytes 327712 | tf_op jit(solution)/shard_map/ppermute | solution.py:577
  55.7 2.5 %collective-permute-done.11.xp_ref = bf16[5,8,32,128]{3,2,1,0:T(8,128)(2,1)S(1)} collective-permute-done((bf16[5,8,32,128]{3,2,1,0:T(8,128)(2,1)S(1)}, bf16[5,8,32,128]{3,2,1,0:T(8,128)(2,1)S(1)}, u32[]{:S(2)}, u32[]{:S(2)}) %collective-permute-start.11) | collective-permute-done | bytes 327712 | tf_op jit(solution)/shard_map/ppermute | solution.py:577
  58.2 7.9 %shard_map.63 = (f32[64,128]{1,0:T(8,128)S(1)}, bf16[32,112,128]{2,1,0:T(8,128)(2,1)S(1)}, f32[32,32,256]{2,1,0:T(8,128)}, f32[32,32,256]{2,1,0:T(8,128)}, f32[3...) custom-call(f32[16,16,128]{2,1,0:T(8,128)S(1)} %get-tuple-element.45, ...), custom_call_target="tpu_custom_call" | custom-call | tf_op jit(solution)/shard_map/pallas_call | solution.py:41
  66.1 22.2 %all_to_all.5.all_ref = bf16[32,112,128]{2,1,0:T(8,128)(2,1)S(1)} all-to-all(bf16[32,112,128]{2,1,0:T(8,128)(2,1)S(1)} %get-tuple-element.54), channel_id=1, replica_groups=mesh['gx'=8,'gy'=4,'gz'=16] {'gx','gy'}, dimensions={0} | all-to-all | bytes 1835008 | tf_op jit(solution)/shard_map/all_to_all | solution.py:628
  88.3 6.4 %shard_map.64 = f32[16,16,128]{2,1,0:T(8,128)} custom-call(s32[2]{0:T(128)S(1)} %pad_add_fusion.place_ref, bf16[32,112,128]{2,1,0:T(8,128)(2,1)S(1)} %all_to_all.5.all_ref, f32[64,128]{1,0:T(8,128)S(1)} %get-tuple-element.55.own_ref, f32[32,32,256]{2,1,0:T(8,128)} %get-tuple-element.56.side_in, f32[32,32,256]{2,1,0:T(8,128)} %get-tuple-element.57.kx_in, ...), custom_call_target="tpu_custom_call" | custom-call | tf_op jit(solution)/shard_map/pallas_call | solution.py:41
  (1 shorter events, 0.0 us)
Async XLA Ops:
  2.2 23.1 %collective-permute-start.2 = (bf16[9,16,128]{2,1,0:T(8,128)(2,1)S(1)}, bf16[9,16,128]{2,1,0:T(8,128)(2,1)S(1)}, u32[]{:S(2)}, u32[]{:S(2)}) collective-permute-start(bf16[9,16,128]{2,1,0:T(8,128)(2,1)S(1)} %get-tuple-element.41.own_yp_ref), channel_id=1, source_target_pairs={{0,16},{16,32},{32,48},{48,0},{1,17},{17,33},{33,49},{49,1},{2,18}... | collective-permute-start | bytes 110600 | tf_op jit(solution)/shard_map/ppermute | solution.py:577
  6.2 22.5 %collective-permute-start.4 = (bf16[17,16,128]{2,1,0:T(8,128)(2,1)S(1)}, bf16[17,16,128]{2,1,0:T(8,128)(2,1)S(1)}, u32[]{:S(2)}, u32[]{:S(2)}) collective-permute-start(bf16[17,16,128]{2,1,0:T(8,128)(2,1)S(1)} %get-tuple-element.43), channel_id=1, source_target_pairs={{0,1},{1,2},{2,3},{3,4},{4,5},{5,6},{6,7},{7,8},{8,9},{9,10},{10,1... | collective-permute-start | bytes 208904 | tf_op jit(solution)/shard_map/ppermute | solution.py:577
  9.7 19.0 %collective-permute-start.5 = (bf16[17,16,128]{2,1,0:T(8,128)(2,1)S(1)}, bf16[17,16,128]{2,1,0:T(8,128)(2,1)S(1)}, u32[]{:S(2)}, u32[]{:S(2)}) collective-permute-start(bf16[17,16,128]{2,1,0:T(8,128)(2,1)S(1)} %get-tuple-element.44), channel_id=1, source_target_pairs={{0,15},{1,0},{2,1},{3,2},{4,3},{5,4},{6,5},{7,6},{8,7},{9,8},{10,9... | collective-permute-start | bytes 208904 | tf_op jit(solution)/shard_map/ppermute | solution.py:577
  19.2 6.1 %collective-permute-start.3 = (bf16[9,16,128]{2,1,0:T(8,128)(2,1)S(1)}, bf16[9,16,128]{2,1,0:T(8,128)(2,1)S(1)}, u32[]{:S(2)}, u32[]{:S(2)}) collective-permute-start(bf16[9,16,128]{2,1,0:T(8,128)(2,1)S(1)} %get-tuple-element.42.own_ym_ref), channel_id=1, source_target_pairs={{0,48},{16,0},{32,16},{48,32},{1,49},{17,1},{33,17},{49,33},{2,50}... | collective-permute-start | bytes 110600 | tf_op jit(solution)/shard_map/ppermute | solution.py:577
  22.6 3.8 %collective-permute-start = (bf16[9,16,128]{2,1,0:T(8,128)(2,1)S(1)}, bf16[9,16,128]{2,1,0:T(8,128)(2,1)S(1)}, u32[]{:S(2)}, u32[]{:S(2)}) collective-permute-start(bf16[9,16,128]{2,1,0:T(8,128)(2,1)S(1)} %get-tuple-element.39), channel_id=1, source_target_pairs={{0,64},{64,128},{128,192},{192,256},{256,320},{320,384},{384,448},... | collective-permute-start | bytes 110600 | tf_op jit(solution)/shard_map/ppermute | solution.py:577
  25.3 3.4 %collective-permute-start.1 = (bf16[9,16,128]{2,1,0:T(8,128)(2,1)S(1)}, bf16[9,16,128]{2,1,0:T(8,128)(2,1)S(1)}, u32[]{:S(2)}, u32[]{:S(2)}) collective-permute-start(bf16[9,16,128]{2,1,0:T(8,128)(2,1)S(1)} %get-tuple-element.40), channel_id=1, source_target_pairs={{0,448},{64,0},{128,64},{192,128},{256,192},{320,256},{384,320},{4... | collective-permute-start | bytes 110600 | tf_op jit(solution)/shard_map/ppermute | solution.py:577
  31.5 6.8 %collective-permute-start.6 = (bf16[16,16,128]{2,1,0:T(8,128)(2,1)S(1)}, bf16[16,16,128]{2,1,0:T(8,128)(2,1)S(1)}, u32[]{:S(2)}, u32[]{:S(2)}) collective-permute-start(bf16[16,16,128]{2,1,0:T(8,128)(2,1)S(1)} %get-tuple-element.46), channel_id=1, source_target_pairs={{0,1},{1,2},{2,3},{3,4},{4,5},{5,6},{6,7},{7,8},{8,9},{9,10},{10,1... | collective-permute-start | bytes 196616 | tf_op jit(solution)/shard_map/ppermute | solution.py:577
  33.4 5.9 %collective-permute-start.7 = (bf16[16,16,128]{2,1,0:T(8,128)(2,1)S(1)}, bf16[16,16,128]{2,1,0:T(8,128)(2,1)S(1)}, u32[]{:S(2)}, u32[]{:S(2)}) collective-permute-start(bf16[16,16,128]{2,1,0:T(8,128)(2,1)S(1)} %get-tuple-element.47), channel_id=1, source_target_pairs={{0,15},{1,0},{2,1},{3,2},{4,3},{5,4},{6,5},{7,6},{8,7},{9,8},{10,9... | collective-permute-start | bytes 196616 | tf_op jit(solution)/shard_map/ppermute | solution.py:577
  39.3 7.6 %collective-permute-start.8 = (bf16[5,16,8,128]{3,2,1,0:T(8,128)(2,1)S(1)}, bf16[5,16,8,128]{3,2,1,0:T(8,128)(2,1)S(1)}, u32[]{:S(2)}, u32[]{:S(2)}) collective-permute-start(bf16[5,16,8,128]{3,2,1,0:T(8,128)(2,1)S(1)} %get-tuple-element.48.high_ref), channel_id=1, source_target_pairs={{0,16},{16,32},{32,48},{48,0},{1,17},{17,33},{33,49},{49,1},{2,18}... | collective-permute-start | bytes 491528 | tf_op jit(solution)/shard_map/ppermute | solution.py:577
  41.3 6.8 %collective-permute-start.9 = (bf16[5,16,8,128]{3,2,1,0:T(8,128)(2,1)S(1)}, bf16[5,16,8,128]{3,2,1,0:T(8,128)(2,1)S(1)}, u32[]{:S(2)}, u32[]{:S(2)}) collective-permute-start(bf16[5,16,8,128]{3,2,1,0:T(8,128)(2,1)S(1)} %get-tuple-element.49.low_ref), channel_id=1, source_target_pairs={{0,48},{16,0},{32,16},{48,32},{1,49},{17,1},{33,17},{49,33},{2,50}... | collective-permute-start | bytes 491528 | tf_op jit(solution)/shard_map/ppermute | solution.py:577
  48.2 7.5 %collective-permute-start.10 = (bf16[5,8,32,128]{3,2,1,0:T(8,128)(2,1)S(1)}, bf16[5,8,32,128]{3,2,1,0:T(8,128)(2,1)S(1)}, u32[]{:S(2)}, u32[]{:S(2)}) collective-permute-start(bf16[5,8,32,128]{3,2,1,0:T(8,128)(2,1)S(1)} %get-tuple-element.50), channel_id=1, source_target_pairs={{0,64},{64,128},{128,192},{192,256},{256,320},{320,384},{384,448},... | collective-permute-start | bytes 983048 | tf_op jit(solution)/shard_map/ppermute | solution.py:577
  51.7 6.5 %collective-permute-start.11 = (bf16[5,8,32,128]{3,2,1,0:T(8,128)(2,1)S(1)}, bf16[5,8,32,128]{3,2,1,0:T(8,128)(2,1)S(1)}, u32[]{:S(2)}, u32[]{:S(2)}) collective-permute-start(bf16[5,8,32,128]{3,2,1,0:T(8,128)(2,1)S(1)} %get-tuple-element.51), channel_id=1, source_target_pairs={{0,448},{64,0},{128,64},{192,128},{256,192},{320,256},{384,320},{4... | collective-permute-start | bytes 983048 | tf_op jit(solution)/shard_map/ppermute | solution.py:577

commit v5 on v4

--- a/solution.py
+++ b/solution.py
@@ -23,7 +23,8 @@
 COARSE_LOW = 10
 MIDDLE = 70
 MIDDLE_LOW = 3
-CHUNK = 112
+HEAD = 26
+CHUNK = 96
 FINE_PLANES = pl.ds(6, 20)
 MIDDLE_PLANES = pl.ds(1, 13)
 
@@ -131,21 +132,19 @@
 
 
 def mobility_kernel(
-    conc_ref, side_ref, order_ref, ids_ref, xm_ref, xp_ref, ym_ref, yp_ref, zm_ref, zp_ref,
-    own_ym_ref, own_yp_ref, mob_ref, keep_ref, zm_out, zp_out, work, weights,
+    conc_ref, side_ref, order_ref, ids_ref, xm_ref, xp_ref, ym_ref, yp_ref,
+    own_ym_ref, own_yp_ref, own_zm_ref, own_zp_ref, mob_ref, zm_out, zp_out, work, weights,
 ):
     own = lane_ids(ids_ref)
     lane = iota((16, LANES), 1)
     row = iota((16, LANES), 0)
     last = lane % BRICK == BRICK - 1
-    edge = last | (lane % BRICK == 0)
+    edge = (last | (lane % BRICK == 0)) & (lane != 0) & (lane != LANES - 1)
 
     lane8 = iota((8, LANES), 1)
-    after = jnp.where(
-        lane8 >= LANES - BRICK, join_ids(zp_ref[16]), roll(own, -BRICK, 1)
-    )
-    before = jnp.where(lane8 < BRICK, join_ids(zm_ref[16]), roll(own, BRICK, 1))
-    beside = jnp.where(lane8 % BRICK == BRICK - 1, after, before)
+    beside = jnp.where(
+        lane8 % BRICK == BRICK - 1, roll(own, -BRICK, 1), roll(own, BRICK, 1)
+    )
     for other in range(SLOTS):
         match = (own == beside[other : other + 1]).astype(F32)
         for slot in range(SLOTS):
@@ -170,8 +169,6 @@
     def plane(x, carry_in):
         conc = conc_ref[x]
         base = 1.0 + 8.0 * square(conc * (1.0 - conc))
-        zlow = zm_ref[x].astype(F32)
-        zhigh = zp_ref[x].astype(F32)
         along_y = jnp.zeros((16, LANES), F32)
         along_z = jnp.zeros((16, LANES), F32)
         along_x = jnp.zeros((16, LANES), F32)
@@ -186,9 +183,7 @@
             along_y = along_y + square(roll(here, -1, 0) - here)
             right = roll(here, -1, 1)
             along_z = along_z + square(right - here)
-            right = jnp.where(lane == LANES - 1, zhigh[:, slot : slot + 1], right)
-            left = jnp.where(lane == 0, zlow[:, slot : slot + 1], roll(here, 1, 1))
-            facing.append(jnp.where(last, right, left))
+            facing.append(jnp.where(last, right, roll(here, 1, 1)))
         along_y = jnp.where(row == 15, 0.0, along_y)
         along_z = jnp.where(last, 0.0, along_z)
         remapped = jnp.zeros((16, LANES), F32)
@@ -219,7 +214,6 @@
         value = value + jnp.where(row == 0, bottom[x : x + 1], 0.0)
         value = value + jnp.where(row == 15, top[x : x + 1], 0.0)
         mob_ref[x] = value
-        keep_ref[x] = value
         conc, side = conc_ref[x], side_ref[x]
         first = jnp.where(
             lane < 43, value, jnp.where(lane < 86, roll(conc, 43, 1), roll(side, 86, 1))
@@ -229,12 +223,49 @@
             lane >= 85, value, jnp.where(lane >= 42, roll(conc, -43, 1), roll(side, -86, 1))
         )
         zp_out[x] = final.astype(BF16)
-
-
-def split_kernel(mob_ref, conc_ref, side_ref, zm_ref, zp_ref, low_ref, high_ref):
-    for place, ref in enumerate((mob_ref, conc_ref, side_ref, zm_ref, zp_ref)):
-        low_ref[place] = ref[:, :8].astype(BF16)
-        high_ref[place] = ref[:, 8:].astype(BF16)
+    zm_out[16:] = own_zm_ref[...]
+    zp_out[16:] = own_zp_ref[...]
+
+
+def facing_squares(near_ref, far_ref, near_lane, far_lane):
+    near = near_ref[:16].reshape(256, LANES)
+    far = far_ref[:16].reshape(256, LANES)
+    near_ids = join_ids(near_ref[16])
+    far_ids = join_ids(far_ref[16])
+    diagonal = iota((8, LANES), 0) == iota((8, LANES), 1)
+    slots = iota((8, LANES), 1) < SLOTS
+
+    def squares(cells, ids, others, other_ids, target):
+        along = jnp.sum(jnp.where(diagonal, ids, 0.0), axis=0, keepdims=True)
+        match = ((other_ids == along) & slots).astype(F32)
+        match = jnp.concatenate([match, jnp.zeros((LANES - 8, LANES), F32)], axis=0)
+        seen = jnp.dot(others, match.astype(BF16), preferred_element_type=F32)
+        place = (iota((LANES, LANES), 1) == target).astype(F32)
+        total = select_dot(square(seen - cells.astype(F32)), place)
+        return total.reshape(16, 16, LANES)
+
+    return (
+        squares(near, near_ids, far, far_ids, near_lane),
+        squares(far, far_ids, near, near_ids, far_lane),
+    )
+
+
+def split_kernel(
+    mob_ref, conc_ref, side_ref, left_ref, right_ref, zm_ref, zp_ref,
+    out_ref, keep_ref, down_ref, up_ref, low_ref, high_ref,
+):
+    own_low, far_low = facing_squares(zm_ref, left_ref.at[16:], 0, LANES - 1)
+    own_high, far_high = facing_squares(zp_ref, right_ref.at[16:], LANES - 1, 0)
+    mob = mob_ref[...] + own_low + own_high
+    out_ref[...] = mob
+    keep_ref[...] = mob
+    down = (left_ref[:16].astype(F32) + far_low).astype(BF16)
+    up = (right_ref[:16].astype(F32) + far_high).astype(BF16)
+    down_ref[...] = down
+    up_ref[...] = up
+    for place, value in enumerate((mob, conc_ref[...], side_ref[...], down, up)):
+        low_ref[place] = value[:, :8].astype(BF16)
+        high_ref[place] = value[:, 8:].astype(BF16)
 
 
 def rows_kernel(below_ref, low_ref, high_ref, above_ref, xl_ref, xh_ref):
@@ -409,9 +440,15 @@
     src = iota((RING, LANES), 0)
     dst = iota((RING, LANES), 1)
     cell = jnp.where(src < 192, src, src - RING)
-    pick_low = (cell == 4 * (dst - COARSE_LOW)) & (dst < COARSE)
-    pick_high = (cell == 4 * (dst - 64 - COARSE_LOW)) & (dst >= 64) & (dst < 64 + COARSE)
-    picks = jnp.concatenate([pick_low.astype(F32), pick_high.astype(F32)], axis=0)
+    coarse = (cell + 4 * COARSE_LOW) // 4
+    there = ((cell & 3) == 0) & (coarse >= 0) & (coarse < COARSE)
+    head = there & (coarse < HEAD)
+    tail = there & (coarse >= HEAD)
+    sides = [there & (coarse == dst), there & (coarse + COARSE == dst)]
+    picks0 = sides + [head & (coarse + 2 * COARSE == dst)]
+    picks1 = sides + [tail & (coarse + 2 * COARSE - HEAD == dst)]
+    picks0 = jnp.concatenate([pick.astype(F32) for pick in picks0], axis=0).astype(BF16)
+    picks1 = jnp.concatenate([pick.astype(F32) for pick in picks1], axis=0).astype(BF16)
     pick_middle = ((cell == 2 * (dst - MIDDLE_LOW)) & (dst < MIDDLE)).astype(F32)
     firsts = []
     seconds = []
@@ -423,18 +460,23 @@
         k2y = upper_of(k2y, 2, 0) * (1.0 / 16.0)
         k2z = pair_sum(k1z_ref[i] + k1z_ref[i + 1], 2, 0)
         k2z = upper_of(k2z, 2, 1) * (1.0 / 16.0)
-        firsts.append(jnp.concatenate([f2[8:24], k2x[8:24]], axis=1))
-        seconds.append(jnp.concatenate([k2y[8:24], k2z[8:24]], axis=1))
-    rows[...] = select_dot(jnp.concatenate(firsts + seconds, axis=0), picks)
+        f2, k2x, k2y, k2z = (cells[8:24] for cells in (f2, k2x, k2y, k2z))
+        k2z = k2z.astype(BF16)
+        high = f2.astype(BF16)
+        low = (f2 - high.astype(F32)).astype(BF16)
+        firsts.append(jnp.concatenate([high, low, k2z], axis=1))
+        seconds.append(jnp.concatenate([k2x.astype(BF16), k2y.astype(BF16), k2z], axis=1))
+    firsts = jnp.concatenate(firsts, axis=0)
+    seconds = jnp.concatenate(seconds, axis=0)
+    rows[pl.ds(0, 64), :] = jnp.dot(firsts, picks0, preferred_element_type=F32)
+    rows[pl.ds(64, 64), :] = jnp.dot(seconds, picks1, preferred_element_type=F32)
     coarse = rows[pl.ds(0, 32, stride=4), :]
     rows[...] = select_dot(
         jnp.concatenate([e1[4 + i, 8:24] for i in range(8)], axis=0), pick_middle
     )
     middle = rows[pl.ds(0, 64, stride=2), :]
     own_ref[...] = middle
-    high = coarse.astype(BF16)
-    low = (coarse[:16] - high[:16].astype(F32)).astype(BF16)
-    chunk = jnp.concatenate([high, low, middle.astype(BF16)], axis=0)
+    chunk = jnp.concatenate([coarse.astype(BF16), middle.astype(BF16)], axis=0)
     for k in range(32):
         chunk_ref[k] = chunk
     for copy in copies:
@@ -475,7 +517,6 @@
         for q in range(4):
             s = source(p - 1, q - 1)
             first = all_ref[s, pl.ds(0, 16), :].astype(F32)
-            first = first + all_ref[s, pl.ds(32, 16), :].astype(F32)
             second = all_ref[s, pl.ds(16, 16), :].astype(F32)
             for i in range(4):
                 pair0[4 * p + i, pl.ds(4 * q, 4), :] = first[4 * i : 4 * i + 4]
@@ -485,7 +526,7 @@
             if p == 0 and q == 0:
                 cells = own_ref[...]
             else:
-                cells = all_ref[source(p, q), pl.ds(48, 64), :].astype(F32)
+                cells = all_ref[source(p, q), pl.ds(32, 64), :].astype(F32)
             for i in range(1, 15):
                 if (i - 4) // 8 != p:
                     continue
@@ -499,14 +540,18 @@
                     mid[i, pl.ds(12, 4), :] = block[:4]
 
     used = iota((16, LANES), 1) < COARSE
+    head = iota((16, LANES), 1) < HEAD
     for x in range(-6, 17):
         k = x % 32
         first = pair0[k]
         second = pair1[k]
-        f2[k] = jnp.where(used, first, 0.0)
-        c2x[k] = jnp.where(used, roll(first, 64, 1), 0.0)
-        c2y[k] = jnp.where(used, second, 0.0)
-        c2z[k] = jnp.where(used, roll(second, 64, 1), 0.0)
+        f2[k] = jnp.where(used, first + roll(first, -COARSE, 1), 0.0)
+        c2x[k] = jnp.where(used, second, 0.0)
+        c2y[k] = jnp.where(used, roll(second, -COARSE, 1), 0.0)
+        last = jnp.where(
+            head, roll(first, -2 * COARSE, 1), roll(second, HEAD - 2 * COARSE, 1)
+        )
+        c2z[k] = jnp.where(used, last, 0.0)
     for xs in groups(range(-5, 17), 11):
         done = []
         for x in xs:
@@ -593,19 +638,22 @@
     faces = (
         shift(xp, "gx", 1), shift(xm, "gx", -1),
         shift(yp, "gy", 1), shift(ym, "gy", -1),
-        shift(zp, "gz", 1), shift(zm, "gz", -1),
     )
     pack = ((16, 16, LANES), BF16)
-    mobility, keep, zm, zp = call(
+    partial, send_zm, send_zp = call(
         mobility_kernel,
-        [brick, brick, pack, pack],
-        (conc, side, order, ids) + faces + (ym, yp),
+        [brick, ((33, 16, LANES), BF16), ((33, 16, LANES), BF16)],
+        (conc, side, order, ids) + faces + (ym, yp, zm, zp),
         scratch=[brick, ((64, 8, LANES), F32)],
     )
-    left = shift(zp, "gz", 1)
-    right = shift(zm, "gz", -1)
+    left = shift(send_zp, "gz", 1)
+    right = shift(send_zm, "gz", -1)
     half = ((5, 16, 8, LANES), BF16)
-    low, high = call(split_kernel, [half, half], (keep, conc, side, left, right))
+    mobility, keep, left, right, low, high = call(
+        split_kernel,
+        [brick, brick, pack, pack, half, half],
+        (partial, conc, side, left, right, zm, zp),
+    )
     below = shift(high, "gy", 1)
     above = shift(low, "gy", -1)
     slab = ((5, 8, 32, LANES), BF16)

time: 95.3 us -> 89.2 us (0.936)
  starting transfers between devices: 39.5 us -> 34.8 us
    ppermute x12 -> x10, starting transfers between devices: 39.5 us -> 34.8 us  [shift(): lax.ppermute(x, axis, [(i, (i + direction) % count) for i in range(count)])]
    ppermute x12 -> x10, waiting for transfers between devices: 13.4 us -> 12.5 us  [shift(): lax.ppermute(x, axis, [(i, (i + direction) % count) for i in range(count)])]
  transfers between devices with their start and end apart: 12 -> 10, of which waited for: 8 -> 8; matrix products, arithmetic and copies ran while one was open for 0% -> 0% of each run, Pallas kernels for 0% -> 0%
where the time goes in v5:
time: 89.2 us; the launch traced here: 88.9 us
  starting transfers between devices  34.8 us (39%)
  blocking collectives  21.3 us (24%)
  Pallas kernels  19.5 us (22%)
  waiting for transfers between devices  12.5 us (14%)
    ppermute x10, starting transfers between devices, shift(): lax.ppermute(x, axis, [(i, (i + direction) % count) for i in range(count)])  34.8 us
    all_to_all x1, blocking collectives, body(): chunks = lax.all_to_all(chunk, ('gx', 'gy'), 0, 0, tiled=True)  21.3 us
    pallas_call x6, Pallas kernels, call(): pl.pallas_call(kernel, out_shape=[pltpu.MemorySpace.HBM(*out) if place is...  19.5 us
    ppermute x10, waiting for transfers between devices, shift(): lax.ppermute(x, axis, [(i, (i + direction) % count) for i in range(count)])  12.5 us
  transfers between devices with their start and end apart: 10, of which 8 were waited for; matrix products, arithmetic and copies ran while one was open for 0% of the time, Pallas kernels for 0%

profile of v5, /device:TPU:1, one launch (start us, length us, event | category | flops | bytes accessed | tf_op | source)
XLA Modules:
  0.0 88.9 jit_solution(4687574135515480640)
XLA Ops:
  0.6 1.6 %shard_map.59 = (f32[16,16,128]{2,1,0:T(8,128)S(1)}, f32[16,16,128]{2,1,0:T(8,128)S(1)}, bf16[8,16,16,128]{3,2,1,0:T(8,128)(2,1)S(1)}, s32[1,1,8,8]{3,2,1,0:T(8,...) custom-call(f32[16,16,128]{2,1,0:T(8,128)} %conc_in.1, ...), custom_call_target="tpu_custom_call" | custom-call | tf_op jit(solution)/shard_map/pallas_call | solution.py:42
  2.2 3.9 %collective-permute-start.2 = (bf16[9,16,128]{2,1,0:T(8,128)(2,1)S(1)}, bf16[9,16,128]{2,1,0:T(8,128)(2,1)S(1)}, u32[]{:S(2)}, u32[]{:S(2)}) collective-permute-start(bf16[9,16,128]{2,1,0:T(8,128)(2,1)S(1)} %get-tuple-element.44.own_yp_ref), channel_id=1, source_target_pairs={{0,16},{16,32},{32,48},{48,0},{1,17},{17,33},{33,49},{49,1},{2,18}... | collective-permute-start | bytes 110600 | tf_op jit(solution)/shard_map/ppermute | solution.py:622
  6.2 3.2 %collective-permute-start.3 = (bf16[9,16,128]{2,1,0:T(8,128)(2,1)S(1)}, bf16[9,16,128]{2,1,0:T(8,128)(2,1)S(1)}, u32[]{:S(2)}, u32[]{:S(2)}) collective-permute-start(bf16[9,16,128]{2,1,0:T(8,128)(2,1)S(1)} %get-tuple-element.45.own_ym_ref), channel_id=1, source_target_pairs={{0,48},{16,0},{32,16},{48,32},{1,49},{17,1},{33,17},{49,33},{2,50}... | collective-permute-start | bytes 110600 | tf_op jit(solution)/shard_map/ppermute | solution.py:622
  9.4 2.6 %collective-permute-start = (bf16[9,16,128]{2,1,0:T(8,128)(2,1)S(1)}, bf16[9,16,128]{2,1,0:T(8,128)(2,1)S(1)}, u32[]{:S(2)}, u32[]{:S(2)}) collective-permute-start(bf16[9,16,128]{2,1,0:T(8,128)(2,1)S(1)} %get-tuple-element.42), channel_id=1, source_target_pairs={{0,64},{64,128},{128,192},{192,256},{256,320},{320,384},{384,448},... | collective-permute-start | bytes 110600 | tf_op jit(solution)/shard_map/ppermute | solution.py:622
  12.0 4.2 %collective-permute-start.1 = (bf16[9,16,128]{2,1,0:T(8,128)(2,1)S(1)}, bf16[9,16,128]{2,1,0:T(8,128)(2,1)S(1)}, u32[]{:S(2)}, u32[]{:S(2)}) collective-permute-start(bf16[9,16,128]{2,1,0:T(8,128)(2,1)S(1)} %get-tuple-element.43), channel_id=1, source_target_pairs={{0,448},{64,0},{128,64},{192,128},{256,192},{320,256},{384,320},{4... | collective-permute-start | bytes 110600 | tf_op jit(solution)/shard_map/ppermute | solution.py:622
  16.2 0.0 collective-permute-done.2.ym_ref
  16.2 0.0 collective-permute-done.3.yp_ref
  16.2 0.7 collective-permute-done.xm_ref
  16.9 0.2 collective-permute-done.1.xp_ref
  17.1 1.9 %shard_map.60 = (f32[16,16,128]{2,1,0:T(8,128)S(1)}, bf16[33,16,128]{2,1,0:T(8,128)(2,1)S(1)}, bf16[33,16,128]{2,1,0:T(8,128)(2,1)S(1)}) custom-call(f32[16,16,128]{2,1,0:T(8,128)S(1)} %get-tuple-element.38.conc_ref.conc_in, f32[16,16,128]{2,1,0:T(8,128)S(1)} %get-tuple-element.39.side_ref.side_in, bf16[8,16,16,128]{3,2,1,0:T(8,128)(2,1)S(1)} %get-tuple-element.40.order_ref, ...), custom_call_target="tpu_custom_call" | custom-call | tf_op jit(solution)/shard_map/pallas_call | solution.py:42
  19.0 1.9 %collective-permute-start.4 = (bf16[33,16,128]{2,1,0:T(8,128)(2,1)S(1)}, bf16[33,16,128]{2,1,0:T(8,128)(2,1)S(1)}, u32[]{:S(2)}, u32[]{:S(2)}) collective-permute-start(bf16[33,16,128]{2,1,0:T(8,128)(2,1)S(1)} %get-tuple-element.49), channel_id=1, source_target_pairs={{0,1},{1,2},{2,3},{3,4},{4,5},{5,6},{6,7},{7,8},{8,9},{9,10},{10,1... | collective-permute-start | bytes 405512 | tf_op jit(solution)/shard_map/ppermute | solution.py:622
  20.9 9.4 %collective-permute-start.5 = (bf16[33,16,128]{2,1,0:T(8,128)(2,1)S(1)}, bf16[33,16,128]{2,1,0:T(8,128)(2,1)S(1)}, u32[]{:S(2)}, u32[]{:S(2)}) collective-permute-start(bf16[33,16,128]{2,1,0:T(8,128)(2,1)S(1)} %get-tuple-element.50), channel_id=1, source_target_pairs={{0,15},{1,0},{2,1},{3,2},{4,3},{5,4},{6,5},{7,6},{8,7},{9,8},{10,9... | collective-permute-start | bytes 405512 | tf_op jit(solution)/shard_map/ppermute | solution.py:622
  30.3 2.0 %collective-permute-done.4.left_ref = bf16[33,16,128]{2,1,0:T(8,128)(2,1)S(1)} collective-permute-done((bf16[33,16,128]{2,1,0:T(8,128)(2,1)S(1)}, bf16[33,16,128]{2,1,0:T(8,128)(2,1)S(1)}, u32[]{:S(2)}, u32[]{:S(2)}) %collective-permute-start.4) | collective-permute-done | bytes 135200 | tf_op jit(solution)/shard_map/ppermute | solution.py:622
  32.3 1.0 %collective-permute-done.5.right_ref = bf16[33,16,128]{2,1,0:T(8,128)(2,1)S(1)} collective-permute-done((bf16[33,16,128]{2,1,0:T(8,128)(2,1)S(1)}, bf16[33,16,128]{2,1,0:T(8,128)(2,1)S(1)}, u32[]{:S(2)}, u32[]{:S(2)}) %collective-permute-start.5) | collective-permute-done | bytes 135200 | tf_op jit(solution)/shard_map/ppermute | solution.py:622
  33.3 1.3 %shard_map.61 = (f32[16,16,128]{2,1,0:T(8,128)}, f32[16,16,128]{2,1,0:T(8,128)S(1)}, bf16[16,16,128]{2,1,0:T(8,128)(2,1)S(1)}, bf16[16,16,128]{2,1,0:T(8,128)(2,...) custom-call(f32[16,16,128]{2,1,0:T(8,128)S(1)} %get-tuple-element.48.mob_ref, ...), custom_call_target="tpu_custom_call" | custom-call | tf_op jit(solution)/shard_map/pallas_call | solution.py:42
  34.6 1.9 %collective-permute-start.6 = (bf16[5,16,8,128]{3,2,1,0:T(8,128)(2,1)S(1)}, bf16[5,16,8,128]{3,2,1,0:T(8,128)(2,1)S(1)}, u32[]{:S(2)}, u32[]{:S(2)}) collective-permute-start(bf16[5,16,8,128]{3,2,1,0:T(8,128)(2,1)S(1)} %get-tuple-element.54.high_ref), channel_id=1, source_target_pairs={{0,16},{16,32},{32,48},{48,0},{1,17},{17,33},{33,49},{49,1},{2,18}... | collective-permute-start | bytes 491528 | tf_op jit(solution)/shard_map/ppermute | solution.py:622
  36.5 4.6 %collective-permute-start.7 = (bf16[5,16,8,128]{3,2,1,0:T(8,128)(2,1)S(1)}, bf16[5,16,8,128]{3,2,1,0:T(8,128)(2,1)S(1)}, u32[]{:S(2)}, u32[]{:S(2)}) collective-permute-start(bf16[5,16,8,128]{3,2,1,0:T(8,128)(2,1)S(1)} %get-tuple-element.55.low_ref), channel_id=1, source_target_pairs={{0,48},{16,0},{32,16},{48,32},{1,49},{17,1},{33,17},{49,33},{2,50}... | collective-permute-start | bytes 491528 | tf_op jit(solution)/shard_map/ppermute | solution.py:622
  41.1 1.5 %collective-permute-done.6.below_ref = bf16[5,16,8,128]{3,2,1,0:T(8,128)(2,1)S(1)} collective-permute-done((bf16[5,16,8,128]{3,2,1,0:T(8,128)(2,1)S(1)}, bf16[5,16,8,128]{3,2,1,0:T(8,128)(2,1)S(1)}, u32[]{:S(2)}, u32[]{:S(2)}) %collective-permute-start.6) | collective-permute-done | bytes 163872 | tf_op jit(solution)/shard_map/ppermute | solution.py:622
  42.6 0.7 collective-permute-done.7.above_ref
  43.3 0.1 shard_map.62
  43.4 3.0 %collective-permute-start.8 = (bf16[5,8,32,128]{3,2,1,0:T(8,128)(2,1)S(1)}, bf16[5,8,32,128]{3,2,1,0:T(8,128)(2,1)S(1)}, u32[]{:S(2)}, u32[]{:S(2)}) collective-permute-start(bf16[5,8,32,128]{3,2,1,0:T(8,128)(2,1)S(1)} %get-tuple-element.56), channel_id=1, source_target_pairs={{0,64},{64,128},{128,192},{192,256},{256,320},{320,384},{384,448},... | collective-permute-start | bytes 983048 | tf_op jit(solution)/shard_map/ppermute | solution.py:622
  46.5 0.0 collective-permute-start.9
  46.5 0.1 pad_add_fusion.place_ref
  46.6 3.9 %collective-permute-done.8.xm_ref = bf16[5,8,32,128]{3,2,1,0:T(8,128)(2,1)S(1)} collective-permute-done((bf16[5,8,32,128]{3,2,1,0:T(8,128)(2,1)S(1)}, bf16[5,8,32,128]{3,2,1,0:T(8,128)(2,1)S(1)}, u32[]{:S(2)}, u32[]{:S(2)}) %collective-permute-start.8) | collective-permute-done | bytes 327712 | tf_op jit(solution)/shard_map/ppermute | solution.py:622
  50.5 2.5 %collective-permute-done.9.xp_ref = bf16[5,8,32,128]{3,2,1,0:T(8,128)(2,1)S(1)} collective-permute-done((bf16[5,8,32,128]{3,2,1,0:T(8,128)(2,1)S(1)}, bf16[5,8,32,128]{3,2,1,0:T(8,128)(2,1)S(1)}, u32[]{:S(2)}, u32[]{:S(2)}) %collective-permute-start.9) | collective-permute-done | bytes 327712 | tf_op jit(solution)/shard_map/ppermute | solution.py:622
  53.0 8.0 %shard_map.63 = (f32[64,128]{1,0:T(8,128)S(1)}, bf16[32,96,128]{2,1,0:T(8,128)(2,1)S(1)}, f32[32,32,256]{2,1,0:T(8,128)}, f32[32,32,256]{2,1,0:T(8,128)}, f32[32...) custom-call(f32[16,16,128]{2,1,0:T(8,128)S(1)} %get-tuple-element.51, ...), custom_call_target="tpu_custom_call" | custom-call | tf_op jit(solution)/shard_map/pallas_call | solution.py:42
  61.0 21.3 %all_to_all.5.all_ref = bf16[32,96,128]{2,1,0:T(8,128)(2,1)S(1)} all-to-all(bf16[32,96,128]{2,1,0:T(8,128)(2,1)S(1)} %get-tuple-element.60), channel_id=1, replica_groups=mesh['gx'=8,'gy'=4,'gz'=16] {'gx','gy'}, dimensions={0} | all-to-all | bytes 1572864 | tf_op jit(solution)/shard_map/all_to_all | solution.py:676
  82.3 6.6 %shard_map.64 = f32[16,16,128]{2,1,0:T(8,128)} custom-call(s32[2]{0:T(128)S(1)} %pad_add_fusion.place_ref, bf16[32,96,128]{2,1,0:T(8,128)(2,1)S(1)} %all_to_all.5.all_ref, f32[64,128]{1,0:T(8,128)S(1)} %get-tuple-element.61.own_ref, f32[32,32,256]{2,1,0:T(8,128)} %get-tuple-element.62.side_in, f32[32,32,256]{2,1,0:T(8,128)} %get-tuple-element.63.kx_in, ...), custom_call_target="tpu_custom_call" | custom-call | tf_op jit(solution)/shard_map/pallas_call | solution.py:42
Async XLA Ops:
  2.2 14.0 %collective-permute-start.2 = (bf16[9,16,128]{2,1,0:T(8,128)(2,1)S(1)}, bf16[9,16,128]{2,1,0:T(8,128)(2,1)S(1)}, u32[]{:S(2)}, u32[]{:S(2)}) collective-permute-start(bf16[9,16,128]{2,1,0:T(8,128)(2,1)S(1)} %get-tuple-element.44.own_yp_ref), channel_id=1, source_target_pairs={{0,16},{16,32},{32,48},{48,0},{1,17},{17,33},{33,49},{49,1},{2,18}... | collective-permute-start | bytes 110600 | tf_op jit(solution)/shard_map/ppermute | solution.py:622
  6.2 10.0 %collective-permute-start.3 = (bf16[9,16,128]{2,1,0:T(8,128)(2,1)S(1)}, bf16[9,16,128]{2,1,0:T(8,128)(2,1)S(1)}, u32[]{:S(2)}, u32[]{:S(2)}) collective-permute-start(bf16[9,16,128]{2,1,0:T(8,128)(2,1)S(1)} %get-tuple-element.45.own_ym_ref), channel_id=1, source_target_pairs={{0,48},{16,0},{32,16},{48,32},{1,49},{17,1},{33,17},{49,33},{2,50}... | collective-permute-start | bytes 110600 | tf_op jit(solution)/shard_map/ppermute | solution.py:622
  9.4 7.5 %collective-permute-start = (bf16[9,16,128]{2,1,0:T(8,128)(2,1)S(1)}, bf16[9,16,128]{2,1,0:T(8,128)(2,1)S(1)}, u32[]{:S(2)}, u32[]{:S(2)}) collective-permute-start(bf16[9,16,128]{2,1,0:T(8,128)(2,1)S(1)} %get-tuple-element.42), channel_id=1, source_target_pairs={{0,64},{64,128},{128,192},{192,256},{256,320},{320,384},{384,448},... | collective-permute-start | bytes 110600 | tf_op jit(solution)/shard_map/ppermute | solution.py:622
  12.0 5.1 %collective-permute-start.1 = (bf16[9,16,128]{2,1,0:T(8,128)(2,1)S(1)}, bf16[9,16,128]{2,1,0:T(8,128)(2,1)S(1)}, u32[]{:S(2)}, u32[]{:S(2)}) collective-permute-start(bf16[9,16,128]{2,1,0:T(8,128)(2,1)S(1)} %get-tuple-element.43), channel_id=1, source_target_pairs={{0,448},{64,0},{128,64},{192,128},{256,192},{320,256},{384,320},{4... | collective-permute-start | bytes 110600 | tf_op jit(solution)/shard_map/ppermute | solution.py:622
  19.0 13.3 %collective-permute-start.4 = (bf16[33,16,128]{2,1,0:T(8,128)(2,1)S(1)}, bf16[33,16,128]{2,1,0:T(8,128)(2,1)S(1)}, u32[]{:S(2)}, u32[]{:S(2)}) collective-permute-start(bf16[33,16,128]{2,1,0:T(8,128)(2,1)S(1)} %get-tuple-element.49), channel_id=1, source_target_pairs={{0,1},{1,2},{2,3},{3,4},{4,5},{5,6},{6,7},{7,8},{8,9},{9,10},{10,1... | collective-permute-start | bytes 405512 | tf_op jit(solution)/shard_map/ppermute | solution.py:622
  20.9 12.4 %collective-permute-start.5 = (bf16[33,16,128]{2,1,0:T(8,128)(2,1)S(1)}, bf16[33,16,128]{2,1,0:T(8,128)(2,1)S(1)}, u32[]{:S(2)}, u32[]{:S(2)}) collective-permute-start(bf16[33,16,128]{2,1,0:T(8,128)(2,1)S(1)} %get-tuple-element.50), channel_id=1, source_target_pairs={{0,15},{1,0},{2,1},{3,2},{4,3},{5,4},{6,5},{7,6},{8,7},{9,8},{10,9... | collective-permute-start | bytes 405512 | tf_op jit(solution)/shard_map/ppermute | solution.py:622
  34.6 8.0 %collective-permute-start.6 = (bf16[5,16,8,128]{3,2,1,0:T(8,128)(2,1)S(1)}, bf16[5,16,8,128]{3,2,1,0:T(8,128)(2,1)S(1)}, u32[]{:S(2)}, u32[]{:S(2)}) collective-permute-start(bf16[5,16,8,128]{3,2,1,0:T(8,128)(2,1)S(1)} %get-tuple-element.54.high_ref), channel_id=1, source_target_pairs={{0,16},{16,32},{32,48},{48,0},{1,17},{17,33},{33,49},{49,1},{2,18}... | collective-permute-start | bytes 491528 | tf_op jit(solution)/shard_map/ppermute | solution.py:622
  36.5 6.8 %collective-permute-start.7 = (bf16[5,16,8,128]{3,2,1,0:T(8,128)(2,1)S(1)}, bf16[5,16,8,128]{3,2,1,0:T(8,128)(2,1)S(1)}, u32[]{:S(2)}, u32[]{:S(2)}) collective-permute-start(bf16[5,16,8,128]{3,2,1,0:T(8,128)(2,1)S(1)} %get-tuple-element.55.low_ref), channel_id=1, source_target_pairs={{0,48},{16,0},{32,16},{48,32},{1,49},{17,1},{33,17},{49,33},{2,50}... | collective-permute-start | bytes 491528 | tf_op jit(solution)/shard_map/ppermute | solution.py:622
  43.4 7.1 %collective-permute-start.8 = (bf16[5,8,32,128]{3,2,1,0:T(8,128)(2,1)S(1)}, bf16[5,8,32,128]{3,2,1,0:T(8,128)(2,1)S(1)}, u32[]{:S(2)}, u32[]{:S(2)}) collective-permute-start(bf16[5,8,32,128]{3,2,1,0:T(8,128)(2,1)S(1)} %get-tuple-element.56), channel_id=1, source_target_pairs={{0,64},{64,128},{128,192},{192,256},{256,320},{320,384},{384,448},... | collective-permute-start | bytes 983048 | tf_op jit(solution)/shard_map/ppermute | solution.py:622
  46.5 6.5 %collective-permute-start.9 = (bf16[5,8,32,128]{3,2,1,0:T(8,128)(2,1)S(1)}, bf16[5,8,32,128]{3,2,1,0:T(8,128)(2,1)S(1)}, u32[]{:S(2)}, u32[]{:S(2)}) collective-permute-start(bf16[5,8,32,128]{3,2,1,0:T(8,128)(2,1)S(1)} %get-tuple-element.57), channel_id=1, source_target_pairs={{0,448},{64,0},{128,64},{192,128},{256,192},{320,256},{384,320},{4... | collective-permute-start | bytes 983048 | tf_op jit(solution)/shard_map/ppermute | solution.py:622

commit v6 on v5

--- a/solution.py
+++ b/solution.py
@@ -22,9 +22,8 @@
 COARSE = 51
 COARSE_LOW = 10
 MIDDLE = 70
-MIDDLE_LOW = 3
 HEAD = 26
-CHUNK = 96
+CHUNK = 64
 FINE_PLANES = pl.ds(6, 20)
 MIDDLE_PLANES = pl.ds(1, 13)
 
@@ -132,8 +131,8 @@
 
 
 def mobility_kernel(
-    conc_ref, side_ref, order_ref, ids_ref, xm_ref, xp_ref, ym_ref, yp_ref,
-    own_ym_ref, own_yp_ref, own_zm_ref, own_zp_ref, mob_ref, zm_out, zp_out, work, weights,
+    conc_ref, side_ref, order_ref, ids_ref, xm_ref, xp_ref, yp_ref,
+    own_yp_ref, own_zm_ref, own_zp_ref, mob_ref, beyond_ref, zm_out, zp_out, work, weights,
 ):
     own = lane_ids(ids_ref)
     lane = iota((16, LANES), 1)
@@ -150,16 +149,16 @@
         for slot in range(SLOTS):
             weights[slot * SLOTS + other] = jnp.broadcast_to(match[slot : slot + 1], (8, LANES))
 
-    def across(face_ref, ids, center):
-        facing = [face_ref[other].astype(F32) for other in range(SLOTS)]
+    def across(center, ids, facing, facing_ids):
+        facing = [facing(other).astype(F32) for other in range(SLOTS)]
         total = None
         for slot in range(SLOTS):
             value = None
             for other in range(SLOTS):
-                match = (own[slot : slot + 1] == ids[other : other + 1]).astype(F32)
-                term = match * facing[other]
+                match = ids[slot : slot + 1] == facing_ids[other : other + 1]
+                term = match.astype(F32) * facing[other]
                 value = term if value is None else value + term
-            part = square(value - center(slot))
+            part = square(value - center(slot).astype(F32))
             total = part if total is None else total + part
         return total
 
@@ -202,16 +201,19 @@
     for x in range(16):
         carry = plane(x, carry)
     work[0] = work[0] + across(
-        xm_ref, join_ids(xm_ref[SLOTS]), lambda s: order_ref[s, 0].astype(F32)
+        lambda k: order_ref[k, 0], own, lambda k: xm_ref[k], join_ids(xm_ref[SLOTS])
     )
     work[15] = work[15] + across(
-        xp_ref, join_ids(xp_ref[SLOTS]), lambda s: order_ref[s, 15].astype(F32)
-    )
-    bottom = across(ym_ref, join_ids(ym_ref[SLOTS]), lambda s: own_ym_ref[s].astype(F32))
-    top = across(yp_ref, join_ids(yp_ref[SLOTS]), lambda s: own_yp_ref[s].astype(F32))
+        lambda k: order_ref[k, 15], own, lambda k: xp_ref[k], join_ids(xp_ref[SLOTS])
+    )
+    above_ids = join_ids(yp_ref[SLOTS])
+    top = across(lambda k: own_yp_ref[k], own, lambda k: yp_ref[k], above_ids)
+    beyond = across(lambda k: yp_ref[k], above_ids, lambda k: own_yp_ref[k], own)
+    beyond_ref[...] = beyond
+    zm_out[33] = beyond.astype(BF16)
+    zp_out[33] = beyond.astype(BF16)
     for x in range(16):
         value = work[x]
-        value = value + jnp.where(row == 0, bottom[x : x + 1], 0.0)
         value = value + jnp.where(row == 15, top[x : x + 1], 0.0)
         mob_ref[x] = value
         conc, side = conc_ref[x], side_ref[x]
@@ -223,8 +225,8 @@
             lane >= 85, value, jnp.where(lane >= 42, roll(conc, -43, 1), roll(side, -86, 1))
         )
         zp_out[x] = final.astype(BF16)
-    zm_out[16:] = own_zm_ref[...]
-    zp_out[16:] = own_zp_ref[...]
+    zm_out[16:33] = own_zm_ref[...]
+    zp_out[16:33] = own_zp_ref[...]
 
 
 def facing_squares(near_ref, far_ref, near_lane, far_lane):
@@ -251,28 +253,65 @@
 
 
 def split_kernel(
-    mob_ref, conc_ref, side_ref, left_ref, right_ref, zm_ref, zp_ref,
-    out_ref, keep_ref, down_ref, up_ref, low_ref, high_ref,
+    mob_ref, conc_ref, side_ref, beyond_ref, left_ref, right_ref, zm_ref, zp_ref,
+    keep_ref, beside_ref, low_ref, high_ref,
 ):
-    own_low, far_low = facing_squares(zm_ref, left_ref.at[16:], 0, LANES - 1)
-    own_high, far_high = facing_squares(zp_ref, right_ref.at[16:], LANES - 1, 0)
+    own_low, far_low = facing_squares(zm_ref, left_ref.at[16:33], 0, LANES - 1)
+    own_high, far_high = facing_squares(zp_ref, right_ref.at[16:33], LANES - 1, 0)
     mob = mob_ref[...] + own_low + own_high
-    out_ref[...] = mob
     keep_ref[...] = mob
     down = (left_ref[:16].astype(F32) + far_low).astype(BF16)
     up = (right_ref[:16].astype(F32) + far_high).astype(BF16)
-    down_ref[...] = down
-    up_ref[...] = up
     for place, value in enumerate((mob, conc_ref[...], side_ref[...], down, up)):
-        low_ref[place] = value[:, :8].astype(BF16)
-        high_ref[place] = value[:, 8:].astype(BF16)
-
-
-def rows_kernel(below_ref, low_ref, high_ref, above_ref, xl_ref, xh_ref):
-    for place, ref in enumerate((below_ref, low_ref, high_ref, above_ref)):
-        rows = pl.ds(8 * place, 8)
-        xl_ref[:, :, rows, :] = ref[:, :8]
-        xh_ref[:, :, rows, :] = ref[:, 8:]
+        planes = pl.ds(16 * place, 16)
+        low_ref[planes] = value[:, :8].astype(BF16)
+        high_ref[planes] = value[:, 8:].astype(BF16)
+    lane = iota((16, LANES), 1)
+    down, up = left_ref[33].astype(F32), right_ref[33].astype(F32)
+    beside = jnp.where(lane < 43, up, jnp.where(lane >= 85, down, 0.0))
+    beside_ref[...] = beside
+    beyond = beyond_ref[...]
+    high = beyond.astype(BF16)
+    rest = (beyond - high.astype(F32)).astype(BF16)
+    for k, value in enumerate((high, rest, beside.astype(BF16))):
+        high_ref[80 + 2 * k] = value[:8]
+        high_ref[81 + 2 * k] = value[8:]
+
+
+def rows_kernel(
+    below_ref, low_ref, high_ref, above_ref, mob_ref, beyond_ref, beside_ref,
+    out_ref, keep_ref, xl_ref, xh_ref,
+):
+    lane = iota((8, LANES), 1)
+    first = iota((8, LANES), 0) == 0
+    got = [
+        jnp.concatenate([below_ref[80 + 2 * k], below_ref[81 + 2 * k]], axis=0).astype(F32)
+        for k in range(3)
+    ]
+    missing = ((got[0] + got[1], got[2]), (beyond_ref[...], beside_ref[...]))
+    for x in range(16):
+        ref = xl_ref if x < 8 else xh_ref
+        lines = []
+        for main, beside in missing:
+            main = jnp.where(first, main[x : x + 1], 0.0)
+            beside = jnp.where(first, beside[x : x + 1], 0.0)
+            down = jnp.where(lane >= 85, beside, 0.0)
+            lines.append((main, None, None, down, jnp.where(lane < 43, beside, 0.0)))
+        own = mob_ref[x, :8] + lines[0][0]
+        for out in (out_ref, keep_ref):
+            out[x, :8] = own
+            out[x, 8:] = mob_ref[x, 8:]
+        for place in range(5):
+            plane = 16 * place + x
+            near, far = low_ref[plane], above_ref[plane]
+            if place == 0:
+                near = own.astype(BF16)
+            elif place >= 3:
+                near = (near.astype(F32) + lines[0][place]).astype(BF16)
+            if place in (0, 3, 4):
+                far = (far.astype(F32) + lines[1][place]).astype(BF16)
+            for k, value in enumerate((below_ref[plane], near, high_ref[plane], far)):
+                ref[place, x % 8, pl.ds(8 * k, 8), :] = value
 
 
 def partner(x, step, axis):
@@ -287,6 +326,13 @@
 def upper_of(x, step, axis):
     upper = (iota(x.shape, axis) & step) != 0
     return jnp.where(upper, x, roll(x, -step, axis))
+
+
+def middle_cell(lane):
+    cell = lane
+    for place, end in enumerate((-2, -1, 64, 65, -3, 66)):
+        cell = jnp.where(lane == 64 + place, end, cell)
+    return cell
 
 
 def groups(items, size):
@@ -315,7 +361,7 @@
 
 
 def down_kernel(
-    mob_in, conc_in, side_in, zm_ref, zp_ref, below_ref, above_ref, xm_ref, xp_ref,
+    mob_in, conc_in, side_in, xl_ref, xh_ref, xm_ref, xp_ref,
     own_ref, chunk_ref, side_out, kx_out, ky_out, kz_out, wd_out, v_out,
     k1x_out, k1y_out, k1z_out, wd1_out, f1_out,
     mob, v0, res, v_ref, side_ref, kx_ref, ky_ref, kz_ref, wd_ref,
@@ -330,19 +376,17 @@
 
     lane = iota((32, LANES), 1)
 
-    def own_plane(x, place, ref):
-        parts = (below_ref[place, x], ref[x], above_ref[place, x])
-        return jnp.concatenate([part.astype(F32) for part in parts], axis=0)
-
-    own = (mob_in, conc_in, side_in, zm_ref, zp_ref)
+    own = (mob_in, conc_in, side_in)
+    slabs = (xm_ref, xl_ref, xh_ref, xp_ref)
     for xs in groups(range(32), 8):
         planes = []
         for x in xs:
+            parts = [slabs[x // 8][place, x % 8].astype(F32) for place in range(5)]
             if 8 <= x < 24:
-                parts = [own_plane(x - 8, place, ref) for place, ref in enumerate(own)]
-            else:
-                ref = xm_ref if x < 8 else xp_ref
-                parts = [ref[place, x % 8].astype(F32) for place in range(5)]
+                for place in range(3):
+                    part = parts[place]
+                    part = [part[:8], own[place][x - 8], part[24:]]
+                    parts[place] = jnp.concatenate(part, axis=0)
             down, up = parts[3], parts[4]
             beyond = jnp.where(lane < 43, up, jnp.where(lane >= 85, down, 1.0))
             iterate = jnp.where(
@@ -449,7 +493,7 @@
     picks1 = sides + [tail & (coarse + 2 * COARSE - HEAD == dst)]
     picks0 = jnp.concatenate([pick.astype(F32) for pick in picks0], axis=0).astype(BF16)
     picks1 = jnp.concatenate([pick.astype(F32) for pick in picks1], axis=0).astype(BF16)
-    pick_middle = ((cell == 2 * (dst - MIDDLE_LOW)) & (dst < MIDDLE)).astype(F32)
+    pick_middle = ((cell == 2 * middle_cell(dst)) & (dst < MIDDLE)).astype(F32)
     firsts = []
     seconds = []
     for j in range(4):
@@ -472,11 +516,23 @@
     rows[pl.ds(64, 64), :] = jnp.dot(seconds, picks1, preferred_element_type=F32)
     coarse = rows[pl.ds(0, 32, stride=4), :]
     rows[...] = select_dot(
-        jnp.concatenate([e1[4 + i, 8:24] for i in range(8)], axis=0), pick_middle
-    )
-    middle = rows[pl.ds(0, 64, stride=2), :]
-    own_ref[...] = middle
-    chunk = jnp.concatenate([coarse.astype(BF16), middle.astype(BF16)], axis=0)
+        jnp.concatenate([e1[i] for i in range(3, 13)], axis=0), pick_middle
+    )
+    own_ref[...] = rows[pl.ds(0, 160, stride=2), :]
+
+    blocks = [own_ref[pl.ds(16 * (1 + x) + 4, 8), :] for x in (1, 2, 5, 6)]
+    for y in (1, 2):
+        lines = [(x, k) for k in (y, y + 4) for x in (0, 3, 4, 7)]
+        lines = [own_ref[pl.ds(16 * (1 + x) + 4 + k, 1), :] for x, k in lines]
+        blocks.append(jnp.concatenate(lines, axis=0))
+    narrow = iota((8, LANES), 1)
+    middle = []
+    for k in (0, 2, 4):
+        middle.append(jnp.where(narrow < 64, blocks[k], roll(blocks[k + 1], 64, 1)))
+    ends = jnp.zeros((8, LANES), F32)
+    for k in range(6):
+        ends = jnp.where(narrow // 4 == k, roll(blocks[k], 4 * k - 64, 1), ends)
+    chunk = jnp.concatenate([coarse] + middle + [ends], axis=0).astype(BF16)
     for k in range(32):
         chunk_ref[k] = chunk
     for copy in copies:
@@ -521,23 +577,48 @@
             for i in range(4):
                 pair0[4 * p + i, pl.ds(4 * q, 4), :] = first[4 * i : 4 * i + 4]
                 pair1[4 * p + i, pl.ds(4 * q, 4), :] = second[4 * i : 4 * i + 4]
+    for i in range(3, 13):
+        mid[i] = own_ref[pl.ds(16 * (i - 3), 16), :]
+    narrow = iota((8, LANES), 1)
     for p in (-1, 0, 1):
         for q in (-1, 0, 1):
             if p == 0 and q == 0:
-                cells = own_ref[...]
-            else:
-                cells = all_ref[source(p, q), pl.ds(32, 64), :].astype(F32)
-            for i in range(1, 15):
-                if (i - 4) // 8 != p:
-                    continue
-                start = 8 * ((i - 4) % 8)
-                block = cells[start : start + 8]
+                continue
+            cells = all_ref[source(p, q), pl.ds(32, 32), :].astype(F32)
+            ends = cells[24:]
+
+            def block(k):
+                main = cells[8 * (k // 2) : 8 * (k // 2) + 8]
+                if k % 2:
+                    main = roll(main, 64, 1)
+                end = jnp.where(narrow < 68, roll(ends, 64 - 4 * k, 1), 0.0)
+                return jnp.where(narrow < 64, main, end)
+
+            for k, i in {-1: ((2, 1), (3, 2)), 0: (), 1: ((0, 13), (1, 14))}[p]:
+                part = block(k)
                 if q == -1:
-                    mid[i, pl.ds(0, 4), :] = block[4:]
+                    mid[i, pl.ds(0, 4), :] = part[4:]
                 elif q == 0:
-                    mid[i, pl.ds(4, 8), :] = block
+                    mid[i, pl.ds(4, 8), :] = part
                 else:
-                    mid[i, pl.ds(12, 4), :] = block[:4]
+                    mid[i, pl.ds(12, 4), :] = part[:4]
+            if q == 0:
+                continue
+            for depth in (0, 1):
+                row = (1 if q == -1 else 13) + depth
+                half = 4 if q == -1 else 0
+                thin = block(4 + depth)
+                for k, x in enumerate((0, 3, 4, 7)):
+                    i = 8 * p + x + 4
+                    if 3 <= i <= 12:
+                        mid[i, pl.ds(row, 1), :] = thin[half + k : half + k + 1]
+            if p == 0:
+                for k, x in enumerate((1, 2, 5, 6)):
+                    line = 5 if q == -1 else 1
+                    part = block(k)
+                    for depth in (0, 1):
+                        row = (1 if q == -1 else 13) + depth
+                        mid[x + 4, pl.ds(row, 1), :] = part[line + depth : line + depth + 1]
 
     used = iota((16, LANES), 1) < COARSE
     head = iota((16, LANES), 1) < HEAD
@@ -591,8 +672,7 @@
     src = iota((LANES, RING), 0)
     dst = iota((LANES, RING), 1)
     cell = jnp.where(dst < 192, dst, dst - RING)
-    middle = (cell >= -2 * MIDDLE_LOW) & (src < MIDDLE)
-    middle = middle & ((cell + 2 * MIDDLE_LOW) // 2 == src)
+    middle = (src < MIDDLE) & ((cell + 64) // 2 - 32 == middle_cell(src))
     coarse = (cell >= -4 * COARSE_LOW) & (src >= MIDDLE) & (src < MIDDLE + COARSE)
     coarse = coarse & ((cell + 4 * COARSE_LOW) // 4 == src - MIDDLE)
     spread = (middle | coarse).astype(F32)
@@ -635,38 +715,41 @@
         specs=[HBM] * 4,
         semaphores=4,
     )
-    faces = (
-        shift(xp, "gx", 1), shift(xm, "gx", -1),
-        shift(yp, "gy", 1), shift(ym, "gy", -1),
-    )
-    pack = ((16, 16, LANES), BF16)
-    partial, send_zm, send_zp = call(
+    above = shift(ym, "gy", -1)
+    before = shift(xp, "gx", 1)
+    after = shift(xm, "gx", -1)
+    line = ((16, LANES), F32)
+    payload = ((34, 16, LANES), BF16)
+    partial, beyond, send_zm, send_zp = call(
         mobility_kernel,
-        [brick, ((33, 16, LANES), BF16), ((33, 16, LANES), BF16)],
-        (conc, side, order, ids) + faces + (ym, yp, zm, zp),
+        [brick, line, payload, payload],
+        (conc, side, order, ids, before, after, above, yp, zm, zp),
         scratch=[brick, ((64, 8, LANES), F32)],
     )
     left = shift(send_zp, "gz", 1)
     right = shift(send_zm, "gz", -1)
-    half = ((5, 16, 8, LANES), BF16)
-    mobility, keep, left, right, low, high = call(
+    keep, beside, low, high = call(
         split_kernel,
-        [brick, brick, pack, pack, half, half],
-        (partial, conc, side, left, right, zm, zp),
+        [brick, line, ((80, 8, LANES), BF16), ((86, 8, LANES), BF16)],
+        (partial, conc, side, beyond, left, right, zm, zp),
     )
     below = shift(high, "gy", 1)
     above = shift(low, "gy", -1)
     slab = ((5, 8, 32, LANES), BF16)
-    xl, xh = call(rows_kernel, [slab, slab], (below, low, high, above))
+    mobility, keep, xl, xh = call(
+        rows_kernel,
+        [brick, brick, slab, slab],
+        (below, low, high, above, keep, beyond, beside),
+    )
     before = shift(xh, "gx", 1)
     after = shift(xl, "gx", -1)
     fine = ((32, 32, RING), F32)
     middle = ((16, 32, RING), F32)
     own, chunk, *kept = call(
         down_kernel,
-        [((64, LANES), F32), ((32, CHUNK, LANES), BF16)] + [fine] * 6 + [middle] * 5,
-        (keep, conc, side, left, right, below, above, before, after),
-        scratch=[fine] * 9 + [middle] * 8 + [((LANES, LANES), F32)],
+        [((160, LANES), F32), ((32, CHUNK, LANES), BF16)] + [fine] * 6 + [middle] * 5,
+        (keep, conc, side, xl, xh, before, after),
+        scratch=[fine] * 9 + [middle] * 8 + [((320, LANES), F32)],
         places=[VMEM] * 2 + [HBM] * 11,
         limit=24,
         semaphores=11,

time: 89.2 us -> 84.1 us (0.943)
  starting transfers between devices: 34.8 us -> 29.8 us
  blocking collectives: 21.3 us -> 19.9 us
  waiting for transfers between devices: 12.5 us -> 13.7 us
    ppermute x10 -> x9, starting transfers between devices: 34.8 us -> 29.8 us  [shift(): lax.ppermute(x, axis, [(i, (i + direction) % count) for i in range(count)])]
    all_to_all x1, blocking collectives: 21.3 us -> 19.9 us  [body(): chunks = lax.all_to_all(chunk, ('gx', 'gy'), 0, 0, tiled=True)]
    ppermute x10 -> x9, waiting for transfers between devices: 12.5 us -> 13.7 us  [shift(): lax.ppermute(x, axis, [(i, (i + direction) % count) for i in range(count)])]
  transfers between devices with their start and end apart: 10 -> 9, of which waited for: 8 -> 6; matrix products, arithmetic and copies ran while one was open for 0% -> 0% of each run, Pallas kernels for 0% -> 0%
where the time goes in v6:
time: 84.1 us; the launch traced here: 83.8 us
  starting transfers between devices  29.8 us (35%)
  blocking collectives  19.9 us (24%)
  Pallas kernels  19.6 us (23%)
  waiting for transfers between devices  13.7 us (16%)
    ppermute x9, starting transfers between devices, shift(): lax.ppermute(x, axis, [(i, (i + direction) % count) for i in range(count)])  29.8 us
    all_to_all x1, blocking collectives, body(): chunks = lax.all_to_all(chunk, ('gx', 'gy'), 0, 0, tiled=True)  19.9 us
    pallas_call x6, Pallas kernels, call(): pl.pallas_call(kernel, out_shape=[pltpu.MemorySpace.HBM(*out) if place is...  19.6 us
    ppermute x9, waiting for transfers between devices, shift(): lax.ppermute(x, axis, [(i, (i + direction) % count) for i in range(count)])  13.7 us
  transfers between devices with their start and end apart: 9, of which 6 were waited for; matrix products, arithmetic and copies ran while one was open for 0% of the time, Pallas kernels for 0%

profile of v6, /device:TPU:1, one launch (start us, length us, event | category | flops | bytes accessed | tf_op | source)
XLA Modules:
  0.0 83.8 jit_solution(6078402402001085692)
XLA Ops:
  0.6 1.6 %shard_map.59 = (f32[16,16,128]{2,1,0:T(8,128)S(1)}, f32[16,16,128]{2,1,0:T(8,128)S(1)}, bf16[8,16,16,128]{3,2,1,0:T(8,128)(2,1)S(1)}, s32[1,1,8,8]{3,2,1,0:T(8,...) custom-call(f32[16,16,128]{2,1,0:T(8,128)} %conc_in.1, ...), custom_call_target="tpu_custom_call" | custom-call | tf_op jit(solution)/shard_map/pallas_call | solution.py:41
  2.2 2.7 %collective-permute-start = (bf16[9,16,128]{2,1,0:T(8,128)(2,1)S(1)}, bf16[9,16,128]{2,1,0:T(8,128)(2,1)S(1)}, u32[]{:S(2)}, u32[]{:S(2)}) collective-permute-start(bf16[9,16,128]{2,1,0:T(8,128)(2,1)S(1)} %get-tuple-element.43), channel_id=1, source_target_pairs={{0,64},{64,128},{128,192},{192,256},{256,320},{320,384},{384,448},... | collective-permute-start | bytes 110600 | tf_op jit(solution)/shard_map/ppermute | solution.py:702
  4.9 4.2 %collective-permute-start.1 = (bf16[9,16,128]{2,1,0:T(8,128)(2,1)S(1)}, bf16[9,16,128]{2,1,0:T(8,128)(2,1)S(1)}, u32[]{:S(2)}, u32[]{:S(2)}) collective-permute-start(bf16[9,16,128]{2,1,0:T(8,128)(2,1)S(1)} %get-tuple-element.44), channel_id=1, source_target_pairs={{0,448},{64,0},{128,64},{192,128},{256,192},{320,256},{384,320},{4... | collective-permute-start | bytes 110600 | tf_op jit(solution)/shard_map/ppermute | solution.py:702
  9.2 1.9 %collective-permute-start.2 = (bf16[9,16,128]{2,1,0:T(8,128)(2,1)S(1)}, bf16[9,16,128]{2,1,0:T(8,128)(2,1)S(1)}, u32[]{:S(2)}, u32[]{:S(2)}) collective-permute-start(bf16[9,16,128]{2,1,0:T(8,128)(2,1)S(1)} %get-tuple-element.45), channel_id=1, source_target_pairs={{0,48},{16,0},{32,16},{48,32},{1,49},{17,1},{33,17},{49,33},{2,50}... | collective-permute-start | bytes 110600 | tf_op jit(solution)/shard_map/ppermute | solution.py:702
  11.1 0.0 collective-permute-done.xm_ref
  11.1 0.0 collective-permute-done.1.xp_ref
  11.1 2.8 %collective-permute-done.2.yp_ref = bf16[9,16,128]{2,1,0:T(8,128)(2,1)S(1)} collective-permute-done((bf16[9,16,128]{2,1,0:T(8,128)(2,1)S(1)}, bf16[9,16,128]{2,1,0:T(8,128)(2,1)S(1)}, u32[]{:S(2)}, u32[]{:S(2)}) %collective-permute-start.2) | collective-permute-done | bytes 36896 | tf_op jit(solution)/shard_map/ppermute | solution.py:702
  13.8 1.9 %shard_map.60 = (f32[16,16,128]{2,1,0:T(8,128)S(1)}, f32[16,128]{1,0:T(8,128)S(1)}, bf16[34,16,128]{2,1,0:T(8,128)(2,1)S(1)}, bf16[34,16,128]{2,1,0:T(8,128)(2,1)S(1)}) custom-call(f32[16,16,128]{2,1,0:T(8,128)S(1)} %get-tuple-element.39.conc_ref.conc_in, f32[16,16,128]{2,1,0:T(8,128)S(1)} %get-tuple-element.40.side_ref.side_in, ...), custom_call_target="tpu_custom_call" | custom-call | tf_op jit(solution)/shard_map/pallas_call | solution.py:41
  15.7 1.9 %collective-permute-start.3 = (bf16[34,16,128]{2,1,0:T(8,128)(2,1)S(1)}, bf16[34,16,128]{2,1,0:T(8,128)(2,1)S(1)}, u32[]{:S(2)}, u32[]{:S(2)}) collective-permute-start(bf16[34,16,128]{2,1,0:T(8,128)(2,1)S(1)} %get-tuple-element.51), channel_id=1, source_target_pairs={{0,1},{1,2},{2,3},{3,4},{4,5},{5,6},{6,7},{7,8},{8,9},{9,10},{10,1... | collective-permute-start | bytes 417800 | tf_op jit(solution)/shard_map/ppermute | solution.py:702
  17.6 7.6 %collective-permute-start.4 = (bf16[34,16,128]{2,1,0:T(8,128)(2,1)S(1)}, bf16[34,16,128]{2,1,0:T(8,128)(2,1)S(1)}, u32[]{:S(2)}, u32[]{:S(2)}) collective-permute-start(bf16[34,16,128]{2,1,0:T(8,128)(2,1)S(1)} %get-tuple-element.52), channel_id=1, source_target_pairs={{0,15},{1,0},{2,1},{3,2},{4,3},{5,4},{6,5},{7,6},{8,7},{9,8},{10,9... | collective-permute-start | bytes 417800 | tf_op jit(solution)/shard_map/ppermute | solution.py:702
  25.3 0.5 collective-permute-done.3.left_ref
  25.8 1.5 %collective-permute-done.4.right_ref = bf16[34,16,128]{2,1,0:T(8,128)(2,1)S(1)} collective-permute-done((bf16[34,16,128]{2,1,0:T(8,128)(2,1)S(1)}, bf16[34,16,128]{2,1,0:T(8,128)(2,1)S(1)}, u32[]{:S(2)}, u32[]{:S(2)}) %collective-permute-start.4) | collective-permute-done | bytes 139296 | tf_op jit(solution)/shard_map/ppermute | solution.py:702
  27.3 0.6 shard_map.61
  27.9 2.4 %collective-permute-start.5 = (bf16[86,8,128]{2,1,0:T(8,128)(2,1)S(1)}, bf16[86,8,128]{2,1,0:T(8,128)(2,1)S(1)}, u32[]{:S(2)}, u32[]{:S(2)}) collective-permute-start(bf16[86,8,128]{2,1,0:T(8,128)(2,1)S(1)} %get-tuple-element.53.high_ref), channel_id=1, source_target_pairs={{0,16},{16,32},{32,48},{48,0},{1,17},{17,33},{33,49},{49,1},{2,18}... | collective-permute-start | bytes 528392 | tf_op jit(solution)/shard_map/ppermute | solution.py:702
  30.3 4.4 %collective-permute-start.6 = (bf16[80,8,128]{2,1,0:T(8,128)(2,1)S(1)}, bf16[80,8,128]{2,1,0:T(8,128)(2,1)S(1)}, u32[]{:S(2)}, u32[]{:S(2)}) collective-permute-start(bf16[80,8,128]{2,1,0:T(8,128)(2,1)S(1)} %get-tuple-element.54.low_ref), channel_id=1, source_target_pairs={{0,48},{16,0},{32,16},{48,32},{1,49},{17,1},{33,17},{49,33},{2,50}... | collective-permute-start | bytes 491528 | tf_op jit(solution)/shard_map/ppermute | solution.py:702
  34.7 2.2 %collective-permute-done.6.above_ref = bf16[80,8,128]{2,1,0:T(8,128)(2,1)S(1)} collective-permute-done((bf16[80,8,128]{2,1,0:T(8,128)(2,1)S(1)}, bf16[80,8,128]{2,1,0:T(8,128)(2,1)S(1)}, u32[]{:S(2)}, u32[]{:S(2)}) %collective-permute-start.6) | collective-permute-done | bytes 163872 | tf_op jit(solution)/shard_map/ppermute | solution.py:702
  37.0 0.0 collective-permute-done.5.below_ref
  37.0 0.8 shard_map.62
  37.8 4.6 %collective-permute-start.7 = (bf16[5,8,32,128]{3,2,1,0:T(8,128)(2,1)S(1)}, bf16[5,8,32,128]{3,2,1,0:T(8,128)(2,1)S(1)}, u32[]{:S(2)}, u32[]{:S(2)}) collective-permute-start(bf16[5,8,32,128]{3,2,1,0:T(8,128)(2,1)S(1)} %get-tuple-element.59.xh_ref), channel_id=1, source_target_pairs={{0,64},{64,128},{128,192},{192,256},{256,320},{320,384},{384,448},... | collective-permute-start | bytes 983048 | tf_op jit(solution)/shard_map/ppermute | solution.py:702
  42.4 0.0 collective-permute-start.8
  42.4 0.1 pad_add_fusion.place_ref
  42.5 3.9 %collective-permute-done.7.xm_ref = bf16[5,8,32,128]{3,2,1,0:T(8,128)(2,1)S(1)} collective-permute-done((bf16[5,8,32,128]{3,2,1,0:T(8,128)(2,1)S(1)}, bf16[5,8,32,128]{3,2,1,0:T(8,128)(2,1)S(1)}, u32[]{:S(2)}, u32[]{:S(2)}) %collective-permute-start.7) | collective-permute-done | bytes 327712 | tf_op jit(solution)/shard_map/ppermute | solution.py:702
  46.4 2.8 %collective-permute-done.8.xp_ref = bf16[5,8,32,128]{3,2,1,0:T(8,128)(2,1)S(1)} collective-permute-done((bf16[5,8,32,128]{3,2,1,0:T(8,128)(2,1)S(1)}, bf16[5,8,32,128]{3,2,1,0:T(8,128)(2,1)S(1)}, u32[]{:S(2)}, u32[]{:S(2)}) %collective-permute-start.8) | collective-permute-done | bytes 327712 | tf_op jit(solution)/shard_map/ppermute | solution.py:702
  49.2 8.0 %shard_map.63 = (f32[160,128]{1,0:T(8,128)S(1)}, bf16[32,64,128]{2,1,0:T(8,128)(2,1)S(1)}, f32[32,32,256]{2,1,0:T(8,128)}, f32[32,32,256]{2,1,0:T(8,128)}, f32[3...) custom-call(f32[16,16,128]{2,1,0:T(8,128)S(1)} %get-tuple-element.57, ...), custom_call_target="tpu_custom_call" | custom-call | tf_op jit(solution)/shard_map/pallas_call | solution.py:41
  57.2 19.9 %all_to_all.5.all_ref = bf16[32,64,128]{2,1,0:T(8,128)(2,1)S(1)} all-to-all(bf16[32,64,128]{2,1,0:T(8,128)(2,1)S(1)} %get-tuple-element.62), channel_id=1, replica_groups=mesh['gx'=8,'gy'=4,'gz'=16] {'gx','gy'}, dimensions={0} | all-to-all | bytes 1048576 | tf_op jit(solution)/shard_map/all_to_all | solution.py:759
  77.1 6.7 %shard_map.64 = f32[16,16,128]{2,1,0:T(8,128)} custom-call(s32[2]{0:T(128)S(1)} %pad_add_fusion.place_ref, bf16[32,64,128]{2,1,0:T(8,128)(2,1)S(1)} %all_to_all.5.all_ref, f32[160,128]{1,0:T(8,128)S(1)} %get-tuple-element.63.own_ref, f32[32,32,256]{2,1,0:T(8,128)} %get-tuple-element.64.side_in, f32[32,32,256]{2,1,0:T(8,128)} %get-tuple-element.65.kx_in, ...), custom_call_target="tpu_custom_call" | custom-call | tf_op jit(solution)/shard_map/pallas_call | solution.py:41
Async XLA Ops:
  2.2 8.8 %collective-permute-start = (bf16[9,16,128]{2,1,0:T(8,128)(2,1)S(1)}, bf16[9,16,128]{2,1,0:T(8,128)(2,1)S(1)}, u32[]{:S(2)}, u32[]{:S(2)}) collective-permute-start(bf16[9,16,128]{2,1,0:T(8,128)(2,1)S(1)} %get-tuple-element.43), channel_id=1, source_target_pairs={{0,64},{64,128},{128,192},{192,256},{256,320},{320,384},{384,448},... | collective-permute-start | bytes 110600 | tf_op jit(solution)/shard_map/ppermute | solution.py:702
  4.9 6.1 %collective-permute-start.1 = (bf16[9,16,128]{2,1,0:T(8,128)(2,1)S(1)}, bf16[9,16,128]{2,1,0:T(8,128)(2,1)S(1)}, u32[]{:S(2)}, u32[]{:S(2)}) collective-permute-start(bf16[9,16,128]{2,1,0:T(8,128)(2,1)S(1)} %get-tuple-element.44), channel_id=1, source_target_pairs={{0,448},{64,0},{128,64},{192,128},{256,192},{320,256},{384,320},{4... | collective-permute-start | bytes 110600 | tf_op jit(solution)/shard_map/ppermute | solution.py:702
  9.2 4.7 %collective-permute-start.2 = (bf16[9,16,128]{2,1,0:T(8,128)(2,1)S(1)}, bf16[9,16,128]{2,1,0:T(8,128)(2,1)S(1)}, u32[]{:S(2)}, u32[]{:S(2)}) collective-permute-start(bf16[9,16,128]{2,1,0:T(8,128)(2,1)S(1)} %get-tuple-element.45), channel_id=1, source_target_pairs={{0,48},{16,0},{32,16},{48,32},{1,49},{17,1},{33,17},{49,33},{2,50}... | collective-permute-start | bytes 110600 | tf_op jit(solution)/shard_map/ppermute | solution.py:702
  15.7 10.1 %collective-permute-start.3 = (bf16[34,16,128]{2,1,0:T(8,128)(2,1)S(1)}, bf16[34,16,128]{2,1,0:T(8,128)(2,1)S(1)}, u32[]{:S(2)}, u32[]{:S(2)}) collective-permute-start(bf16[34,16,128]{2,1,0:T(8,128)(2,1)S(1)} %get-tuple-element.51), channel_id=1, source_target_pairs={{0,1},{1,2},{2,3},{3,4},{4,5},{5,6},{6,7},{7,8},{8,9},{9,10},{10,1... | collective-permute-start | bytes 417800 | tf_op jit(solution)/shard_map/ppermute | solution.py:702
  17.6 9.7 %collective-permute-start.4 = (bf16[34,16,128]{2,1,0:T(8,128)(2,1)S(1)}, bf16[34,16,128]{2,1,0:T(8,128)(2,1)S(1)}, u32[]{:S(2)}, u32[]{:S(2)}) collective-permute-start(bf16[34,16,128]{2,1,0:T(8,128)(2,1)S(1)} %get-tuple-element.52), channel_id=1, source_target_pairs={{0,15},{1,0},{2,1},{3,2},{4,3},{5,4},{6,5},{7,6},{8,7},{9,8},{10,9... | collective-permute-start | bytes 417800 | tf_op jit(solution)/shard_map/ppermute | solution.py:702
  27.9 9.0 %collective-permute-start.5 = (bf16[86,8,128]{2,1,0:T(8,128)(2,1)S(1)}, bf16[86,8,128]{2,1,0:T(8,128)(2,1)S(1)}, u32[]{:S(2)}, u32[]{:S(2)}) collective-permute-start(bf16[86,8,128]{2,1,0:T(8,128)(2,1)S(1)} %get-tuple-element.53.high_ref), channel_id=1, source_target_pairs={{0,16},{16,32},{32,48},{48,0},{1,17},{17,33},{33,49},{49,1},{2,18}... | collective-permute-start | bytes 528392 | tf_op jit(solution)/shard_map/ppermute | solution.py:702
  30.3 6.6 %collective-permute-start.6 = (bf16[80,8,128]{2,1,0:T(8,128)(2,1)S(1)}, bf16[80,8,128]{2,1,0:T(8,128)(2,1)S(1)}, u32[]{:S(2)}, u32[]{:S(2)}) collective-permute-start(bf16[80,8,128]{2,1,0:T(8,128)(2,1)S(1)} %get-tuple-element.54.low_ref), channel_id=1, source_target_pairs={{0,48},{16,0},{32,16},{48,32},{1,49},{17,1},{33,17},{49,33},{2,50}... | collective-permute-start | bytes 491528 | tf_op jit(solution)/shard_map/ppermute | solution.py:702
  37.8 8.6 %collective-permute-start.7 = (bf16[5,8,32,128]{3,2,1,0:T(8,128)(2,1)S(1)}, bf16[5,8,32,128]{3,2,1,0:T(8,128)(2,1)S(1)}, u32[]{:S(2)}, u32[]{:S(2)}) collective-permute-start(bf16[5,8,32,128]{3,2,1,0:T(8,128)(2,1)S(1)} %get-tuple-element.59.xh_ref), channel_id=1, source_target_pairs={{0,64},{64,128},{128,192},{192,256},{256,320},{320,384},{384,448},... | collective-permute-start | bytes 983048 | tf_op jit(solution)/shard_map/ppermute | solution.py:702
  42.4 6.8 %collective-permute-start.8 = (bf16[5,8,32,128]{3,2,1,0:T(8,128)(2,1)S(1)}, bf16[5,8,32,128]{3,2,1,0:T(8,128)(2,1)S(1)}, u32[]{:S(2)}, u32[]{:S(2)}) collective-permute-start(bf16[5,8,32,128]{3,2,1,0:T(8,128)(2,1)S(1)} %get-tuple-element.58.xl_ref), channel_id=1, source_target_pairs={{0,448},{64,0},{128,64},{192,128},{256,192},{320,256},{384,320},{4... | collective-permute-start | bytes 983048 | tf_op jit(solution)/shard_map/ppermute | solution.py:702

commit v7 on v6

--- a/solution.py
+++ b/solution.py
@@ -24,8 +24,6 @@
 MIDDLE = 70
 HEAD = 26
 CHUNK = 64
-FINE_PLANES = pl.ds(6, 20)
-MIDDLE_PLANES = pl.ds(1, 13)
 
 
 def call(kernel, outs, args, scratch=(), specs=None, places=None, limit=16, semaphores=0):
@@ -91,7 +89,7 @@
 
 def faces_kernel(
     conc_in, side_in, order_in, ids_in,
-    conc_ref, side_ref, order_ref, ids_ref, xm_ref, xp_ref, ym_ref, yp_ref, zm_ref, zp_ref, sems,
+    conc_ref, side_ref, order_ref, ids_ref, xm_ref, xp_ref, ym_ref, sems,
 ):
     pairs = (
         (ids_in, ids_ref), (order_in, order_ref), (conc_in, conc_ref), (side_in, side_ref),
@@ -103,37 +101,39 @@
     copies[1].wait()
     grains = lane_ids(ids_ref)
     packed = split_ids(grains)
-    for ref in (xm_ref, xp_ref, ym_ref, yp_ref):
+    for ref in (xm_ref, xp_ref, ym_ref):
         ref[SLOTS] = packed
+    for slot in range(SLOTS):
+        xm_ref[slot] = order_ref[slot, 0]
+        xp_ref[slot] = order_ref[slot, 15]
+        ym_ref[slot] = order_ref[slot].astype(F32)[:, 0, :].astype(BF16)
+    copies[2].wait()
+    copies[3].wait()
+
+
+def square(x):
+    return x * x
+
+
+def inner_kernel(
+    conc_ref, order_ref, ids_ref, work, yp_ref, zm_ref, zp_ref, weights,
+):
+    grains = lane_ids(ids_ref)
     zm_ref[16] = split_ids(jnp.broadcast_to(grains[:, 0:1], (8, LANES)))
     zp_ref[16] = split_ids(jnp.broadcast_to(grains[:, LANES - 1 :], (8, LANES)))
-    lane = iota((16, LANES), 1)
+    slots = iota((16, LANES), 1)
     low = [jnp.zeros((16, LANES), F32)] * 16
     high = [jnp.zeros((16, LANES), F32)] * 16
     for slot in range(SLOTS):
         cells = order_ref[slot].astype(F32)
-        xm_ref[slot] = order_ref[slot, 0]
-        xp_ref[slot] = order_ref[slot, 15]
-        ym_ref[slot] = cells[:, 0, :].astype(BF16)
         yp_ref[slot] = cells[:, 15, :].astype(BF16)
         for x in range(16):
-            low[x] = jnp.where(lane == slot, cells[x, :, 0:1], low[x])
-            high[x] = jnp.where(lane == slot, cells[x, :, LANES - 1 :], high[x])
+            low[x] = jnp.where(slots == slot, cells[x, :, 0:1], low[x])
+            high[x] = jnp.where(slots == slot, cells[x, :, LANES - 1 :], high[x])
     for x in range(16):
         zm_ref[x] = low[x].astype(BF16)
         zp_ref[x] = high[x].astype(BF16)
-    copies[2].wait()
-    copies[3].wait()
-
-
-def square(x):
-    return x * x
-
-
-def mobility_kernel(
-    conc_ref, side_ref, order_ref, ids_ref, xm_ref, xp_ref, yp_ref,
-    own_yp_ref, own_zm_ref, own_zp_ref, mob_ref, beyond_ref, zm_out, zp_out, work, weights,
-):
+
     own = lane_ids(ids_ref)
     lane = iota((16, LANES), 1)
     row = iota((16, LANES), 0)
@@ -148,19 +148,6 @@
         match = (own == beside[other : other + 1]).astype(F32)
         for slot in range(SLOTS):
             weights[slot * SLOTS + other] = jnp.broadcast_to(match[slot : slot + 1], (8, LANES))
-
-    def across(center, ids, facing, facing_ids):
-        facing = [facing(other).astype(F32) for other in range(SLOTS)]
-        total = None
-        for slot in range(SLOTS):
-            value = None
-            for other in range(SLOTS):
-                match = ids[slot : slot + 1] == facing_ids[other : other + 1]
-                term = match.astype(F32) * facing[other]
-                value = term if value is None else value + term
-            part = square(value - center(slot).astype(F32))
-            total = part if total is None else total + part
-        return total
 
     def doubled(block):
         return jnp.concatenate([block, block], axis=0)
@@ -200,10 +187,32 @@
     carry = jnp.zeros((16, LANES), F32)
     for x in range(16):
         carry = plane(x, carry)
-    work[0] = work[0] + across(
+
+def outer_kernel(
+    work, conc_ref, side_ref, order_ref, ids_ref, xm_ref, xp_ref, yp_ref,
+    own_yp_ref, own_zm_ref, own_zp_ref, mob_ref, beyond_ref, zm_out, zp_out,
+):
+    own = lane_ids(ids_ref)
+    lane = iota((16, LANES), 1)
+    row = iota((16, LANES), 0)
+
+    def across(center, ids, facing, facing_ids):
+        facing = [facing(other).astype(F32) for other in range(SLOTS)]
+        total = None
+        for slot in range(SLOTS):
+            value = None
+            for other in range(SLOTS):
+                match = ids[slot : slot + 1] == facing_ids[other : other + 1]
+                term = match.astype(F32) * facing[other]
+                value = term if value is None else value + term
+            part = square(value - center(slot).astype(F32))
+            total = part if total is None else total + part
+        return total
+
+    first = work[0] + across(
         lambda k: order_ref[k, 0], own, lambda k: xm_ref[k], join_ids(xm_ref[SLOTS])
     )
-    work[15] = work[15] + across(
+    final = work[15] + across(
         lambda k: order_ref[k, 15], own, lambda k: xp_ref[k], join_ids(xp_ref[SLOTS])
     )
     above_ids = join_ids(yp_ref[SLOTS])
@@ -213,18 +222,18 @@
     zm_out[33] = beyond.astype(BF16)
     zp_out[33] = beyond.astype(BF16)
     for x in range(16):
-        value = work[x]
+        value = first if x == 0 else final if x == 15 else work[x]
         value = value + jnp.where(row == 15, top[x : x + 1], 0.0)
         mob_ref[x] = value
         conc, side = conc_ref[x], side_ref[x]
-        first = jnp.where(
+        down = jnp.where(
             lane < 43, value, jnp.where(lane < 86, roll(conc, 43, 1), roll(side, 86, 1))
         )
-        zm_out[x] = first.astype(BF16)
-        final = jnp.where(
+        zm_out[x] = down.astype(BF16)
+        up = jnp.where(
             lane >= 85, value, jnp.where(lane >= 42, roll(conc, -43, 1), roll(side, -86, 1))
         )
-        zp_out[x] = final.astype(BF16)
+        zp_out[x] = up.astype(BF16)
     zm_out[16:33] = own_zm_ref[...]
     zp_out[16:33] = own_zp_ref[...]
 
@@ -362,18 +371,10 @@
 
 def down_kernel(
     mob_in, conc_in, side_in, xl_ref, xh_ref, xm_ref, xp_ref,
-    own_ref, chunk_ref, side_out, kx_out, ky_out, kz_out, wd_out, v_out,
-    k1x_out, k1y_out, k1z_out, wd1_out, f1_out,
-    mob, v0, res, v_ref, side_ref, kx_ref, ky_ref, kz_ref, wd_ref,
-    f1_ref, k1x_ref, k1y_ref, k1z_ref, wd1_ref, e0, e1, r1, rows, sems,
+    own_ref, chunk_ref, side_ref, kx_ref, ky_ref, kz_ref, wd_ref, v_ref,
+    k1x_ref, k1y_ref, k1z_ref, wd1_ref, f1_ref,
+    mob, v0, res, e0, e1, r1, rows,
 ):
-    copies = []
-
-    def store(source, target, planes):
-        copy = pltpu.make_async_copy(source.at[planes], target.at[planes], sems.at[len(copies)])
-        copy.start()
-        copies.append(copy)
-
     lane = iota((32, LANES), 1)
 
     own = (mob_in, conc_in, side_in)
@@ -423,11 +424,6 @@
             kx_ref[x], ky_ref[x], wd_ref[x] = done[k]
             kz_ref[x] = kz[k]
 
-    store(side_ref, side_out, FINE_PLANES)
-    store(kx_ref, kx_out, FINE_PLANES)
-    store(ky_ref, ky_out, FINE_PLANES)
-    store(kz_ref, kz_out, FINE_PLANES)
-    store(wd_ref, wd_out, FINE_PLANES)
 
     def smooth(target, weight):
         def use(x, value, left):
@@ -438,7 +434,6 @@
     sweep_planes(2, 29, v0, side_ref, kx_ref, ky_ref, kz_ref, 1, smooth(res, wd_ref))
     sweep_planes(3, 28, res, side_ref, kx_ref, ky_ref, kz_ref, 1, smooth(v_ref, wd_ref))
 
-    store(v_ref, v_out, FINE_PLANES)
 
     def keep(x, value, left):
         res[x] = left
@@ -469,11 +464,6 @@
             done.append((f1, k1y, k1z, weight, weight * f1))
         for i, value in zip(xs, done):
             f1_ref[i], k1y_ref[i], k1z_ref[i], wd1_ref[i], e0[i] = value
-    store(k1x_ref, k1x_out, MIDDLE_PLANES)
-    store(k1y_ref, k1y_out, MIDDLE_PLANES)
-    store(k1z_ref, k1z_out, MIDDLE_PLANES)
-    store(wd1_ref, wd1_out, MIDDLE_PLANES)
-    store(f1_ref, f1_out, MIDDLE_PLANES)
     sweep_planes(3, 12, e0, f1_ref, k1x_ref, k1y_ref, k1z_ref, 2, smooth(e1, wd1_ref))
 
     def keep_middle(x, value, left):
@@ -535,34 +525,14 @@
     chunk = jnp.concatenate([coarse] + middle + [ends], axis=0).astype(BF16)
     for k in range(32):
         chunk_ref[k] = chunk
-    for copy in copies:
-        copy.wait()
 
 
 def up_kernel(
-    place_ref, all_ref, own_ref, side_in, kx_in, ky_in, kz_in, wd_in, v_in,
-    k1x_in, k1y_in, k1z_in, wd1_in, f1_in,
+    place_ref, all_ref, own_ref, side_ref, kx_ref, ky_ref, kz_ref, wd_ref, v_ref,
+    k1x_ref, k1y_ref, k1z_ref, wd1_ref, f1_ref,
     out_ref,
-    side_ref, kx_ref, ky_ref, kz_ref, wd_ref, v_ref, k1x_ref, k1y_ref, k1z_ref, wd1_ref, f1_ref,
-    pair0, pair1, c2x, c2y, c2z, wd2, f2, ea, eb, mid, tall, lean, e1a, e1b, va, vb, sems,
+    pair0, pair1, c2x, c2y, c2z, wd2, f2, ea, eb, mid, tall, lean, e1a, e1b, va, vb,
 ):
-    copies = []
-    for planes, moves in (
-        (MIDDLE_PLANES, (
-            (k1x_in, k1x_ref), (k1y_in, k1y_ref), (k1z_in, k1z_ref), (wd1_in, wd1_ref),
-            (f1_in, f1_ref),
-        )),
-        (FINE_PLANES, (
-            (v_in, v_ref), (side_in, side_ref), (kx_in, kx_ref), (ky_in, ky_ref),
-            (kz_in, kz_ref), (wd_in, wd_ref),
-        )),
-    ):
-        for a, b in moves:
-            copies.append(
-                pltpu.make_async_copy(a.at[planes], b.at[planes], sems.at[len(copies)])
-            )
-    for copy in copies:
-        copy.start()
     gx = place_ref[0]
     gy = place_ref[1]
 
@@ -682,8 +652,6 @@
     for i in range(1, 15):
         e1a[i] = widened[32 * (i - 1) : 32 * i]
 
-    for copy in copies:
-        copy.wait()
     sweep_planes(2, 13, e1a, f1_ref, k1x_ref, k1y_ref, k1z_ref, 2, smooth(e1b, wd1_ref))
     sweep_planes(3, 12, e1b, f1_ref, k1x_ref, k1y_ref, k1z_ref, 2, smooth(e1a, wd1_ref))
     for x in range(6, 26):
@@ -706,11 +674,9 @@
     face = ((9, 16, LANES), BF16)
     zface = ((17, 16, LANES), BF16)
     brick = ((16, 16, LANES), F32)
-    conc, side, order, ids, xm, xp, ym, yp, zm, zp = call(
+    conc, side, order, ids, xm, xp, ym = call(
         faces_kernel,
-        [brick, brick, ((8, 16, 16, LANES), BF16), ((1, 1, 8, 8), jnp.int32)]
-        + [face] * 4
-        + [zface] * 2,
+        [brick, brick, ((8, 16, 16, LANES), BF16), ((1, 1, 8, 8), jnp.int32)] + [face] * 3,
         (conc, right_side, order_field, grain_ids),
         specs=[HBM] * 4,
         semaphores=4,
@@ -718,13 +684,18 @@
     above = shift(ym, "gy", -1)
     before = shift(xp, "gx", 1)
     after = shift(xm, "gx", -1)
+    inner, yp, zm, zp = call(
+        inner_kernel,
+        [brick, ((8, 16, LANES), BF16), zface, zface],
+        (conc, order, ids),
+        scratch=[((64, 8, LANES), F32)],
+    )
     line = ((16, LANES), F32)
     payload = ((34, 16, LANES), BF16)
     partial, beyond, send_zm, send_zp = call(
-        mobility_kernel,
+        outer_kernel,
         [brick, line, payload, payload],
-        (conc, side, order, ids, before, after, above, yp, zm, zp),
-        scratch=[brick, ((64, 8, LANES), F32)],
+        (inner, conc, side, order, ids, before, after, above, yp, zm, zp),
     )
     left = shift(send_zp, "gz", 1)
     right = shift(send_zm, "gz", -1)
@@ -749,10 +720,7 @@
         down_kernel,
         [((160, LANES), F32), ((32, CHUNK, LANES), BF16)] + [fine] * 6 + [middle] * 5,
         (keep, conc, side, xl, xh, before, after),
-        scratch=[fine] * 9 + [middle] * 8 + [((320, LANES), F32)],
-        places=[VMEM] * 2 + [HBM] * 11,
-        limit=24,
-        semaphores=11,
+        scratch=[fine] * 3 + [middle] * 3 + [((320, LANES), F32)],
     )
     place = jnp.stack([lax.axis_index("gx"), lax.axis_index("gy")]).astype(jnp.int32)
     chunk, place = lax.optimization_barrier((chunk, place))
@@ -762,15 +730,11 @@
         up_kernel,
         [brick],
         (place, chunks, own) + tuple(kept),
-        scratch=[fine] * 6
-        + [middle] * 5
-        + [plane] * 9
+        scratch=[plane] * 9
         + [brick, ((16, 32, LANES), F32), ((8, 32, LANES), F32)]
         + [middle] * 2
         + [fine] * 2,
-        specs=[SMEM] + [VMEM] * 2 + [HBM] * 11,
-        limit=24,
-        semaphores=11,
+        specs=[SMEM] + [VMEM] * 13,
     )
     return out, mobility
 

time: 84.1 us -> 77.1 us (0.917)
  Pallas kernels: 19.6 us -> 14.6 us
  waiting for transfers between devices: 13.7 us -> 11.8 us
    pallas_call x6 -> x7, Pallas kernels: 19.6 us -> 14.6 us  [call(): pl.pallas_call(kernel, out_shape=[pltpu.MemorySpace.HBM(*out) if place is...]
    ppermute x9, waiting for transfers between devices: 13.7 us -> 11.8 us  [shift(): lax.ppermute(x, axis, [(i, (i + direction) % count) for i in range(count)])]
  transfers between devices with their start and end apart: 9 -> 9, of which waited for: 6 -> 6; matrix products, arithmetic and copies ran while one was open for 0% -> 0% of each run, Pallas kernels for 0% -> 3%
where the time goes in v7:
time: 77.1 us; the launch traced here: 76.8 us
  starting transfers between devices  30 us (39%)
  blocking collectives  19.7 us (26%)
  Pallas kernels  14.6 us (19%)
  waiting for transfers between devices  11.8 us (15%)
    ppermute x9, starting transfers between devices, shift(): lax.ppermute(x, axis, [(i, (i + direction) % count) for i in range(count)])  30 us
    all_to_all x1, blocking collectives, body(): chunks = lax.all_to_all(chunk, ('gx', 'gy'), 0, 0, tiled=True)  19.7 us
    pallas_call x7, Pallas kernels, call(): pl.pallas_call(kernel, out_shape=[pltpu.MemorySpace.HBM(*out) if place is...  14.6 us
    ppermute x9, waiting for transfers between devices, shift(): lax.ppermute(x, axis, [(i, (i + direction) % count) for i in range(count)])  11.8 us
  transfers between devices with their start and end apart: 9, of which 6 were waited for; matrix products, arithmetic and copies ran while one was open for 0% of the time, Pallas kernels for 3%

profile of v7, /device:TPU:1, one launch (start us, length us, event | category | flops | bytes accessed | tf_op | source)
XLA Modules:
  0.0 76.8 jit_solution(14456203802765490291)
XLA Ops:
  0.6 1.3 %shard_map.59 = (f32[16,16,128]{2,1,0:T(8,128)S(1)}, f32[16,16,128]{2,1,0:T(8,128)S(1)}, bf16[8,16,16,128]{3,2,1,0:T(8,128)(2,1)S(1)}, s32[1,1,8,8]{3,2,1,0:T(8,...) custom-call(f32[16,16,128]{2,1,0:T(8,128)} %conc_in.1, ...), custom_call_target="tpu_custom_call" | custom-call | tf_op jit(solution)/shard_map/pallas_call | solution.py:39
  2.0 2.7 %collective-permute-start = (bf16[9,16,128]{2,1,0:T(8,128)(2,1)S(1)}, bf16[9,16,128]{2,1,0:T(8,128)(2,1)S(1)}, u32[]{:S(2)}, u32[]{:S(2)}) collective-permute-start(bf16[9,16,128]{2,1,0:T(8,128)(2,1)S(1)} %get-tuple-element.45), channel_id=1, source_target_pairs={{0,64},{64,128},{128,192},{192,256},{256,320},{320,384},{384,448},... | collective-permute-start | bytes 110600 | tf_op jit(solution)/shard_map/ppermute | solution.py:670
  4.7 4.2 %collective-permute-start.1 = (bf16[9,16,128]{2,1,0:T(8,128)(2,1)S(1)}, bf16[9,16,128]{2,1,0:T(8,128)(2,1)S(1)}, u32[]{:S(2)}, u32[]{:S(2)}) collective-permute-start(bf16[9,16,128]{2,1,0:T(8,128)(2,1)S(1)} %get-tuple-element.46), channel_id=1, source_target_pairs={{0,448},{64,0},{128,64},{192,128},{256,192},{320,256},{384,320},{4... | collective-permute-start | bytes 110600 | tf_op jit(solution)/shard_map/ppermute | solution.py:670
  8.9 1.9 %collective-permute-start.2 = (bf16[9,16,128]{2,1,0:T(8,128)(2,1)S(1)}, bf16[9,16,128]{2,1,0:T(8,128)(2,1)S(1)}, u32[]{:S(2)}, u32[]{:S(2)}) collective-permute-start(bf16[9,16,128]{2,1,0:T(8,128)(2,1)S(1)} %get-tuple-element.47), channel_id=1, source_target_pairs={{0,48},{16,0},{32,16},{48,32},{1,49},{17,1},{33,17},{49,33},{2,50}... | collective-permute-start | bytes 110600 | tf_op jit(solution)/shard_map/ppermute | solution.py:670
  10.8 1.9 %shard_map.60 = (f32[16,16,128]{2,1,0:T(8,128)S(1)}, bf16[8,16,128]{2,1,0:T(8,128)(2,1)S(1)}, bf16[17,16,128]{2,1,0:T(8,128)(2,1)S(1)}, bf16[17,16,128]{2,1,0:T(8,128)(2,1)S(1)}) custom-call(f32[16,16,128]{2,1,0:T(8,128)S(1)} %get-tuple-element.40.conc_ref.conc_in, bf16[8,16,16,128]{3,2,1,0:T(8,128)(2,1)S(1)} %get-tuple-element.41.order_ref, ...), custom_call_target="tpu_custom_call" | custom-call | tf_op jit(solution)/shard_map/pallas_call | solution.py:39
  12.7 0.0 collective-permute-done.xm_ref
  12.7 0.0 collective-permute-done.1.xp_ref
  12.8 0.8 %collective-permute-done.2.yp_ref = bf16[9,16,128]{2,1,0:T(8,128)(2,1)S(1)} collective-permute-done((bf16[9,16,128]{2,1,0:T(8,128)(2,1)S(1)}, bf16[9,16,128]{2,1,0:T(8,128)(2,1)S(1)}, u32[]{:S(2)}, u32[]{:S(2)}) %collective-permute-start.2) | collective-permute-done | bytes 36896 | tf_op jit(solution)/shard_map/ppermute | solution.py:670
  13.6 0.4 shard_map.61
  14.0 1.9 %collective-permute-start.3 = (bf16[34,16,128]{2,1,0:T(8,128)(2,1)S(1)}, bf16[34,16,128]{2,1,0:T(8,128)(2,1)S(1)}, u32[]{:S(2)}, u32[]{:S(2)}) collective-permute-start(bf16[34,16,128]{2,1,0:T(8,128)(2,1)S(1)} %get-tuple-element.53), channel_id=1, source_target_pairs={{0,1},{1,2},{2,3},{3,4},{4,5},{5,6},{6,7},{7,8},{8,9},{9,10},{10,1... | collective-permute-start | bytes 417800 | tf_op jit(solution)/shard_map/ppermute | solution.py:670
  15.9 8.6 %collective-permute-start.4 = (bf16[34,16,128]{2,1,0:T(8,128)(2,1)S(1)}, bf16[34,16,128]{2,1,0:T(8,128)(2,1)S(1)}, u32[]{:S(2)}, u32[]{:S(2)}) collective-permute-start(bf16[34,16,128]{2,1,0:T(8,128)(2,1)S(1)} %get-tuple-element.54), channel_id=1, source_target_pairs={{0,15},{1,0},{2,1},{3,2},{4,3},{5,4},{6,5},{7,6},{8,7},{9,8},{10,9... | collective-permute-start | bytes 417800 | tf_op jit(solution)/shard_map/ppermute | solution.py:670
  24.5 0.5 collective-permute-done.3.left_ref
  25.0 1.5 %collective-permute-done.4.right_ref = bf16[34,16,128]{2,1,0:T(8,128)(2,1)S(1)} collective-permute-done((bf16[34,16,128]{2,1,0:T(8,128)(2,1)S(1)}, bf16[34,16,128]{2,1,0:T(8,128)(2,1)S(1)}, u32[]{:S(2)}, u32[]{:S(2)}) %collective-permute-start.4) | collective-permute-done | bytes 139296 | tf_op jit(solution)/shard_map/ppermute | solution.py:670
  26.5 0.6 shard_map.62
  27.2 1.9 %collective-permute-start.5 = (bf16[86,8,128]{2,1,0:T(8,128)(2,1)S(1)}, bf16[86,8,128]{2,1,0:T(8,128)(2,1)S(1)}, u32[]{:S(2)}, u32[]{:S(2)}) collective-permute-start(bf16[86,8,128]{2,1,0:T(8,128)(2,1)S(1)} %get-tuple-element.55.high_ref), channel_id=1, source_target_pairs={{0,16},{16,32},{32,48},{48,0},{1,17},{17,33},{33,49},{49,1},{2,18}... | collective-permute-start | bytes 528392 | tf_op jit(solution)/shard_map/ppermute | solution.py:670
  29.1 4.6 %collective-permute-start.6 = (bf16[80,8,128]{2,1,0:T(8,128)(2,1)S(1)}, bf16[80,8,128]{2,1,0:T(8,128)(2,1)S(1)}, u32[]{:S(2)}, u32[]{:S(2)}) collective-permute-start(bf16[80,8,128]{2,1,0:T(8,128)(2,1)S(1)} %get-tuple-element.56.low_ref), channel_id=1, source_target_pairs={{0,48},{16,0},{32,16},{48,32},{1,49},{17,1},{33,17},{49,33},{2,50}... | collective-permute-start | bytes 491528 | tf_op jit(solution)/shard_map/ppermute | solution.py:670
  33.7 2.2 %collective-permute-done.6.above_ref = bf16[80,8,128]{2,1,0:T(8,128)(2,1)S(1)} collective-permute-done((bf16[80,8,128]{2,1,0:T(8,128)(2,1)S(1)}, bf16[80,8,128]{2,1,0:T(8,128)(2,1)S(1)}, u32[]{:S(2)}, u32[]{:S(2)}) %collective-permute-start.6) | collective-permute-done | bytes 163872 | tf_op jit(solution)/shard_map/ppermute | solution.py:670
  35.9 0.0 collective-permute-done.5.below_ref
  35.9 0.8 %shard_map.63 = (f32[16,16,128]{2,1,0:T(8,128)}, f32[16,16,128]{2,1,0:T(8,128)S(1)}, bf16[5,8,32,128]{3,2,1,0:T(8,128)(2,1)S(1)}, bf16[5,8,32,128]{3,2,1,0:T(8,128)(2,1)S(1)}) custom-call(bf16[86,8,128]{2,1,0:T(8,128)(2,1)S(1)} %collective-permute-done.5.below_ref, bf16[80,8,128]{2,1,0:T(8,128)(2,1)S(1)} %get-tuple-element.56.low_ref, ...), custom_call_target="tpu_custom_call" | custom-call | tf_op jit(solution)/shard_map/pallas_call | solution.py:39
  36.7 4.2 %collective-permute-start.7 = (bf16[5,8,32,128]{3,2,1,0:T(8,128)(2,1)S(1)}, bf16[5,8,32,128]{3,2,1,0:T(8,128)(2,1)S(1)}, u32[]{:S(2)}, u32[]{:S(2)}) collective-permute-start(bf16[5,8,32,128]{3,2,1,0:T(8,128)(2,1)S(1)} %get-tuple-element.61.xh_ref), channel_id=1, source_target_pairs={{0,64},{64,128},{128,192},{192,256},{256,320},{320,384},{384,448},... | collective-permute-start | bytes 983048 | tf_op jit(solution)/shard_map/ppermute | solution.py:670
  40.9 0.0 collective-permute-start.8
  40.9 0.1 pad_add_fusion.place_ref
  41.0 3.9 %collective-permute-done.7.xm_ref = bf16[5,8,32,128]{3,2,1,0:T(8,128)(2,1)S(1)} collective-permute-done((bf16[5,8,32,128]{3,2,1,0:T(8,128)(2,1)S(1)}, bf16[5,8,32,128]{3,2,1,0:T(8,128)(2,1)S(1)}, u32[]{:S(2)}, u32[]{:S(2)}) %collective-permute-start.7) | collective-permute-done | bytes 327712 | tf_op jit(solution)/shard_map/ppermute | solution.py:670
  44.9 2.8 %collective-permute-done.8.xp_ref = bf16[5,8,32,128]{3,2,1,0:T(8,128)(2,1)S(1)} collective-permute-done((bf16[5,8,32,128]{3,2,1,0:T(8,128)(2,1)S(1)}, bf16[5,8,32,128]{3,2,1,0:T(8,128)(2,1)S(1)}, u32[]{:S(2)}, u32[]{:S(2)}) %collective-permute-start.8) | collective-permute-done | bytes 327712 | tf_op jit(solution)/shard_map/ppermute | solution.py:670
  47.7 5.6 %shard_map.64 = (f32[160,128]{1,0:T(8,128)S(1)}, bf16[32,64,128]{2,1,0:T(8,128)(2,1)S(1)}, f32[32,32,256]{2,1,0:T(8,128)S(1)}, f32[32,32,256]{2,1,0:T(8,128)S(1)...) custom-call(f32[16,16,128]{2,1,0:T(8,128)S(1)} %get-tuple-element.59, ...), custom_call_target="tpu_custom_call" | custom-call | tf_op jit(solution)/shard_map/pallas_call | solution.py:39
  53.3 19.7 %all_to_all.5.all_ref = bf16[32,64,128]{2,1,0:T(8,128)(2,1)S(1)} all-to-all(bf16[32,64,128]{2,1,0:T(8,128)(2,1)S(1)} %get-tuple-element.64), channel_id=1, replica_groups=mesh['gx'=8,'gy'=4,'gz'=16] {'gx','gy'}, dimensions={0} | all-to-all | bytes 1048576 | tf_op jit(solution)/shard_map/all_to_all | solution.py:727
  72.9 3.9 %shard_map.65 = f32[16,16,128]{2,1,0:T(8,128)} custom-call(s32[2]{0:T(128)S(1)} %pad_add_fusion.place_ref, bf16[32,64,128]{2,1,0:T(8,128)(2,1)S(1)} %all_to_all.5.all_ref, f32[160,128]{1,0:T(8,128)S(1)} %get-tuple-element.65.own_ref, f32[32,32,256]{2,1,0:T(8,128)S(1)} %get-tuple-element.66.side_ref, f32[32,32,256]{2,1,0:T(8,128)S(1)} %get-tuple-element.67.kx_ref, ...), custom_call_target="tpu_custom_call" | custom-call | tf_op jit(solution)/shard_map/pallas_call | solution.py:39
Async XLA Ops:
  2.0 10.8 %collective-permute-start = (bf16[9,16,128]{2,1,0:T(8,128)(2,1)S(1)}, bf16[9,16,128]{2,1,0:T(8,128)(2,1)S(1)}, u32[]{:S(2)}, u32[]{:S(2)}) collective-permute-start(bf16[9,16,128]{2,1,0:T(8,128)(2,1)S(1)} %get-tuple-element.45), channel_id=1, source_target_pairs={{0,64},{64,128},{128,192},{192,256},{256,320},{320,384},{384,448},... | collective-permute-start | bytes 110600 | tf_op jit(solution)/shard_map/ppermute | solution.py:670
  4.7 8.1 %collective-permute-start.1 = (bf16[9,16,128]{2,1,0:T(8,128)(2,1)S(1)}, bf16[9,16,128]{2,1,0:T(8,128)(2,1)S(1)}, u32[]{:S(2)}, u32[]{:S(2)}) collective-permute-start(bf16[9,16,128]{2,1,0:T(8,128)(2,1)S(1)} %get-tuple-element.46), channel_id=1, source_target_pairs={{0,448},{64,0},{128,64},{192,128},{256,192},{320,256},{384,320},{4... | collective-permute-start | bytes 110600 | tf_op jit(solution)/shard_map/ppermute | solution.py:670
  8.9 4.7 %collective-permute-start.2 = (bf16[9,16,128]{2,1,0:T(8,128)(2,1)S(1)}, bf16[9,16,128]{2,1,0:T(8,128)(2,1)S(1)}, u32[]{:S(2)}, u32[]{:S(2)}) collective-permute-start(bf16[9,16,128]{2,1,0:T(8,128)(2,1)S(1)} %get-tuple-element.47), channel_id=1, source_target_pairs={{0,48},{16,0},{32,16},{48,32},{1,49},{17,1},{33,17},{49,33},{2,50}... | collective-permute-start | bytes 110600 | tf_op jit(solution)/shard_map/ppermute | solution.py:670
  14.0 11.0 %collective-permute-start.3 = (bf16[34,16,128]{2,1,0:T(8,128)(2,1)S(1)}, bf16[34,16,128]{2,1,0:T(8,128)(2,1)S(1)}, u32[]{:S(2)}, u32[]{:S(2)}) collective-permute-start(bf16[34,16,128]{2,1,0:T(8,128)(2,1)S(1)} %get-tuple-element.53), channel_id=1, source_target_pairs={{0,1},{1,2},{2,3},{3,4},{4,5},{5,6},{6,7},{7,8},{8,9},{9,10},{10,1... | collective-permute-start | bytes 417800 | tf_op jit(solution)/shard_map/ppermute | solution.py:670
  15.9 10.6 %collective-permute-start.4 = (bf16[34,16,128]{2,1,0:T(8,128)(2,1)S(1)}, bf16[34,16,128]{2,1,0:T(8,128)(2,1)S(1)}, u32[]{:S(2)}, u32[]{:S(2)}) collective-permute-start(bf16[34,16,128]{2,1,0:T(8,128)(2,1)S(1)} %get-tuple-element.54), channel_id=1, source_target_pairs={{0,15},{1,0},{2,1},{3,2},{4,3},{5,4},{6,5},{7,6},{8,7},{9,8},{10,9... | collective-permute-start | bytes 417800 | tf_op jit(solution)/shard_map/ppermute | solution.py:670
  27.2 8.8 %collective-permute-start.5 = (bf16[86,8,128]{2,1,0:T(8,128)(2,1)S(1)}, bf16[86,8,128]{2,1,0:T(8,128)(2,1)S(1)}, u32[]{:S(2)}, u32[]{:S(2)}) collective-permute-start(bf16[86,8,128]{2,1,0:T(8,128)(2,1)S(1)} %get-tuple-element.55.high_ref), channel_id=1, source_target_pairs={{0,16},{16,32},{32,48},{48,0},{1,17},{17,33},{33,49},{49,1},{2,18}... | collective-permute-start | bytes 528392 | tf_op jit(solution)/shard_map/ppermute | solution.py:670
  29.1 6.8 %collective-permute-start.6 = (bf16[80,8,128]{2,1,0:T(8,128)(2,1)S(1)}, bf16[80,8,128]{2,1,0:T(8,128)(2,1)S(1)}, u32[]{:S(2)}, u32[]{:S(2)}) collective-permute-start(bf16[80,8,128]{2,1,0:T(8,128)(2,1)S(1)} %get-tuple-element.56.low_ref), channel_id=1, source_target_pairs={{0,48},{16,0},{32,16},{48,32},{1,49},{17,1},{33,17},{49,33},{2,50}... | collective-permute-start | bytes 491528 | tf_op jit(solution)/shard_map/ppermute | solution.py:670
  36.7 8.2 %collective-permute-start.7 = (bf16[5,8,32,128]{3,2,1,0:T(8,128)(2,1)S(1)}, bf16[5,8,32,128]{3,2,1,0:T(8,128)(2,1)S(1)}, u32[]{:S(2)}, u32[]{:S(2)}) collective-permute-start(bf16[5,8,32,128]{3,2,1,0:T(8,128)(2,1)S(1)} %get-tuple-element.61.xh_ref), channel_id=1, source_target_pairs={{0,64},{64,128},{128,192},{192,256},{256,320},{320,384},{384,448},... | collective-permute-start | bytes 983048 | tf_op jit(solution)/shard_map/ppermute | solution.py:670
  40.9 6.8 %collective-permute-start.8 = (bf16[5,8,32,128]{3,2,1,0:T(8,128)(2,1)S(1)}, bf16[5,8,32,128]{3,2,1,0:T(8,128)(2,1)S(1)}, u32[]{:S(2)}, u32[]{:S(2)}) collective-permute-start(bf16[5,8,32,128]{3,2,1,0:T(8,128)(2,1)S(1)} %get-tuple-element.60.xl_ref), channel_id=1, source_target_pairs={{0,448},{64,0},{128,64},{192,128},{256,192},{320,256},{384,320},{4... | collective-permute-start | bytes 983048 | tf_op jit(solution)/shard_map/ppermute | solution.py:670

commit v8 on v7

--- a/solution.py
+++ b/solution.py
@@ -369,25 +369,48 @@
             use(at(x), cells[k], left[k])
 
 
-def down_kernel(
-    mob_in, conc_in, side_in, xl_ref, xh_ref, xm_ref, xp_ref,
-    own_ref, chunk_ref, side_ref, kx_ref, ky_ref, kz_ref, wd_ref, v_ref,
-    k1x_ref, k1y_ref, k1z_ref, wd1_ref, f1_ref,
-    mob, v0, res, e0, e1, r1, rows,
-):
+INNER = {
+    "side": (8, 16), "kx": (8, 15), "ky": (9, 14), "kz": (9, 14), "wd": (9, 14), "v": (10, 12),
+    "k1x": (4, 7), "k1y": (5, 6), "k1z": (5, 6), "wd1": (5, 6), "f1": (6, 4),
+    "mob": (8, 16), "v0": (8, 16), "s1": (9, 14), "r0": (11, 10),
+}
+KEPT = ("side", "kx", "ky", "kz", "wd", "v", "k1x", "k1y", "k1z", "wd1", "f1")
+MIDDLE_ARRAYS = ("k1x", "k1y", "k1z", "wd1", "f1")
+
+
+class Inner:
+    def __init__(self, name, ref):
+        self.low, self.count = INNER[name]
+        self.ref = ref
+
+    def __contains__(self, x):
+        return self.low <= x < self.low + self.count
+
+    def __getitem__(self, x):
+        return self.ref[x - self.low]
+
+    def __setitem__(self, x, value):
+        self.ref[x - self.low] = value
+
+
+class Joined:
+    def __init__(self, inner, outer):
+        self.inner = inner
+        self.outer = outer
+
+    def __getitem__(self, x):
+        return self.inner[x] if x in self.inner else self.outer[x]
+
+    def __setitem__(self, x, value):
+        self.outer[x] = value
+
+
+def assemble(xs, parts_of, mob, v0, side):
     lane = iota((32, LANES), 1)
-
-    own = (mob_in, conc_in, side_in)
-    slabs = (xm_ref, xl_ref, xh_ref, xp_ref)
-    for xs in groups(range(32), 8):
+    for some in groups(xs, 8):
         planes = []
-        for x in xs:
-            parts = [slabs[x // 8][place, x % 8].astype(F32) for place in range(5)]
-            if 8 <= x < 24:
-                for place in range(3):
-                    part = parts[place]
-                    part = [part[:8], own[place][x - 8], part[24:]]
-                    parts[place] = jnp.concatenate(part, axis=0)
+        for x in some:
+            parts = parts_of(x)
             down, up = parts[3], parts[4]
             beyond = jnp.where(lane < 43, up, jnp.where(lane >= 85, down, 1.0))
             iterate = jnp.where(
@@ -396,74 +419,129 @@
             right = jnp.where(
                 lane < 42, roll(up, -86, 1), jnp.where(lane >= 86, roll(down, 86, 1), 0.0)
             )
-            planes.append((parts, beyond, iterate, right))
-        for x, (parts, beyond, iterate, right) in zip(xs, planes):
-            mob[x, :, :LANES] = parts[0]
-            v0[x, :, :LANES] = parts[1]
-            side_ref[x, :, :LANES] = parts[2]
-            mob[x, :, LANES:] = beyond
-            v0[x, :, LANES:] = iterate
-            side_ref[x, :, LANES:] = right
-
+            planes.append(zip(parts, (beyond, iterate, right)))
+        for x, plane in zip(some, planes):
+            for target, pair in zip((mob, v0, side), plane):
+                target[x] = jnp.concatenate(pair, axis=1)
+
+
+def descend(a, coeffs, sweeps, middle_x, middle, middle_f):
     half = TAU / 2
-
-    before = half * (mob[1] + mob[2])
-    kx_ref[1] = before
-    for xs in groups(range(2, 30), 7):
-        here = [mob[x] for x in xs + [xs[-1] + 1]]
-        kz = [half * (cells + roll(cells, -1, 1)) for cells in here[:-1]]
-        back = [roll(k, 1, 1) for k in kz]
-        done = []
-        for k, x in enumerate(xs):
-            kx = half * (here[k] + here[k + 1])
-            ky = half * (here[k] + roll(here[k], -1, 0))
-            total = (kx + before) + (ky + roll(ky, 1, 0)) + (kz[k] + back[k])
-            done.append((kx, ky, OMEGA / (1.0 + total)))
-            before = kx
-        for k, x in enumerate(xs):
-            kx_ref[x], ky_ref[x], wd_ref[x] = done[k]
-            kz_ref[x] = kz[k]
-
-
-    def smooth(target, weight):
+    mob, kx_ref, ky_ref, kz_ref, wd_ref = (a[k] for k in ("mob", "kx", "ky", "kz", "wd"))
+    for first, last in coeffs:
+        before = half * (mob[first - 1] + mob[first])
+        kx_ref[first - 1] = before
+        for xs in groups(range(first, last + 1), 7):
+            here = [mob[x] for x in xs + [xs[-1] + 1]]
+            kz = [half * (cells + roll(cells, -1, 1)) for cells in here[:-1]]
+            back = [roll(k, 1, 1) for k in kz]
+            done = []
+            for k, x in enumerate(xs):
+                kx = half * (here[k] + here[k + 1])
+                ky = half * (here[k] + roll(here[k], -1, 0))
+                total = (kx + before) + (ky + roll(ky, 1, 0)) + (kz[k] + back[k])
+                done.append((kx, ky, OMEGA / (1.0 + total)))
+                before = kx
+            for k, x in enumerate(xs):
+                kx_ref[x], ky_ref[x], wd_ref[x] = done[k]
+                kz_ref[x] = kz[k]
+
+    def smooth(target):
         def use(x, value, left):
-            target[x] = value + weight[x] * left
+            target[x] = value + wd_ref[x] * left
 
         return use
 
-    sweep_planes(2, 29, v0, side_ref, kx_ref, ky_ref, kz_ref, 1, smooth(res, wd_ref))
-    sweep_planes(3, 28, res, side_ref, kx_ref, ky_ref, kz_ref, 1, smooth(v_ref, wd_ref))
-
-
     def keep(x, value, left):
-        res[x] = left
-
-    sweep_planes(4, 27, v_ref, side_ref, kx_ref, ky_ref, kz_ref, 1, keep)
+        a["r0"][x] = left
+
+    steps = (("v0", smooth(a["s1"])), ("s1", smooth(a["v"])), ("v", keep))
+    for (name, use), runs in zip(steps, sweeps):
+        for first, last in runs:
+            sweep_planes(first, last, a[name], a["side"], kx_ref, ky_ref, kz_ref, 1, use)
 
     def pool(x):
         return pair_sum(pair_sum(x, 1, 0), 1, 1)
 
-    for xs in groups(range(1, 14), 7):
+    k1x_ref = a["k1x"]
+    for xs in groups(middle_x, 7):
         done = [pool(kx_ref[2 * i + 1]) * (1.0 / 16.0) for i in xs]
         for i, value in zip(xs, done):
             k1x_ref[i] = value
-    for ref in (f1_ref, k1y_ref, k1z_ref, wd1_ref):
-        ref[1] = jnp.zeros((32, RING), F32)
-    for xs in groups(range(2, 14), 6):
+    for xs in groups(middle, 6):
         done = []
         for i in xs:
             x = 2 * i
-            f1 = pool(res[x] + res[x + 1]) * 0.125
             along_y = pair_sum(ky_ref[x] + ky_ref[x + 1], 1, 1)
             k1y = upper_of(along_y, 1, 0) * (1.0 / 16.0)
             along_z = pair_sum(kz_ref[x] + kz_ref[x + 1], 1, 0)
             k1z = upper_of(along_z, 1, 1) * (1.0 / 16.0)
             total = k1x_ref[i] + k1x_ref[i - 1]
             total = total + (k1y + roll(k1y, 2, 0)) + (k1z + roll(k1z, 2, 1))
-            weight = OMEGA / (1.0 + total)
-            done.append((f1, k1y, k1z, weight, weight * f1))
+            done.append((k1y, k1z, OMEGA / (1.0 + total)))
         for i, value in zip(xs, done):
-            f1_ref[i], k1y_ref[i], k1z_ref[i], wd1_ref[i], e0[i] = value
+            a["k1y"][i], a["k1z"][i], a["wd1"][i] = value
+    res = a["r0"]
+    for xs in groups(middle_f, 8):
+        done = [pool(res[2 * i] + res[2 * i + 1]) * 0.125 for i in xs]
+        for i, value in zip(xs, done):
+            a["f1"][i] = value
+
+
+def near_kernel(mob_in, conc_in, side_in, xl_ref, xh_ref, *refs):
+    a = {name: Inner(name, ref) for name, ref in zip(INNER, refs)}
+    own = (mob_in, conc_in, side_in)
+
+    def parts_of(x):
+        ref = xl_ref if x < 16 else xh_ref
+        parts = [ref[place, x % 8].astype(F32) for place in range(5)]
+        for place in range(3):
+            part = parts[place]
+            part = [part[:8], own[place][x - 8], part[24:]]
+            parts[place] = jnp.concatenate(part, axis=0)
+        return parts
+
+    assemble(range(8, 24), parts_of, a["mob"], a["v0"], a["side"])
+    descend(
+        a, [(9, 22)], [[(9, 22)], [(10, 21)], [(11, 20)]], range(4, 11), range(5, 11), range(6, 10)
+    )
+
+
+def down_kernel(xm_ref, xp_ref, *refs):
+    count = len(INNER)
+    inner, refs = refs[:count], refs[count:]
+    own_ref, chunk_ref, *outer = refs[: 2 + count]
+    e0, e1, r1, rows = refs[2 + count :]
+    a = {
+        name: Joined(Inner(name, near), far) for name, near, far in zip(INNER, inner, outer)
+    }
+
+    def parts_of(x):
+        ref = xm_ref if x < 8 else xp_ref
+        return [ref[place, x % 8].astype(F32) for place in range(5)]
+
+    outside = list(range(8)) + list(range(24, 32))
+    assemble(outside, parts_of, a["mob"], a["v0"], a["side"])
+    descend(
+        a,
+        [(2, 8), (23, 29)],
+        [[(2, 8), (23, 29)], [(3, 9), (22, 28)], [(4, 10), (21, 27)]],
+        [1, 2, 3, 11, 12, 13],
+        [2, 3, 4, 11, 12, 13],
+        [2, 3, 4, 5, 10, 11, 12, 13],
+    )
+    f1_ref, k1x_ref, k1y_ref, k1z_ref, wd1_ref = (
+        a[k] for k in ("f1", "k1x", "k1y", "k1z", "wd1")
+    )
+    for i in range(2, 14):
+        e0[i] = wd1_ref[i] * f1_ref[i]
+
+    def smooth(target, weight):
+        def use(x, value, left):
+            target[x] = value + weight[x] * left
+
+        return use
+
     sweep_planes(3, 12, e0, f1_ref, k1x_ref, k1y_ref, k1z_ref, 2, smooth(e1, wd1_ref))
 
     def keep_middle(x, value, left):
@@ -528,11 +606,17 @@
 
 
 def up_kernel(
-    place_ref, all_ref, own_ref, side_ref, kx_ref, ky_ref, kz_ref, wd_ref, v_ref,
-    k1x_ref, k1y_ref, k1z_ref, wd1_ref, f1_ref,
-    out_ref,
-    pair0, pair1, c2x, c2y, c2z, wd2, f2, ea, eb, mid, tall, lean, e1a, e1b, va, vb,
+    place_ref, all_ref, own_ref, *refs
 ):
+    count = len(KEPT)
+    joined = [
+        Joined(Inner(name, near), far)
+        for name, near, far in zip(KEPT, refs[:count], refs[count : 2 * count])
+    ]
+    side_ref, kx_ref, ky_ref, kz_ref, wd_ref, v_ref = joined[:6]
+    k1x_ref, k1y_ref, k1z_ref, wd1_ref, f1_ref = joined[6:]
+    out_ref, pair0, pair1, c2x, c2y, c2z, wd2, f2, ea, eb = refs[2 * count : 2 * count + 10]
+    mid, tall, lean, e1a, e1b, va, vb = refs[2 * count + 10 :]
     gx = place_ref[0]
     gy = place_ref[1]
 
@@ -716,12 +800,19 @@
     after = shift(xl, "gx", -1)
     fine = ((32, 32, RING), F32)
     middle = ((16, 32, RING), F32)
-    own, chunk, *kept = call(
+    inner = call(
+        near_kernel,
+        [((INNER[name][1], 32, RING), F32) for name in INNER],
+        (keep, conc, side, xl, xh),
+    )
+    outer = [middle if name in MIDDLE_ARRAYS else fine for name in INNER]
+    own, chunk, *outer = call(
         down_kernel,
-        [((160, LANES), F32), ((32, CHUNK, LANES), BF16)] + [fine] * 6 + [middle] * 5,
-        (keep, conc, side, xl, xh, before, after),
-        scratch=[fine] * 3 + [middle] * 3 + [((320, LANES), F32)],
-    )
+        [((160, LANES), F32), ((32, CHUNK, LANES), BF16)] + outer[: len(KEPT)],
+        (before, after) + tuple(inner),
+        scratch=outer[len(KEPT) :] + [middle] * 3 + [((320, LANES), F32)],
+    )
+    kept = tuple(inner[: len(KEPT)]) + tuple(outer)
     place = jnp.stack([lax.axis_index("gx"), lax.axis_index("gy")]).astype(jnp.int32)
     chunk, place = lax.optimization_barrier((chunk, place))
     chunks = lax.all_to_all(chunk, ("gx", "gy"), 0, 0, tiled=True)
@@ -729,12 +820,12 @@
     (out,) = call(
         up_kernel,
         [brick],
-        (place, chunks, own) + tuple(kept),
+        (place, chunks, own) + kept,
         scratch=[plane] * 9
         + [brick, ((16, 32, LANES), F32), ((8, 32, LANES), F32)]
         + [middle] * 2
         + [fine] * 2,
-        specs=[SMEM] + [VMEM] * 13,
+        specs=[SMEM] + [VMEM] * (2 + len(kept)),
     )
     return out, mobility
 

time: 77.1 us -> 75 us (0.973)
  waiting for transfers between devices: 11.8 us -> 9.55 us
    ppermute x9, waiting for transfers between devices: 11.8 us -> 9.55 us  [shift(): lax.ppermute(x, axis, [(i, (i + direction) % count) for i in range(count)])]
    pallas_call x7 -> x8, Pallas kernels: 14.6 us -> 14.7 us  [call(): pl.pallas_call(kernel, out_shape=[pltpu.MemorySpace.HBM(*out) if place is...]
  transfers between devices with their start and end apart: 9 -> 9, of which waited for: 6 -> 6; matrix products, arithmetic and copies ran while one was open for 0% -> 0% of each run, Pallas kernels for 3% -> 6%
where the time goes in v8:
time: 75 us; the launch traced here: 74.7 us
  starting transfers between devices  30 us (40%)
  blocking collectives  19.7 us (26%)
  Pallas kernels  14.7 us (20%)
  waiting for transfers between devices  9.55 us (13%)
    ppermute x9, starting transfers between devices, shift(): lax.ppermute(x, axis, [(i, (i + direction) % count) for i in range(count)])  30 us
    all_to_all x1, blocking collectives, body(): chunks = lax.all_to_all(chunk, ('gx', 'gy'), 0, 0, tiled=True)  19.7 us
    pallas_call x8, Pallas kernels, call(): pl.pallas_call(kernel, out_shape=[pltpu.MemorySpace.HBM(*out) if place is...  14.7 us
    ppermute x9, waiting for transfers between devices, shift(): lax.ppermute(x, axis, [(i, (i + direction) % count) for i in range(count)])  9.55 us
  transfers between devices with their start and end apart: 9, of which 6 were waited for; matrix products, arithmetic and copies ran while one was open for 0% of the time, Pallas kernels for 6%

profile of v8, /device:TPU:1, one launch (start us, length us, event | category | flops | bytes accessed | tf_op | source)
XLA Modules:
  0.0 74.7 jit_solution(8029642305753429352)
XLA Ops:
  0.6 1.3 %shard_map.59 = (f32[16,16,128]{2,1,0:T(8,128)S(1)}, f32[16,16,128]{2,1,0:T(8,128)S(1)}, bf16[8,16,16,128]{3,2,1,0:T(8,128)(2,1)S(1)}, s32[1,1,8,8]{3,2,1,0:T(8,...) custom-call(f32[16,16,128]{2,1,0:T(8,128)} %conc_in.1, ...), custom_call_target="tpu_custom_call" | custom-call | tf_op jit(solution)/shard_map/pallas_call | solution.py:39
  2.0 2.7 %collective-permute-start = (bf16[9,16,128]{2,1,0:T(8,128)(2,1)S(1)}, bf16[9,16,128]{2,1,0:T(8,128)(2,1)S(1)}, u32[]{:S(2)}, u32[]{:S(2)}) collective-permute-start(bf16[9,16,128]{2,1,0:T(8,128)(2,1)S(1)} %get-tuple-element.60), channel_id=1, source_target_pairs={{0,64},{64,128},{128,192},{192,256},{256,320},{320,384},{384,448},... | collective-permute-start | bytes 110600 | tf_op jit(solution)/shard_map/ppermute | solution.py:754
  4.7 4.2 %collective-permute-start.1 = (bf16[9,16,128]{2,1,0:T(8,128)(2,1)S(1)}, bf16[9,16,128]{2,1,0:T(8,128)(2,1)S(1)}, u32[]{:S(2)}, u32[]{:S(2)}) collective-permute-start(bf16[9,16,128]{2,1,0:T(8,128)(2,1)S(1)} %get-tuple-element.61), channel_id=1, source_target_pairs={{0,448},{64,0},{128,64},{192,128},{256,192},{320,256},{384,320},{4... | collective-permute-start | bytes 110600 | tf_op jit(solution)/shard_map/ppermute | solution.py:754
  8.9 1.9 %collective-permute-start.2 = (bf16[9,16,128]{2,1,0:T(8,128)(2,1)S(1)}, bf16[9,16,128]{2,1,0:T(8,128)(2,1)S(1)}, u32[]{:S(2)}, u32[]{:S(2)}) collective-permute-start(bf16[9,16,128]{2,1,0:T(8,128)(2,1)S(1)} %get-tuple-element.62), channel_id=1, source_target_pairs={{0,48},{16,0},{32,16},{48,32},{1,49},{17,1},{33,17},{49,33},{2,50}... | collective-permute-start | bytes 110600 | tf_op jit(solution)/shard_map/ppermute | solution.py:754
  10.8 1.9 %shard_map.60 = (f32[16,16,128]{2,1,0:T(8,128)S(1)}, bf16[8,16,128]{2,1,0:T(8,128)(2,1)S(1)}, bf16[17,16,128]{2,1,0:T(8,128)(2,1)S(1)}, bf16[17,16,128]{2,1,0:T(8,128)(2,1)S(1)}) custom-call(f32[16,16,128]{2,1,0:T(8,128)S(1)} %get-tuple-element.55.conc_ref.conc_in, bf16[8,16,16,128]{3,2,1,0:T(8,128)(2,1)S(1)} %get-tuple-element.56.order_ref, ...), custom_call_target="tpu_custom_call" | custom-call | tf_op jit(solution)/shard_map/pallas_call | solution.py:39
  12.7 0.0 collective-permute-done.xm_ref
  12.7 0.0 collective-permute-done.1.xp_ref
  12.8 0.8 %collective-permute-done.2.yp_ref = bf16[9,16,128]{2,1,0:T(8,128)(2,1)S(1)} collective-permute-done((bf16[9,16,128]{2,1,0:T(8,128)(2,1)S(1)}, bf16[9,16,128]{2,1,0:T(8,128)(2,1)S(1)}, u32[]{:S(2)}, u32[]{:S(2)}) %collective-permute-start.2) | collective-permute-done | bytes 36896 | tf_op jit(solution)/shard_map/ppermute | solution.py:754
  13.6 0.4 shard_map.61
  14.0 1.9 %collective-permute-start.3 = (bf16[34,16,128]{2,1,0:T(8,128)(2,1)S(1)}, bf16[34,16,128]{2,1,0:T(8,128)(2,1)S(1)}, u32[]{:S(2)}, u32[]{:S(2)}) collective-permute-start(bf16[34,16,128]{2,1,0:T(8,128)(2,1)S(1)} %get-tuple-element.68), channel_id=1, source_target_pairs={{0,1},{1,2},{2,3},{3,4},{4,5},{5,6},{6,7},{7,8},{8,9},{9,10},{10,1... | collective-permute-start | bytes 417800 | tf_op jit(solution)/shard_map/ppermute | solution.py:754
  15.9 8.6 %collective-permute-start.4 = (bf16[34,16,128]{2,1,0:T(8,128)(2,1)S(1)}, bf16[34,16,128]{2,1,0:T(8,128)(2,1)S(1)}, u32[]{:S(2)}, u32[]{:S(2)}) collective-permute-start(bf16[34,16,128]{2,1,0:T(8,128)(2,1)S(1)} %get-tuple-element.69), channel_id=1, source_target_pairs={{0,15},{1,0},{2,1},{3,2},{4,3},{5,4},{6,5},{7,6},{8,7},{9,8},{10,9... | collective-permute-start | bytes 417800 | tf_op jit(solution)/shard_map/ppermute | solution.py:754
  24.5 0.5 collective-permute-done.3.left_ref
  25.0 1.5 %collective-permute-done.4.right_ref = bf16[34,16,128]{2,1,0:T(8,128)(2,1)S(1)} collective-permute-done((bf16[34,16,128]{2,1,0:T(8,128)(2,1)S(1)}, bf16[34,16,128]{2,1,0:T(8,128)(2,1)S(1)}, u32[]{:S(2)}, u32[]{:S(2)}) %collective-permute-start.4) | collective-permute-done | bytes 139296 | tf_op jit(solution)/shard_map/ppermute | solution.py:754
  26.5 0.6 shard_map.62
  27.2 1.9 %collective-permute-start.5 = (bf16[86,8,128]{2,1,0:T(8,128)(2,1)S(1)}, bf16[86,8,128]{2,1,0:T(8,128)(2,1)S(1)}, u32[]{:S(2)}, u32[]{:S(2)}) collective-permute-start(bf16[86,8,128]{2,1,0:T(8,128)(2,1)S(1)} %get-tuple-element.70.high_ref), channel_id=1, source_target_pairs={{0,16},{16,32},{32,48},{48,0},{1,17},{17,33},{33,49},{49,1},{2,18}... | collective-permute-start | bytes 528392 | tf_op jit(solution)/shard_map/ppermute | solution.py:754
  29.1 4.6 %collective-permute-start.6 = (bf16[80,8,128]{2,1,0:T(8,128)(2,1)S(1)}, bf16[80,8,128]{2,1,0:T(8,128)(2,1)S(1)}, u32[]{:S(2)}, u32[]{:S(2)}) collective-permute-start(bf16[80,8,128]{2,1,0:T(8,128)(2,1)S(1)} %get-tuple-element.71.low_ref), channel_id=1, source_target_pairs={{0,48},{16,0},{32,16},{48,32},{1,49},{17,1},{33,17},{49,33},{2,50}... | collective-permute-start | bytes 491528 | tf_op jit(solution)/shard_map/ppermute | solution.py:754
  33.7 2.2 %collective-permute-done.6.above_ref = bf16[80,8,128]{2,1,0:T(8,128)(2,1)S(1)} collective-permute-done((bf16[80,8,128]{2,1,0:T(8,128)(2,1)S(1)}, bf16[80,8,128]{2,1,0:T(8,128)(2,1)S(1)}, u32[]{:S(2)}, u32[]{:S(2)}) %collective-permute-start.6) | collective-permute-done | bytes 163872 | tf_op jit(solution)/shard_map/ppermute | solution.py:754
  35.9 0.0 collective-permute-done.5.below_ref
  35.9 0.8 %shard_map.63 = (f32[16,16,128]{2,1,0:T(8,128)}, f32[16,16,128]{2,1,0:T(8,128)S(1)}, bf16[5,8,32,128]{3,2,1,0:T(8,128)(2,1)S(1)}, bf16[5,8,32,128]{3,2,1,0:T(8,128)(2,1)S(1)}) custom-call(bf16[86,8,128]{2,1,0:T(8,128)(2,1)S(1)} %collective-permute-done.5.below_ref, bf16[80,8,128]{2,1,0:T(8,128)(2,1)S(1)} %get-tuple-element.71.low_ref, ...), custom_call_target="tpu_custom_call" | custom-call | tf_op jit(solution)/shard_map/pallas_call | solution.py:39
  36.7 4.2 %collective-permute-start.7 = (bf16[5,8,32,128]{3,2,1,0:T(8,128)(2,1)S(1)}, bf16[5,8,32,128]{3,2,1,0:T(8,128)(2,1)S(1)}, u32[]{:S(2)}, u32[]{:S(2)}) collective-permute-start(bf16[5,8,32,128]{3,2,1,0:T(8,128)(2,1)S(1)} %get-tuple-element.74.xh_ref), channel_id=1, source_target_pairs={{0,64},{64,128},{128,192},{192,256},{256,320},{320,384},{384,448},... | collective-permute-start | bytes 983048 | tf_op jit(solution)/shard_map/ppermute | solution.py:754
  40.9 0.0 collective-permute-start.8
  40.9 0.1 pad_add_fusion.place_ref
  41.0 2.2 %shard_map.64 = (f32[16,32,256]{2,1,0:T(8,128)S(1)}, f32[15,32,256]{2,1,0:T(8,128)S(1)}, f32[14,32,256]{2,1,0:T(8,128)S(1)}, f32[14,32,256]{2,1,0:T(8,128)S(1)},...) custom-call(f32[16,16,128]{2,1,0:T(8,128)S(1)} %get-tuple-element.76, ...), custom_call_target="tpu_custom_call" | custom-call | tf_op jit(solution)/shard_map/pallas_call | solution.py:39
  43.2 1.7 %collective-permute-done.7.xm_ref = bf16[5,8,32,128]{3,2,1,0:T(8,128)(2,1)S(1)} collective-permute-done((bf16[5,8,32,128]{3,2,1,0:T(8,128)(2,1)S(1)}, bf16[5,8,32,128]{3,2,1,0:T(8,128)(2,1)S(1)}, u32[]{:S(2)}, u32[]{:S(2)}) %collective-permute-start.7) | collective-permute-done | bytes 327712 | tf_op jit(solution)/shard_map/ppermute | solution.py:754
  44.9 2.8 %collective-permute-done.8.xp_ref = bf16[5,8,32,128]{3,2,1,0:T(8,128)(2,1)S(1)} collective-permute-done((bf16[5,8,32,128]{3,2,1,0:T(8,128)(2,1)S(1)}, bf16[5,8,32,128]{3,2,1,0:T(8,128)(2,1)S(1)}, u32[]{:S(2)}, u32[]{:S(2)}) %collective-permute-start.8) | collective-permute-done | bytes 327712 | tf_op jit(solution)/shard_map/ppermute | solution.py:754
  47.7 3.5 %shard_map.65 = (f32[160,128]{1,0:T(8,128)S(1)}, bf16[32,64,128]{2,1,0:T(8,128)(2,1)S(1)}, f32[32,32,256]{2,1,0:T(8,128)S(1)}, f32[32,32,256]{2,1,0:T(8,128)S(1)...) custom-call(bf16[5,8,32,128]{3,2,1,0:T(8,128)(2,1)S(1)} %collective-, ...), custom_call_target="tpu_custom_call" | custom-call | tf_op jit(solution)/shard_map/pallas_call | solution.py:39
  51.2 19.7 %all_to_all.5.all_ref = bf16[32,64,128]{2,1,0:T(8,128)(2,1)S(1)} all-to-all(bf16[32,64,128]{2,1,0:T(8,128)(2,1)S(1)} %get-tuple-element.94), channel_id=1, replica_groups=mesh['gx'=8,'gy'=4,'gz'=16] {'gx','gy'}, dimensions={0} | all-to-all | bytes 1048576 | tf_op jit(solution)/shard_map/all_to_all | solution.py:818
  70.9 3.8 %shard_map.66 = f32[16,16,128]{2,1,0:T(8,128)} custom-call(s32[2]{0:T(128)S(1)} %pad_add_fusion.place_ref, bf16[32,64,128]{2,1,0:T(8,128)(2,1)S(1)} %all_to_all.5.all_ref, f32[160,128]{1,0:T(8,128)S(1)} %get-tuple-element.95.own_ref, f32[16,32,256]{2,1,0:T(8,128)S(1)} %get-tuple-element.77.refs_0_, f32[15,32,256]{2,1,0:T(8,128)S(1)} %get-tuple-element.78.refs_1_, ...), custom_call_target="tpu_custom_call" | custom-call | tf_op jit(solution)/shard_map/pallas_call | solution.py:39
Async XLA Ops:
  2.0 10.8 %collective-permute-start = (bf16[9,16,128]{2,1,0:T(8,128)(2,1)S(1)}, bf16[9,16,128]{2,1,0:T(8,128)(2,1)S(1)}, u32[]{:S(2)}, u32[]{:S(2)}) collective-permute-start(bf16[9,16,128]{2,1,0:T(8,128)(2,1)S(1)} %get-tuple-element.60), channel_id=1, source_target_pairs={{0,64},{64,128},{128,192},{192,256},{256,320},{320,384},{384,448},... | collective-permute-start | bytes 110600 | tf_op jit(solution)/shard_map/ppermute | solution.py:754
  4.7 8.1 %collective-permute-start.1 = (bf16[9,16,128]{2,1,0:T(8,128)(2,1)S(1)}, bf16[9,16,128]{2,1,0:T(8,128)(2,1)S(1)}, u32[]{:S(2)}, u32[]{:S(2)}) collective-permute-start(bf16[9,16,128]{2,1,0:T(8,128)(2,1)S(1)} %get-tuple-element.61), channel_id=1, source_target_pairs={{0,448},{64,0},{128,64},{192,128},{256,192},{320,256},{384,320},{4... | collective-permute-start | bytes 110600 | tf_op jit(solution)/shard_map/ppermute | solution.py:754
  8.9 4.7 %collective-permute-start.2 = (bf16[9,16,128]{2,1,0:T(8,128)(2,1)S(1)}, bf16[9,16,128]{2,1,0:T(8,128)(2,1)S(1)}, u32[]{:S(2)}, u32[]{:S(2)}) collective-permute-start(bf16[9,16,128]{2,1,0:T(8,128)(2,1)S(1)} %get-tuple-element.62), channel_id=1, source_target_pairs={{0,48},{16,0},{32,16},{48,32},{1,49},{17,1},{33,17},{49,33},{2,50}... | collective-permute-start | bytes 110600 | tf_op jit(solution)/shard_map/ppermute | solution.py:754
  14.0 11.0 %collective-permute-start.3 = (bf16[34,16,128]{2,1,0:T(8,128)(2,1)S(1)}, bf16[34,16,128]{2,1,0:T(8,128)(2,1)S(1)}, u32[]{:S(2)}, u32[]{:S(2)}) collective-permute-start(bf16[34,16,128]{2,1,0:T(8,128)(2,1)S(1)} %get-tuple-element.68), channel_id=1, source_target_pairs={{0,1},{1,2},{2,3},{3,4},{4,5},{5,6},{6,7},{7,8},{8,9},{9,10},{10,1... | collective-permute-start | bytes 417800 | tf_op jit(solution)/shard_map/ppermute | solution.py:754
  15.9 10.6 %collective-permute-start.4 = (bf16[34,16,128]{2,1,0:T(8,128)(2,1)S(1)}, bf16[34,16,128]{2,1,0:T(8,128)(2,1)S(1)}, u32[]{:S(2)}, u32[]{:S(2)}) collective-permute-start(bf16[34,16,128]{2,1,0:T(8,128)(2,1)S(1)} %get-tuple-element.69), channel_id=1, source_target_pairs={{0,15},{1,0},{2,1},{3,2},{4,3},{5,4},{6,5},{7,6},{8,7},{9,8},{10,9... | collective-permute-start | bytes 417800 | tf_op jit(solution)/shard_map/ppermute | solution.py:754
  27.2 8.8 %collective-permute-start.5 = (bf16[86,8,128]{2,1,0:T(8,128)(2,1)S(1)}, bf16[86,8,128]{2,1,0:T(8,128)(2,1)S(1)}, u32[]{:S(2)}, u32[]{:S(2)}) collective-permute-start(bf16[86,8,128]{2,1,0:T(8,128)(2,1)S(1)} %get-tuple-element.70.high_ref), channel_id=1, source_target_pairs={{0,16},{16,32},{32,48},{48,0},{1,17},{17,33},{33,49},{49,1},{2,18}... | collective-permute-start | bytes 528392 | tf_op jit(solution)/shard_map/ppermute | solution.py:754
  29.1 6.8 %collective-permute-start.6 = (bf16[80,8,128]{2,1,0:T(8,128)(2,1)S(1)}, bf16[80,8,128]{2,1,0:T(8,128)(2,1)S(1)}, u32[]{:S(2)}, u32[]{:S(2)}) collective-permute-start(bf16[80,8,128]{2,1,0:T(8,128)(2,1)S(1)} %get-tuple-element.71.low_ref), channel_id=1, source_target_pairs={{0,48},{16,0},{32,16},{48,32},{1,49},{17,1},{33,17},{49,33},{2,50}... | collective-permute-start | bytes 491528 | tf_op jit(solution)/shard_map/ppermute | solution.py:754
  36.7 8.2 %collective-permute-start.7 = (bf16[5,8,32,128]{3,2,1,0:T(8,128)(2,1)S(1)}, bf16[5,8,32,128]{3,2,1,0:T(8,128)(2,1)S(1)}, u32[]{:S(2)}, u32[]{:S(2)}) collective-permute-start(bf16[5,8,32,128]{3,2,1,0:T(8,128)(2,1)S(1)} %get-tuple-element.74.xh_ref), channel_id=1, source_target_pairs={{0,64},{64,128},{128,192},{192,256},{256,320},{320,384},{384,448},... | collective-permute-start | bytes 983048 | tf_op jit(solution)/shard_map/ppermute | solution.py:754
  40.9 6.8 %collective-permute-start.8 = (bf16[5,8,32,128]{3,2,1,0:T(8,128)(2,1)S(1)}, bf16[5,8,32,128]{3,2,1,0:T(8,128)(2,1)S(1)}, u32[]{:S(2)}, u32[]{:S(2)}) collective-permute-start(bf16[5,8,32,128]{3,2,1,0:T(8,128)(2,1)S(1)} %get-tuple-element.75.xl_ref), channel_id=1, source_target_pairs={{0,448},{64,0},{128,64},{192,128},{256,192},{320,256},{384,320},{4... | collective-permute-start | bytes 983048 | tf_op jit(solution)/shard_map/ppermute | solution.py:754

commit v9 on v8

--- a/solution.py
+++ b/solution.py
@@ -289,7 +289,7 @@
 
 def rows_kernel(
     below_ref, low_ref, high_ref, above_ref, mob_ref, beyond_ref, beside_ref,
-    out_ref, keep_ref, xl_ref, xh_ref,
+    keep_ref, xl_ref, xh_ref,
 ):
     lane = iota((8, LANES), 1)
     first = iota((8, LANES), 0) == 0
@@ -307,9 +307,8 @@
             down = jnp.where(lane >= 85, beside, 0.0)
             lines.append((main, None, None, down, jnp.where(lane < 43, beside, 0.0)))
         own = mob_ref[x, :8] + lines[0][0]
-        for out in (out_ref, keep_ref):
-            out[x, :8] = own
-            out[x, 8:] = mob_ref[x, 8:]
+        keep_ref[x, :8] = own
+        keep_ref[x, 8:] = mob_ref[x, 8:]
         for place in range(5):
             plane = 16 * place + x
             near, far = low_ref[plane], above_ref[plane]
@@ -488,67 +487,7 @@
             a["f1"][i] = value
 
 
-def near_kernel(mob_in, conc_in, side_in, xl_ref, xh_ref, *refs):
-    a = {name: Inner(name, ref) for name, ref in zip(INNER, refs)}
-    own = (mob_in, conc_in, side_in)
-
-    def parts_of(x):
-        ref = xl_ref if x < 16 else xh_ref
-        parts = [ref[place, x % 8].astype(F32) for place in range(5)]
-        for place in range(3):
-            part = parts[place]
-            part = [part[:8], own[place][x - 8], part[24:]]
-            parts[place] = jnp.concatenate(part, axis=0)
-        return parts
-
-    assemble(range(8, 24), parts_of, a["mob"], a["v0"], a["side"])
-    descend(
-        a, [(9, 22)], [[(9, 22)], [(10, 21)], [(11, 20)]], range(4, 11), range(5, 11), range(6, 10)
-    )
-
-
-def down_kernel(xm_ref, xp_ref, *refs):
-    count = len(INNER)
-    inner, refs = refs[:count], refs[count:]
-    own_ref, chunk_ref, *outer = refs[: 2 + count]
-    e0, e1, r1, rows = refs[2 + count :]
-    a = {
-        name: Joined(Inner(name, near), far) for name, near, far in zip(INNER, inner, outer)
-    }
-
-    def parts_of(x):
-        ref = xm_ref if x < 8 else xp_ref
-        return [ref[place, x % 8].astype(F32) for place in range(5)]
-
-    outside = list(range(8)) + list(range(24, 32))
-    assemble(outside, parts_of, a["mob"], a["v0"], a["side"])
-    descend(
-        a,
-        [(2, 8), (23, 29)],
-        [[(2, 8), (23, 29)], [(3, 9), (22, 28)], [(4, 10), (21, 27)]],
-        [1, 2, 3, 11, 12, 13],
-        [2, 3, 4, 11, 12, 13],
-        [2, 3, 4, 5, 10, 11, 12, 13],
-    )
-    f1_ref, k1x_ref, k1y_ref, k1z_ref, wd1_ref = (
-        a[k] for k in ("f1", "k1x", "k1y", "k1z", "wd1")
-    )
-    for i in range(2, 14):
-        e0[i] = wd1_ref[i] * f1_ref[i]
-
-    def smooth(target, weight):
-        def use(x, value, left):
-            target[x] = value + weight[x] * left
-
-        return use
-
-    sweep_planes(3, 12, e0, f1_ref, k1x_ref, k1y_ref, k1z_ref, 2, smooth(e1, wd1_ref))
-
-    def keep_middle(x, value, left):
-        r1[x] = left
-
-    sweep_planes(4, 11, e1, f1_ref, k1x_ref, k1y_ref, k1z_ref, 2, keep_middle)
-
+def selection_matrices(picks0_ref, picks1_ref, middle_ref, spread_ref):
     src = iota((RING, LANES), 0)
     dst = iota((RING, LANES), 1)
     cell = jnp.where(src < 192, src, src - RING)
@@ -559,9 +498,82 @@
     sides = [there & (coarse == dst), there & (coarse + COARSE == dst)]
     picks0 = sides + [head & (coarse + 2 * COARSE == dst)]
     picks1 = sides + [tail & (coarse + 2 * COARSE - HEAD == dst)]
-    picks0 = jnp.concatenate([pick.astype(F32) for pick in picks0], axis=0).astype(BF16)
-    picks1 = jnp.concatenate([pick.astype(F32) for pick in picks1], axis=0).astype(BF16)
-    pick_middle = ((cell == 2 * middle_cell(dst)) & (dst < MIDDLE)).astype(F32)
+    picks0_ref[...] = jnp.concatenate([pick.astype(F32) for pick in picks0], axis=0).astype(BF16)
+    picks1_ref[...] = jnp.concatenate([pick.astype(F32) for pick in picks1], axis=0).astype(BF16)
+    pick_middle = (cell == 2 * middle_cell(dst)) & (dst < MIDDLE)
+    middle_ref[...] = pick_middle.astype(F32).astype(BF16)
+    src = iota((LANES, RING), 0)
+    dst = iota((LANES, RING), 1)
+    cell = jnp.where(dst < 192, dst, dst - RING)
+    middle = (src < MIDDLE) & ((cell + 64) // 2 - 32 == middle_cell(src))
+    coarse = (cell >= -4 * COARSE_LOW) & (src >= MIDDLE) & (src < MIDDLE + COARSE)
+    coarse = coarse & ((cell + 4 * COARSE_LOW) // 4 == src - MIDDLE)
+    spread_ref[...] = (middle | coarse).astype(F32).astype(BF16)
+
+
+def near_kernel(mob_in, conc_in, side_in, xl_ref, xh_ref, *refs):
+    a = {name: Inner(name, ref) for name, ref in zip(INNER, refs)}
+    refs[len(INNER)][...] = mob_in[...]
+    selection_matrices(*refs[len(INNER) + 1 :])
+    own = (mob_in, conc_in, side_in)
+
+    def parts_of(x):
+        ref = xl_ref if x < 16 else xh_ref
+        parts = [ref[place, x % 8].astype(F32) for place in range(5)]
+        for place in range(3):
+            part = parts[place]
+            part = [part[:8], own[place][x - 8], part[24:]]
+            parts[place] = jnp.concatenate(part, axis=0)
+        return parts
+
+    assemble(range(8, 24), parts_of, a["mob"], a["v0"], a["side"])
+    descend(
+        a, [(9, 22)], [[(9, 22)], [(10, 21)], [(11, 20)]], range(4, 11), range(5, 11), range(6, 10)
+    )
+
+
+def down_kernel(xm_ref, xp_ref, picks0_ref, picks1_ref, pick_middle_ref, *refs):
+    count = len(INNER)
+    inner, refs = refs[:count], refs[count:]
+    own_ref, chunk_ref, *outer = refs[: 2 + count]
+    e0, e1, r1, rows = refs[2 + count :]
+    a = {
+        name: Joined(Inner(name, near), far) for name, near, far in zip(INNER, inner, outer)
+    }
+
+    def parts_of(x):
+        ref = xm_ref if x < 8 else xp_ref
+        return [ref[place, x % 8].astype(F32) for place in range(5)]
+
+    outside = list(range(8)) + list(range(24, 32))
+    assemble(outside, parts_of, a["mob"], a["v0"], a["side"])
+    descend(
+        a,
+        [(2, 8), (23, 29)],
+        [[(2, 8), (23, 29)], [(3, 9), (22, 28)], [(4, 10), (21, 27)]],
+        [1, 2, 3, 11, 12, 13],
+        [2, 3, 4, 11, 12, 13],
+        [2, 3, 4, 5, 10, 11, 12, 13],
+    )
+    f1_ref, k1x_ref, k1y_ref, k1z_ref, wd1_ref = (
+        a[k] for k in ("f1", "k1x", "k1y", "k1z", "wd1")
+    )
+    for i in range(2, 14):
+        e0[i] = wd1_ref[i] * f1_ref[i]
+
+    def smooth(target, weight):
+        def use(x, value, left):
+            target[x] = value + weight[x] * left
+
+        return use
+
+    sweep_planes(3, 12, e0, f1_ref, k1x_ref, k1y_ref, k1z_ref, 2, smooth(e1, wd1_ref))
+
+    def keep_middle(x, value, left):
+        r1[x] = left
+
+    sweep_planes(4, 11, e1, f1_ref, k1x_ref, k1y_ref, k1z_ref, 2, keep_middle)
+
     firsts = []
     seconds = []
     for j in range(4):
@@ -580,11 +592,11 @@
         seconds.append(jnp.concatenate([k2x.astype(BF16), k2y.astype(BF16), k2z], axis=1))
     firsts = jnp.concatenate(firsts, axis=0)
     seconds = jnp.concatenate(seconds, axis=0)
-    rows[pl.ds(0, 64), :] = jnp.dot(firsts, picks0, preferred_element_type=F32)
-    rows[pl.ds(64, 64), :] = jnp.dot(seconds, picks1, preferred_element_type=F32)
+    rows[pl.ds(0, 64), :] = jnp.dot(firsts, picks0_ref[...], preferred_element_type=F32)
+    rows[pl.ds(64, 64), :] = jnp.dot(seconds, picks1_ref[...], preferred_element_type=F32)
     coarse = rows[pl.ds(0, 32, stride=4), :]
     rows[...] = select_dot(
-        jnp.concatenate([e1[i] for i in range(3, 13)], axis=0), pick_middle
+        jnp.concatenate([e1[i] for i in range(3, 13)], axis=0), pick_middle_ref[...]
     )
     own_ref[...] = rows[pl.ds(0, 160, stride=2), :]
 
@@ -606,7 +618,7 @@
 
 
 def up_kernel(
-    place_ref, all_ref, own_ref, *refs
+    place_ref, all_ref, own_ref, spread_ref, *refs
 ):
     count = len(KEPT)
     joined = [
@@ -723,16 +735,9 @@
         line = mid[i]
         for k in range(2):
             tall[i, pl.ds(k, 16, stride=2), :] = line
-    src = iota((LANES, RING), 0)
-    dst = iota((LANES, RING), 1)
-    cell = jnp.where(dst < 192, dst, dst - RING)
-    middle = (src < MIDDLE) & ((cell + 64) // 2 - 32 == middle_cell(src))
-    coarse = (cell >= -4 * COARSE_LOW) & (src >= MIDDLE) & (src < MIDDLE + COARSE)
-    coarse = coarse & ((cell + 4 * COARSE_LOW) // 4 == src - MIDDLE)
-    spread = (middle | coarse).astype(F32)
     narrow = iota((32, LANES), 1) < MIDDLE
     packed = [jnp.where(narrow, tall[i], lean[i // 2]) for i in range(1, 15)]
-    widened = select_dot(jnp.concatenate(packed, axis=0), spread)
+    widened = select_dot(jnp.concatenate(packed, axis=0), spread_ref[...])
     for i in range(1, 15):
         e1a[i] = widened[32 * (i - 1) : 32 * i]
 
@@ -791,25 +796,28 @@
     below = shift(high, "gy", 1)
     above = shift(low, "gy", -1)
     slab = ((5, 8, 32, LANES), BF16)
-    mobility, keep, xl, xh = call(
+    keep, xl, xh = call(
         rows_kernel,
-        [brick, brick, slab, slab],
+        [brick, slab, slab],
         (below, low, high, above, keep, beyond, beside),
     )
     before = shift(xh, "gx", 1)
     after = shift(xl, "gx", -1)
     fine = ((32, 32, RING), F32)
     middle = ((16, 32, RING), F32)
-    inner = call(
+    *inner, mobility, picks0, picks1, pick_middle, spread = call(
         near_kernel,
-        [((INNER[name][1], 32, RING), F32) for name in INNER],
+        [((INNER[name][1], 32, RING), F32) for name in INNER]
+        + [brick]
+        + [((3 * RING, LANES), BF16)] * 2
+        + [((RING, LANES), BF16), ((LANES, RING), BF16)],
         (keep, conc, side, xl, xh),
     )
     outer = [middle if name in MIDDLE_ARRAYS else fine for name in INNER]
     own, chunk, *outer = call(
         down_kernel,
         [((160, LANES), F32), ((32, CHUNK, LANES), BF16)] + outer[: len(KEPT)],
-        (before, after) + tuple(inner),
+        (before, after, picks0, picks1, pick_middle) + tuple(inner),
         scratch=outer[len(KEPT) :] + [middle] * 3 + [((320, LANES), F32)],
     )
     kept = tuple(inner[: len(KEPT)]) + tuple(outer)
@@ -820,12 +828,12 @@
     (out,) = call(
         up_kernel,
         [brick],
-        (place, chunks, own) + kept,
+        (place, chunks, own, spread) + kept,
         scratch=[plane] * 9
         + [brick, ((16, 32, LANES), F32), ((8, 32, LANES), F32)]
         + [middle] * 2
         + [fine] * 2,
-        specs=[SMEM] + [VMEM] * (2 + len(kept)),
+        specs=[SMEM] + [VMEM] * (3 + len(kept)),
     )
     return out, mobility
 

time: 75 us -> 74.4 us (level)
  waiting for transfers between devices: 9.55 us -> 8.79 us
    ppermute x9, waiting for transfers between devices: 9.55 us -> 8.79 us  [shift(): lax.ppermute(x, axis, [(i, (i + direction) % count) for i in range(count)])]
  transfers between devices with their start and end apart: 9 -> 9, of which waited for: 6 -> 6; matrix products, arithmetic and copies ran while one was open for 0% -> 0% of each run, Pallas kernels for 6% -> 7%
where the time goes in v9:
time: 74.4 us; the launch traced here: 74.1 us
  starting transfers between devices  30 us (40%)
  blocking collectives  19.7 us (26%)
  Pallas kernels  14.8 us (20%)
  waiting for transfers between devices  8.79 us (12%)
    ppermute x9, starting transfers between devices, shift(): lax.ppermute(x, axis, [(i, (i + direction) % count) for i in range(count)])  30 us
    all_to_all x1, blocking collectives, body(): chunks = lax.all_to_all(chunk, ('gx', 'gy'), 0, 0, tiled=True)  19.7 us
    pallas_call x8, Pallas kernels, call(): pl.pallas_call(kernel, out_shape=[pltpu.MemorySpace.HBM(*out) if place is...  14.8 us
    ppermute x9, waiting for transfers between devices, shift(): lax.ppermute(x, axis, [(i, (i + direction) % count) for i in range(count)])  8.79 us
  transfers between devices with their start and end apart: 9, of which 6 were waited for; matrix products, arithmetic and copies ran while one was open for 0% of the time, Pallas kernels for 7%

profile of v9, /device:TPU:1, one launch (start us, length us, event | category | flops | bytes accessed | tf_op | source)
XLA Modules:
  0.0 74.1 jit_solution(8799178695095463087)
XLA Ops:
  0.6 1.3 %shard_map.59 = (f32[16,16,128]{2,1,0:T(8,128)S(1)}, f32[16,16,128]{2,1,0:T(8,128)S(1)}, bf16[8,16,16,128]{3,2,1,0:T(8,128)(2,1)S(1)}, s32[1,1,8,8]{3,2,1,0:T(8,...) custom-call(f32[16,16,128]{2,1,0:T(8,128)} %conc_in.1, ...), custom_call_target="tpu_custom_call" | custom-call | tf_op jit(solution)/shard_map/pallas_call | solution.py:39
  2.0 2.7 %collective-permute-start = (bf16[9,16,128]{2,1,0:T(8,128)(2,1)S(1)}, bf16[9,16,128]{2,1,0:T(8,128)(2,1)S(1)}, u32[]{:S(2)}, u32[]{:S(2)}) collective-permute-start(bf16[9,16,128]{2,1,0:T(8,128)(2,1)S(1)} %get-tuple-element.64), channel_id=1, source_target_pairs={{0,64},{64,128},{128,192},{192,256},{256,320},{320,384},{384,448},... | collective-permute-start | bytes 110600 | tf_op jit(solution)/shard_map/ppermute | solution.py:759
  4.7 4.2 %collective-permute-start.1 = (bf16[9,16,128]{2,1,0:T(8,128)(2,1)S(1)}, bf16[9,16,128]{2,1,0:T(8,128)(2,1)S(1)}, u32[]{:S(2)}, u32[]{:S(2)}) collective-permute-start(bf16[9,16,128]{2,1,0:T(8,128)(2,1)S(1)} %get-tuple-element.65), channel_id=1, source_target_pairs={{0,448},{64,0},{128,64},{192,128},{256,192},{320,256},{384,320},{4... | collective-permute-start | bytes 110600 | tf_op jit(solution)/shard_map/ppermute | solution.py:759
  8.9 1.9 %collective-permute-start.2 = (bf16[9,16,128]{2,1,0:T(8,128)(2,1)S(1)}, bf16[9,16,128]{2,1,0:T(8,128)(2,1)S(1)}, u32[]{:S(2)}, u32[]{:S(2)}) collective-permute-start(bf16[9,16,128]{2,1,0:T(8,128)(2,1)S(1)} %get-tuple-element.66), channel_id=1, source_target_pairs={{0,48},{16,0},{32,16},{48,32},{1,49},{17,1},{33,17},{49,33},{2,50}... | collective-permute-start | bytes 110600 | tf_op jit(solution)/shard_map/ppermute | solution.py:759
  10.8 1.9 %shard_map.60 = (f32[16,16,128]{2,1,0:T(8,128)S(1)}, bf16[8,16,128]{2,1,0:T(8,128)(2,1)S(1)}, bf16[17,16,128]{2,1,0:T(8,128)(2,1)S(1)}, bf16[17,16,128]{2,1,0:T(8,128)(2,1)S(1)}) custom-call(f32[16,16,128]{2,1,0:T(8,128)S(1)} %get-tuple-element.59.conc_ref.conc_in, bf16[8,16,16,128]{3,2,1,0:T(8,128)(2,1)S(1)} %get-tuple-element.60.order_ref, ...), custom_call_target="tpu_custom_call" | custom-call | tf_op jit(solution)/shard_map/pallas_call | solution.py:39
  12.7 0.0 collective-permute-done.xm_ref
  12.7 0.0 collective-permute-done.1.xp_ref
  12.8 0.8 %collective-permute-done.2.yp_ref = bf16[9,16,128]{2,1,0:T(8,128)(2,1)S(1)} collective-permute-done((bf16[9,16,128]{2,1,0:T(8,128)(2,1)S(1)}, bf16[9,16,128]{2,1,0:T(8,128)(2,1)S(1)}, u32[]{:S(2)}, u32[]{:S(2)}) %collective-permute-start.2) | collective-permute-done | bytes 36896 | tf_op jit(solution)/shard_map/ppermute | solution.py:759
  13.6 0.4 shard_map.61
  14.0 1.9 %collective-permute-start.3 = (bf16[34,16,128]{2,1,0:T(8,128)(2,1)S(1)}, bf16[34,16,128]{2,1,0:T(8,128)(2,1)S(1)}, u32[]{:S(2)}, u32[]{:S(2)}) collective-permute-start(bf16[34,16,128]{2,1,0:T(8,128)(2,1)S(1)} %get-tuple-element.72), channel_id=1, source_target_pairs={{0,1},{1,2},{2,3},{3,4},{4,5},{5,6},{6,7},{7,8},{8,9},{9,10},{10,1... | collective-permute-start | bytes 417800 | tf_op jit(solution)/shard_map/ppermute | solution.py:759
  15.9 8.6 %collective-permute-start.4 = (bf16[34,16,128]{2,1,0:T(8,128)(2,1)S(1)}, bf16[34,16,128]{2,1,0:T(8,128)(2,1)S(1)}, u32[]{:S(2)}, u32[]{:S(2)}) collective-permute-start(bf16[34,16,128]{2,1,0:T(8,128)(2,1)S(1)} %get-tuple-element.73), channel_id=1, source_target_pairs={{0,15},{1,0},{2,1},{3,2},{4,3},{5,4},{6,5},{7,6},{8,7},{9,8},{10,9... | collective-permute-start | bytes 417800 | tf_op jit(solution)/shard_map/ppermute | solution.py:759
  24.5 0.5 collective-permute-done.3.left_ref
  25.0 1.5 %collective-permute-done.4.right_ref = bf16[34,16,128]{2,1,0:T(8,128)(2,1)S(1)} collective-permute-done((bf16[34,16,128]{2,1,0:T(8,128)(2,1)S(1)}, bf16[34,16,128]{2,1,0:T(8,128)(2,1)S(1)}, u32[]{:S(2)}, u32[]{:S(2)}) %collective-permute-start.4) | collective-permute-done | bytes 139296 | tf_op jit(solution)/shard_map/ppermute | solution.py:759
  26.5 0.6 shard_map.62
  27.2 1.9 %collective-permute-start.5 = (bf16[86,8,128]{2,1,0:T(8,128)(2,1)S(1)}, bf16[86,8,128]{2,1,0:T(8,128)(2,1)S(1)}, u32[]{:S(2)}, u32[]{:S(2)}) collective-permute-start(bf16[86,8,128]{2,1,0:T(8,128)(2,1)S(1)} %get-tuple-element.74.high_ref), channel_id=1, source_target_pairs={{0,16},{16,32},{32,48},{48,0},{1,17},{17,33},{33,49},{49,1},{2,18}... | collective-permute-start | bytes 528392 | tf_op jit(solution)/shard_map/ppermute | solution.py:759
  29.1 4.6 %collective-permute-start.6 = (bf16[80,8,128]{2,1,0:T(8,128)(2,1)S(1)}, bf16[80,8,128]{2,1,0:T(8,128)(2,1)S(1)}, u32[]{:S(2)}, u32[]{:S(2)}) collective-permute-start(bf16[80,8,128]{2,1,0:T(8,128)(2,1)S(1)} %get-tuple-element.75.low_ref), channel_id=1, source_target_pairs={{0,48},{16,0},{32,16},{48,32},{1,49},{17,1},{33,17},{49,33},{2,50}... | collective-permute-start | bytes 491528 | tf_op jit(solution)/shard_map/ppermute | solution.py:759
  33.7 2.2 %collective-permute-done.6.above_ref = bf16[80,8,128]{2,1,0:T(8,128)(2,1)S(1)} collective-permute-done((bf16[80,8,128]{2,1,0:T(8,128)(2,1)S(1)}, bf16[80,8,128]{2,1,0:T(8,128)(2,1)S(1)}, u32[]{:S(2)}, u32[]{:S(2)}) %collective-permute-start.6) | collective-permute-done | bytes 163872 | tf_op jit(solution)/shard_map/ppermute | solution.py:759
  35.9 0.0 collective-permute-done.5.below_ref
  35.9 0.1 shard_map.63
  36.1 4.2 %collective-permute-start.7 = (bf16[5,8,32,128]{3,2,1,0:T(8,128)(2,1)S(1)}, bf16[5,8,32,128]{3,2,1,0:T(8,128)(2,1)S(1)}, u32[]{:S(2)}, u32[]{:S(2)}) collective-permute-start(bf16[5,8,32,128]{3,2,1,0:T(8,128)(2,1)S(1)} %get-tuple-element.78.xh_ref), channel_id=1, source_target_pairs={{0,64},{64,128},{128,192},{192,256},{256,320},{320,384},{384,448},... | collective-permute-start | bytes 983048 | tf_op jit(solution)/shard_map/ppermute | solution.py:759
  40.3 0.0 collective-permute-start.8
  40.3 0.1 pad_add_fusion.place_ref
  40.4 3.0 %shard_map.64 = (f32[16,32,256]{2,1,0:T(8,128)S(1)}, f32[15,32,256]{2,1,0:T(8,128)S(1)}, f32[14,32,256]{2,1,0:T(8,128)S(1)}, f32[14,32,256]{2,1,0:T(8,128)S(1)},...) custom-call(f32[16,16,128]{2,1,0:T(8,128)S(1)} %get-tuple-element.80, ...), custom_call_target="tpu_custom_call" | custom-call | tf_op jit(solution)/shard_map/pallas_call | solution.py:39
  43.3 1.0 %collective-permute-done.7.xm_ref = bf16[5,8,32,128]{3,2,1,0:T(8,128)(2,1)S(1)} collective-permute-done((bf16[5,8,32,128]{3,2,1,0:T(8,128)(2,1)S(1)}, bf16[5,8,32,128]{3,2,1,0:T(8,128)(2,1)S(1)}, u32[]{:S(2)}, u32[]{:S(2)}) %collective-permute-start.7) | collective-permute-done | bytes 327712 | tf_op jit(solution)/shard_map/ppermute | solution.py:759
  44.3 2.8 %collective-permute-done.8.xp_ref = bf16[5,8,32,128]{3,2,1,0:T(8,128)(2,1)S(1)} collective-permute-done((bf16[5,8,32,128]{3,2,1,0:T(8,128)(2,1)S(1)}, bf16[5,8,32,128]{3,2,1,0:T(8,128)(2,1)S(1)}, u32[]{:S(2)}, u32[]{:S(2)}) %collective-permute-start.8) | collective-permute-done | bytes 327712 | tf_op jit(solution)/shard_map/ppermute | solution.py:759
  47.1 3.5 %shard_map.65 = (f32[160,128]{1,0:T(8,128)S(1)}, bf16[32,64,128]{2,1,0:T(8,128)(2,1)S(1)}, f32[32,32,256]{2,1,0:T(8,128)S(1)}, f32[32,32,256]{2,1,0:T(8,128)S(1)...) custom-call(bf16[5,8,32,128]{3,2,1,0:T(8,128)(2,1)S(1)} %collective-, ...), custom_call_target="tpu_custom_call" | custom-call | tf_op jit(solution)/shard_map/pallas_call | solution.py:39
  50.5 19.7 %all_to_all.5.all_ref = bf16[32,64,128]{2,1,0:T(8,128)(2,1)S(1)} all-to-all(bf16[32,64,128]{2,1,0:T(8,128)(2,1)S(1)} %get-tuple-element.101), channel_id=1, replica_groups=mesh['gx'=8,'gy'=4,'gz'=16] {'gx','gy'}, dimensions={0} | all-to-all | bytes 1048576 | tf_op jit(solution)/shard_map/all_to_all | solution.py:826
  70.2 3.9 %shard_map.66 = f32[16,16,128]{2,1,0:T(8,128)} custom-call(s32[2]{0:T(128)S(1)} %pad_add_fusion.place_ref, bf16[32,64,128]{2,1,0:T(8,128)(2,1)S(1)} %all_to_all.5.all_ref, f32[160,128]{1,0:T(8,128)S(1)} %get-tuple-element.102.own_ref, bf16[128,256]{1,0:T(8,128)(2,1)S(1)} %get-tuple-element.103.spread_ref, f32[16,32,256]{2,1,0:T(8,128)S(1)} %get-tuple-element.84.refs_0_, ...), custom_call_target="tpu_custom_call" | custom-call | tf_op jit(solution)/shard_map/pallas_call | solution.py:39
Async XLA Ops:
  2.0 10.8 %collective-permute-start = (bf16[9,16,128]{2,1,0:T(8,128)(2,1)S(1)}, bf16[9,16,128]{2,1,0:T(8,128)(2,1)S(1)}, u32[]{:S(2)}, u32[]{:S(2)}) collective-permute-start(bf16[9,16,128]{2,1,0:T(8,128)(2,1)S(1)} %get-tuple-element.64), channel_id=1, source_target_pairs={{0,64},{64,128},{128,192},{192,256},{256,320},{320,384},{384,448},... | collective-permute-start | bytes 110600 | tf_op jit(solution)/shard_map/ppermute | solution.py:759
  4.7 8.1 %collective-permute-start.1 = (bf16[9,16,128]{2,1,0:T(8,128)(2,1)S(1)}, bf16[9,16,128]{2,1,0:T(8,128)(2,1)S(1)}, u32[]{:S(2)}, u32[]{:S(2)}) collective-permute-start(bf16[9,16,128]{2,1,0:T(8,128)(2,1)S(1)} %get-tuple-element.65), channel_id=1, source_target_pairs={{0,448},{64,0},{128,64},{192,128},{256,192},{320,256},{384,320},{4... | collective-permute-start | bytes 110600 | tf_op jit(solution)/shard_map/ppermute | solution.py:759
  8.9 4.7 %collective-permute-start.2 = (bf16[9,16,128]{2,1,0:T(8,128)(2,1)S(1)}, bf16[9,16,128]{2,1,0:T(8,128)(2,1)S(1)}, u32[]{:S(2)}, u32[]{:S(2)}) collective-permute-start(bf16[9,16,128]{2,1,0:T(8,128)(2,1)S(1)} %get-tuple-element.66), channel_id=1, source_target_pairs={{0,48},{16,0},{32,16},{48,32},{1,49},{17,1},{33,17},{49,33},{2,50}... | collective-permute-start | bytes 110600 | tf_op jit(solution)/shard_map/ppermute | solution.py:759
  14.0 11.0 %collective-permute-start.3 = (bf16[34,16,128]{2,1,0:T(8,128)(2,1)S(1)}, bf16[34,16,128]{2,1,0:T(8,128)(2,1)S(1)}, u32[]{:S(2)}, u32[]{:S(2)}) collective-permute-start(bf16[34,16,128]{2,1,0:T(8,128)(2,1)S(1)} %get-tuple-element.72), channel_id=1, source_target_pairs={{0,1},{1,2},{2,3},{3,4},{4,5},{5,6},{6,7},{7,8},{8,9},{9,10},{10,1... | collective-permute-start | bytes 417800 | tf_op jit(solution)/shard_map/ppermute | solution.py:759
  15.9 10.6 %collective-permute-start.4 = (bf16[34,16,128]{2,1,0:T(8,128)(2,1)S(1)}, bf16[34,16,128]{2,1,0:T(8,128)(2,1)S(1)}, u32[]{:S(2)}, u32[]{:S(2)}) collective-permute-start(bf16[34,16,128]{2,1,0:T(8,128)(2,1)S(1)} %get-tuple-element.73), channel_id=1, source_target_pairs={{0,15},{1,0},{2,1},{3,2},{4,3},{5,4},{6,5},{7,6},{8,7},{9,8},{10,9... | collective-permute-start | bytes 417800 | tf_op jit(solution)/shard_map/ppermute | solution.py:759
  27.2 8.8 %collective-permute-start.5 = (bf16[86,8,128]{2,1,0:T(8,128)(2,1)S(1)}, bf16[86,8,128]{2,1,0:T(8,128)(2,1)S(1)}, u32[]{:S(2)}, u32[]{:S(2)}) collective-permute-start(bf16[86,8,128]{2,1,0:T(8,128)(2,1)S(1)} %get-tuple-element.74.high_ref), channel_id=1, source_target_pairs={{0,16},{16,32},{32,48},{48,0},{1,17},{17,33},{33,49},{49,1},{2,18}... | collective-permute-start | bytes 528392 | tf_op jit(solution)/shard_map/ppermute | solution.py:759
  29.1 6.8 %collective-permute-start.6 = (bf16[80,8,128]{2,1,0:T(8,128)(2,1)S(1)}, bf16[80,8,128]{2,1,0:T(8,128)(2,1)S(1)}, u32[]{:S(2)}, u32[]{:S(2)}) collective-permute-start(bf16[80,8,128]{2,1,0:T(8,128)(2,1)S(1)} %get-tuple-element.75.low_ref), channel_id=1, source_target_pairs={{0,48},{16,0},{32,16},{48,32},{1,49},{17,1},{33,17},{49,33},{2,50}... | collective-permute-start | bytes 491528 | tf_op jit(solution)/shard_map/ppermute | solution.py:759
  36.1 8.2 %collective-permute-start.7 = (bf16[5,8,32,128]{3,2,1,0:T(8,128)(2,1)S(1)}, bf16[5,8,32,128]{3,2,1,0:T(8,128)(2,1)S(1)}, u32[]{:S(2)}, u32[]{:S(2)}) collective-permute-start(bf16[5,8,32,128]{3,2,1,0:T(8,128)(2,1)S(1)} %get-tuple-element.78.xh_ref), channel_id=1, source_target_pairs={{0,64},{64,128},{128,192},{192,256},{256,320},{320,384},{384,448},... | collective-permute-start | bytes 983048 | tf_op jit(solution)/shard_map/ppermute | solution.py:759
  40.3 6.8 %collective-permute-start.8 = (bf16[5,8,32,128]{3,2,1,0:T(8,128)(2,1)S(1)}, bf16[5,8,32,128]{3,2,1,0:T(8,128)(2,1)S(1)}, u32[]{:S(2)}, u32[]{:S(2)}) collective-permute-start(bf16[5,8,32,128]{3,2,1,0:T(8,128)(2,1)S(1)} %get-tuple-element.79.xl_ref), channel_id=1, source_target_pairs={{0,448},{64,0},{128,64},{192,128},{256,192},{320,256},{384,320},{4... | collective-permute-start | bytes 983048 | tf_op jit(solution)/shard_map/ppermute | solution.py:759

commit v10 on v9

--- a/solution.py
+++ b/solution.py
@@ -88,9 +88,10 @@
 
 
 def faces_kernel(
-    conc_in, side_in, order_in, ids_in,
-    conc_ref, side_ref, order_ref, ids_ref, xm_ref, xp_ref, ym_ref, sems,
+    place_ref, conc_in, side_in, order_in, ids_in,
+    conc_ref, side_ref, order_ref, ids_ref, xa_ref, xb_ref, ym_ref, sems,
 ):
+    odd = place_ref[0] & 1
     pairs = (
         (ids_in, ids_ref), (order_in, order_ref), (conc_in, conc_ref), (side_in, side_ref),
     )
@@ -101,11 +102,11 @@
     copies[1].wait()
     grains = lane_ids(ids_ref)
     packed = split_ids(grains)
-    for ref in (xm_ref, xp_ref, ym_ref):
+    for ref in (xa_ref, xb_ref, ym_ref):
         ref[SLOTS] = packed
     for slot in range(SLOTS):
-        xm_ref[slot] = order_ref[slot, 0]
-        xp_ref[slot] = order_ref[slot, 15]
+        xa_ref[slot] = order_ref[slot, 15 * odd]
+        xb_ref[slot] = order_ref[slot, 15 - 15 * odd]
         ym_ref[slot] = order_ref[slot].astype(F32)[:, 0, :].astype(BF16)
     copies[2].wait()
     copies[3].wait()
@@ -189,7 +190,7 @@
         carry = plane(x, carry)
 
 def outer_kernel(
-    work, conc_ref, side_ref, order_ref, ids_ref, xm_ref, xp_ref, yp_ref,
+    place_ref, work, conc_ref, side_ref, order_ref, ids_ref, xa_ref, xb_ref, yp_ref,
     own_yp_ref, own_zm_ref, own_zp_ref, mob_ref, beyond_ref, zm_out, zp_out,
 ):
     own = lane_ids(ids_ref)
@@ -209,12 +210,15 @@
             total = part if total is None else total + part
         return total
 
-    first = work[0] + across(
-        lambda k: order_ref[k, 0], own, lambda k: xm_ref[k], join_ids(xm_ref[SLOTS])
-    )
-    final = work[15] + across(
-        lambda k: order_ref[k, 15], own, lambda k: xp_ref[k], join_ids(xp_ref[SLOTS])
-    )
+    odd = place_ref[0] & 1
+    side_a = across(
+        lambda k: order_ref[k, 15 * odd], own, lambda k: xa_ref[k], join_ids(xa_ref[SLOTS])
+    )
+    side_b = across(
+        lambda k: order_ref[k, 15 - 15 * odd], own, lambda k: xb_ref[k], join_ids(xb_ref[SLOTS])
+    )
+    first = work[0] + jnp.where(odd == 0, side_a, side_b)
+    final = work[15] + jnp.where(odd == 0, side_b, side_a)
     above_ids = join_ids(yp_ref[SLOTS])
     top = across(lambda k: own_yp_ref[k], own, lambda k: yp_ref[k], above_ids)
     beyond = across(lambda k: yp_ref[k], above_ids, lambda k: own_yp_ref[k], own)
@@ -288,8 +292,8 @@
 
 
 def rows_kernel(
-    below_ref, low_ref, high_ref, above_ref, mob_ref, beyond_ref, beside_ref,
-    keep_ref, xl_ref, xh_ref,
+    place_ref, below_ref, low_ref, high_ref, above_ref, mob_ref, beyond_ref, beside_ref,
+    keep_ref, xl_ref, xh_ref, xa_ref, xb_ref,
 ):
     lane = iota((8, LANES), 1)
     first = iota((8, LANES), 0) == 0
@@ -320,6 +324,17 @@
                 far = (far.astype(F32) + lines[1][place]).astype(BF16)
             for k, value in enumerate((below_ref[plane], near, high_ref[plane], far)):
                 ref[place, x % 8, pl.ds(8 * k, 8), :] = value
+    odd = place_ref[0] & 1
+
+    @pl.when(odd == 0)
+    def _():
+        xa_ref[...] = xl_ref[...]
+        xb_ref[...] = xh_ref[...]
+
+    @pl.when(odd == 1)
+    def _():
+        xa_ref[...] = xh_ref[...]
+        xb_ref[...] = xl_ref[...]
 
 
 def partner(x, step, axis):
@@ -532,7 +547,7 @@
     )
 
 
-def down_kernel(xm_ref, xp_ref, picks0_ref, picks1_ref, pick_middle_ref, *refs):
+def down_kernel(place_ref, xa_ref, xb_ref, picks0_ref, picks1_ref, pick_middle_ref, *refs):
     count = len(INNER)
     inner, refs = refs[:count], refs[count:]
     own_ref, chunk_ref, *outer = refs[: 2 + count]
@@ -541,12 +556,18 @@
         name: Joined(Inner(name, near), far) for name, near, far in zip(INNER, inner, outer)
     }
 
-    def parts_of(x):
-        ref = xm_ref if x < 8 else xp_ref
-        return [ref[place, x % 8].astype(F32) for place in range(5)]
-
     outside = list(range(8)) + list(range(24, 32))
-    assemble(outside, parts_of, a["mob"], a["v0"], a["side"])
+
+    def fill(xm_ref, xp_ref):
+        def parts_of(x):
+            ref = xm_ref if x < 8 else xp_ref
+            return [ref[place, x % 8].astype(F32) for place in range(5)]
+
+        assemble(outside, parts_of, a["mob"], a["v0"], a["side"])
+
+    odd = place_ref[0] & 1
+    pl.when(odd == 0)(lambda: fill(xa_ref, xb_ref))
+    pl.when(odd == 1)(lambda: fill(xb_ref, xa_ref))
     descend(
         a,
         [(2, 8), (23, 29)],
@@ -754,6 +775,14 @@
     sweep_planes(8, 23, vb, side_ref, kx_ref, ky_ref, kz_ref, 1, finish)
 
 
+def swap(x, axis, upper):
+    count = lax.axis_size(axis)
+    step = 1 if upper else -1
+    return lax.ppermute(
+        x, axis, [(i, (i + (step if i % 2 == 0 else -step)) % count) for i in range(count)]
+    )
+
+
 def shift(x, axis, direction):
     count = lax.axis_size(axis)
     return lax.ppermute(x, axis, [(i, (i + direction) % count) for i in range(count)])
@@ -763,16 +792,17 @@
     face = ((9, 16, LANES), BF16)
     zface = ((17, 16, LANES), BF16)
     brick = ((16, 16, LANES), F32)
-    conc, side, order, ids, xm, xp, ym = call(
+    place = jnp.stack([lax.axis_index("gx"), lax.axis_index("gy")]).astype(jnp.int32)
+    conc, side, order, ids, xa, xb, ym = call(
         faces_kernel,
         [brick, brick, ((8, 16, 16, LANES), BF16), ((1, 1, 8, 8), jnp.int32)] + [face] * 3,
-        (conc, right_side, order_field, grain_ids),
-        specs=[HBM] * 4,
+        (place, conc, right_side, order_field, grain_ids),
+        specs=[SMEM] + [HBM] * 4,
         semaphores=4,
     )
+    beside_b = swap(xb, "gx", True)
+    beside_a = swap(xa, "gx", False)
     above = shift(ym, "gy", -1)
-    before = shift(xp, "gx", 1)
-    after = shift(xm, "gx", -1)
     inner, yp, zm, zp = call(
         inner_kernel,
         [brick, ((8, 16, LANES), BF16), zface, zface],
@@ -784,7 +814,8 @@
     partial, beyond, send_zm, send_zp = call(
         outer_kernel,
         [brick, line, payload, payload],
-        (inner, conc, side, order, ids, before, after, above, yp, zm, zp),
+        (place, inner, conc, side, order, ids, beside_a, beside_b, above, yp, zm, zp),
+        specs=[SMEM] + [VMEM] * 11,
     )
     left = shift(send_zp, "gz", 1)
     right = shift(send_zm, "gz", -1)
@@ -796,13 +827,14 @@
     below = shift(high, "gy", 1)
     above = shift(low, "gy", -1)
     slab = ((5, 8, 32, LANES), BF16)
-    keep, xl, xh = call(
+    keep, xl, xh, xa, xb = call(
         rows_kernel,
-        [brick, slab, slab],
-        (below, low, high, above, keep, beyond, beside),
-    )
-    before = shift(xh, "gx", 1)
-    after = shift(xl, "gx", -1)
+        [brick, slab, slab, slab, slab],
+        (place, below, low, high, above, keep, beyond, beside),
+        specs=[SMEM] + [VMEM] * 7,
+    )
+    beside_b = swap(xb, "gx", True)
+    beside_a = swap(xa, "gx", False)
     fine = ((32, 32, RING), F32)
     middle = ((16, 32, RING), F32)
     *inner, mobility, picks0, picks1, pick_middle, spread = call(
@@ -817,12 +849,11 @@
     own, chunk, *outer = call(
         down_kernel,
         [((160, LANES), F32), ((32, CHUNK, LANES), BF16)] + outer[: len(KEPT)],
-        (before, after, picks0, picks1, pick_middle) + tuple(inner),
+        (place, beside_a, beside_b, picks0, picks1, pick_middle) + tuple(inner),
+        specs=[SMEM] + [VMEM] * (5 + len(inner)),
         scratch=outer[len(KEPT) :] + [middle] * 3 + [((320, LANES), F32)],
     )
     kept = tuple(inner[: len(KEPT)]) + tuple(outer)
-    place = jnp.stack([lax.axis_index("gx"), lax.axis_index("gy")]).astype(jnp.int32)
-    chunk, place = lax.optimization_barrier((chunk, place))
     chunks = lax.all_to_all(chunk, ("gx", "gy"), 0, 0, tiled=True)
     plane = ((32, 16, LANES), F32)
     (out,) = call(

time: 74.4 us -> 80.8 us (1.086)
  starting transfers between devices: 30 us -> 37 us
  waiting for transfers between devices: 8.79 us -> 5.8 us
  Pallas kernels: 14.8 us -> 17.7 us
    ppermute x0 -> x4, starting transfers between devices: none -> 16.8 us  [swap(): lax.ppermute(x, axis, [(i, (i + (step if i % 2 == 0 else -step)) % count)...]
    ppermute x9 -> x5, starting transfers between devices: 30 us -> 20.2 us  [shift(): lax.ppermute(x, axis, [(i, (i + direction) % count) for i in range(count)])]
    ppermute x9 -> x5, waiting for transfers between devices: 8.79 us -> 5.79 us  [shift(): lax.ppermute(x, axis, [(i, (i + direction) % count) for i in range(count)])]
    pallas_call x8, Pallas kernels: 14.8 us -> 17.7 us  [call(): pl.pallas_call(kernel, out_shape=[pltpu.MemorySpace.HBM(*out) if place is...]
  transfers between devices with their start and end apart: 9 -> 9, of which waited for: 6 -> 4; matrix products, arithmetic and copies ran while one was open for 0% -> 0% of each run, Pallas kernels for 7% -> 6%
where the time goes in v10:
time: 80.8 us; the launch traced here: 80.4 us
  starting transfers between devices  37 us (46%)
  blocking collectives  19.1 us (24%)
  Pallas kernels  17.7 us (22%)
  waiting for transfers between devices  5.8 us (7%)
    ppermute x5, starting transfers between devices, shift(): lax.ppermute(x, axis, [(i, (i + direction) % count) for i in range(count)])  20.2 us
    all_to_all x1, blocking collectives, body(): chunks = lax.all_to_all(chunk, ('gx', 'gy'), 0, 0, tiled=True)  19.1 us
    pallas_call x8, Pallas kernels, call(): pl.pallas_call(kernel, out_shape=[pltpu.MemorySpace.HBM(*out) if place is...  17.7 us
    ppermute x4, starting transfers between devices, swap(): lax.ppermute(x, axis, [(i, (i + (step if i % 2 == 0 else -step)) % count)...  16.8 us
    ppermute x5, waiting for transfers between devices, shift(): lax.ppermute(x, axis, [(i, (i + direction) % count) for i in range(count)])  5.79 us
  transfers between devices with their start and end apart: 9, of which 4 were waited for; matrix products, arithmetic and copies ran while one was open for 0% of the time, Pallas kernels for 6%

profile of v10, /device:TPU:1, one launch (start us, length us, event | category | flops | bytes accessed | tf_op | source)
XLA Modules:
  0.0 80.4 jit_solution(5453556234637539960)
XLA Ops:
  0.6 0.1 pad_add_fusion.place_ref
  0.7 1.9 %shard_map.59 = (f32[16,16,128]{2,1,0:T(8,128)S(1)}, f32[16,16,128]{2,1,0:T(8,128)S(1)}, bf16[8,16,16,128]{3,2,1,0:T(8,128)(2,1)S(1)}, s32[1,1,8,8]{3,2,1,0:T(8,...) custom-call(s32[2]{0:T(128)S(1)} %pad_add_fusion.place_ref, ...), custom_call_target="tpu_custom_call" | custom-call | tf_op jit(solution)/shard_map/pallas_call | solution.py:39
  2.6 4.6 %collective-permute-start = (bf16[9,16,128]{2,1,0:T(8,128)(2,1)S(1)}, bf16[9,16,128]{2,1,0:T(8,128)(2,1)S(1)}, u32[]{:S(2)}, u32[]{:S(2)}) collective-permute-start(bf16[9,16,128]{2,1,0:T(8,128)(2,1)S(1)} %get-tuple-element.64), channel_id=1, source_target_pairs={{0,448},{64,128},{128,64},{192,256},{256,192},{320,384},{384,320},... | collective-permute-start | bytes 110600 | tf_op jit(solution)/shard_map/ppermute | solution.py:781
  7.2 6.1 %collective-permute-start.1 = (bf16[9,16,128]{2,1,0:T(8,128)(2,1)S(1)}, bf16[9,16,128]{2,1,0:T(8,128)(2,1)S(1)}, u32[]{:S(2)}, u32[]{:S(2)}) collective-permute-start(bf16[9,16,128]{2,1,0:T(8,128)(2,1)S(1)} %get-tuple-element.65), channel_id=1, source_target_pairs={{0,64},{64,0},{128,192},{192,128},{256,320},{320,256},{384,448},{4... | collective-permute-start | bytes 110600 | tf_op jit(solution)/shard_map/ppermute | solution.py:781
  13.3 1.9 %collective-permute-start.2 = (bf16[9,16,128]{2,1,0:T(8,128)(2,1)S(1)}, bf16[9,16,128]{2,1,0:T(8,128)(2,1)S(1)}, u32[]{:S(2)}, u32[]{:S(2)}) collective-permute-start(bf16[9,16,128]{2,1,0:T(8,128)(2,1)S(1)} %get-tuple-element.66), channel_id=1, source_target_pairs={{0,48},{16,0},{32,16},{48,32},{1,49},{17,1},{33,17},{49,33},{2,50}... | collective-permute-start | bytes 110600 | tf_op jit(solution)/shard_map/ppermute | solution.py:788
  15.2 2.0 %shard_map.60 = (f32[16,16,128]{2,1,0:T(8,128)S(1)}, bf16[8,16,128]{2,1,0:T(8,128)(2,1)S(1)}, bf16[17,16,128]{2,1,0:T(8,128)(2,1)S(1)}, bf16[17,16,128]{2,1,0:T(8,128)(2,1)S(1)}) custom-call(f32[16,16,128]{2,1,0:T(8,128)S(1)} %get-tuple-element.59.conc_ref.conc_in, bf16[8,16,16,128]{3,2,1,0:T(8,128)(2,1)S(1)} %get-tuple-element.60.order_ref, ...), custom_call_target="tpu_custom_call" | custom-call | tf_op jit(solution)/shard_map/pallas_call | solution.py:39
  17.2 0.0 collective-permute-done.xa_ref
  17.2 0.0 collective-permute-done.1.xb_ref
  17.2 0.8 collective-permute-done.2.yp_ref
  18.0 1.0 %shard_map.61 = (f32[16,16,128]{2,1,0:T(8,128)S(1)}, f32[16,128]{1,0:T(8,128)S(1)}, bf16[34,16,128]{2,1,0:T(8,128)(2,1)S(1)}, bf16[34,16,128]{2,1,0:T(8,128)(2,1)S(1)}) custom-call(s32[2]{0:T(128)S(1)} %pad_add_fusion.place_ref, f32[16,16,128]{2,1,0:T(8,128)S(1)} %get-tuple-element.62.work, f32[16,16,128]{2,1,0:T(8,128)S(1)} %get-tuple-element.59.conc_ref.conc_in, ...), custom_call_target="tpu_custom_call" | custom-call | tf_op jit(solution)/shard_map/pallas_call | solution.py:39
  19.0 2.3 %collective-permute-start.3 = (bf16[34,16,128]{2,1,0:T(8,128)(2,1)S(1)}, bf16[34,16,128]{2,1,0:T(8,128)(2,1)S(1)}, u32[]{:S(2)}, u32[]{:S(2)}) collective-permute-start(bf16[34,16,128]{2,1,0:T(8,128)(2,1)S(1)} %get-tuple-element.72), channel_id=1, source_target_pairs={{0,1},{1,2},{2,3},{3,4},{4,5},{5,6},{6,7},{7,8},{8,9},{9,10},{10,1... | collective-permute-start | bytes 417800 | tf_op jit(solution)/shard_map/ppermute | solution.py:788
  21.3 9.5 %collective-permute-start.4 = (bf16[34,16,128]{2,1,0:T(8,128)(2,1)S(1)}, bf16[34,16,128]{2,1,0:T(8,128)(2,1)S(1)}, u32[]{:S(2)}, u32[]{:S(2)}) collective-permute-start(bf16[34,16,128]{2,1,0:T(8,128)(2,1)S(1)} %get-tuple-element.73), channel_id=1, source_target_pairs={{0,15},{1,0},{2,1},{3,2},{4,3},{5,4},{6,5},{7,6},{8,7},{9,8},{10,9... | collective-permute-start | bytes 417800 | tf_op jit(solution)/shard_map/ppermute | solution.py:788
  30.8 1.9 %collective-permute-done.3.left_ref = bf16[34,16,128]{2,1,0:T(8,128)(2,1)S(1)} collective-permute-done((bf16[34,16,128]{2,1,0:T(8,128)(2,1)S(1)}, bf16[34,16,128]{2,1,0:T(8,128)(2,1)S(1)}, u32[]{:S(2)}, u32[]{:S(2)}) %collective-permute-start.3) | collective-permute-done | bytes 139296 | tf_op jit(solution)/shard_map/ppermute | solution.py:788
  32.7 0.9 %collective-permute-done.4.right_ref = bf16[34,16,128]{2,1,0:T(8,128)(2,1)S(1)} collective-permute-done((bf16[34,16,128]{2,1,0:T(8,128)(2,1)S(1)}, bf16[34,16,128]{2,1,0:T(8,128)(2,1)S(1)}, u32[]{:S(2)}, u32[]{:S(2)}) %collective-permute-start.4) | collective-permute-done | bytes 139296 | tf_op jit(solution)/shard_map/ppermute | solution.py:788
  33.6 0.6 shard_map.62
  34.2 1.9 %collective-permute-start.5 = (bf16[86,8,128]{2,1,0:T(8,128)(2,1)S(1)}, bf16[86,8,128]{2,1,0:T(8,128)(2,1)S(1)}, u32[]{:S(2)}, u32[]{:S(2)}) collective-permute-start(bf16[86,8,128]{2,1,0:T(8,128)(2,1)S(1)} %get-tuple-element.74.high_ref), channel_id=1, source_target_pairs={{0,16},{16,32},{32,48},{48,0},{1,17},{17,33},{33,49},{49,1},{2,18}... | collective-permute-start | bytes 528392 | tf_op jit(solution)/shard_map/ppermute | solution.py:788
  36.2 4.6 %collective-permute-start.6 = (bf16[80,8,128]{2,1,0:T(8,128)(2,1)S(1)}, bf16[80,8,128]{2,1,0:T(8,128)(2,1)S(1)}, u32[]{:S(2)}, u32[]{:S(2)}) collective-permute-start(bf16[80,8,128]{2,1,0:T(8,128)(2,1)S(1)} %get-tuple-element.75.low_ref), channel_id=1, source_target_pairs={{0,48},{16,0},{32,16},{48,32},{1,49},{17,1},{33,17},{49,33},{2,50}... | collective-permute-start | bytes 491528 | tf_op jit(solution)/shard_map/ppermute | solution.py:788
  40.7 2.2 %collective-permute-done.6.above_ref = bf16[80,8,128]{2,1,0:T(8,128)(2,1)S(1)} collective-permute-done((bf16[80,8,128]{2,1,0:T(8,128)(2,1)S(1)}, bf16[80,8,128]{2,1,0:T(8,128)(2,1)S(1)}, u32[]{:S(2)}, u32[]{:S(2)}) %collective-permute-start.6) | collective-permute-done | bytes 163872 | tf_op jit(solution)/shard_map/ppermute | solution.py:788
  43.0 0.0 collective-permute-done.5.below_ref
  43.0 0.7 shard_map.63
  43.7 4.1 %collective-permute-start.7 = (bf16[5,8,32,128]{3,2,1,0:T(8,128)(2,1)S(1)}, bf16[5,8,32,128]{3,2,1,0:T(8,128)(2,1)S(1)}, u32[]{:S(2)}, u32[]{:S(2)}) collective-permute-start(bf16[5,8,32,128]{3,2,1,0:T(8,128)(2,1)S(1)} %get-tuple-element.78), channel_id=1, source_target_pairs={{0,448},{64,128},{128,64},{192,256},{256,192},{320,384},{384,320},... | collective-permute-start | bytes 983048 | tf_op jit(solution)/shard_map/ppermute | solution.py:781
  47.8 2.0 %collective-permute-start.8 = (bf16[5,8,32,128]{3,2,1,0:T(8,128)(2,1)S(1)}, bf16[5,8,32,128]{3,2,1,0:T(8,128)(2,1)S(1)}, u32[]{:S(2)}, u32[]{:S(2)}) collective-permute-start(bf16[5,8,32,128]{3,2,1,0:T(8,128)(2,1)S(1)} %get-tuple-element.79), channel_id=1, source_target_pairs={{0,64},{64,0},{128,192},{192,128},{256,320},{320,256},{384,448},{4... | collective-permute-start | bytes 983048 | tf_op jit(solution)/shard_map/ppermute | solution.py:781
  49.8 3.1 %shard_map.64 = (f32[16,32,256]{2,1,0:T(8,128)S(1)}, f32[15,32,256]{2,1,0:T(8,128)S(1)}, f32[14,32,256]{2,1,0:T(8,128)S(1)}, f32[14,32,256]{2,1,0:T(8,128)S(1)},...) custom-call(f32[16,16,128]{2,1,0:T(8,128)S(1)} %get-tuple-element.80, ...), custom_call_target="tpu_custom_call" | custom-call | tf_op jit(solution)/shard_map/pallas_call | solution.py:39
  53.0 0.0 collective-permute-done.7.xa_ref
  53.0 0.0 collective-permute-done.8.xb_ref
  53.0 4.3 %shard_map.65 = (f32[160,128]{1,0:T(8,128)S(1)}, bf16[32,64,128]{2,1,0:T(8,128)(2,1)S(1)}, f32[32,32,256]{2,1,0:T(8,128)S(1)}, f32[32,32,256]{2,1,0:T(8,128)S(1)...) custom-call(s32[2]{0:T(128)S(1)} %pad_add_fusion.place_ref, ...), custom_call_target="tpu_custom_call" | custom-call | tf_op jit(solution)/shard_map/pallas_call | solution.py:39
  57.3 19.1 %all_to_all.5.all_ref = bf16[32,64,128]{2,1,0:T(8,128)(2,1)S(1)} all-to-all(bf16[32,64,128]{2,1,0:T(8,128)(2,1)S(1)} %get-tuple-element.101), channel_id=1, replica_groups=mesh['gx'=8,'gy'=4,'gz'=16] {'gx','gy'}, dimensions={0} | all-to-all | bytes 1048576 | tf_op jit(solution)/shard_map/all_to_all | solution.py:857
  76.4 4.0 %shard_map.66 = f32[16,16,128]{2,1,0:T(8,128)} custom-call(s32[2]{0:T(128)S(1)} %pad_add_fusion.place_ref, bf16[32,64,128]{2,1,0:T(8,128)(2,1)S(1)} %all_to_all.5.all_ref, f32[160,128]{1,0:T(8,128)S(1)} %get-tuple-element.102.own_ref, bf16[128,256]{1,0:T(8,128)(2,1)S(1)} %get-tuple-element.103.spread_ref, f32[16,32,256]{2,1,0:T(8,128)S(1)} %get-tuple-element.86.refs_0_, ...), custom_call_target="tpu_custom_call" | custom-call | tf_op jit(solution)/shard_map/pallas_call | solution.py:39
Async XLA Ops:
  2.6 14.6 %collective-permute-start = (bf16[9,16,128]{2,1,0:T(8,128)(2,1)S(1)}, bf16[9,16,128]{2,1,0:T(8,128)(2,1)S(1)}, u32[]{:S(2)}, u32[]{:S(2)}) collective-permute-start(bf16[9,16,128]{2,1,0:T(8,128)(2,1)S(1)} %get-tuple-element.64), channel_id=1, source_target_pairs={{0,448},{64,128},{128,64},{192,256},{256,192},{320,384},{384,320},... | collective-permute-start | bytes 110600 | tf_op jit(solution)/shard_map/ppermute | solution.py:781
  7.2 10.0 %collective-permute-start.1 = (bf16[9,16,128]{2,1,0:T(8,128)(2,1)S(1)}, bf16[9,16,128]{2,1,0:T(8,128)(2,1)S(1)}, u32[]{:S(2)}, u32[]{:S(2)}) collective-permute-start(bf16[9,16,128]{2,1,0:T(8,128)(2,1)S(1)} %get-tuple-element.65), channel_id=1, source_target_pairs={{0,64},{64,0},{128,192},{192,128},{256,320},{320,256},{384,448},{4... | collective-permute-start | bytes 110600 | tf_op jit(solution)/shard_map/ppermute | solution.py:781
  13.3 4.7 %collective-permute-start.2 = (bf16[9,16,128]{2,1,0:T(8,128)(2,1)S(1)}, bf16[9,16,128]{2,1,0:T(8,128)(2,1)S(1)}, u32[]{:S(2)}, u32[]{:S(2)}) collective-permute-start(bf16[9,16,128]{2,1,0:T(8,128)(2,1)S(1)} %get-tuple-element.66), channel_id=1, source_target_pairs={{0,48},{16,0},{32,16},{48,32},{1,49},{17,1},{33,17},{49,33},{2,50}... | collective-permute-start | bytes 110600 | tf_op jit(solution)/shard_map/ppermute | solution.py:788
  19.0 13.7 %collective-permute-start.3 = (bf16[34,16,128]{2,1,0:T(8,128)(2,1)S(1)}, bf16[34,16,128]{2,1,0:T(8,128)(2,1)S(1)}, u32[]{:S(2)}, u32[]{:S(2)}) collective-permute-start(bf16[34,16,128]{2,1,0:T(8,128)(2,1)S(1)} %get-tuple-element.72), channel_id=1, source_target_pairs={{0,1},{1,2},{2,3},{3,4},{4,5},{5,6},{6,7},{7,8},{8,9},{9,10},{10,1... | collective-permute-start | bytes 417800 | tf_op jit(solution)/shard_map/ppermute | solution.py:788
  21.3 12.3 %collective-permute-start.4 = (bf16[34,16,128]{2,1,0:T(8,128)(2,1)S(1)}, bf16[34,16,128]{2,1,0:T(8,128)(2,1)S(1)}, u32[]{:S(2)}, u32[]{:S(2)}) collective-permute-start(bf16[34,16,128]{2,1,0:T(8,128)(2,1)S(1)} %get-tuple-element.73), channel_id=1, source_target_pairs={{0,15},{1,0},{2,1},{3,2},{4,3},{5,4},{6,5},{7,6},{8,7},{9,8},{10,9... | collective-permute-start | bytes 417800 | tf_op jit(solution)/shard_map/ppermute | solution.py:788
  34.2 8.8 %collective-permute-start.5 = (bf16[86,8,128]{2,1,0:T(8,128)(2,1)S(1)}, bf16[86,8,128]{2,1,0:T(8,128)(2,1)S(1)}, u32[]{:S(2)}, u32[]{:S(2)}) collective-permute-start(bf16[86,8,128]{2,1,0:T(8,128)(2,1)S(1)} %get-tuple-element.74.high_ref), channel_id=1, source_target_pairs={{0,16},{16,32},{32,48},{48,0},{1,17},{17,33},{33,49},{49,1},{2,18}... | collective-permute-start | bytes 528392 | tf_op jit(solution)/shard_map/ppermute | solution.py:788
  36.2 6.8 %collective-permute-start.6 = (bf16[80,8,128]{2,1,0:T(8,128)(2,1)S(1)}, bf16[80,8,128]{2,1,0:T(8,128)(2,1)S(1)}, u32[]{:S(2)}, u32[]{:S(2)}) collective-permute-start(bf16[80,8,128]{2,1,0:T(8,128)(2,1)S(1)} %get-tuple-element.75.low_ref), channel_id=1, source_target_pairs={{0,48},{16,0},{32,16},{48,32},{1,49},{17,1},{33,17},{49,33},{2,50}... | collective-permute-start | bytes 491528 | tf_op jit(solution)/shard_map/ppermute | solution.py:788
  43.7 9.2 %collective-permute-start.7 = (bf16[5,8,32,128]{3,2,1,0:T(8,128)(2,1)S(1)}, bf16[5,8,32,128]{3,2,1,0:T(8,128)(2,1)S(1)}, u32[]{:S(2)}, u32[]{:S(2)}) collective-permute-start(bf16[5,8,32,128]{3,2,1,0:T(8,128)(2,1)S(1)} %get-tuple-element.78), channel_id=1, source_target_pairs={{0,448},{64,128},{128,64},{192,256},{256,192},{320,384},{384,320},... | collective-permute-start | bytes 983048 | tf_op jit(solution)/shard_map/ppermute | solution.py:781
  47.8 5.2 %collective-permute-start.8 = (bf16[5,8,32,128]{3,2,1,0:T(8,128)(2,1)S(1)}, bf16[5,8,32,128]{3,2,1,0:T(8,128)(2,1)S(1)}, u32[]{:S(2)}, u32[]{:S(2)}) collective-permute-start(bf16[5,8,32,128]{3,2,1,0:T(8,128)(2,1)S(1)} %get-tuple-element.79), channel_id=1, source_target_pairs={{0,64},{64,0},{128,192},{192,128},{256,320},{320,256},{384,448},{4... | collective-permute-start | bytes 983048 | tf_op jit(solution)/shard_map/ppermute | solution.py:781

commit v11 on v9

--- a/solution.py
+++ b/solution.py
@@ -89,7 +89,7 @@
 
 def faces_kernel(
     conc_in, side_in, order_in, ids_in,
-    conc_ref, side_ref, order_ref, ids_ref, xm_ref, xp_ref, ym_ref, sems,
+    conc_ref, side_ref, order_ref, ids_ref, ym_ref, sems,
 ):
     pairs = (
         (ids_in, ids_ref), (order_in, order_ref), (conc_in, conc_ref), (side_in, side_ref),
@@ -101,11 +101,8 @@
     copies[1].wait()
     grains = lane_ids(ids_ref)
     packed = split_ids(grains)
-    for ref in (xm_ref, xp_ref, ym_ref):
-        ref[SLOTS] = packed
+    ym_ref[SLOTS] = packed
     for slot in range(SLOTS):
-        xm_ref[slot] = order_ref[slot, 0]
-        xp_ref[slot] = order_ref[slot, 15]
         ym_ref[slot] = order_ref[slot].astype(F32)[:, 0, :].astype(BF16)
     copies[2].wait()
     copies[3].wait()
@@ -113,6 +110,13 @@
 
 def square(x):
     return x * x
+
+
+def sides_kernel(order_ref, ym_ref, xm_ref, xp_ref):
+    for x, ref in ((0, xm_ref), (15, xp_ref)):
+        ref[SLOTS] = ym_ref[SLOTS]
+        for slot in range(SLOTS):
+            ref[slot] = order_ref[slot, x]
 
 
 def inner_kernel(
@@ -188,37 +192,43 @@
     for x in range(16):
         carry = plane(x, carry)
 
+def across(center, ids, facing, facing_ids):
+    facing = [facing(other).astype(F32) for other in range(SLOTS)]
+    total = None
+    for slot in range(SLOTS):
+        value = None
+        for other in range(SLOTS):
+            match = ids[slot : slot + 1] == facing_ids[other : other + 1]
+            term = match.astype(F32) * facing[other]
+            value = term if value is None else value + term
+        part = square(value - center(slot).astype(F32))
+        total = part if total is None else total + part
+    return total
+
+
+def upper_kernel(ids_ref, yp_ref, own_yp_ref, top_ref, beyond_ref):
+    own = lane_ids(ids_ref)
+    above_ids = join_ids(yp_ref[SLOTS])
+    top_ref[...] = across(lambda k: own_yp_ref[k], own, lambda k: yp_ref[k], above_ids)
+    beyond_ref[...] = across(lambda k: yp_ref[k], above_ids, lambda k: own_yp_ref[k], own)
+
+
 def outer_kernel(
-    work, conc_ref, side_ref, order_ref, ids_ref, xm_ref, xp_ref, yp_ref,
-    own_yp_ref, own_zm_ref, own_zp_ref, mob_ref, beyond_ref, zm_out, zp_out,
+    work, conc_ref, side_ref, order_ref, ids_ref, xm_ref, xp_ref, top_ref, beyond_ref,
+    own_zm_ref, own_zp_ref, mob_ref, zm_out, zp_out,
 ):
     own = lane_ids(ids_ref)
     lane = iota((16, LANES), 1)
     row = iota((16, LANES), 0)
 
-    def across(center, ids, facing, facing_ids):
-        facing = [facing(other).astype(F32) for other in range(SLOTS)]
-        total = None
-        for slot in range(SLOTS):
-            value = None
-            for other in range(SLOTS):
-                match = ids[slot : slot + 1] == facing_ids[other : other + 1]
-                term = match.astype(F32) * facing[other]
-                value = term if value is None else value + term
-            part = square(value - center(slot).astype(F32))
-            total = part if total is None else total + part
-        return total
-
     first = work[0] + across(
         lambda k: order_ref[k, 0], own, lambda k: xm_ref[k], join_ids(xm_ref[SLOTS])
     )
     final = work[15] + across(
         lambda k: order_ref[k, 15], own, lambda k: xp_ref[k], join_ids(xp_ref[SLOTS])
     )
-    above_ids = join_ids(yp_ref[SLOTS])
-    top = across(lambda k: own_yp_ref[k], own, lambda k: yp_ref[k], above_ids)
-    beyond = across(lambda k: yp_ref[k], above_ids, lambda k: own_yp_ref[k], own)
-    beyond_ref[...] = beyond
+    top = top_ref[...]
+    beyond = beyond_ref[...]
     zm_out[33] = beyond.astype(BF16)
     zp_out[33] = beyond.astype(BF16)
     for x in range(16):
@@ -763,14 +773,15 @@
     face = ((9, 16, LANES), BF16)
     zface = ((17, 16, LANES), BF16)
     brick = ((16, 16, LANES), F32)
-    conc, side, order, ids, xm, xp, ym = call(
+    conc, side, order, ids, ym = call(
         faces_kernel,
-        [brick, brick, ((8, 16, 16, LANES), BF16), ((1, 1, 8, 8), jnp.int32)] + [face] * 3,
+        [brick, brick, ((8, 16, 16, LANES), BF16), ((1, 1, 8, 8), jnp.int32), face],
         (conc, right_side, order_field, grain_ids),
         specs=[HBM] * 4,
         semaphores=4,
     )
     above = shift(ym, "gy", -1)
+    xm, xp = call(sides_kernel, [face, face], (order, ym))
     before = shift(xp, "gx", 1)
     after = shift(xm, "gx", -1)
     inner, yp, zm, zp = call(
@@ -781,10 +792,11 @@
     )
     line = ((16, LANES), F32)
     payload = ((34, 16, LANES), BF16)
-    partial, beyond, send_zm, send_zp = call(
+    top, beyond = call(upper_kernel, [line, line], (ids, above, yp))
+    partial, send_zm, send_zp = call(
         outer_kernel,
-        [brick, line, payload, payload],
-        (inner, conc, side, order, ids, before, after, above, yp, zm, zp),
+        [brick, payload, payload],
+        (inner, conc, side, order, ids, before, after, top, beyond, zm, zp),
     )
     left = shift(send_zp, "gz", 1)
     right = shift(send_zm, "gz", -1)

time: 74.4 us -> 75.1 us (level)
  starting transfers between devices: 30 us -> 32.5 us
  blocking collectives: 19.7 us -> 18.5 us
  waiting for transfers between devices: 8.79 us -> 7.98 us
    ppermute x9, starting transfers between devices: 30 us -> 32.5 us  [shift(): lax.ppermute(x, axis, [(i, (i + direction) % count) for i in range(count)])]
    all_to_all x1, blocking collectives: 19.7 us -> 18.5 us  [body(): chunks = lax.all_to_all(chunk, ('gx', 'gy'), 0, 0, tiled=True)]
    ppermute x9, waiting for transfers between devices: 8.79 us -> 7.98 us  [shift(): lax.ppermute(x, axis, [(i, (i + direction) % count) for i in range(count)])]
    pallas_call x8 -> x10, Pallas kernels: 14.8 us -> 15 us  [call(): pl.pallas_call(kernel, out_shape=[pltpu.MemorySpace.HBM(*out) if place is...]
  transfers between devices with their start and end apart: 9 -> 9, of which waited for: 6 -> 5; matrix products, arithmetic and copies ran while one was open for 0% -> 0% of each run, Pallas kernels for 7% -> 7%
where the time goes in v11:
time: 75.1 us; the launch traced here: 74.8 us
  starting transfers between devices  32.5 us (43%)
  blocking collectives  18.5 us (25%)
  Pallas kernels  15 us (20%)
  waiting for transfers between devices  7.98 us (11%)
    ppermute x9, starting transfers between devices, shift(): lax.ppermute(x, axis, [(i, (i + direction) % count) for i in range(count)])  32.5 us
    all_to_all x1, blocking collectives, body(): chunks = lax.all_to_all(chunk, ('gx', 'gy'), 0, 0, tiled=True)  18.5 us
    pallas_call x10, Pallas kernels, call(): pl.pallas_call(kernel, out_shape=[pltpu.MemorySpace.HBM(*out) if place is...  15 us
    ppermute x9, waiting for transfers between devices, shift(): lax.ppermute(x, axis, [(i, (i + direction) % count) for i in range(count)])  7.98 us
  transfers between devices with their start and end apart: 9, of which 5 were waited for; matrix products, arithmetic and copies ran while one was open for 0% of the time, Pallas kernels for 7%

profile of v11, /device:TPU:1, one launch (start us, length us, event | category | flops | bytes accessed | tf_op | source)
XLA Modules:
  0.0 74.8 jit_solution(7955011058884645835)
XLA Ops:
  0.6 1.3 %shard_map.59 = (f32[16,16,128]{2,1,0:T(8,128)S(1)}, f32[16,16,128]{2,1,0:T(8,128)S(1)}, bf16[8,16,16,128]{3,2,1,0:T(8,128)(2,1)S(1)}, s32[1,1,8,8]{3,2,1,0:T(8,128)S(1)}, bf16[9,16,128]{2,1,0:T(8,128)(2,1)S(1)}) custom-call(f32[16,16,128]{2,1,0:T(8,128)} %conc_in.1, f32[16,16,128]{2,1,0:T(8,128)} %side_in.1, bf16[8,16,16,128]{3,2,1,0:T(8,128)(2,1)} %order_in.1, ...), custom_call_target="tpu_custom_call" | custom-call | tf_op jit(solution)/shard_map/pallas_call | solution.py:39
  1.9 5.2 %collective-permute-start.2 = (bf16[9,16,128]{2,1,0:T(8,128)(2,1)S(1)}, bf16[9,16,128]{2,1,0:T(8,128)(2,1)S(1)}, u32[]{:S(2)}, u32[]{:S(2)}) collective-permute-start(bf16[9,16,128]{2,1,0:T(8,128)(2,1)S(1)} %get-tuple-element.65.ym_ref), channel_id=1, source_target_pairs={{0,48},{16,0},{32,16},{48,32},{1,49},{17,1},{33,17},{49,33},{2,50}... | collective-permute-start | bytes 110600 | tf_op jit(solution)/shard_map/ppermute | solution.py:769
  7.2 2.1 %collective-permute-start = (bf16[9,16,128]{2,1,0:T(8,128)(2,1)S(1)}, bf16[9,16,128]{2,1,0:T(8,128)(2,1)S(1)}, u32[]{:S(2)}, u32[]{:S(2)}) collective-permute-start(bf16[9,16,128]{2,1,0:T(8,128)(2,1)S(1)} %get-tuple-element.66), channel_id=1, source_target_pairs={{0,64},{64,128},{128,192},{192,256},{256,320},{320,384},{384,448},... | collective-permute-start | bytes 110600 | tf_op jit(solution)/shard_map/ppermute | solution.py:769
  9.3 1.5 %collective-permute-start.1 = (bf16[9,16,128]{2,1,0:T(8,128)(2,1)S(1)}, bf16[9,16,128]{2,1,0:T(8,128)(2,1)S(1)}, u32[]{:S(2)}, u32[]{:S(2)}) collective-permute-start(bf16[9,16,128]{2,1,0:T(8,128)(2,1)S(1)} %get-tuple-element.67), channel_id=1, source_target_pairs={{0,448},{64,0},{128,64},{192,128},{256,192},{320,256},{384,320},{4... | collective-permute-start | bytes 110600 | tf_op jit(solution)/shard_map/ppermute | solution.py:769
  10.8 2.0 %shard_map.60 = (f32[16,16,128]{2,1,0:T(8,128)S(1)}, bf16[8,16,128]{2,1,0:T(8,128)(2,1)S(1)}, bf16[17,16,128]{2,1,0:T(8,128)(2,1)S(1)}, bf16[17,16,128]{2,1,0:T(8,128)(2,1)S(1)}) custom-call(f32[16,16,128]{2,1,0:T(8,128)S(1)} %get-tuple-element.60.conc_ref.conc_in, bf16[8,16,16,128]{3,2,1,0:T(8,128)(2,1)S(1)} %get-tuple-element.61.order_ref, ...), custom_call_target="tpu_custom_call" | custom-call | tf_op jit(solution)/shard_map/pallas_call | solution.py:39
  12.8 0.0 collective-permute-done.2.yp_ref
  12.8 0.3 shard_map.62
  13.1 0.0 collective-permute-done.xm_ref
  13.1 0.0 collective-permute-done.1.xp_ref
  13.1 0.3 shard_map.63
  13.4 3.2 %collective-permute-start.3 = (bf16[34,16,128]{2,1,0:T(8,128)(2,1)S(1)}, bf16[34,16,128]{2,1,0:T(8,128)(2,1)S(1)}, u32[]{:S(2)}, u32[]{:S(2)}) collective-permute-start(bf16[34,16,128]{2,1,0:T(8,128)(2,1)S(1)} %get-tuple-element.74), channel_id=1, source_target_pairs={{0,1},{1,2},{2,3},{3,4},{4,5},{5,6},{6,7},{7,8},{8,9},{9,10},{10,1... | collective-permute-start | bytes 417800 | tf_op jit(solution)/shard_map/ppermute | solution.py:769
  16.6 9.5 %collective-permute-start.4 = (bf16[34,16,128]{2,1,0:T(8,128)(2,1)S(1)}, bf16[34,16,128]{2,1,0:T(8,128)(2,1)S(1)}, u32[]{:S(2)}, u32[]{:S(2)}) collective-permute-start(bf16[34,16,128]{2,1,0:T(8,128)(2,1)S(1)} %get-tuple-element.75), channel_id=1, source_target_pairs={{0,15},{1,0},{2,1},{3,2},{4,3},{5,4},{6,5},{7,6},{8,7},{9,8},{10,9... | collective-permute-start | bytes 417800 | tf_op jit(solution)/shard_map/ppermute | solution.py:769
  26.1 1.4 %collective-permute-done.3.left_ref = bf16[34,16,128]{2,1,0:T(8,128)(2,1)S(1)} collective-permute-done((bf16[34,16,128]{2,1,0:T(8,128)(2,1)S(1)}, bf16[34,16,128]{2,1,0:T(8,128)(2,1)S(1)}, u32[]{:S(2)}, u32[]{:S(2)}) %collective-permute-start.3) | collective-permute-done | bytes 139296 | tf_op jit(solution)/shard_map/ppermute | solution.py:769
  27.5 0.9 %collective-permute-done.4.right_ref = bf16[34,16,128]{2,1,0:T(8,128)(2,1)S(1)} collective-permute-done((bf16[34,16,128]{2,1,0:T(8,128)(2,1)S(1)}, bf16[34,16,128]{2,1,0:T(8,128)(2,1)S(1)}, u32[]{:S(2)}, u32[]{:S(2)}) %collective-permute-start.4) | collective-permute-done | bytes 139296 | tf_op jit(solution)/shard_map/ppermute | solution.py:769
  28.4 0.6 shard_map.64
  29.1 1.9 %collective-permute-start.5 = (bf16[86,8,128]{2,1,0:T(8,128)(2,1)S(1)}, bf16[86,8,128]{2,1,0:T(8,128)(2,1)S(1)}, u32[]{:S(2)}, u32[]{:S(2)}) collective-permute-start(bf16[86,8,128]{2,1,0:T(8,128)(2,1)S(1)} %get-tuple-element.76.high_ref), channel_id=1, source_target_pairs={{0,16},{16,32},{32,48},{48,0},{1,17},{17,33},{33,49},{49,1},{2,18}... | collective-permute-start | bytes 528392 | tf_op jit(solution)/shard_map/ppermute | solution.py:769
  31.0 4.6 %collective-permute-start.6 = (bf16[80,8,128]{2,1,0:T(8,128)(2,1)S(1)}, bf16[80,8,128]{2,1,0:T(8,128)(2,1)S(1)}, u32[]{:S(2)}, u32[]{:S(2)}) collective-permute-start(bf16[80,8,128]{2,1,0:T(8,128)(2,1)S(1)} %get-tuple-element.77.low_ref), channel_id=1, source_target_pairs={{0,48},{16,0},{32,16},{48,32},{1,49},{17,1},{33,17},{49,33},{2,50}... | collective-permute-start | bytes 491528 | tf_op jit(solution)/shard_map/ppermute | solution.py:769
  35.6 2.2 %collective-permute-done.6.above_ref = bf16[80,8,128]{2,1,0:T(8,128)(2,1)S(1)} collective-permute-done((bf16[80,8,128]{2,1,0:T(8,128)(2,1)S(1)}, bf16[80,8,128]{2,1,0:T(8,128)(2,1)S(1)}, u32[]{:S(2)}, u32[]{:S(2)}) %collective-permute-start.6) | collective-permute-done | bytes 163872 | tf_op jit(solution)/shard_map/ppermute | solution.py:769
  37.8 0.0 collective-permute-done.5.below_ref
  37.8 0.1 shard_map.65
  37.9 4.5 %collective-permute-start.7 = (bf16[5,8,32,128]{3,2,1,0:T(8,128)(2,1)S(1)}, bf16[5,8,32,128]{3,2,1,0:T(8,128)(2,1)S(1)}, u32[]{:S(2)}, u32[]{:S(2)}) collective-permute-start(bf16[5,8,32,128]{3,2,1,0:T(8,128)(2,1)S(1)} %get-tuple-element.80.xh_ref), channel_id=1, source_target_pairs={{0,64},{64,128},{128,192},{192,256},{256,320},{320,384},{384,448},... | collective-permute-start | bytes 983048 | tf_op jit(solution)/shard_map/ppermute | solution.py:769
  42.5 0.0 collective-permute-start.8
  42.5 0.1 pad_add_fusion.place_ref
  42.5 3.0 %shard_map.66 = (f32[16,32,256]{2,1,0:T(8,128)S(1)}, f32[15,32,256]{2,1,0:T(8,128)S(1)}, f32[14,32,256]{2,1,0:T(8,128)S(1)}, f32[14,32,256]{2,1,0:T(8,128)S(1)},...) custom-call(f32[16,16,128]{2,1,0:T(8,128)S(1)} %get-tuple-element.82, ...), custom_call_target="tpu_custom_call" | custom-call | tf_op jit(solution)/shard_map/pallas_call | solution.py:39
  45.5 1.0 %collective-permute-done.7.xm_ref = bf16[5,8,32,128]{3,2,1,0:T(8,128)(2,1)S(1)} collective-permute-done((bf16[5,8,32,128]{3,2,1,0:T(8,128)(2,1)S(1)}, bf16[5,8,32,128]{3,2,1,0:T(8,128)(2,1)S(1)}, u32[]{:S(2)}, u32[]{:S(2)}) %collective-permute-start.7) | collective-permute-done | bytes 327712 | tf_op jit(solution)/shard_map/ppermute | solution.py:769
  46.5 2.5 %collective-permute-done.8.xp_ref = bf16[5,8,32,128]{3,2,1,0:T(8,128)(2,1)S(1)} collective-permute-done((bf16[5,8,32,128]{3,2,1,0:T(8,128)(2,1)S(1)}, bf16[5,8,32,128]{3,2,1,0:T(8,128)(2,1)S(1)}, u32[]{:S(2)}, u32[]{:S(2)}) %collective-permute-start.8) | collective-permute-done | bytes 327712 | tf_op jit(solution)/shard_map/ppermute | solution.py:769
  49.0 3.5 %shard_map.67 = (f32[160,128]{1,0:T(8,128)S(1)}, bf16[32,64,128]{2,1,0:T(8,128)(2,1)S(1)}, f32[32,32,256]{2,1,0:T(8,128)S(1)}, f32[32,32,256]{2,1,0:T(8,128)S(1)...) custom-call(bf16[5,8,32,128]{3,2,1,0:T(8,128)(2,1)S(1)} %collective-, ...), custom_call_target="tpu_custom_call" | custom-call | tf_op jit(solution)/shard_map/pallas_call | solution.py:39
  52.4 18.5 %all_to_all.5.all_ref = bf16[32,64,128]{2,1,0:T(8,128)(2,1)S(1)} all-to-all(bf16[32,64,128]{2,1,0:T(8,128)(2,1)S(1)} %get-tuple-element.103), channel_id=1, replica_groups=mesh['gx'=8,'gy'=4,'gz'=16] {'gx','gy'}, dimensions={0} | all-to-all | bytes 1048576 | tf_op jit(solution)/shard_map/all_to_all | solution.py:838
  71.0 3.9 %shard_map.68 = f32[16,16,128]{2,1,0:T(8,128)} custom-call(s32[2]{0:T(128)S(1)} %pad_add_fusion.place_ref, bf16[32,64,128]{2,1,0:T(8,128)(2,1)S(1)} %all_to_all.5.all_ref, f32[160,128]{1,0:T(8,128)S(1)} %get-tuple-element.104.own_ref, bf16[128,256]{1,0:T(8,128)(2,1)S(1)} %get-tuple-element.105.spread_ref, f32[16,32,256]{2,1,0:T(8,128)S(1)} %get-tuple-element.86.refs_0_, ...), custom_call_target="tpu_custom_call" | custom-call | tf_op jit(solution)/shard_map/pallas_call | solution.py:39
  (1 shorter events, 0.0 us)
Async XLA Ops:
  1.9 10.8 %collective-permute-start.2 = (bf16[9,16,128]{2,1,0:T(8,128)(2,1)S(1)}, bf16[9,16,128]{2,1,0:T(8,128)(2,1)S(1)}, u32[]{:S(2)}, u32[]{:S(2)}) collective-permute-start(bf16[9,16,128]{2,1,0:T(8,128)(2,1)S(1)} %get-tuple-element.65.ym_ref), channel_id=1, source_target_pairs={{0,48},{16,0},{32,16},{48,32},{1,49},{17,1},{33,17},{49,33},{2,50}... | collective-permute-start | bytes 110600 | tf_op jit(solution)/shard_map/ppermute | solution.py:769
  7.2 5.9 %collective-permute-start = (bf16[9,16,128]{2,1,0:T(8,128)(2,1)S(1)}, bf16[9,16,128]{2,1,0:T(8,128)(2,1)S(1)}, u32[]{:S(2)}, u32[]{:S(2)}) collective-permute-start(bf16[9,16,128]{2,1,0:T(8,128)(2,1)S(1)} %get-tuple-element.66), channel_id=1, source_target_pairs={{0,64},{64,128},{128,192},{192,256},{256,320},{320,384},{384,448},... | collective-permute-start | bytes 110600 | tf_op jit(solution)/shard_map/ppermute | solution.py:769
  9.3 3.8 %collective-permute-start.1 = (bf16[9,16,128]{2,1,0:T(8,128)(2,1)S(1)}, bf16[9,16,128]{2,1,0:T(8,128)(2,1)S(1)}, u32[]{:S(2)}, u32[]{:S(2)}) collective-permute-start(bf16[9,16,128]{2,1,0:T(8,128)(2,1)S(1)} %get-tuple-element.67), channel_id=1, source_target_pairs={{0,448},{64,0},{128,64},{192,128},{256,192},{320,256},{384,320},{4... | collective-permute-start | bytes 110600 | tf_op jit(solution)/shard_map/ppermute | solution.py:769
  13.4 14.1 %collective-permute-start.3 = (bf16[34,16,128]{2,1,0:T(8,128)(2,1)S(1)}, bf16[34,16,128]{2,1,0:T(8,128)(2,1)S(1)}, u32[]{:S(2)}, u32[]{:S(2)}) collective-permute-start(bf16[34,16,128]{2,1,0:T(8,128)(2,1)S(1)} %get-tuple-element.74), channel_id=1, source_target_pairs={{0,1},{1,2},{2,3},{3,4},{4,5},{5,6},{6,7},{7,8},{8,9},{9,10},{10,1... | collective-permute-start | bytes 417800 | tf_op jit(solution)/shard_map/ppermute | solution.py:769
  16.6 11.8 %collective-permute-start.4 = (bf16[34,16,128]{2,1,0:T(8,128)(2,1)S(1)}, bf16[34,16,128]{2,1,0:T(8,128)(2,1)S(1)}, u32[]{:S(2)}, u32[]{:S(2)}) collective-permute-start(bf16[34,16,128]{2,1,0:T(8,128)(2,1)S(1)} %get-tuple-element.75), channel_id=1, source_target_pairs={{0,15},{1,0},{2,1},{3,2},{4,3},{5,4},{6,5},{7,6},{8,7},{9,8},{10,9... | collective-permute-start | bytes 417800 | tf_op jit(solution)/shard_map/ppermute | solution.py:769
  29.1 8.8 %collective-permute-start.5 = (bf16[86,8,128]{2,1,0:T(8,128)(2,1)S(1)}, bf16[86,8,128]{2,1,0:T(8,128)(2,1)S(1)}, u32[]{:S(2)}, u32[]{:S(2)}) collective-permute-start(bf16[86,8,128]{2,1,0:T(8,128)(2,1)S(1)} %get-tuple-element.76.high_ref), channel_id=1, source_target_pairs={{0,16},{16,32},{32,48},{48,0},{1,17},{17,33},{33,49},{49,1},{2,18}... | collective-permute-start | bytes 528392 | tf_op jit(solution)/shard_map/ppermute | solution.py:769
  31.0 6.8 %collective-permute-start.6 = (bf16[80,8,128]{2,1,0:T(8,128)(2,1)S(1)}, bf16[80,8,128]{2,1,0:T(8,128)(2,1)S(1)}, u32[]{:S(2)}, u32[]{:S(2)}) collective-permute-start(bf16[80,8,128]{2,1,0:T(8,128)(2,1)S(1)} %get-tuple-element.77.low_ref), channel_id=1, source_target_pairs={{0,48},{16,0},{32,16},{48,32},{1,49},{17,1},{33,17},{49,33},{2,50}... | collective-permute-start | bytes 491528 | tf_op jit(solution)/shard_map/ppermute | solution.py:769
  37.9 8.5 %collective-permute-start.7 = (bf16[5,8,32,128]{3,2,1,0:T(8,128)(2,1)S(1)}, bf16[5,8,32,128]{3,2,1,0:T(8,128)(2,1)S(1)}, u32[]{:S(2)}, u32[]{:S(2)}) collective-permute-start(bf16[5,8,32,128]{3,2,1,0:T(8,128)(2,1)S(1)} %get-tuple-element.80.xh_ref), channel_id=1, source_target_pairs={{0,64},{64,128},{128,192},{192,256},{256,320},{320,384},{384,448},... | collective-permute-start | bytes 983048 | tf_op jit(solution)/shard_map/ppermute | solution.py:769
  42.5 6.5 %collective-permute-start.8 = (bf16[5,8,32,128]{3,2,1,0:T(8,128)(2,1)S(1)}, bf16[5,8,32,128]{3,2,1,0:T(8,128)(2,1)S(1)}, u32[]{:S(2)}, u32[]{:S(2)}) collective-permute-start(bf16[5,8,32,128]{3,2,1,0:T(8,128)(2,1)S(1)} %get-tuple-element.81.xl_ref), channel_id=1, source_target_pairs={{0,448},{64,0},{128,64},{192,128},{256,192},{320,256},{384,320},{4... | collective-permute-start | bytes 983048 | tf_op jit(solution)/shard_map/ppermute | solution.py:769
